TPU v7x, 256 devices: a whole 4x4x8 slice. The times are simulated.
256 devices in a mesh: grp: 8 (over z_hi, core), mem: 32 (over z_lo, x, y).
Axes of the slice: x: 4, y: 4, z: 8 (z_hi: 4, z_lo: 2; z = z_hi * 2 + z_lo), core: 2. Of those that a mesh axis runs over, the one named last changes fastest.
Arguments:
- spectra: bfloat16 [2048, 2, 16, 512], P(('grp', 'mem')), may hold values from -40 to 40
- partners: int32 [2, 32], replicated, may hold values from 0 to 7, as said below
Outputs:
- correlations: bfloat16 [2048, 2, 256, 513], P(('grp', 'mem'))
Inputs may be any that keep to these rules, and one draw needn't show every extreme that they name: For each member index k the offsets partners[r, k] of the rounds are distinct (offset 0 pairs a block with its own group).
All inputs are finite; a program needn't handle non-finite values.
Results may differ from a plain program's by a relative error of at most 0.0068.
Values may be sent and summed in bfloat16 or wider, within the bound.
No kernel may reach another device: no remote copies, remote signals or barrier semaphores. Data moves between devices by JAX's collectives and lax.ppermute only.
A program may use at most 128 MiB of HBM per device.

v0:
```python
import math

import jax
import jax.numpy as jnp
from jax import lax
from jax.sharding import PartitionSpec as P

SMOOTH = 32


def from_partner(array, axis, distance):
    return lax.ppermute(array, axis, [(i, i ^ 1 << distance) for i in range(lax.axis_size(axis))])


def whiten(spectra, half_width):
    components = spectra.astype(jnp.float32)
    power_sum = components[:, 0] * components[:, 0] + components[:, 1] * components[:, 1]
    bin_count = power_sum.shape[-1]
    positions = jnp.arange(bin_count, dtype=jnp.int32)
    band_matrix = (jnp.abs(positions[:, None] - positions[None, :]) <= half_width).astype(
        jnp.float32
    )
    smooth = jnp.dot(power_sum.reshape(-1, bin_count), band_matrix, precision=lax.Precision.HIGHEST)
    smooth = smooth.reshape(power_sum.shape) / (2 * half_width + 1)
    inv_level = lax.rsqrt(smooth + 1e-05)
    return (components * inv_level[:, None]).astype(jnp.bfloat16)


def lag_table(bin_count):
    centre = bin_count // 2
    frequency = jnp.arange(bin_count, dtype=jnp.int32)[:, None]
    lag_offset = jnp.arange(bin_count + 1, dtype=jnp.int32)[None, :] - centre
    angles = jnp.mod(frequency * lag_offset, 2 * bin_count).astype(jnp.float32) * (
        math.pi / bin_count
    )
    return jnp.stack([jnp.cos(angles), -jnp.sin(angles)], 0).astype(jnp.bfloat16)


def pair_lags(own_block, partner_block, transform):
    factor = math.sqrt(2.0 / (own_block.shape[3] * own_block.shape[2]))
    rotated = jnp.stack([own_block, jnp.stack([own_block[:, 1], -own_block[:, 0]], 1)], 0)
    cross_spectra = jnp.einsum(
        "oicsf,jcsf->ofij", rotated, partner_block, preferred_element_type=jnp.float32
    ).astype(jnp.bfloat16)
    lag_sums = jnp.einsum(
        "ofij,ofl->ijl", cross_spectra, transform, preferred_element_type=jnp.float32
    )
    return (lag_sums * factor).astype(jnp.bfloat16)


def correlate_piece(own_block, transform, received):
    return pair_lags(own_block, received, transform)


def route_shard(payload, offset, levels):
    for level in range(levels):
        swapped = from_partner(payload, "grp", level)
        payload = jnp.where(offset // 2**level % 2 == 1, swapped, payload)
    return payload


def on_device(spectra, partners):
    whitened = whiten(spectra, SMOOTH)
    transform = lag_table(spectra.shape[3])
    rounds = partners.shape[0]
    member_index = lax.axis_index("mem")
    levels = lax.axis_size("grp").bit_length() - 1
    outputs = []
    for round_index in range(rounds):
        own_offset = partners[round_index, member_index]
        source = route_shard(whitened, own_offset, levels)
        outputs.append(
            correlate_piece(whitened, transform, lax.all_gather(source, "mem", axis=0, tiled=True))
        )
    return jnp.stack(outputs, 1)


def solution(mesh):
    placed = (P(("grp", "mem"), None, None, None), P())
    return jax.shard_map(
        on_device,
        mesh=mesh,
        in_specs=placed,
        out_specs=P(("grp", "mem"), None, None, None),
        check_vma=False,
    )
```

profile of v0, /device:TPU:8, one launch (start us, length us, event | category | flops | bytes accessed | tf_op | source)
XLA Modules:
  0.0 450.0 jit_solution(15983893650686171145)
XLA Ops:
  6.5 0.0 all-gather.3.cloned.1.call-start
  6.5 1.0 convert_element_type.42
  7.5 0.0 copy-start
  7.6 0.4 fusion.15
  8.0 1.0 multiply_convert_fusion
  9.0 0.1 collective-permute-start
  9.1 1.3 constant_dynamic-slice_fusion.1
  14.1 0.0 collective-permute-done
  14.2 1.1 broadcast_select_fusion.3
  15.2 3.4 collective-permute-start.1
  19.3 11.9 %collective-permute-done.1 = bf16[8,2,16,512]{3,2,1,0:T(8,128)(2,1)S(1)} collective-permute-done((bf16[8,2,16,512]{3,2,1,0:T(8,128)(2,1)S(1)}, bf16[8,2,16,512]{3,2,1,0:T(8,128)(2,1)S(1)}, u32[]{:S(2)}, u32[]{:S(2)}) %collective-permute-start.1) | collective-permute-done | bytes 262176 | tf_op jit(solution)/shard_map/ppermute | solution.py:12
  31.2 6.6 %collective-permute-start.2 = (bf16[8,2,16,512]{3,2,1,0:T(8,128)(2,1)S(1)}, bf16[8,2,16,512]{3,2,1,0:T(8,128)(2,1)S(1)}, u32[]{:S(2)}, u32[]{:S(2)}) collective-permute-start(bf16[8,2,16,512]{3,2,1,0:T(8,128)(2,1)S(1)} %broadcast_select_fusion.4), channel_id=1, source_target_pairs={{0,128},{32,160},{64,192},{96,224},{128,0},{160,32},{192,64},{224,... | collective-permute-start | bytes 786440 | tf_op jit(solution)/shard_map/ppermute | solution.py:12
  37.9 11.9 %collective-permute-done.2 = bf16[8,2,16,512]{3,2,1,0:T(8,128)(2,1)S(1)} collective-permute-done((bf16[8,2,16,512]{3,2,1,0:T(8,128)(2,1)S(1)}, bf16[8,2,16,512]{3,2,1,0:T(8,128)(2,1)S(1)}, u32[]{:S(2)}, u32[]{:S(2)}) %collective-permute-start.2) | collective-permute-done | bytes 262176 | tf_op jit(solution)/shard_map/ppermute | solution.py:12
  49.7 0.7 broadcast_select_fusion.5
  50.4 0.0 all-gather.3.cloned.1.call-update
  50.5 0.0 all-gather.5.cloned.1.call-start
  50.5 0.1 collective-permute-start.3
  51.2 10.8 %collective-permute-done.3 = bf16[8,2,16,512]{3,2,1,0:T(8,128)(2,1)S(1)} collective-permute-done((bf16[8,2,16,512]{3,2,1,0:T(8,128)(2,1)S(1)}, bf16[8,2,16,512]{3,2,1,0:T(8,128)(2,1)S(1)}, u32[]{:S(2)}, u32[]{:S(2)}) %collective-permute-start.3) | collective-permute-done | bytes 262176 | tf_op jit(solution)/shard_map/ppermute | solution.py:12
  62.1 5.1 %collective-permute-start.4 = (bf16[8,2,16,512]{3,2,1,0:T(8,128)(2,1)S(1)}, bf16[8,2,16,512]{3,2,1,0:T(8,128)(2,1)S(1)}, u32[]{:S(2)}, u32[]{:S(2)}) collective-permute-start(bf16[8,2,16,512]{3,2,1,0:T(8,128)(2,1)S(1)} %broadcast_select_fusion.1), channel_id=1, source_target_pairs={{0,128},{32,160},{64,192},{96,224},{128,0},{160,32},{192,64},{224,... | collective-permute-start | bytes 786440 | tf_op jit(solution)/shard_map/ppermute | solution.py:12
  67.2 11.3 %collective-permute-done.4 = bf16[8,2,16,512]{3,2,1,0:T(8,128)(2,1)S(1)} collective-permute-done((bf16[8,2,16,512]{3,2,1,0:T(8,128)(2,1)S(1)}, bf16[8,2,16,512]{3,2,1,0:T(8,128)(2,1)S(1)}, u32[]{:S(2)}, u32[]{:S(2)}) %collective-permute-start.4) | collective-permute-done | bytes 262176 | tf_op jit(solution)/shard_map/ppermute | solution.py:12
  78.5 0.7 broadcast_select_fusion.2
  79.2 0.0 all-gather.5.cloned.1.call-update
  79.3 0.0 copy-done
  79.3 0.1 fusion.38
  79.4 0.1 pad_maximum_fusion.1
  79.4 6.4 %copy.6 = bf16[2,8,2,16,512]{3,1,2,0,4:T(8,128)(2,1)} copy(bf16[2,8,2,16,512]{4,3,2,1,0:T(8,128)(2,1)S(1)} %pad_maximum_fusion.1) | data formatting | bytes 1048576 | tf_op jit(solution)/shard_map/stack | solution.py:41
  85.9 4.7 %cosine_convert_fusion = (bf16[1,512,513]{1,2,0:T(8,128)(2,1)S(1)}, bf16[1,512,513]{1,2,0:T(8,128)(2,1)S(1)}) fusion(s32[513]{0:T(1024)S(1)} %iota_add_fusion), kind=kLoop, calls=%fused_computation.24 | loop fusion | flops 4465152 | bytes 1052676 | tf_op jit(solution)/shard_map/convert
  90.6 132.0 %all-gather.3.cloned.1.call-done = bf16[256,2,16,512]{3,2,1,0:T(8,128)(2,1)} async-done(((bf16[8,2,16,512]{3,2,1,0:T(8,128)(2,1)}), bf16[256,2,16,512]{3,2,1,0:T(8,128)(2,1)}) %all-gather.3.cloned.1.call-update) | async-done | bytes 8388624 | tf_op jit(solution)/shard_map/all_gather | solution.py:73
  222.6 15.9 %copy.5 = bf16[256,2,16,512,1]{0,2,1,4,3:T(8,128)(2,1)} copy(bf16[256,2,16,512,1]{3,2,1,0,4:T(8,128)(2,1)} %bitcast.64) | data formatting | bytes 16777216 | tf_op jit(solution)/shard_map/all_gather | solution.py:73
  238.6 158.3 %all-gather.5.cloned.1.call-done = bf16[256,2,16,512]{3,2,1,0:T(8,128)(2,1)} async-done(((bf16[8,2,16,512]{3,2,1,0:T(8,128)(2,1)}), bf16[256,2,16,512]{3,2,1,0:T(8,128)(2,1)}) %all-gather.5.cloned.1.call-update) | async-done | bytes 8388624 | tf_op jit(solution)/shard_map/all_gather | solution.py:73
  396.9 16.0 %copy.9 = bf16[256,2,16,512,1]{0,2,1,4,3:T(8,128)(2,1)} copy(bf16[256,2,16,512,1]{3,2,1,0,4:T(8,128)(2,1)} %bitcast.65) | data formatting | bytes 16777216 | tf_op jit(solution)/shard_map/all_gather | solution.py:73
  412.9 8.0 %fusion.32 = bf16[512,256,2,8,1]{1,3,4,2,0:T(8,128)(2,1)} fusion(bf16[256,2,16,512,1]{0,2,1,4,3:T(8,128)(2,1)} %copy.5, bf16[2,8,2,16,512]{3,1,2,0,4:T(8,128)(2,1)} %copy.6), kind=kOutput, calls=%fused_computation.52 | convolution fusion | flops 134217728 | bytes 13107200 | tf_op jit(solution)/shard_map/oicsf,jcsf->ofij/dot_general | solution.py:42
  420.8 7.9 %fusion.33 = bf16[512,256,2,8,1]{1,3,4,2,0:T(8,128)(2,1)} fusion(bf16[256,2,16,512,1]{0,2,1,4,3:T(8,128)(2,1)} %copy.9, bf16[2,8,2,16,512]{3,1,2,0,4:T(8,128)(2,1)} %copy.6), kind=kOutput, calls=%fused_computation.53 | convolution fusion | flops 134217728 | bytes 13107200 | tf_op jit(solution)/shard_map/oicsf,jcsf->ofij/dot_general | solution.py:42
  428.8 0.0 copy-start.1
  428.8 5.0 %fusion.8 = bf16[8,1,256,513]{2,3,0,1:T(8,128)(2,1)S(1)} fusion(bf16[512,256,2,8,1]{1,3,4,2,0:T(8,128)(2,1)} %fusion.32, bf16[1,512,513]{1,2,0:T(8,128)(2,1)S(1)} %get-tuple-element.10, bf16[1,512,513]{1,2,0:T(8,128)(2,1)S(1)} %get-tuple-element.9), kind=kOutput, calls=%fused_computation.11 | convolution fusion | flops 2154304512 | bytes 7346176 | tf_op jit(solution)/shard_map/ofij,ofl->ijl/dot_general | solution.py:45
  433.7 0.0 copy-done.1
  433.8 2.7 fusion.9
  436.5 0.4 pad_maximum_fusion
  436.8 6.3 %copy.4 = bf16[8,2,256,513]{2,1,3,0:T(2,128)(2,1)} copy(bf16[8,2,256,513]{2,3,0,1:T(8,128)(2,1)S(1)} %pad_maximum_fusion) | data formatting | bytes 8404992 | tf_op jit(solution)/shard_map/stack | solution.py:75
  (5 shorter events, 0.1 us)
Async XLA Ops:
  6.5 216.1 %all-gather.3.cloned.1.call-start = ((), (), s32[]{:S(2)}) async-start(), calls=%async_computation | async-start | bytes 8650752 | tf_op jit(solution)/shard_map/all_gather | solution.py:73
  7.5 71.8 %copy-start = (bf16[8,2,16,512]{3,2,1,0:T(8,128)(2,1)S(1)}, bf16[8,2,16,512]{3,2,1,0:T(8,128)(2,1)}, u32[]{:S(2)}) copy-start(bf16[8,2,16,512]{3,2,1,0:T(8,128)(2,1)} %param.2) | copy-start | bytes 786436
  9.0 5.1 %collective-permute-start = (bf16[8,2,16,512]{3,2,1,0:T(8,128)(2,1)S(1)}, bf16[8,2,16,512]{3,2,1,0:T(8,128)(2,1)S(1)}, u32[]{:S(2)}, u32[]{:S(2)}) collective-permute-start(bf16[8,2,16,512]{3,2,1,0:T(8,128)(2,1)S(1)} %multiply_convert_fusion), channel_id=1, source_target_pairs={{0,32},{32,0},{64,96},{96,64},{128,160},{160,128},{192,224},{224,1... | collective-permute-start | bytes 786440 | tf_op jit(solution)/shard_map/ppermute | solution.py:12
  15.2 15.9 %collective-permute-start.1 = (bf16[8,2,16,512]{3,2,1,0:T(8,128)(2,1)S(1)}, bf16[8,2,16,512]{3,2,1,0:T(8,128)(2,1)S(1)}, u32[]{:S(2)}, u32[]{:S(2)}) collective-permute-start(bf16[8,2,16,512]{3,2,1,0:T(8,128)(2,1)S(1)} %get-tuple-element.5), channel_id=1, source_target_pairs={{0,64},{32,96},{64,0},{96,32},{128,192},{160,224},{192,128},{224,1... | collective-permute-start | bytes 786440 | tf_op jit(solution)/shard_map/ppermute | solution.py:12
  31.2 18.5 %collective-permute-start.2 = (bf16[8,2,16,512]{3,2,1,0:T(8,128)(2,1)S(1)}, bf16[8,2,16,512]{3,2,1,0:T(8,128)(2,1)S(1)}, u32[]{:S(2)}, u32[]{:S(2)}) collective-permute-start(bf16[8,2,16,512]{3,2,1,0:T(8,128)(2,1)S(1)} %broadcast_select_fusion.4), channel_id=1, source_target_pairs={{0,128},{32,160},{64,192},{96,224},{128,0},{160,32},{192,64},{224,... | collective-permute-start | bytes 786440 | tf_op jit(solution)/shard_map/ppermute | solution.py:12
  50.5 346.4 %all-gather.5.cloned.1.call-start = ((), (), s32[]{:S(2)}) async-start(), calls=%async_computation.1 | async-start | bytes 8650752 | tf_op jit(solution)/shard_map/all_gather | solution.py:73
  50.5 11.5 %collective-permute-start.3 = (bf16[8,2,16,512]{3,2,1,0:T(8,128)(2,1)S(1)}, bf16[8,2,16,512]{3,2,1,0:T(8,128)(2,1)S(1)}, u32[]{:S(2)}, u32[]{:S(2)}) collective-permute-start(bf16[8,2,16,512]{3,2,1,0:T(8,128)(2,1)S(1)} %get-tuple-element.6), channel_id=1, source_target_pairs={{0,64},{32,96},{64,0},{96,32},{128,192},{160,224},{192,128},{224,1... | collective-permute-start | bytes 786440 | tf_op jit(solution)/shard_map/ppermute | solution.py:12
  62.1 16.4 %collective-permute-start.4 = (bf16[8,2,16,512]{3,2,1,0:T(8,128)(2,1)S(1)}, bf16[8,2,16,512]{3,2,1,0:T(8,128)(2,1)S(1)}, u32[]{:S(2)}, u32[]{:S(2)}) collective-permute-start(bf16[8,2,16,512]{3,2,1,0:T(8,128)(2,1)S(1)} %broadcast_select_fusion.1), channel_id=1, source_target_pairs={{0,128},{32,160},{64,192},{96,224},{128,0},{160,32},{192,64},{224,... | collective-permute-start | bytes 786440 | tf_op jit(solution)/shard_map/ppermute | solution.py:12
  428.8 5.0 %copy-start.1 = (bf16[512,256,2,8,1]{1,3,4,2,0:T(8,128)(2,1)S(1)}, bf16[512,256,2,8,1]{1,3,4,2,0:T(8,128)(2,1)}, u32[]{:S(2)}) copy-start(bf16[512,256,2,8,1]{1,3,4,2,0:T(8,128)(2,1)} %fusion.33) | copy-start | bytes 12582916
Sparse Core Ops, SparseCore 0:
  50.6 171.9 all-gather.2
  224.4 172.4 all-gather.4
where the time goes:
time: 451 us; the launch traced here: 450 us
  waiting for transfers between devices  336 us (75%)
  local copies, waits for them, and re-layouts  46 us (10%)
  matrix products  24 us (5%)
  between operations  18.5 us (4%)
  starting transfers between devices  15.3 us (3%)
  other arithmetic  9.86 us (2%)
    all_gather x2, waiting for transfers between devices, on_device(): lax.all_gather(source, 'mem', axis=0, tiled=True)  290 us
    ppermute x5, waiting for transfers between devices, from_partner(): lax.ppermute(array, axis, [(i, i ^ 1 << distance) for i in range(lax.axis...  45.9 us
    all_gather x2, local copies, waits for them, and re-layouts, on_device(): lax.all_gather(source, 'mem', axis=0, tiled=True)  31.9 us
    dot_general x2, matrix products, pair_lags(): jnp.einsum('oicsf,jcsf->ofij', rotated, partner_block, preferred_element_...  15.9 us
    ppermute x5, starting transfers between devices, from_partner(): lax.ppermute(array, axis, [(i, i ^ 1 << distance) for i in range(lax.axis...  15.3 us
  transfers between devices with their start and end apart: 7, of which 6 were waited for; matrix products, arithmetic and copies ran while one was open for 7% of the time, Pallas kernels for 0%

commit v1 on v0

v1 whole, which is shorter than its diff:
```python
import math

import jax
import jax.numpy as jnp
from jax import lax
from jax.experimental import pallas as pl
from jax.experimental.pallas import tpu as pltpu
from jax.sharding import PartitionSpec as P

SMOOTH = 32
CH = 8
COMP = 32
BINS = 512
LANE = 128
TAPS = BINS // LANE
LAGS = BINS + 1
LAG_ROWS = 520
PARAMS = pltpu.CompilerParams(vmem_limit_bytes=56 * 1024 * 1024)


def xor_perm(array, axis, mask):
    return lax.ppermute(array, axis, [(i, i ^ mask) for i in range(lax.axis_size(axis))])


def whiten_kernel(spectra_ref, out_ref, rows):
    comps = spectra_ref[...].astype(jnp.float32)
    power = (comps[:, 0] * comps[:, 0] + comps[:, 1] * comps[:, 1]).reshape(-1, BINS)
    row = lax.broadcasted_iota(jnp.int32, (BINS, BINS), 0)
    col = lax.broadcasted_iota(jnp.int32, (BINS, BINS), 1)
    band = (jnp.abs(row - col) <= SMOOTH).astype(jnp.float32)
    smooth = jnp.dot(
        power, band, precision=lax.Precision.HIGHEST, preferred_element_type=jnp.float32
    )
    inv = lax.rsqrt(smooth / (2 * SMOOTH + 1) + 1e-05)
    segs = COMP // 2
    for ch in range(CH):
        level = inv[ch * segs : (ch + 1) * segs]
        white = jnp.concatenate([comps[ch, 0] * level, comps[ch, 1] * level], 0)
        taps = jnp.concatenate([white[:, k * LANE : (k + 1) * LANE] for k in range(TAPS)], 0)
        rows[pl.ds(ch, LANE, stride=CH), :] = taps.T
    out_ref[...] = rows[...].reshape(LANE, CH, LANE).astype(jnp.bfloat16)


def whiten(spectra):
    return pl.pallas_call(
        whiten_kernel,
        out_shape=jax.ShapeDtypeStruct((LANE, CH, LANE), jnp.bfloat16),
        scratch_shapes=[pltpu.VMEM((LANE * CH, LANE), jnp.float32)],
        compiler_params=PARAMS,
        name="whiten",
    )(spectra)


def corr_kernel(factor, *refs):
    row_refs, col_refs, table_ref = refs[:4], refs[4:12], refs[12]
    out_refs, rows, cross = refs[13:17], refs[17], refs[18]
    lane = lax.broadcasted_iota(jnp.int32, (CH * LANE, LANE), 1)
    imag = lane // 16 % 2 == 1
    for d in range(4):
        own = row_refs[d][...].astype(jnp.float32).reshape(CH * LANE, LANE)
        rows[pl.ds(d * 1024, 1024), :] = own
        rows[pl.ds(4096 + d * 1024, 1024), :] = jnp.where(
            imag, -pltpu.roll(own, 16, 1), pltpu.roll(own, LANE - 16, 1)
        )
    sub = lax.broadcasted_iota(jnp.int32, (8, LANE), 0)
    tap = lax.broadcasted_iota(jnp.int32, (8, LANE), 1) // COMP
    pick_re = sub == tap
    pick_im = sub - TAPS == tap
    blank = jnp.zeros((64, LANE), jnp.bfloat16)

    def step(g, carry):
        cols = jnp.concatenate([c[g].astype(jnp.float32) for c in col_refs], 0).astype(jnp.bfloat16)
        rhs = jnp.concatenate(
            [jnp.concatenate([cols, blank], 1), jnp.concatenate([blank, cols], 1)], 0
        )
        pairs = []
        for pair in range(16):
            halves = []
            for half in range(2):
                i = 2 * pair + half
                at = (i // 8) * 1024 + g * 8 + i % 8
                re = jnp.broadcast_to(rows[pl.ds(at, 1), :], (8, LANE))
                im = jnp.broadcast_to(rows[pl.ds(4096 + at, 1), :], (8, LANE))
                halves.append(jnp.where(pick_re, re, jnp.where(pick_im, im, 0.0)))
            pairs.append(jnp.concatenate(halves, 1))
        lhs = jnp.concatenate(pairs, 0).astype(jnp.bfloat16)
        prod = lax.dot_general(
            lhs, rhs, (((1,), (1,)), ((), ())), preferred_element_type=jnp.float32
        )
        at = pl.multiple_of(g * 8, 8)
        for pair in range(16):
            cross[pair, pl.ds(at, 8), :] = prod[pair * 8 : pair * 8 + 8]
        return carry

    lax.fori_loop(0, LANE, step, 0)
    table = table_ref[...]
    for d in range(4):
        for quad in range(2):
            pair = d * 4 + quad * 2
            weights = jnp.concatenate([cross[pair], cross[pair + 1]], 1).astype(jnp.bfloat16)
            lags = jnp.dot(table, weights, preferred_element_type=jnp.float32)
            out_refs[d][quad] = (lags * factor).astype(jnp.bfloat16)


def correlate(row_blocks, col_blocks, table, factor):
    def body(*refs):
        corr_kernel(factor, *refs)

    return pl.pallas_call(
        body,
        out_shape=[jax.ShapeDtypeStruct((2, LAG_ROWS, 256), jnp.bfloat16)] * 4,
        scratch_shapes=[
            pltpu.VMEM((8 * 1024, LANE), jnp.float32),
            pltpu.VMEM((16, 1024, LANE), jnp.float32),
        ],
        compiler_params=PARAMS,
        name="correlate",
    )(*row_blocks, *col_blocks, table)


def finish_kernel(*refs):
    parts, order_ref, out_ref, buf = refs[:8], refs[8], refs[9], refs[10]
    for i2 in range(4):
        for half in range(2):
            i = i2 * 2 + half
            quad, at = i // 4, (i // 2) % 2 * LANE
            for r in range(2):
                wide = jnp.concatenate(
                    [parts[r * 4 + d][quad, :, at : at + LANE] for d in range(4)], 1
                )
                ordered = jnp.dot(wide, order_ref[r, half], preferred_element_type=jnp.float32)
                for tile in range(2):
                    buf[pl.ds(half * 4 * LAGS + tile * 2 + r, LAGS, stride=4), :] = ordered[
                        :LAGS, tile * LANE : (tile + 1) * LANE
                    ]
        out_ref[i2] = buf[...].astype(jnp.bfloat16)


def finish(parts, order):
    return pl.pallas_call(
        finish_kernel,
        out_shape=jax.ShapeDtypeStruct((4, 8 * LAGS, LANE), jnp.bfloat16),
        scratch_shapes=[pltpu.VMEM((8 * LAGS, LANE), jnp.float32)],
        compiler_params=PARAMS,
        name="finish",
    )(*parts, order)


def lag_table():
    lag = jnp.arange(LAG_ROWS, dtype=jnp.int32)[:, None]
    k = jnp.arange(2 * BINS, dtype=jnp.int32)[None, :]
    frequency = k % TAPS * LANE + k // 8
    angles = jnp.mod(frequency * (lag - BINS // 2), 2 * BINS).astype(jnp.float32) * (math.pi / BINS)
    values = jnp.where(k // TAPS % 2 == 0, jnp.cos(angles), -jnp.sin(angles))
    return jnp.where(lag < LAGS, values, 0.0).astype(jnp.bfloat16)


def column_order(member):
    z, x, y = member // 16, member // 4 % 4, member % 4
    at = jnp.arange(512, dtype=jnp.int32)
    d, half, block, ch = at // 128, at // 64 % 2, at // 8 % 8, at % 8
    ez, e = block // 4, block % 4
    first = (z ^ ez) * 128 + (x ^ d) * 32 + (y ^ e) * 8 + ch
    second = (z ^ ez) * 128 + (x ^ e) * 32 + (y ^ d) * 8 + ch
    target = jnp.stack([first, second], 0)[:, None, :, None]
    column = jnp.arange(256, dtype=jnp.int32)[None, None, None, :]
    side = jnp.arange(2, dtype=jnp.int32)[None, :, None, None]
    return ((target == column) & (half[None, None, :, None] == side)).astype(jnp.bfloat16)


def on_device(spectra, partners):
    member = lax.axis_index("mem").astype(jnp.int32)
    white = whiten(spectra)
    planes = [white] + [xor_perm(white, "grp", 2 * d) for d in range(1, 4)]
    row_masks, col_masks = (4, 1), (1, 4)
    rows = [[white] + [xor_perm(white, "mem", d * m) for d in range(1, 4)] for m in row_masks]
    table = lag_table()
    order = column_order(member)
    factor = math.sqrt(2.0 / (BINS * (COMP // 2)))
    cols = []
    for r in range(2):
        offset = partners[r, member]
        plane = offset >> 1
        mine = jnp.where(
            plane == 0,
            planes[0],
            jnp.where(plane == 1, planes[1], jnp.where(plane == 2, planes[2], planes[3])),
        )
        other = xor_perm(mine, "grp", 1)
        block = jnp.where((offset & 1) == 1, other, mine)
        far = xor_perm(block, "mem", 16)
        cols.append(
            [block]
            + [xor_perm(block, "mem", e * col_masks[r]) for e in range(1, 4)]
            + [far]
            + [xor_perm(far, "mem", e * col_masks[r]) for e in range(1, 4)]
        )
    parts = []
    for r in range(2):
        sums = correlate(rows[r], cols[r], table, factor)
        parts += [sums[0]] + [xor_perm(sums[d], "mem", d * row_masks[r]) for d in range(1, 4)]
    packed = finish(parts, order)
    result = packed.reshape(CH, LAGS, 2, 2, LANE)
    return jnp.transpose(result, (0, 3, 2, 4, 1)).reshape(CH, 2, 256, LAGS)


def solution(mesh):
    placed = (P(("grp", "mem"), None, None, None), P())
    return jax.shard_map(
        on_device,
        mesh=mesh,
        in_specs=placed,
        out_specs=P(("grp", "mem"), None, None, None),
        check_vma=False,
    )
```

time: 451 us -> 214 us (0.47)
  waiting for transfers between devices: 336 us -> 79.1 us
  Pallas kernels: 0 us -> 65.1 us
  local copies, waits for them, and re-layouts: 46 us -> 3.62 us
  starting transfers between devices: 15.3 us -> 50.9 us
  matrix products: 24 us -> 0 us
  between operations: 18.5 us -> 2.92 us
    all_gather x2 -> x0, waiting for transfers between devices: 290 us -> none  [on_device(): lax.all_gather(source, 'mem', axis=0, tiled=True)]
    pallas_call x0 -> x4, Pallas kernels: none -> 65.1 us  [the longest x2 55.2 us: correlate(): pl.pallas_call(body, out_shape=[jax.ShapeDtypeStruct((2, LAG_ROWS, 256),...]
    ppermute x5 -> x31, starting transfers between devices: 15.3 us -> 50.9 us  [xor_perm(): lax.ppermute(array, axis, [(i, i ^ mask) for i in range(lax.axis_size(axi...]
    ppermute x5 -> x31, waiting for transfers between devices: 45.9 us -> 79.1 us  [xor_perm(): lax.ppermute(array, axis, [(i, i ^ mask) for i in range(lax.axis_size(axi...]
    all_gather x2 -> x0, local copies, waits for them, and re-layouts: 31.9 us -> none  [on_device(): lax.all_gather(source, 'mem', axis=0, tiled=True)]
    dot_general x5 -> x0, matrix products: 24 us -> none  [the longest x2 15.9 us: pair_lags(): jnp.einsum('oicsf,jcsf->ofij', rotated, partner_block, preferred_element_...]
    another operation x2 -> x0, local copies, waits for them, and re-layouts: 12.8 us -> none  [the longest x1 6.44 us: pair_lags(): jnp.stack([own_block, jnp.stack([own_block[:, 1], -own_block[:, 0]], 1)], 0)]
    convert_element_type x2, other arithmetic: 2 us -> 11 us  [the longest x1 9.8 us: lag_table(): return jnp.where(lag < LAGS, values, 0.0).astype(jnp.bfloat16)]
  transfers between devices with their start and end apart: 7 -> 31, of which waited for: 6 -> 15; matrix products, arithmetic and copies ran while one was open for 7% -> 6% of each run, Pallas kernels for 0% -> 26%
where the time goes in v1:
time: 214 us
  waiting for transfers between devices  79.1 us (37%)
  Pallas kernels  65.1 us (30%)
  starting transfers between devices  50.9 us (24%)
  other arithmetic  12.4 us (6%)
  local copies, waits for them, and re-layouts  3.62 us (2%)
  between operations  2.92 us (1%)
    ppermute x31, waiting for transfers between devices, xor_perm(): lax.ppermute(array, axis, [(i, i ^ mask) for i in range(lax.axis_size(axi...  79.1 us
    pallas_call x2, Pallas kernels, correlate(): pl.pallas_call(body, out_shape=[jax.ShapeDtypeStruct((2, LAG_ROWS, 256),...  55.2 us
    ppermute x31, starting transfers between devices, xor_perm(): lax.ppermute(array, axis, [(i, i ^ mask) for i in range(lax.axis_size(axi...  50.9 us
    convert_element_type x1, other arithmetic, lag_table(): return jnp.where(lag < LAGS, values, 0.0).astype(jnp.bfloat16)  9.8 us
    pallas_call x1, Pallas kernels, finish(): pl.pallas_call(finish_kernel, out_shape=jax.ShapeDtypeStruct((4, 8 * LAGS...  7.38 us
  transfers between devices with their start and end apart: 31, of which 15 were waited for; matrix products, arithmetic and copies ran while one was open for 6% of the time, Pallas kernels for 26%

profile of v1, /device:TPU:8, one launch (start us, length us, event | category | flops | bytes accessed | tf_op | source)
XLA Modules:
  0.0 214.0 jit_solution(1371588322956363638)
XLA Ops:
  0.0 2.5 %whiten.1.refs_0_ = bf16[128,8,128]{2,1,0:T(8,128)(2,1)} custom-call(bf16[8,2,16,512]{3,2,1,0:T(8,128)(2,1)} %spectra_ref.1), custom_call_target="tpu_custom_call" | custom-call | tf_op jit(solution)/shard_map/whiten/pallas_call | solution.py:45
  2.5 3.3 %collective-permute-start.3 = (bf16[128,8,128]{2,1,0:T(8,128)(2,1)}, bf16[128,8,128]{2,1,0:T(8,128)(2,1)S(1)}, u32[]{:S(2)}, u32[]{:S(2)}) collective-permute-start(bf16[128,8,128]{2,1,0:T(8,128)(2,1)} %whiten.1.refs_0_), channel_id=1, source_target_pairs={{0,64},{32,96},{64,0},{96,32},{128,192},{160,224},{192,128},{224,1... | collective-permute-start | bytes 786440 | tf_op jit(solution)/shard_map/ppermute | solution.py:22
  5.8 5.4 %collective-permute-start.4 = (bf16[128,8,128]{2,1,0:T(8,128)(2,1)}, bf16[128,8,128]{2,1,0:T(8,128)(2,1)S(1)}, u32[]{:S(2)}, u32[]{:S(2)}) collective-permute-start(bf16[128,8,128]{2,1,0:T(8,128)(2,1)} %whiten.1.refs_0_), channel_id=1, source_target_pairs={{0,128},{32,160},{64,192},{96,224},{128,0},{160,32},{192,64},{224,... | collective-permute-start | bytes 786440 | tf_op jit(solution)/shard_map/ppermute | solution.py:22
  11.2 0.0 collective-permute-start.5
  11.2 1.4 constant_dynamic-slice_fusion
  13.8 15.4 %collective-permute-done.3 = bf16[128,8,128]{2,1,0:T(8,128)(2,1)S(1)} collective-permute-done((bf16[128,8,128]{2,1,0:T(8,128)(2,1)}, bf16[128,8,128]{2,1,0:T(8,128)(2,1)S(1)}, u32[]{:S(2)}, u32[]{:S(2)}) %collective-permute-start.3) | collective-permute-done | bytes 262176 | tf_op jit(solution)/shard_map/ppermute | solution.py:22
  29.2 5.1 %collective-permute-done.4 = bf16[128,8,128]{2,1,0:T(8,128)(2,1)S(1)} collective-permute-done((bf16[128,8,128]{2,1,0:T(8,128)(2,1)}, bf16[128,8,128]{2,1,0:T(8,128)(2,1)S(1)}, u32[]{:S(2)}, u32[]{:S(2)}) %collective-permute-start.4) | collective-permute-done | bytes 262176 | tf_op jit(solution)/shard_map/ppermute | solution.py:22
  34.3 1.0 select_select_fusion
  35.3 0.1 collective-permute-start.20
  35.4 0.5 collective-permute-start.17
  35.9 2.6 %collective-permute-start.18 = (bf16[128,8,128]{2,1,0:T(8,128)(2,1)}, bf16[128,8,128]{2,1,0:T(8,128)(2,1)S(1)}, u32[]{:S(2)}, u32[]{:S(2)}) collective-permute-start(bf16[128,8,128]{2,1,0:T(8,128)(2,1)} %whiten.1.refs_0_), channel_id=1, source_target_pairs={{0,2},{1,3},{2,0},{3,1},{4,6},{5,7},{6,4},{7,5},{8,10},{9,11},{10,... | collective-permute-start | bytes 786440 | tf_op jit(solution)/shard_map/ppermute | solution.py:22
  38.5 0.4 collective-permute-start.19
  39.0 1.5 collective-permute-start
  41.1 0.0 collective-permute-done.20
  41.1 0.1 collective-permute-start.6
  41.3 3.5 %collective-permute-done.17.refs_1_ = bf16[128,8,128]{2,1,0:T(8,128)(2,1)S(1)} collective-permute-done((bf16[128,8,128]{2,1,0:T(8,128)(2,1)}, bf16[128,8,128]{2,1,0:T(8,128)(2,1)S(1)}, u32[]{:S(2)}, u32[]{:S(2)}) %collective-permute-start.17) | collective-permute-done | bytes 262176 | tf_op jit(solution)/shard_map/ppermute | solution.py:22
  44.8 0.9 collective-permute-start.24
  45.7 5.4 %collective-permute-done.18.refs_2_ = bf16[128,8,128]{2,1,0:T(8,128)(2,1)S(1)} collective-permute-done((bf16[128,8,128]{2,1,0:T(8,128)(2,1)}, bf16[128,8,128]{2,1,0:T(8,128)(2,1)S(1)}, u32[]{:S(2)}, u32[]{:S(2)}) %collective-permute-start.18) | collective-permute-done | bytes 262176 | tf_op jit(solution)/shard_map/ppermute | solution.py:22
  51.1 1.5 collective-permute-start.21
  52.6 0.0 collective-permute-done.19.refs_3_
  52.6 2.9 %collective-permute-start.22 = (bf16[128,8,128]{2,1,0:T(8,128)(2,1)S(1)}, bf16[128,8,128]{2,1,0:T(8,128)(2,1)S(1)}, u32[]{:S(2)}, u32[]{:S(2)}) collective-permute-start(bf16[128,8,128]{2,1,0:T(8,128)(2,1)S(1)} %broadcast_select_fusion.refs_4_), channel_id=1, source_target_pairs={{0,8},{1,9},{2,10},{3,11},{4,12},{5,13},{6,14},{7,15},{8,0},{9,1},... | collective-permute-start | bytes 786440 | tf_op jit(solution)/shard_map/ppermute | solution.py:22
  55.5 0.0 collective-permute-done.refs_1_
  55.5 1.1 collective-permute-start.23
  56.6 0.0 collective-permute-done.24.refs_8_
  56.6 0.0 collective-permute-done.6
  56.6 3.5 %collective-permute-start.26 = (bf16[128,8,128]{2,1,0:T(8,128)(2,1)S(1)}, bf16[128,8,128]{2,1,0:T(8,128)(2,1)S(1)}, u32[]{:S(2)}, u32[]{:S(2)}) collective-permute-start(bf16[128,8,128]{2,1,0:T(8,128)(2,1)S(1)} %collective-permute-done.24.refs_8_), channel_id=1, source_target_pairs={{0,8},{1,9},{2,10},{3,11},{4,12},{5,13},{6,14},{7,15},{8,0},{9,1},... | collective-permute-start | bytes 786440 | tf_op jit(solution)/shard_map/ppermute | solution.py:22
  60.2 0.1 collective-permute-done.21.refs_5_
  60.3 2.8 %collective-permute-start.27 = (bf16[128,8,128]{2,1,0:T(8,128)(2,1)S(1)}, bf16[128,8,128]{2,1,0:T(8,128)(2,1)S(1)}, u32[]{:S(2)}, u32[]{:S(2)}) collective-permute-start(bf16[128,8,128]{2,1,0:T(8,128)(2,1)S(1)} %collective-permute-done.24.refs_8_), channel_id=1, source_target_pairs={{0,12},{1,13},{2,14},{3,15},{4,8},{5,9},{6,10},{7,11},{8,4},{9,5},... | collective-permute-start | bytes 786440 | tf_op jit(solution)/shard_map/ppermute | solution.py:22
  63.8 4.4 %collective-permute-done.22.refs_6_ = bf16[128,8,128]{2,1,0:T(8,128)(2,1)S(1)} collective-permute-done((bf16[128,8,128]{2,1,0:T(8,128)(2,1)S(1)}, bf16[128,8,128]{2,1,0:T(8,128)(2,1)S(1)}, u32[]{:S(2)}, u32[]{:S(2)}) %collective-permute-start.22) | collective-permute-done | bytes 262176 | tf_op jit(solution)/shard_map/ppermute | solution.py:22
  68.2 0.8 collective-permute-start.1
  69.0 2.6 %collective-permute-done.23.refs_7_ = bf16[128,8,128]{2,1,0:T(8,128)(2,1)S(1)} collective-permute-done((bf16[128,8,128]{2,1,0:T(8,128)(2,1)S(1)}, bf16[128,8,128]{2,1,0:T(8,128)(2,1)S(1)}, u32[]{:S(2)}, u32[]{:S(2)}) %collective-permute-start.23) | collective-permute-done | bytes 262176 | tf_op jit(solution)/shard_map/ppermute | solution.py:22
  71.6 1.1 collective-permute-start.2
  72.7 0.9 collective-permute-start.10
  73.6 5.9 %collective-permute-done.26.refs_10_ = bf16[128,8,128]{2,1,0:T(8,128)(2,1)S(1)} collective-permute-done((bf16[128,8,128]{2,1,0:T(8,128)(2,1)S(1)}, bf16[128,8,128]{2,1,0:T(8,128)(2,1)S(1)}, u32[]{:S(2)}, u32[]{:S(2)}) %collective-permute-start.26) | collective-permute-done | bytes 262176 | tf_op jit(solution)/shard_map/ppermute | solution.py:22
  79.5 1.9 collective-permute-start.7
  81.4 6.7 %collective-permute-done.27.refs_11_ = bf16[128,8,128]{2,1,0:T(8,128)(2,1)S(1)} collective-permute-done((bf16[128,8,128]{2,1,0:T(8,128)(2,1)S(1)}, bf16[128,8,128]{2,1,0:T(8,128)(2,1)S(1)}, u32[]{:S(2)}, u32[]{:S(2)}) %collective-permute-start.27) | collective-permute-done | bytes 262176 | tf_op jit(solution)/shard_map/ppermute | solution.py:22
  88.1 1.6 collective-permute-start.8
  89.7 9.8 %select_convert_fusion.refs_12_ = bf16[520,1024]{1,0:T(8,128)(2,1)} fusion(s32[520]{0:T(1024)S(1)} %iota_add_fusion, s32[1024]{0:T(1024)S(1)} %fusion.12, pred[520]{0:T(1024)(128)(4,1)S(1)} %iota_compare_fusion.2, pred[1024]{0:T(1024)(128)(4,1)S(1)} %fusion.10), kind=kLoop, calls=%fused_computation.8 | loop fusion | flops 9584640 | bytes 1072680 | tf_op jit(solution)/shard_map/convert_element_type | solution.py:155
  99.6 27.6 %correlate.3 = (bf16[2,520,256]{2,1,0:T(8,128)(2,1)}, bf16[2,520,256]{2,1,0:T(8,128)(2,1)}, bf16[2,520,256]{2,1,0:T(8,128)(2,1)}, bf16[2,520,256]{2,1,0:T(8,128)(2,1)}) custom-call(bf16[128,8,128]{2,1,0:T(8,128)(2,1)} %whiten.1.refs_0_, bf16[128,8,128]{2,1,0:T(8,128)(2,1)} %copy-done.15, bf16[128,8,128]{2,1,0:T(8,128)(2,1)} %copy-done.16, ...), custom_call_target="tpu_custom_call" | custom-call | tf_op jit(solution)/shard_map/correlate/pallas_call | solution.py:109
  127.2 0.0 collective-permute-done.1.refs_2_
  127.2 1.0 collective-permute-start.28
  128.2 0.0 collective-permute-done.2.refs_3_
  128.3 1.7 collective-permute-start.9
  129.9 2.5 %collective-permute-start.11 = (bf16[128,8,128]{2,1,0:T(8,128)(2,1)S(1)}, bf16[128,8,128]{2,1,0:T(8,128)(2,1)S(1)}, u32[]{:S(2)}, u32[]{:S(2)}) collective-permute-start(bf16[128,8,128]{2,1,0:T(8,128)(2,1)S(1)} %collective-permute-done.10.refs_8_), channel_id=1, source_target_pairs={{0,1},{1,0},{2,3},{3,2},{4,5},{5,4},{6,7},{7,6},{8,9},{9,8},{10,11... | collective-permute-start | bytes 786440 | tf_op jit(solution)/shard_map/ppermute | solution.py:22
  132.4 0.0 collective-permute-done.7.refs_5_
  132.4 0.0 collective-permute-start.12
  132.5 1.5 collective-permute-start.13
  134.0 3.0 %collective-permute-done.9.refs_7_ = bf16[128,8,128]{2,1,0:T(8,128)(2,1)S(1)} collective-permute-done((bf16[128,8,128]{2,1,0:T(8,128)(2,1)S(1)}, bf16[128,8,128]{2,1,0:T(8,128)(2,1)S(1)}, u32[]{:S(2)}, u32[]{:S(2)}) %collective-permute-start.9) | collective-permute-done | bytes 262176 | tf_op jit(solution)/shard_map/ppermute | solution.py:22
  137.0 4.3 %collective-permute-start.29 = (bf16[2,520,256]{2,1,0:T(8,128)(2,1)}, bf16[2,520,256]{2,1,0:T(8,128)(2,1)S(1)}, u32[]{:S(2)}, u32[]{:S(2)}) collective-permute-start(bf16[2,520,256]{2,1,0:T(8,128)(2,1)} %get-tuple-element.19), channel_id=1, source_target_pairs={{0,2},{1,3},{2,0},{3,1},{4,6},{5,7},{6,4},{7,5},{8,10},{9,11},{10,... | collective-permute-start | bytes 1597448 | tf_op jit(solution)/shard_map/ppermute | solution.py:22
  141.3 6.8 %collective-permute-done.11.refs_9_ = bf16[128,8,128]{2,1,0:T(8,128)(2,1)S(1)} collective-permute-done((bf16[128,8,128]{2,1,0:T(8,128)(2,1)S(1)}, bf16[128,8,128]{2,1,0:T(8,128)(2,1)S(1)}, u32[]{:S(2)}, u32[]{:S(2)}) %collective-permute-start.11) | collective-permute-done | bytes 262176 | tf_op jit(solution)/shard_map/ppermute | solution.py:22
  148.1 2.4 %collective-permute-start.30 = (bf16[2,520,256]{2,1,0:T(8,128)(2,1)}, bf16[2,520,256]{2,1,0:T(8,128)(2,1)S(1)}, u32[]{:S(2)}, u32[]{:S(2)}) collective-permute-start(bf16[2,520,256]{2,1,0:T(8,128)(2,1)} %get-tuple-element.20), channel_id=1, source_target_pairs={{0,3},{1,2},{2,1},{3,0},{4,7},{5,6},{6,5},{7,4},{8,11},{9,10},{10,... | collective-permute-start | bytes 1597448 | tf_op jit(solution)/shard_map/ppermute | solution.py:22
  150.5 5.2 %collective-permute-done.12.refs_10_ = bf16[128,8,128]{2,1,0:T(8,128)(2,1)S(1)} collective-permute-done((bf16[128,8,128]{2,1,0:T(8,128)(2,1)S(1)}, bf16[128,8,128]{2,1,0:T(8,128)(2,1)S(1)}, u32[]{:S(2)}, u32[]{:S(2)}) %collective-permute-start.12) | collective-permute-done | bytes 262176 | tf_op jit(solution)/shard_map/ppermute | solution.py:22
  155.7 0.6 copy-done.27
  156.4 0.8 copy-done.28
  157.1 27.6 %correlate.2 = (bf16[2,520,256]{2,1,0:T(8,128)(2,1)}, bf16[2,520,256]{2,1,0:T(8,128)(2,1)}, bf16[2,520,256]{2,1,0:T(8,128)(2,1)}, bf16[2,520,256]{2,1,0:T(8,128)(2,1)}) custom-call(bf16[128,8,128]{2,1,0:T(8,128)(2,1)} %whiten.1.refs_0_, bf16[128,8,128]{2,1,0:T(8,128)(2,1)} %copy-done.9, bf16[128,8,128]{2,1,0:T(8,128)(2,1)} %copy-done.10, ...), custom_call_target="tpu_custom_call" | custom-call | tf_op jit(solution)/shard_map/correlate/pallas_call | solution.py:109
  184.7 2.3 %collective-permute-start.15 = (bf16[2,520,256]{2,1,0:T(8,128)(2,1)}, bf16[2,520,256]{2,1,0:T(8,128)(2,1)S(1)}, u32[]{:S(2)}, u32[]{:S(2)}) collective-permute-start(bf16[2,520,256]{2,1,0:T(8,128)(2,1)} %get-tuple-element.15), channel_id=1, source_target_pairs={{0,8},{1,9},{2,10},{3,11},{4,12},{5,13},{6,14},{7,15},{8,0},{9,1},... | collective-permute-start | bytes 1597448 | tf_op jit(solution)/shard_map/ppermute | solution.py:22
  187.0 2.4 %collective-permute-start.16 = (bf16[2,520,256]{2,1,0:T(8,128)(2,1)}, bf16[2,520,256]{2,1,0:T(8,128)(2,1)S(1)}, u32[]{:S(2)}, u32[]{:S(2)}) collective-permute-start(bf16[2,520,256]{2,1,0:T(8,128)(2,1)} %get-tuple-element.16), channel_id=1, source_target_pairs={{0,12},{1,13},{2,14},{3,15},{4,8},{5,9},{6,10},{7,11},{8,4},{9,5},... | collective-permute-start | bytes 1597448 | tf_op jit(solution)/shard_map/ppermute | solution.py:22
  189.4 0.2 iota_compare_fusion
  189.6 1.2 and_convert_fusion.refs_8_
  190.9 5.5 %collective-permute-done.14.refs_1_ = bf16[2,520,256]{2,1,0:T(8,128)(2,1)S(1)} collective-permute-done((bf16[2,520,256]{2,1,0:T(8,128)(2,1)}, bf16[2,520,256]{2,1,0:T(8,128)(2,1)S(1)}, u32[]{:S(2)}, u32[]{:S(2)}) %collective-permute-start.14) | collective-permute-done | bytes 532512 | tf_op jit(solution)/shard_map/ppermute | solution.py:22
  196.4 6.9 %collective-permute-done.15.refs_2_ = bf16[2,520,256]{2,1,0:T(8,128)(2,1)S(1)} collective-permute-done((bf16[2,520,256]{2,1,0:T(8,128)(2,1)}, bf16[2,520,256]{2,1,0:T(8,128)(2,1)S(1)}, u32[]{:S(2)}, u32[]{:S(2)}) %collective-permute-start.15) | collective-permute-done | bytes 532512 | tf_op jit(solution)/shard_map/ppermute | solution.py:22
  203.3 2.5 %collective-permute-done.16.refs_3_ = bf16[2,520,256]{2,1,0:T(8,128)(2,1)S(1)} collective-permute-done((bf16[2,520,256]{2,1,0:T(8,128)(2,1)}, bf16[2,520,256]{2,1,0:T(8,128)(2,1)S(1)}, u32[]{:S(2)}, u32[]{:S(2)}) %collective-permute-start.16) | collective-permute-done | bytes 532512 | tf_op jit(solution)/shard_map/ppermute | solution.py:22
  205.9 0.8 copy-done.8
  206.6 7.4 %finish.1 = bf16[4,4104,128]{2,1,0:T(8,128)(2,1)} custom-call(bf16[2,520,256]{2,1,0:T(8,128)(2,1)} %get-tuple-element.13.refs_0_, bf16[2,520,256]{2,1,0:T(8,128)(2,1)} %copy-done.6, bf16[2,520,256]{2,1,0:T(8,128)(2,1)} %copy-done.7, bf16[2,520,256]{2,1,0:T(8,128)(2,1)} %copy-done.8, bf16[2,520,256]{2,1,0:T(8,128)(2,1)} %get-tuple-element.17.refs_4_, ...), custom_call_target="tpu_custom_call" | custom-call | tf_op jit(solution)/shard_map/finish/pallas_call | solution.py:140
  (75 shorter events, 0.3 us)
Async XLA Ops:
  2.5 65.7 %copy-start = (bf16[128,8,128]{2,1,0:T(8,128)(2,1)S(1)}, bf16[128,8,128]{2,1,0:T(8,128)(2,1)}, u32[]{:S(2)}) copy-start(bf16[128,8,128]{2,1,0:T(8,128)(2,1)} %whiten.1.refs_0_) | copy-start | bytes 786436
  2.5 26.7 %collective-permute-start.3 = (bf16[128,8,128]{2,1,0:T(8,128)(2,1)}, bf16[128,8,128]{2,1,0:T(8,128)(2,1)S(1)}, u32[]{:S(2)}, u32[]{:S(2)}) collective-permute-start(bf16[128,8,128]{2,1,0:T(8,128)(2,1)} %whiten.1.refs_0_), channel_id=1, source_target_pairs={{0,64},{32,96},{64,0},{96,32},{128,192},{160,224},{192,128},{224,1... | collective-permute-start | bytes 786440 | tf_op jit(solution)/shard_map/ppermute | solution.py:22
  5.8 28.5 %collective-permute-start.4 = (bf16[128,8,128]{2,1,0:T(8,128)(2,1)}, bf16[128,8,128]{2,1,0:T(8,128)(2,1)S(1)}, u32[]{:S(2)}, u32[]{:S(2)}) collective-permute-start(bf16[128,8,128]{2,1,0:T(8,128)(2,1)} %whiten.1.refs_0_), channel_id=1, source_target_pairs={{0,128},{32,160},{64,192},{96,224},{128,0},{160,32},{192,64},{224,... | collective-permute-start | bytes 786440 | tf_op jit(solution)/shard_map/ppermute | solution.py:22
  11.2 23.1 %collective-permute-start.5 = (bf16[128,8,128]{2,1,0:T(8,128)(2,1)}, bf16[128,8,128]{2,1,0:T(8,128)(2,1)S(1)}, u32[]{:S(2)}, u32[]{:S(2)}) collective-permute-start(bf16[128,8,128]{2,1,0:T(8,128)(2,1)} %whiten.1.refs_0_), channel_id=1, source_target_pairs={{0,192},{32,224},{64,128},{96,160},{128,64},{160,96},{192,0},{224,... | collective-permute-start | bytes 786440 | tf_op jit(solution)/shard_map/ppermute | solution.py:22
  35.3 5.8 %collective-permute-start.20 = (bf16[128,8,128]{2,1,0:T(8,128)(2,1)S(1)}, bf16[128,8,128]{2,1,0:T(8,128)(2,1)S(1)}, u32[]{:S(2)}, u32[]{:S(2)}) collective-permute-start(bf16[128,8,128]{2,1,0:T(8,128)(2,1)S(1)} %get-tuple-element.21), channel_id=1, source_target_pairs={{0,32},{32,0},{64,96},{96,64},{128,160},{160,128},{192,224},{224,1... | collective-permute-start | bytes 786440 | tf_op jit(solution)/shard_map/ppermute | solution.py:22
  35.4 9.4 %collective-permute-start.17 = (bf16[128,8,128]{2,1,0:T(8,128)(2,1)}, bf16[128,8,128]{2,1,0:T(8,128)(2,1)S(1)}, u32[]{:S(2)}, u32[]{:S(2)}) collective-permute-start(bf16[128,8,128]{2,1,0:T(8,128)(2,1)} %whiten.1.refs_0_), channel_id=1, source_target_pairs={{0,1},{1,0},{2,3},{3,2},{4,5},{5,4},{6,7},{7,6},{8,9},{9,8},{10,11... | collective-permute-start | bytes 786440 | tf_op jit(solution)/shard_map/ppermute | solution.py:22
  35.9 15.1 %collective-permute-start.18 = (bf16[128,8,128]{2,1,0:T(8,128)(2,1)}, bf16[128,8,128]{2,1,0:T(8,128)(2,1)S(1)}, u32[]{:S(2)}, u32[]{:S(2)}) collective-permute-start(bf16[128,8,128]{2,1,0:T(8,128)(2,1)} %whiten.1.refs_0_), channel_id=1, source_target_pairs={{0,2},{1,3},{2,0},{3,1},{4,6},{5,7},{6,4},{7,5},{8,10},{9,11},{10,... | collective-permute-start | bytes 786440 | tf_op jit(solution)/shard_map/ppermute | solution.py:22
  38.5 14.1 %collective-permute-start.19 = (bf16[128,8,128]{2,1,0:T(8,128)(2,1)}, bf16[128,8,128]{2,1,0:T(8,128)(2,1)S(1)}, u32[]{:S(2)}, u32[]{:S(2)}) collective-permute-start(bf16[128,8,128]{2,1,0:T(8,128)(2,1)} %whiten.1.refs_0_), channel_id=1, source_target_pairs={{0,3},{1,2},{2,1},{3,0},{4,7},{5,6},{6,5},{7,4},{8,11},{9,10},{10,... | collective-permute-start | bytes 786440 | tf_op jit(solution)/shard_map/ppermute | solution.py:22
  39.0 16.5 %collective-permute-start = (bf16[128,8,128]{2,1,0:T(8,128)(2,1)}, bf16[128,8,128]{2,1,0:T(8,128)(2,1)S(1)}, u32[]{:S(2)}, u32[]{:S(2)}) collective-permute-start(bf16[128,8,128]{2,1,0:T(8,128)(2,1)} %whiten.1.refs_0_), channel_id=1, source_target_pairs={{0,4},{1,5},{2,6},{3,7},{4,0},{5,1},{6,2},{7,3},{8,12},{9,13},{10,... | collective-permute-start | bytes 786440 | tf_op jit(solution)/shard_map/ppermute | solution.py:22
  41.1 15.5 %collective-permute-start.6 = (bf16[128,8,128]{2,1,0:T(8,128)(2,1)S(1)}, bf16[128,8,128]{2,1,0:T(8,128)(2,1)S(1)}, u32[]{:S(2)}, u32[]{:S(2)}) collective-permute-start(bf16[128,8,128]{2,1,0:T(8,128)(2,1)S(1)} %get-tuple-element.22), channel_id=1, source_target_pairs={{0,32},{32,0},{64,96},{96,64},{128,160},{160,128},{192,224},{224,1... | collective-permute-start | bytes 786440 | tf_op jit(solution)/shard_map/ppermute | solution.py:22
  41.3 58.2 %copy-start.2 = (bf16[128,8,128]{2,1,0:T(8,128)(2,1)}, bf16[128,8,128]{2,1,0:T(8,128)(2,1)S(1)}, u32[]{:S(2)}) copy-start(bf16[128,8,128]{2,1,0:T(8,128)(2,1)S(1)} %broadcast_select_fusion.refs_4_) | copy-start | bytes 786436
  44.8 54.7 %copy-start.15 = (bf16[128,8,128]{2,1,0:T(8,128)(2,1)}, bf16[128,8,128]{2,1,0:T(8,128)(2,1)S(1)}, u32[]{:S(2)}) copy-start(bf16[128,8,128]{2,1,0:T(8,128)(2,1)S(1)} %collective-permute-done.17.refs_1_) | copy-start | bytes 786436
  44.8 11.8 %collective-permute-start.24 = (bf16[128,8,128]{2,1,0:T(8,128)(2,1)S(1)}, bf16[128,8,128]{2,1,0:T(8,128)(2,1)S(1)}, u32[]{:S(2)}, u32[]{:S(2)}) collective-permute-start(bf16[128,8,128]{2,1,0:T(8,128)(2,1)S(1)} %broadcast_select_fusion.refs_4_), channel_id=1, source_target_pairs={{0,16},{1,17},{2,18},{3,19},{4,20},{5,21},{6,22},{7,23},{8,24},{9,... | collective-permute-start | bytes 786440 | tf_op jit(solution)/shard_map/ppermute | solution.py:22
  51.1 48.4 %copy-start.16 = (bf16[128,8,128]{2,1,0:T(8,128)(2,1)}, bf16[128,8,128]{2,1,0:T(8,128)(2,1)S(1)}, u32[]{:S(2)}) copy-start(bf16[128,8,128]{2,1,0:T(8,128)(2,1)S(1)} %collective-permute-done.18.refs_2_) | copy-start | bytes 786436
  51.1 9.2 %collective-permute-start.21 = (bf16[128,8,128]{2,1,0:T(8,128)(2,1)S(1)}, bf16[128,8,128]{2,1,0:T(8,128)(2,1)S(1)}, u32[]{:S(2)}, u32[]{:S(2)}) collective-permute-start(bf16[128,8,128]{2,1,0:T(8,128)(2,1)S(1)} %broadcast_select_fusion.refs_4_), channel_id=1, source_target_pairs={{0,4},{1,5},{2,6},{3,7},{4,0},{5,1},{6,2},{7,3},{8,12},{9,13},{10,... | collective-permute-start | bytes 786440 | tf_op jit(solution)/shard_map/ppermute | solution.py:22
  52.6 46.9 %copy-start.17 = (bf16[128,8,128]{2,1,0:T(8,128)(2,1)}, bf16[128,8,128]{2,1,0:T(8,128)(2,1)S(1)}, u32[]{:S(2)}) copy-start(bf16[128,8,128]{2,1,0:T(8,128)(2,1)S(1)} %collective-permute-done.19.refs_3_) | copy-start | bytes 786436
  52.6 15.6 %collective-permute-start.22 = (bf16[128,8,128]{2,1,0:T(8,128)(2,1)S(1)}, bf16[128,8,128]{2,1,0:T(8,128)(2,1)S(1)}, u32[]{:S(2)}, u32[]{:S(2)}) collective-permute-start(bf16[128,8,128]{2,1,0:T(8,128)(2,1)S(1)} %broadcast_select_fusion.refs_4_), channel_id=1, source_target_pairs={{0,8},{1,9},{2,10},{3,11},{4,12},{5,13},{6,14},{7,15},{8,0},{9,1},... | collective-permute-start | bytes 786440 | tf_op jit(solution)/shard_map/ppermute | solution.py:22
  55.5 71.7 %copy-start.9 = (bf16[128,8,128]{2,1,0:T(8,128)(2,1)}, bf16[128,8,128]{2,1,0:T(8,128)(2,1)S(1)}, u32[]{:S(2)}) copy-start(bf16[128,8,128]{2,1,0:T(8,128)(2,1)S(1)} %collective-permute-done.refs_1_) | copy-start | bytes 786436
  55.5 16.1 %collective-permute-start.23 = (bf16[128,8,128]{2,1,0:T(8,128)(2,1)S(1)}, bf16[128,8,128]{2,1,0:T(8,128)(2,1)S(1)}, u32[]{:S(2)}, u32[]{:S(2)}) collective-permute-start(bf16[128,8,128]{2,1,0:T(8,128)(2,1)S(1)} %broadcast_select_fusion.refs_4_), channel_id=1, source_target_pairs={{0,12},{1,13},{2,14},{3,15},{4,8},{5,9},{6,10},{7,11},{8,4},{9,5},... | collective-permute-start | bytes 786440 | tf_op jit(solution)/shard_map/ppermute | solution.py:22
  56.6 42.9 %copy-start.18 = (bf16[128,8,128]{2,1,0:T(8,128)(2,1)}, bf16[128,8,128]{2,1,0:T(8,128)(2,1)S(1)}, u32[]{:S(2)}) copy-start(bf16[128,8,128]{2,1,0:T(8,128)(2,1)S(1)} %collective-permute-done.24.refs_8_) | copy-start | bytes 786436
  56.6 16.1 %collective-permute-start.25 = (bf16[128,8,128]{2,1,0:T(8,128)(2,1)S(1)}, bf16[128,8,128]{2,1,0:T(8,128)(2,1)S(1)}, u32[]{:S(2)}, u32[]{:S(2)}) collective-permute-start(bf16[128,8,128]{2,1,0:T(8,128)(2,1)S(1)} %collective-permute-done.24.refs_8_), channel_id=1, source_target_pairs={{0,4},{1,5},{2,6},{3,7},{4,0},{5,1},{6,2},{7,3},{8,12},{9,13},{10,... | collective-permute-start | bytes 786440 | tf_op jit(solution)/shard_map/ppermute | solution.py:22
  56.6 22.9 %collective-permute-start.26 = (bf16[128,8,128]{2,1,0:T(8,128)(2,1)S(1)}, bf16[128,8,128]{2,1,0:T(8,128)(2,1)S(1)}, u32[]{:S(2)}, u32[]{:S(2)}) collective-permute-start(bf16[128,8,128]{2,1,0:T(8,128)(2,1)S(1)} %collective-permute-done.24.refs_8_), channel_id=1, source_target_pairs={{0,8},{1,9},{2,10},{3,11},{4,12},{5,13},{6,14},{7,15},{8,0},{9,1},... | collective-permute-start | bytes 786440 | tf_op jit(solution)/shard_map/ppermute | solution.py:22
  60.3 39.2 %copy-start.19 = (bf16[128,8,128]{2,1,0:T(8,128)(2,1)}, bf16[128,8,128]{2,1,0:T(8,128)(2,1)S(1)}, u32[]{:S(2)}) copy-start(bf16[128,8,128]{2,1,0:T(8,128)(2,1)S(1)} %collective-permute-done.21.refs_5_) | copy-start | bytes 786436
  60.3 27.8 %collective-permute-start.27 = (bf16[128,8,128]{2,1,0:T(8,128)(2,1)S(1)}, bf16[128,8,128]{2,1,0:T(8,128)(2,1)S(1)}, u32[]{:S(2)}, u32[]{:S(2)}) collective-permute-start(bf16[128,8,128]{2,1,0:T(8,128)(2,1)S(1)} %collective-permute-done.24.refs_8_), channel_id=1, source_target_pairs={{0,12},{1,13},{2,14},{3,15},{4,8},{5,9},{6,10},{7,11},{8,4},{9,5},... | collective-permute-start | bytes 786440 | tf_op jit(solution)/shard_map/ppermute | solution.py:22
  63.7 64.5 %copy-start.1 = (bf16[128,8,128]{2,1,0:T(8,128)(2,1)}, bf16[128,8,128]{2,1,0:T(8,128)(2,1)S(1)}, u32[]{:S(2)}) copy-start(bf16[128,8,128]{2,1,0:T(8,128)(2,1)S(1)} %broadcast_select_fusion.1.refs_4_) | copy-start | bytes 786436
  68.2 31.3 %copy-start.20 = (bf16[128,8,128]{2,1,0:T(8,128)(2,1)}, bf16[128,8,128]{2,1,0:T(8,128)(2,1)S(1)}, u32[]{:S(2)}) copy-start(bf16[128,8,128]{2,1,0:T(8,128)(2,1)S(1)} %collective-permute-done.22.refs_6_) | copy-start | bytes 786436
  68.2 59.0 %collective-permute-start.1 = (bf16[128,8,128]{2,1,0:T(8,128)(2,1)S(1)}, bf16[128,8,128]{2,1,0:T(8,128)(2,1)S(1)}, u32[]{:S(2)}, u32[]{:S(2)}) collective-permute-start(bf16[128,8,128]{2,1,0:T(8,128)(2,1)S(1)} %copy-done), channel_id=1, source_target_pairs={{0,8},{1,9},{2,10},{3,11},{4,12},{5,13},{6,14},{7,15},{8,0},{9,1},... | collective-permute-start | bytes 786440 | tf_op jit(solution)/shard_map/ppermute | solution.py:22
  71.6 28.0 %copy-start.21 = (bf16[128,8,128]{2,1,0:T(8,128)(2,1)}, bf16[128,8,128]{2,1,0:T(8,128)(2,1)S(1)}, u32[]{:S(2)}) copy-start(bf16[128,8,128]{2,1,0:T(8,128)(2,1)S(1)} %collective-permute-done.23.refs_7_) | copy-start | bytes 786436
  71.6 56.7 %collective-permute-start.2 = (bf16[128,8,128]{2,1,0:T(8,128)(2,1)S(1)}, bf16[128,8,128]{2,1,0:T(8,128)(2,1)S(1)}, u32[]{:S(2)}, u32[]{:S(2)}) collective-permute-start(bf16[128,8,128]{2,1,0:T(8,128)(2,1)S(1)} %copy-done), channel_id=1, source_target_pairs={{0,12},{1,13},{2,14},{3,15},{4,8},{5,9},{6,10},{7,11},{8,4},{9,5},... | collective-permute-start | bytes 786440 | tf_op jit(solution)/shard_map/ppermute | solution.py:22
  72.7 26.8 %copy-start.22 = (bf16[128,8,128]{2,1,0:T(8,128)(2,1)}, bf16[128,8,128]{2,1,0:T(8,128)(2,1)S(1)}, u32[]{:S(2)}) copy-start(bf16[128,8,128]{2,1,0:T(8,128)(2,1)S(1)} %collective-permute-done.25.refs_9_) | copy-start | bytes 786436
  72.7 57.2 %collective-permute-start.10 = (bf16[128,8,128]{2,1,0:T(8,128)(2,1)S(1)}, bf16[128,8,128]{2,1,0:T(8,128)(2,1)S(1)}, u32[]{:S(2)}, u32[]{:S(2)}) collective-permute-start(bf16[128,8,128]{2,1,0:T(8,128)(2,1)S(1)} %broadcast_select_fusion.1.refs_4_), channel_id=1, source_target_pairs={{0,16},{1,17},{2,18},{3,19},{4,20},{5,21},{6,22},{7,23},{8,24},{9,... | collective-permute-start | bytes 786440 | tf_op jit(solution)/shard_map/ppermute | solution.py:22
  79.5 20.0 %copy-start.23 = (bf16[128,8,128]{2,1,0:T(8,128)(2,1)}, bf16[128,8,128]{2,1,0:T(8,128)(2,1)S(1)}, u32[]{:S(2)}) copy-start(bf16[128,8,128]{2,1,0:T(8,128)(2,1)S(1)} %collective-permute-done.26.refs_10_) | copy-start | bytes 786436
  79.5 52.9 %collective-permute-start.7 = (bf16[128,8,128]{2,1,0:T(8,128)(2,1)S(1)}, bf16[128,8,128]{2,1,0:T(8,128)(2,1)S(1)}, u32[]{:S(2)}, u32[]{:S(2)}) collective-permute-start(bf16[128,8,128]{2,1,0:T(8,128)(2,1)S(1)} %broadcast_select_fusion.1.refs_4_), channel_id=1, source_target_pairs={{0,1},{1,0},{2,3},{3,2},{4,5},{5,4},{6,7},{7,6},{8,9},{9,8},{10,11... | collective-permute-start | bytes 786440 | tf_op jit(solution)/shard_map/ppermute | solution.py:22
  88.1 11.5 %copy-start.24 = (bf16[128,8,128]{2,1,0:T(8,128)(2,1)}, bf16[128,8,128]{2,1,0:T(8,128)(2,1)S(1)}, u32[]{:S(2)}) copy-start(bf16[128,8,128]{2,1,0:T(8,128)(2,1)S(1)} %collective-permute-done.27.refs_11_) | copy-start | bytes 786436
  88.1 44.4 %collective-permute-start.8 = (bf16[128,8,128]{2,1,0:T(8,128)(2,1)S(1)}, bf16[128,8,128]{2,1,0:T(8,128)(2,1)S(1)}, u32[]{:S(2)}, u32[]{:S(2)}) collective-permute-start(bf16[128,8,128]{2,1,0:T(8,128)(2,1)S(1)} %broadcast_select_fusion.1.refs_4_), channel_id=1, source_target_pairs={{0,2},{1,3},{2,0},{3,1},{4,6},{5,7},{6,4},{7,5},{8,10},{9,11},{10,... | collective-permute-start | bytes 786440 | tf_op jit(solution)/shard_map/ppermute | solution.py:22
  127.2 28.5 %copy-start.10 = (bf16[128,8,128]{2,1,0:T(8,128)(2,1)}, bf16[128,8,128]{2,1,0:T(8,128)(2,1)S(1)}, u32[]{:S(2)}) copy-start(bf16[128,8,128]{2,1,0:T(8,128)(2,1)S(1)} %collective-permute-done.1.refs_2_) | copy-start | bytes 786436
  127.2 59.8 %collective-permute-start.28 = (bf16[2,520,256]{2,1,0:T(8,128)(2,1)}, bf16[2,520,256]{2,1,0:T(8,128)(2,1)S(1)}, u32[]{:S(2)}, u32[]{:S(2)}) collective-permute-start(bf16[2,520,256]{2,1,0:T(8,128)(2,1)} %get-tuple-element.18), channel_id=1, source_target_pairs={{0,1},{1,0},{2,3},{3,2},{4,5},{5,4},{6,7},{7,6},{8,9},{9,8},{10,11... | collective-permute-start | bytes 1597448 | tf_op jit(solution)/shard_map/ppermute | solution.py:22
  128.3 27.4 %copy-start.11 = (bf16[128,8,128]{2,1,0:T(8,128)(2,1)}, bf16[128,8,128]{2,1,0:T(8,128)(2,1)S(1)}, u32[]{:S(2)}) copy-start(bf16[128,8,128]{2,1,0:T(8,128)(2,1)S(1)} %collective-permute-done.2.refs_3_) | copy-start | bytes 786436
  128.3 8.7 %collective-permute-start.9 = (bf16[128,8,128]{2,1,0:T(8,128)(2,1)S(1)}, bf16[128,8,128]{2,1,0:T(8,128)(2,1)S(1)}, u32[]{:S(2)}, u32[]{:S(2)}) collective-permute-start(bf16[128,8,128]{2,1,0:T(8,128)(2,1)S(1)} %broadcast_select_fusion.1.refs_4_), channel_id=1, source_target_pairs={{0,3},{1,2},{2,1},{3,0},{4,7},{5,6},{6,5},{7,4},{8,11},{9,10},{10,... | collective-permute-start | bytes 786440 | tf_op jit(solution)/shard_map/ppermute | solution.py:22
  129.9 25.7 %copy-start.12 = (bf16[128,8,128]{2,1,0:T(8,128)(2,1)}, bf16[128,8,128]{2,1,0:T(8,128)(2,1)S(1)}, u32[]{:S(2)}) copy-start(bf16[128,8,128]{2,1,0:T(8,128)(2,1)S(1)} %collective-permute-done.10.refs_8_) | copy-start | bytes 786436
  129.9 18.2 %collective-permute-start.11 = (bf16[128,8,128]{2,1,0:T(8,128)(2,1)S(1)}, bf16[128,8,128]{2,1,0:T(8,128)(2,1)S(1)}, u32[]{:S(2)}, u32[]{:S(2)}) collective-permute-start(bf16[128,8,128]{2,1,0:T(8,128)(2,1)S(1)} %collective-permute-done.10.refs_8_), channel_id=1, source_target_pairs={{0,1},{1,0},{2,3},{3,2},{4,5},{5,4},{6,7},{7,6},{8,9},{9,8},{10,11... | collective-permute-start | bytes 786440 | tf_op jit(solution)/shard_map/ppermute | solution.py:22
  132.4 23.3 %copy-start.13 = (bf16[128,8,128]{2,1,0:T(8,128)(2,1)}, bf16[128,8,128]{2,1,0:T(8,128)(2,1)S(1)}, u32[]{:S(2)}) copy-start(bf16[128,8,128]{2,1,0:T(8,128)(2,1)S(1)} %collective-permute-done.7.refs_5_) | copy-start | bytes 786436
  132.4 23.2 %collective-permute-start.12 = (bf16[128,8,128]{2,1,0:T(8,128)(2,1)S(1)}, bf16[128,8,128]{2,1,0:T(8,128)(2,1)S(1)}, u32[]{:S(2)}, u32[]{:S(2)}) collective-permute-start(bf16[128,8,128]{2,1,0:T(8,128)(2,1)S(1)} %collective-permute-done.10.refs_8_), channel_id=1, source_target_pairs={{0,2},{1,3},{2,0},{3,1},{4,6},{5,7},{6,4},{7,5},{8,10},{9,11},{10,... | collective-permute-start | bytes 786440 | tf_op jit(solution)/shard_map/ppermute | solution.py:22
  132.5 23.3 %copy-start.14 = (bf16[128,8,128]{2,1,0:T(8,128)(2,1)}, bf16[128,8,128]{2,1,0:T(8,128)(2,1)S(1)}, u32[]{:S(2)}) copy-start(bf16[128,8,128]{2,1,0:T(8,128)(2,1)S(1)} %collective-permute-done.8.refs_6_) | copy-start | bytes 786436
  132.5 23.2 %collective-permute-start.13 = (bf16[128,8,128]{2,1,0:T(8,128)(2,1)S(1)}, bf16[128,8,128]{2,1,0:T(8,128)(2,1)S(1)}, u32[]{:S(2)}, u32[]{:S(2)}) collective-permute-start(bf16[128,8,128]{2,1,0:T(8,128)(2,1)S(1)} %collective-permute-done.10.refs_8_), channel_id=1, source_target_pairs={{0,3},{1,2},{2,1},{3,0},{4,7},{5,6},{6,5},{7,4},{8,11},{9,10},{10,... | collective-permute-start | bytes 786440 | tf_op jit(solution)/shard_map/ppermute | solution.py:22
  137.0 18.7 %copy-start.25 = (bf16[128,8,128]{2,1,0:T(8,128)(2,1)}, bf16[128,8,128]{2,1,0:T(8,128)(2,1)S(1)}, u32[]{:S(2)}) copy-start(bf16[128,8,128]{2,1,0:T(8,128)(2,1)S(1)} %collective-permute-done.9.refs_7_) | copy-start | bytes 786436
  137.0 53.9 %collective-permute-start.29 = (bf16[2,520,256]{2,1,0:T(8,128)(2,1)}, bf16[2,520,256]{2,1,0:T(8,128)(2,1)S(1)}, u32[]{:S(2)}, u32[]{:S(2)}) collective-permute-start(bf16[2,520,256]{2,1,0:T(8,128)(2,1)} %get-tuple-element.19), channel_id=1, source_target_pairs={{0,2},{1,3},{2,0},{3,1},{4,6},{5,7},{6,4},{7,5},{8,10},{9,11},{10,... | collective-permute-start | bytes 1597448 | tf_op jit(solution)/shard_map/ppermute | solution.py:22
  148.1 7.6 %copy-start.26 = (bf16[128,8,128]{2,1,0:T(8,128)(2,1)}, bf16[128,8,128]{2,1,0:T(8,128)(2,1)S(1)}, u32[]{:S(2)}) copy-start(bf16[128,8,128]{2,1,0:T(8,128)(2,1)S(1)} %collective-permute-done.11.refs_9_) | copy-start | bytes 786436
  148.1 42.7 %collective-permute-start.30 = (bf16[2,520,256]{2,1,0:T(8,128)(2,1)}, bf16[2,520,256]{2,1,0:T(8,128)(2,1)S(1)}, u32[]{:S(2)}, u32[]{:S(2)}) collective-permute-start(bf16[2,520,256]{2,1,0:T(8,128)(2,1)} %get-tuple-element.20), channel_id=1, source_target_pairs={{0,3},{1,2},{2,1},{3,0},{4,7},{5,6},{6,5},{7,4},{8,11},{9,10},{10,... | collective-permute-start | bytes 1597448 | tf_op jit(solution)/shard_map/ppermute | solution.py:22
  155.7 0.7 copy-start.27
  156.4 0.8 copy-start.28
  184.7 11.7 %collective-permute-start.14 = (bf16[2,520,256]{2,1,0:T(8,128)(2,1)}, bf16[2,520,256]{2,1,0:T(8,128)(2,1)S(1)}, u32[]{:S(2)}, u32[]{:S(2)}) collective-permute-start(bf16[2,520,256]{2,1,0:T(8,128)(2,1)} %get-tuple-element.14), channel_id=1, source_target_pairs={{0,4},{1,5},{2,6},{3,7},{4,0},{5,1},{6,2},{7,3},{8,12},{9,13},{10,... | collective-permute-start | bytes 1597448 | tf_op jit(solution)/shard_map/ppermute | solution.py:22
  184.7 18.6 %collective-permute-start.15 = (bf16[2,520,256]{2,1,0:T(8,128)(2,1)}, bf16[2,520,256]{2,1,0:T(8,128)(2,1)S(1)}, u32[]{:S(2)}, u32[]{:S(2)}) collective-permute-start(bf16[2,520,256]{2,1,0:T(8,128)(2,1)} %get-tuple-element.15), channel_id=1, source_target_pairs={{0,8},{1,9},{2,10},{3,11},{4,12},{5,13},{6,14},{7,15},{8,0},{9,1},... | collective-permute-start | bytes 1597448 | tf_op jit(solution)/shard_map/ppermute | solution.py:22
  187.0 18.8 %copy-start.3 = (bf16[2,520,256]{2,1,0:T(8,128)(2,1)}, bf16[2,520,256]{2,1,0:T(8,128)(2,1)S(1)}, u32[]{:S(2)}) copy-start(bf16[2,520,256]{2,1,0:T(8,128)(2,1)S(1)} %collective-permute-done.28.refs_5_) | copy-start | bytes 1597444
  187.0 18.8 %collective-permute-start.16 = (bf16[2,520,256]{2,1,0:T(8,128)(2,1)}, bf16[2,520,256]{2,1,0:T(8,128)(2,1)S(1)}, u32[]{:S(2)}, u32[]{:S(2)}) collective-permute-start(bf16[2,520,256]{2,1,0:T(8,128)(2,1)} %get-tuple-element.16), channel_id=1, source_target_pairs={{0,12},{1,13},{2,14},{3,15},{4,8},{5,9},{6,10},{7,11},{8,4},{9,5},... | collective-permute-start | bytes 1597448 | tf_op jit(solution)/shard_map/ppermute | solution.py:22
  190.9 14.9 %copy-start.4 = (bf16[2,520,256]{2,1,0:T(8,128)(2,1)}, bf16[2,520,256]{2,1,0:T(8,128)(2,1)S(1)}, u32[]{:S(2)}) copy-start(bf16[2,520,256]{2,1,0:T(8,128)(2,1)S(1)} %collective-permute-done.29.refs_6_) | copy-start | bytes 1597444
  190.9 14.9 %copy-start.5 = (bf16[2,520,256]{2,1,0:T(8,128)(2,1)}, bf16[2,520,256]{2,1,0:T(8,128)(2,1)S(1)}, u32[]{:S(2)}) copy-start(bf16[2,520,256]{2,1,0:T(8,128)(2,1)S(1)} %collective-permute-done.30.refs_7_) | copy-start | bytes 1597444
  196.4 9.4 %copy-start.6 = (bf16[2,520,256]{2,1,0:T(8,128)(2,1)}, bf16[2,520,256]{2,1,0:T(8,128)(2,1)S(1)}, u32[]{:S(2)}) copy-start(bf16[2,520,256]{2,1,0:T(8,128)(2,1)S(1)} %collective-permute-done.14.refs_1_) | copy-start | bytes 1597444
  203.3 2.6 %copy-start.7 = (bf16[2,520,256]{2,1,0:T(8,128)(2,1)}, bf16[2,520,256]{2,1,0:T(8,128)(2,1)S(1)}, u32[]{:S(2)}) copy-start(bf16[2,520,256]{2,1,0:T(8,128)(2,1)S(1)} %collective-permute-done.15.refs_2_) | copy-start | bytes 1597444
  205.8 0.8 copy-start.8

commit v2 on v1

--- a/solution.py
+++ b/solution.py
@@ -15,7 +15,11 @@
 TAPS = BINS // LANE
 LAGS = BINS + 1
 LAG_ROWS = 520
-PARAMS = pltpu.CompilerParams(vmem_limit_bytes=56 * 1024 * 1024)
+UNROLL = 16
+
+
+def vmem(mib):
+    return pltpu.CompilerParams(vmem_limit_bytes=mib * 1024 * 1024)
 
 
 def xor_perm(array, axis, mask):
@@ -46,7 +50,7 @@
         whiten_kernel,
         out_shape=jax.ShapeDtypeStruct((LANE, CH, LANE), jnp.bfloat16),
         scratch_shapes=[pltpu.VMEM((LANE * CH, LANE), jnp.float32)],
-        compiler_params=PARAMS,
+        compiler_params=vmem(12),
         name="whiten",
     )(spectra)
 
@@ -68,7 +72,7 @@
     pick_im = sub - TAPS == tap
     blank = jnp.zeros((64, LANE), jnp.bfloat16)
 
-    def step(g, carry):
+    def step(g):
         cols = jnp.concatenate([c[g].astype(jnp.float32) for c in col_refs], 0).astype(jnp.bfloat16)
         rhs = jnp.concatenate(
             [jnp.concatenate([cols, blank], 1), jnp.concatenate([blank, cols], 1)], 0
@@ -79,8 +83,8 @@
             for half in range(2):
                 i = 2 * pair + half
                 at = (i // 8) * 1024 + g * 8 + i % 8
-                re = jnp.broadcast_to(rows[pl.ds(at, 1), :], (8, LANE))
-                im = jnp.broadcast_to(rows[pl.ds(4096 + at, 1), :], (8, LANE))
+                re = rows[pl.ds(at, 8, stride=0), :]
+                im = rows[pl.ds(4096 + at, 8, stride=0), :]
                 halves.append(jnp.where(pick_re, re, jnp.where(pick_im, im, 0.0)))
             pairs.append(jnp.concatenate(halves, 1))
         lhs = jnp.concatenate(pairs, 0).astype(jnp.bfloat16)
@@ -90,9 +94,13 @@
         at = pl.multiple_of(g * 8, 8)
         for pair in range(16):
             cross[pair, pl.ds(at, 8), :] = prod[pair * 8 : pair * 8 + 8]
+
+    def steps(k, carry):
+        for u in range(UNROLL):
+            step(k * UNROLL + u)
         return carry
 
-    lax.fori_loop(0, LANE, step, 0)
+    lax.fori_loop(0, LANE // UNROLL, steps, 0)
     table = table_ref[...]
     for d in range(4):
         for quad in range(2):
@@ -113,7 +121,7 @@
             pltpu.VMEM((8 * 1024, LANE), jnp.float32),
             pltpu.VMEM((16, 1024, LANE), jnp.float32),
         ],
-        compiler_params=PARAMS,
+        compiler_params=vmem(30),
         name="correlate",
     )(*row_blocks, *col_blocks, table)
 
@@ -141,7 +149,7 @@
         finish_kernel,
         out_shape=jax.ShapeDtypeStruct((4, 8 * LAGS, LANE), jnp.bfloat16),
         scratch_shapes=[pltpu.VMEM((8 * LAGS, LANE), jnp.float32)],
-        compiler_params=PARAMS,
+        compiler_params=vmem(24),
         name="finish",
     )(*parts, order)
 
@@ -173,28 +181,42 @@
     white = whiten(spectra)
     planes = [white] + [xor_perm(white, "grp", 2 * d) for d in range(1, 4)]
     row_masks, col_masks = (4, 1), (1, 4)
-    rows = [[white] + [xor_perm(white, "mem", d * m) for d in range(1, 4)] for m in row_masks]
+    order = column_order(member)
+    source, order = lax.optimization_barrier((white, order))
+    rows = [[white, None, None, None], [white, None, None, None]]
+    for d in (1, 3, 2):
+        sent = [xor_perm(source, "mem", d * m) for m in row_masks]
+        source, sent = lax.optimization_barrier((source, sent))
+        rows[0][d], rows[1][d] = sent
     table = lag_table()
-    order = column_order(member)
     factor = math.sqrt(2.0 / (BINS * (COMP // 2)))
-    cols = []
+    planes, rows, table, order = lax.optimization_barrier((planes, rows, table, order))
+    mine = []
     for r in range(2):
-        offset = partners[r, member]
-        plane = offset >> 1
-        mine = jnp.where(
-            plane == 0,
-            planes[0],
-            jnp.where(plane == 1, planes[1], jnp.where(plane == 2, planes[2], planes[3])),
-        )
-        other = xor_perm(mine, "grp", 1)
-        block = jnp.where((offset & 1) == 1, other, mine)
-        far = xor_perm(block, "mem", 16)
-        cols.append(
-            [block]
-            + [xor_perm(block, "mem", e * col_masks[r]) for e in range(1, 4)]
-            + [far]
-            + [xor_perm(far, "mem", e * col_masks[r]) for e in range(1, 4)]
-        )
+        plane = partners[r, member] >> 1
+        mine.append(
+            jnp.where(
+                plane == 0,
+                planes[0],
+                jnp.where(plane == 1, planes[1], jnp.where(plane == 2, planes[2], planes[3])),
+            )
+        )
+    other = [xor_perm(m, "grp", 1) for m in mine]
+    near = [jnp.where((partners[r, member] & 1) == 1, other[r], mine[r]) for r in range(2)]
+    far = [xor_perm(b, "mem", 16) for b in near]
+    cols = [[None] * 8, [None] * 8]
+    sent = [[], []]
+    for block, sources in ((0, near), (4, far)):
+        for r in range(2):
+            cols[r][block] = sources[r]
+        for e in (1, 3, 2):
+            for r in range(2):
+                source = sources[r]
+                if len(sent[r]) >= 2:
+                    source, _ = lax.optimization_barrier((source, sent[r][-2]))
+                cols[r][block + e] = xor_perm(source, "mem", e * col_masks[r])
+                sent[r].append(cols[r][block + e])
+    cols = lax.optimization_barrier(cols)
     parts = []
     for r in range(2):
         sums = correlate(rows[r], cols[r], table, factor)

time: 214 us -> 128 us (0.60)
  Pallas kernels: 65.1 us -> 19.1 us
  waiting for transfers between devices: 79.1 us -> 42.7 us
  other arithmetic: 12.4 us -> 9.81 us
    pallas_call x2, Pallas kernels: 55.2 us -> 13.4 us  [correlate(): pl.pallas_call(body, out_shape=[jax.ShapeDtypeStruct((2, LAG_ROWS, 256),...]
    ppermute x31, waiting for transfers between devices: 79.1 us -> 42.7 us  [xor_perm(): lax.ppermute(array, axis, [(i, i ^ mask) for i in range(lax.axis_size(axi...]
    pallas_call x1, Pallas kernels: 7.38 us -> 4.92 us  [finish(): pl.pallas_call(finish_kernel, out_shape=jax.ShapeDtypeStruct((4, 8 * LAGS...]
  transfers between devices with their start and end apart: 31 -> 31, of which waited for: 15 -> 17; matrix products, arithmetic and copies ran while one was open for 6% -> 8% of each run, Pallas kernels for 26% -> 5%
where the time goes in v2:
time: 128 us; the launch traced here: 127 us
  starting transfers between devices  50.5 us (39%)
  waiting for transfers between devices  42.7 us (33%)
  Pallas kernels  19.1 us (15%)
  other arithmetic  9.81 us (8%)
  between operations  2.86 us (2%)
  local copies, waits for them, and re-layouts  1.6 us (1%)
    ppermute x31, starting transfers between devices, xor_perm(): lax.ppermute(array, axis, [(i, i ^ mask) for i in range(lax.axis_size(axi...  50.5 us
    ppermute x31, waiting for transfers between devices, xor_perm(): lax.ppermute(array, axis, [(i, i ^ mask) for i in range(lax.axis_size(axi...  42.7 us
    pallas_call x2, Pallas kernels, correlate(): pl.pallas_call(body, out_shape=[jax.ShapeDtypeStruct((2, LAG_ROWS, 256),...  13.4 us
    convert_element_type x1, other arithmetic, lag_table(): return jnp.where(lag < LAGS, values, 0.0).astype(jnp.bfloat16)  9.13 us
    pallas_call x1, Pallas kernels, finish(): pl.pallas_call(finish_kernel, out_shape=jax.ShapeDtypeStruct((4, 8 * LAGS...  4.92 us
  transfers between devices with their start and end apart: 31, of which 17 were waited for; matrix products, arithmetic and copies ran while one was open for 8% of the time, Pallas kernels for 5%

profile of v2, /device:TPU:8, one launch (start us, length us, event | category | flops | bytes accessed | tf_op | source)
XLA Modules:
  0.0 126.6 jit_solution(10256855631383487063)
XLA Ops:
  0.1 0.2 iota_compare_fusion
  0.3 0.0 copy-start
  0.3 0.9 copy-done
  1.3 0.8 whiten.1.refs_0_
  2.1 0.3 and_convert_fusion.refs_8_
  2.4 2.3 %collective-permute-start.4 = (bf16[128,8,128]{2,1,0:T(8,128)(2,1)S(1)}, bf16[128,8,128]{2,1,0:T(8,128)(2,1)S(1)}, u32[]{:S(2)}, u32[]{:S(2)}) collective-permute-start(bf16[128,8,128]{2,1,0:T(8,128)(2,1)S(1)} %whiten.1.refs_0_), channel_id=1, source_target_pairs={{0,1},{1,0},{2,3},{3,2},{4,5},{5,4},{6,7},{7,6},{8,9},{9,8},{10,11... | collective-permute-start | bytes 786440 | tf_op jit(solution)/shard_map/ppermute | solution.py:26
  4.7 6.1 %collective-permute-start.2 = (bf16[128,8,128]{2,1,0:T(8,128)(2,1)S(1)}, bf16[128,8,128]{2,1,0:T(8,128)(2,1)S(1)}, u32[]{:S(2)}, u32[]{:S(2)}) collective-permute-start(bf16[128,8,128]{2,1,0:T(8,128)(2,1)S(1)} %whiten.1.refs_0_), channel_id=1, source_target_pairs={{0,192},{32,224},{64,128},{96,160},{128,64},{160,96},{192,0},{224,... | collective-permute-start | bytes 786440 | tf_op jit(solution)/shard_map/ppermute | solution.py:26
  10.7 0.9 collective-permute-start.1
  11.6 1.5 %collective-permute-start = (bf16[128,8,128]{2,1,0:T(8,128)(2,1)S(1)}, bf16[128,8,128]{2,1,0:T(8,128)(2,1)S(1)}, u32[]{:S(2)}, u32[]{:S(2)}) collective-permute-start(bf16[128,8,128]{2,1,0:T(8,128)(2,1)S(1)} %whiten.1.refs_0_), channel_id=1, source_target_pairs={{0,64},{32,96},{64,0},{96,32},{128,192},{160,224},{192,128},{224,1... | collective-permute-start | bytes 786440 | tf_op jit(solution)/shard_map/ppermute | solution.py:26
  13.1 0.0 collective-permute-done.4.refs_1_
  13.1 2.5 %collective-permute-start.6 = (bf16[128,8,128]{2,1,0:T(8,128)(2,1)S(1)}, bf16[128,8,128]{2,1,0:T(8,128)(2,1)S(1)}, u32[]{:S(2)}, u32[]{:S(2)}) collective-permute-start(bf16[128,8,128]{2,1,0:T(8,128)(2,1)S(1)} %whiten.1.refs_0_), channel_id=1, source_target_pairs={{0,3},{1,2},{2,1},{3,0},{4,7},{5,6},{6,5},{7,4},{8,11},{9,10},{10,... | collective-permute-start | bytes 786440 | tf_op jit(solution)/shard_map/ppermute | solution.py:26
  15.6 2.1 %collective-permute-start.5 = (bf16[128,8,128]{2,1,0:T(8,128)(2,1)S(1)}, bf16[128,8,128]{2,1,0:T(8,128)(2,1)S(1)}, u32[]{:S(2)}, u32[]{:S(2)}) collective-permute-start(bf16[128,8,128]{2,1,0:T(8,128)(2,1)S(1)} %whiten.1.refs_0_), channel_id=1, source_target_pairs={{0,12},{1,13},{2,14},{3,15},{4,8},{5,9},{6,10},{7,11},{8,4},{9,5},... | collective-permute-start | bytes 786440 | tf_op jit(solution)/shard_map/ppermute | solution.py:26
  17.7 0.7 constant_dynamic-slice_fusion.1
  19.7 1.1 collective-permute-done.6.refs_3_
  20.8 2.7 %collective-permute-done.5.refs_3_ = bf16[128,8,128]{2,1,0:T(8,128)(2,1)S(1)} collective-permute-done((bf16[128,8,128]{2,1,0:T(8,128)(2,1)S(1)}, bf16[128,8,128]{2,1,0:T(8,128)(2,1)S(1)}, u32[]{:S(2)}, u32[]{:S(2)}) %collective-permute-start.5) | collective-permute-done | bytes 262176 | tf_op jit(solution)/shard_map/ppermute | solution.py:26
  23.4 1.2 collective-permute-start.8
  24.7 2.0 %collective-permute-start.7 = (bf16[128,8,128]{2,1,0:T(8,128)(2,1)S(1)}, bf16[128,8,128]{2,1,0:T(8,128)(2,1)S(1)}, u32[]{:S(2)}, u32[]{:S(2)}) collective-permute-start(bf16[128,8,128]{2,1,0:T(8,128)(2,1)S(1)} %whiten.1.refs_0_), channel_id=1, source_target_pairs={{0,8},{1,9},{2,10},{3,11},{4,12},{5,13},{6,14},{7,15},{8,0},{9,1},... | collective-permute-start | bytes 786440 | tf_op jit(solution)/shard_map/ppermute | solution.py:26
  26.6 9.1 %select_convert_fusion.refs_12_ = bf16[520,1024]{1,0:T(8,128)(2,1)S(1)} fusion(s32[520]{0:T(1024)S(1)} %iota_add_fusion, s32[1024]{0:T(1024)S(1)} %fusion.12, pred[520]{0:T(1024)(128)(4,1)S(1)} %iota_compare_fusion.1, pred[1024]{0:T(1024)(128)(4,1)S(1)} %fusion.10), kind=kLoop, calls=%fused_computation.8 | loop fusion | flops 9584640 | bytes 1072680 | tf_op jit(solution)/shard_map/convert_element_type | solution.py:163
  35.8 0.0 collective-permute-done.7.refs_2_
  35.8 0.0 collective-permute-done.2
  35.8 0.1 collective-permute-done
  35.9 0.1 select_select_fusion
  36.0 0.1 collective-permute-start.17
  36.1 0.5 collective-permute-start.9
  37.2 0.4 collective-permute-done.17
  37.6 1.0 collective-permute-start.21
  39.3 1.2 collective-permute-start.20
  40.6 0.6 collective-permute-start.18
  41.2 0.0 collective-permute-done.9
  41.2 2.1 %collective-permute-start.13 = (bf16[128,8,128]{2,1,0:T(8,128)(2,1)S(1)}, bf16[128,8,128]{2,1,0:T(8,128)(2,1)S(1)}, u32[]{:S(2)}, u32[]{:S(2)}) collective-permute-start(bf16[128,8,128]{2,1,0:T(8,128)(2,1)S(1)} %broadcast_select_fusion.1.refs_4_), channel_id=1, source_target_pairs={{0,16},{1,17},{2,18},{3,19},{4,20},{5,21},{6,22},{7,23},{8,24},{9,... | collective-permute-start | bytes 786440 | tf_op jit(solution)/shard_map/ppermute | solution.py:26
  43.3 2.4 %collective-permute-start.12 = (bf16[128,8,128]{2,1,0:T(8,128)(2,1)S(1)}, bf16[128,8,128]{2,1,0:T(8,128)(2,1)S(1)}, u32[]{:S(2)}, u32[]{:S(2)}) collective-permute-start(bf16[128,8,128]{2,1,0:T(8,128)(2,1)S(1)} %broadcast_select_fusion.1.refs_4_), channel_id=1, source_target_pairs={{0,3},{1,2},{2,1},{3,0},{4,7},{5,6},{6,5},{7,4},{8,11},{9,10},{10,... | collective-permute-start | bytes 786440 | tf_op jit(solution)/shard_map/ppermute | solution.py:26
  45.7 1.1 collective-permute-done.21.refs_8_
  46.8 1.6 %collective-permute-start.10 = (bf16[128,8,128]{2,1,0:T(8,128)(2,1)S(1)}, bf16[128,8,128]{2,1,0:T(8,128)(2,1)S(1)}, u32[]{:S(2)}, u32[]{:S(2)}) collective-permute-start(bf16[128,8,128]{2,1,0:T(8,128)(2,1)S(1)} %broadcast_select_fusion.1.refs_4_), channel_id=1, source_target_pairs={{0,1},{1,0},{2,3},{3,2},{4,5},{5,4},{6,7},{7,6},{8,9},{9,8},{10,11... | collective-permute-start | bytes 786440 | tf_op jit(solution)/shard_map/ppermute | solution.py:26
  48.4 0.3 collective-permute-done.20.refs_7_
  48.7 0.3 collective-permute-start.22
  49.0 0.0 collective-permute-done.18.refs_5_
  49.0 3.0 %collective-permute-start.19 = (bf16[128,8,128]{2,1,0:T(8,128)(2,1)S(1)}, bf16[128,8,128]{2,1,0:T(8,128)(2,1)S(1)}, u32[]{:S(2)}, u32[]{:S(2)}) collective-permute-start(bf16[128,8,128]{2,1,0:T(8,128)(2,1)S(1)} %broadcast_select_fusion.refs_4_), channel_id=1, source_target_pairs={{0,8},{1,9},{2,10},{3,11},{4,12},{5,13},{6,14},{7,15},{8,0},{9,1},... | collective-permute-start | bytes 786440 | tf_op jit(solution)/shard_map/ppermute | solution.py:26
  52.0 0.0 collective-permute-done.13.refs_8_
  52.0 1.3 %collective-permute-start.14 = (bf16[128,8,128]{2,1,0:T(8,128)(2,1)S(1)}, bf16[128,8,128]{2,1,0:T(8,128)(2,1)S(1)}, u32[]{:S(2)}, u32[]{:S(2)}) collective-permute-start(bf16[128,8,128]{2,1,0:T(8,128)(2,1)S(1)} %collective-permute-done.13.refs_8_), channel_id=1, source_target_pairs={{0,1},{1,0},{2,3},{3,2},{4,5},{5,4},{6,7},{7,6},{8,9},{9,8},{10,11... | collective-permute-start | bytes 786440 | tf_op jit(solution)/shard_map/ppermute | solution.py:26
  53.3 0.2 collective-permute-done.10.refs_5_
  53.6 2.6 %collective-permute-start.11 = (bf16[128,8,128]{2,1,0:T(8,128)(2,1)S(1)}, bf16[128,8,128]{2,1,0:T(8,128)(2,1)S(1)}, u32[]{:S(2)}, u32[]{:S(2)}) collective-permute-start(bf16[128,8,128]{2,1,0:T(8,128)(2,1)S(1)} %broadcast_select_fusion.1.refs_4_), channel_id=1, source_target_pairs={{0,2},{1,3},{2,0},{3,1},{4,6},{5,7},{6,4},{7,5},{8,10},{9,11},{10,... | collective-permute-start | bytes 786440 | tf_op jit(solution)/shard_map/ppermute | solution.py:26
  56.2 1.8 %collective-permute-done.22.refs_9_ = bf16[128,8,128]{2,1,0:T(8,128)(2,1)S(1)} collective-permute-done((bf16[128,8,128]{2,1,0:T(8,128)(2,1)S(1)}, bf16[128,8,128]{2,1,0:T(8,128)(2,1)S(1)}, u32[]{:S(2)}, u32[]{:S(2)}) %collective-permute-start.22) | collective-permute-done | bytes 262176 | tf_op jit(solution)/shard_map/ppermute | solution.py:26
  58.0 2.5 %collective-permute-start.23 = (bf16[128,8,128]{2,1,0:T(8,128)(2,1)S(1)}, bf16[128,8,128]{2,1,0:T(8,128)(2,1)S(1)}, u32[]{:S(2)}, u32[]{:S(2)}) collective-permute-start(bf16[128,8,128]{2,1,0:T(8,128)(2,1)S(1)} %collective-permute-done.21.refs_8_), channel_id=1, source_target_pairs={{0,8},{1,9},{2,10},{3,11},{4,12},{5,13},{6,14},{7,15},{8,0},{9,1},... | collective-permute-start | bytes 786440 | tf_op jit(solution)/shard_map/ppermute | solution.py:26
  60.4 4.5 %collective-permute-done.19.refs_6_ = bf16[128,8,128]{2,1,0:T(8,128)(2,1)S(1)} collective-permute-done((bf16[128,8,128]{2,1,0:T(8,128)(2,1)S(1)}, bf16[128,8,128]{2,1,0:T(8,128)(2,1)S(1)}, u32[]{:S(2)}, u32[]{:S(2)}) %collective-permute-start.19) | collective-permute-done | bytes 262176 | tf_op jit(solution)/shard_map/ppermute | solution.py:26
  64.9 1.4 %collective-permute-start.24 = (bf16[128,8,128]{2,1,0:T(8,128)(2,1)S(1)}, bf16[128,8,128]{2,1,0:T(8,128)(2,1)S(1)}, u32[]{:S(2)}, u32[]{:S(2)}) collective-permute-start(bf16[128,8,128]{2,1,0:T(8,128)(2,1)S(1)} %collective-permute-done.21.refs_8_), channel_id=1, source_target_pairs={{0,12},{1,13},{2,14},{3,15},{4,8},{5,9},{6,10},{7,11},{8,4},{9,5},... | collective-permute-start | bytes 786440 | tf_op jit(solution)/shard_map/ppermute | solution.py:26
  66.3 2.0 %collective-permute-start.15 = (bf16[128,8,128]{2,1,0:T(8,128)(2,1)S(1)}, bf16[128,8,128]{2,1,0:T(8,128)(2,1)S(1)}, u32[]{:S(2)}, u32[]{:S(2)}) collective-permute-start(bf16[128,8,128]{2,1,0:T(8,128)(2,1)S(1)} %collective-permute-done.13.refs_8_), channel_id=1, source_target_pairs={{0,2},{1,3},{2,0},{3,1},{4,6},{5,7},{6,4},{7,5},{8,10},{9,11},{10,... | collective-permute-start | bytes 786440 | tf_op jit(solution)/shard_map/ppermute | solution.py:26
  68.3 0.3 collective-permute-start.16
  68.6 5.3 %collective-permute-done.24.refs_11_ = bf16[128,8,128]{2,1,0:T(8,128)(2,1)S(1)} collective-permute-done((bf16[128,8,128]{2,1,0:T(8,128)(2,1)S(1)}, bf16[128,8,128]{2,1,0:T(8,128)(2,1)S(1)}, u32[]{:S(2)}, u32[]{:S(2)}) %collective-permute-start.24) | collective-permute-done | bytes 262176 | tf_op jit(solution)/shard_map/ppermute | solution.py:26
  73.9 0.3 collective-permute-done.15.refs_10_
  74.2 3.6 %collective-permute-done.16.refs_11_ = bf16[128,8,128]{2,1,0:T(8,128)(2,1)S(1)} collective-permute-done((bf16[128,8,128]{2,1,0:T(8,128)(2,1)S(1)}, bf16[128,8,128]{2,1,0:T(8,128)(2,1)S(1)}, u32[]{:S(2)}, u32[]{:S(2)}) %collective-permute-start.16) | collective-permute-done | bytes 262176 | tf_op jit(solution)/shard_map/ppermute | solution.py:26
  77.9 6.7 %correlate.2 = (bf16[2,520,256]{2,1,0:T(8,128)(2,1)S(1)}, bf16[2,520,256]{2,1,0:T(8,128)(2,1)S(1)}, bf16[2,520,256]{2,1,0:T(8,128)(2,1)S(1)}, bf16[2,520,256]{2,1,0:T(8,128)(2,1)S(1)}) custom-call(bf16[128,8,128]{2,1,0:T(8,128)(2,1)S(1)} %whiten.1.refs_0_, bf16[128,8,128]{2,1,0:T(8,128)(2,1)S(1)} %collective-permute-done.3.refs_1_, ...), custom_call_target="tpu_custom_call" | custom-call | tf_op jit(solution)/shard_map/correlate/pallas_call | solution.py:117
  84.6 0.6 collective-permute-start.25
  85.2 3.0 %collective-permute-start.26 = (bf16[2,520,256]{2,1,0:T(8,128)(2,1)S(1)}, bf16[2,520,256]{2,1,0:T(8,128)(2,1)S(1)}, u32[]{:S(2)}, u32[]{:S(2)}) collective-permute-start(bf16[2,520,256]{2,1,0:T(8,128)(2,1)S(1)} %get-tuple-element.98), channel_id=1, source_target_pairs={{0,8},{1,9},{2,10},{3,11},{4,12},{5,13},{6,14},{7,15},{8,0},{9,1},... | collective-permute-start | bytes 1597448 | tf_op jit(solution)/shard_map/ppermute | solution.py:26
  88.2 1.1 collective-permute-start.27
  89.4 6.7 %correlate.3 = (bf16[2,520,256]{2,1,0:T(8,128)(2,1)S(1)}, bf16[2,520,256]{2,1,0:T(8,128)(2,1)S(1)}, bf16[2,520,256]{2,1,0:T(8,128)(2,1)S(1)}, bf16[2,520,256]{2,1,0:T(8,128)(2,1)S(1)}) custom-call(bf16[128,8,128]{2,1,0:T(8,128)(2,1)S(1)} %whiten.1.refs_0_, bf16[128,8,128]{2,1,0:T(8,128)(2,1)S(1)} %collective-permute-done.4.refs_1_, ...), custom_call_target="tpu_custom_call" | custom-call | tf_op jit(solution)/shard_map/correlate/pallas_call | solution.py:117
  96.1 1.7 %collective-permute-start.28 = (bf16[2,520,256]{2,1,0:T(8,128)(2,1)S(1)}, bf16[2,520,256]{2,1,0:T(8,128)(2,1)S(1)}, u32[]{:S(2)}, u32[]{:S(2)}) collective-permute-start(bf16[2,520,256]{2,1,0:T(8,128)(2,1)S(1)} %get-tuple-element.113), channel_id=1, source_target_pairs={{0,1},{1,0},{2,3},{3,2},{4,5},{5,4},{6,7},{7,6},{8,9},{9,8},{10,11... | collective-permute-start | bytes 1597448 | tf_op jit(solution)/shard_map/ppermute | solution.py:26
  97.7 1.4 %collective-permute-start.29 = (bf16[2,520,256]{2,1,0:T(8,128)(2,1)S(1)}, bf16[2,520,256]{2,1,0:T(8,128)(2,1)S(1)}, u32[]{:S(2)}, u32[]{:S(2)}) collective-permute-start(bf16[2,520,256]{2,1,0:T(8,128)(2,1)S(1)} %get-tuple-element.114), channel_id=1, source_target_pairs={{0,2},{1,3},{2,0},{3,1},{4,6},{5,7},{6,4},{7,5},{8,10},{9,11},{10,... | collective-permute-start | bytes 1597448 | tf_op jit(solution)/shard_map/ppermute | solution.py:26
  99.1 0.6 collective-permute-done.25.refs_1_
  99.7 1.3 collective-permute-start.30
  101.0 9.7 %collective-permute-done.26.refs_2_ = bf16[2,520,256]{2,1,0:T(8,128)(2,1)S(1)} collective-permute-done((bf16[2,520,256]{2,1,0:T(8,128)(2,1)S(1)}, bf16[2,520,256]{2,1,0:T(8,128)(2,1)S(1)}, u32[]{:S(2)}, u32[]{:S(2)}) %collective-permute-start.26) | collective-permute-done | bytes 532512 | tf_op jit(solution)/shard_map/ppermute | solution.py:26
  110.7 2.7 %collective-permute-done.27.refs_3_ = bf16[2,520,256]{2,1,0:T(8,128)(2,1)S(1)} collective-permute-done((bf16[2,520,256]{2,1,0:T(8,128)(2,1)S(1)}, bf16[2,520,256]{2,1,0:T(8,128)(2,1)S(1)}, u32[]{:S(2)}, u32[]{:S(2)}) %collective-permute-start.27) | collective-permute-done | bytes 532512 | tf_op jit(solution)/shard_map/ppermute | solution.py:26
  113.4 7.0 %collective-permute-done.29.refs_6_ = bf16[2,520,256]{2,1,0:T(8,128)(2,1)S(1)} collective-permute-done((bf16[2,520,256]{2,1,0:T(8,128)(2,1)S(1)}, bf16[2,520,256]{2,1,0:T(8,128)(2,1)S(1)}, u32[]{:S(2)}, u32[]{:S(2)}) %collective-permute-start.29) | collective-permute-done | bytes 532512 | tf_op jit(solution)/shard_map/ppermute | solution.py:26
  120.4 1.4 %collective-permute-done.30.refs_7_ = bf16[2,520,256]{2,1,0:T(8,128)(2,1)S(1)} collective-permute-done((bf16[2,520,256]{2,1,0:T(8,128)(2,1)S(1)}, bf16[2,520,256]{2,1,0:T(8,128)(2,1)S(1)}, u32[]{:S(2)}, u32[]{:S(2)}) %collective-permute-start.30) | collective-permute-done | bytes 532512 | tf_op jit(solution)/shard_map/ppermute | solution.py:26
  121.7 4.9 %finish.1 = bf16[4,4104,128]{2,1,0:T(8,128)(2,1)} custom-call(bf16[2,520,256]{2,1,0:T(8,128)(2,1)S(1)} %get-tuple-element.96.refs_0_, bf16[2,520,256]{2,1,0:T(8,128)(2,1)S(1)} %collective-permute-done.25.refs_1_, bf16[2,520,256]{2,1,0:T(8,128)(2,1)S(1)} %collective-permute-done.26.refs_2_, bf16[2,520,256]{2,1,0:T(8,128)(2,1)S(1)} %collective-permute-done.27.refs_3_, ...), custom_call_target="tpu_custom_call" | custom-call | tf_op jit(solution)/shard_map/finish/pallas_call | solution.py:148
  (21 shorter events, 0.2 us)
Async XLA Ops:
  0.0 17.7 %copy-start.1 = (s32[2,32]{1,0:T(2,128)S(1)}, s32[2,32]{1,0:T(2,128)}, u32[]{:S(2)}) copy-start(s32[2,32]{1,0:T(2,128)} %param.3) | copy-start | bytes 772
  0.3 1.0 copy-start
  2.4 10.7 %collective-permute-start.4 = (bf16[128,8,128]{2,1,0:T(8,128)(2,1)S(1)}, bf16[128,8,128]{2,1,0:T(8,128)(2,1)S(1)}, u32[]{:S(2)}, u32[]{:S(2)}) collective-permute-start(bf16[128,8,128]{2,1,0:T(8,128)(2,1)S(1)} %whiten.1.refs_0_), channel_id=1, source_target_pairs={{0,1},{1,0},{2,3},{3,2},{4,5},{5,4},{6,7},{7,6},{8,9},{9,8},{10,11... | collective-permute-start | bytes 786440 | tf_op jit(solution)/shard_map/ppermute | solution.py:26
  4.7 8.4 %collective-permute-start.3 = (bf16[128,8,128]{2,1,0:T(8,128)(2,1)S(1)}, bf16[128,8,128]{2,1,0:T(8,128)(2,1)S(1)}, u32[]{:S(2)}, u32[]{:S(2)}) collective-permute-start(bf16[128,8,128]{2,1,0:T(8,128)(2,1)S(1)} %whiten.1.refs_0_), channel_id=1, source_target_pairs={{0,4},{1,5},{2,6},{3,7},{4,0},{5,1},{6,2},{7,3},{8,12},{9,13},{10,... | collective-permute-start | bytes 786440 | tf_op jit(solution)/shard_map/ppermute | solution.py:26
  4.7 31.1 %collective-permute-start.2 = (bf16[128,8,128]{2,1,0:T(8,128)(2,1)S(1)}, bf16[128,8,128]{2,1,0:T(8,128)(2,1)S(1)}, u32[]{:S(2)}, u32[]{:S(2)}) collective-permute-start(bf16[128,8,128]{2,1,0:T(8,128)(2,1)S(1)} %whiten.1.refs_0_), channel_id=1, source_target_pairs={{0,192},{32,224},{64,128},{96,160},{128,64},{160,96},{192,0},{224,... | collective-permute-start | bytes 786440 | tf_op jit(solution)/shard_map/ppermute | solution.py:26
  10.7 25.1 %collective-permute-start.1 = (bf16[128,8,128]{2,1,0:T(8,128)(2,1)S(1)}, bf16[128,8,128]{2,1,0:T(8,128)(2,1)S(1)}, u32[]{:S(2)}, u32[]{:S(2)}) collective-permute-start(bf16[128,8,128]{2,1,0:T(8,128)(2,1)S(1)} %whiten.1.refs_0_), channel_id=1, source_target_pairs={{0,128},{32,160},{64,192},{96,224},{128,0},{160,32},{192,64},{224,... | collective-permute-start | bytes 786440 | tf_op jit(solution)/shard_map/ppermute | solution.py:26
  11.6 24.3 %collective-permute-start = (bf16[128,8,128]{2,1,0:T(8,128)(2,1)S(1)}, bf16[128,8,128]{2,1,0:T(8,128)(2,1)S(1)}, u32[]{:S(2)}, u32[]{:S(2)}) collective-permute-start(bf16[128,8,128]{2,1,0:T(8,128)(2,1)S(1)} %whiten.1.refs_0_), channel_id=1, source_target_pairs={{0,64},{32,96},{64,0},{96,32},{128,192},{160,224},{192,128},{224,1... | collective-permute-start | bytes 786440 | tf_op jit(solution)/shard_map/ppermute | solution.py:26
  13.1 7.7 %collective-permute-start.6 = (bf16[128,8,128]{2,1,0:T(8,128)(2,1)S(1)}, bf16[128,8,128]{2,1,0:T(8,128)(2,1)S(1)}, u32[]{:S(2)}, u32[]{:S(2)}) collective-permute-start(bf16[128,8,128]{2,1,0:T(8,128)(2,1)S(1)} %whiten.1.refs_0_), channel_id=1, source_target_pairs={{0,3},{1,2},{2,1},{3,0},{4,7},{5,6},{6,5},{7,4},{8,11},{9,10},{10,... | collective-permute-start | bytes 786440 | tf_op jit(solution)/shard_map/ppermute | solution.py:26
  15.6 7.9 %collective-permute-start.5 = (bf16[128,8,128]{2,1,0:T(8,128)(2,1)S(1)}, bf16[128,8,128]{2,1,0:T(8,128)(2,1)S(1)}, u32[]{:S(2)}, u32[]{:S(2)}) collective-permute-start(bf16[128,8,128]{2,1,0:T(8,128)(2,1)S(1)} %whiten.1.refs_0_), channel_id=1, source_target_pairs={{0,12},{1,13},{2,14},{3,15},{4,8},{5,9},{6,10},{7,11},{8,4},{9,5},... | collective-permute-start | bytes 786440 | tf_op jit(solution)/shard_map/ppermute | solution.py:26
  23.4 12.3 %collective-permute-start.8 = (bf16[128,8,128]{2,1,0:T(8,128)(2,1)S(1)}, bf16[128,8,128]{2,1,0:T(8,128)(2,1)S(1)}, u32[]{:S(2)}, u32[]{:S(2)}) collective-permute-start(bf16[128,8,128]{2,1,0:T(8,128)(2,1)S(1)} %whiten.1.refs_0_), channel_id=1, source_target_pairs={{0,2},{1,3},{2,0},{3,1},{4,6},{5,7},{6,4},{7,5},{8,10},{9,11},{10,... | collective-permute-start | bytes 786440 | tf_op jit(solution)/shard_map/ppermute | solution.py:26
  24.7 11.1 %collective-permute-start.7 = (bf16[128,8,128]{2,1,0:T(8,128)(2,1)S(1)}, bf16[128,8,128]{2,1,0:T(8,128)(2,1)S(1)}, u32[]{:S(2)}, u32[]{:S(2)}) collective-permute-start(bf16[128,8,128]{2,1,0:T(8,128)(2,1)S(1)} %whiten.1.refs_0_), channel_id=1, source_target_pairs={{0,8},{1,9},{2,10},{3,11},{4,12},{5,13},{6,14},{7,15},{8,0},{9,1},... | collective-permute-start | bytes 786440 | tf_op jit(solution)/shard_map/ppermute | solution.py:26
  36.0 1.6 %collective-permute-start.17 = (bf16[128,8,128]{2,1,0:T(8,128)(2,1)S(1)}, bf16[128,8,128]{2,1,0:T(8,128)(2,1)S(1)}, u32[]{:S(2)}, u32[]{:S(2)}) collective-permute-start(bf16[128,8,128]{2,1,0:T(8,128)(2,1)S(1)} %get-tuple-element.117), channel_id=1, source_target_pairs={{0,32},{32,0},{64,96},{96,64},{128,160},{160,128},{192,224},{224,1... | collective-permute-start | bytes 786440 | tf_op jit(solution)/shard_map/ppermute | solution.py:26
  36.1 5.1 %collective-permute-start.9 = (bf16[128,8,128]{2,1,0:T(8,128)(2,1)S(1)}, bf16[128,8,128]{2,1,0:T(8,128)(2,1)S(1)}, u32[]{:S(2)}, u32[]{:S(2)}) collective-permute-start(bf16[128,8,128]{2,1,0:T(8,128)(2,1)S(1)} %get-tuple-element.118), channel_id=1, source_target_pairs={{0,32},{32,0},{64,96},{96,64},{128,160},{160,128},{192,224},{224,1... | collective-permute-start | bytes 786440 | tf_op jit(solution)/shard_map/ppermute | solution.py:26
  37.6 9.2 %collective-permute-start.21 = (bf16[128,8,128]{2,1,0:T(8,128)(2,1)S(1)}, bf16[128,8,128]{2,1,0:T(8,128)(2,1)S(1)}, u32[]{:S(2)}, u32[]{:S(2)}) collective-permute-start(bf16[128,8,128]{2,1,0:T(8,128)(2,1)S(1)} %broadcast_select_fusion.refs_4_), channel_id=1, source_target_pairs={{0,16},{1,17},{2,18},{3,19},{4,20},{5,21},{6,22},{7,23},{8,24},{9,... | collective-permute-start | bytes 786440 | tf_op jit(solution)/shard_map/ppermute | solution.py:26
  39.3 9.4 %collective-permute-start.20 = (bf16[128,8,128]{2,1,0:T(8,128)(2,1)S(1)}, bf16[128,8,128]{2,1,0:T(8,128)(2,1)S(1)}, u32[]{:S(2)}, u32[]{:S(2)}) collective-permute-start(bf16[128,8,128]{2,1,0:T(8,128)(2,1)S(1)} %broadcast_select_fusion.refs_4_), channel_id=1, source_target_pairs={{0,12},{1,13},{2,14},{3,15},{4,8},{5,9},{6,10},{7,11},{8,4},{9,5},... | collective-permute-start | bytes 786440 | tf_op jit(solution)/shard_map/ppermute | solution.py:26
  40.6 8.4 %collective-permute-start.18 = (bf16[128,8,128]{2,1,0:T(8,128)(2,1)S(1)}, bf16[128,8,128]{2,1,0:T(8,128)(2,1)S(1)}, u32[]{:S(2)}, u32[]{:S(2)}) collective-permute-start(bf16[128,8,128]{2,1,0:T(8,128)(2,1)S(1)} %broadcast_select_fusion.refs_4_), channel_id=1, source_target_pairs={{0,4},{1,5},{2,6},{3,7},{4,0},{5,1},{6,2},{7,3},{8,12},{9,13},{10,... | collective-permute-start | bytes 786440 | tf_op jit(solution)/shard_map/ppermute | solution.py:26
  41.2 10.8 %collective-permute-start.13 = (bf16[128,8,128]{2,1,0:T(8,128)(2,1)S(1)}, bf16[128,8,128]{2,1,0:T(8,128)(2,1)S(1)}, u32[]{:S(2)}, u32[]{:S(2)}) collective-permute-start(bf16[128,8,128]{2,1,0:T(8,128)(2,1)S(1)} %broadcast_select_fusion.1.refs_4_), channel_id=1, source_target_pairs={{0,16},{1,17},{2,18},{3,19},{4,20},{5,21},{6,22},{7,23},{8,24},{9,... | collective-permute-start | bytes 786440 | tf_op jit(solution)/shard_map/ppermute | solution.py:26
  43.3 8.7 %collective-permute-start.12 = (bf16[128,8,128]{2,1,0:T(8,128)(2,1)S(1)}, bf16[128,8,128]{2,1,0:T(8,128)(2,1)S(1)}, u32[]{:S(2)}, u32[]{:S(2)}) collective-permute-start(bf16[128,8,128]{2,1,0:T(8,128)(2,1)S(1)} %broadcast_select_fusion.1.refs_4_), channel_id=1, source_target_pairs={{0,3},{1,2},{2,1},{3,0},{4,7},{5,6},{6,5},{7,4},{8,11},{9,10},{10,... | collective-permute-start | bytes 786440 | tf_op jit(solution)/shard_map/ppermute | solution.py:26
  46.8 6.7 %collective-permute-start.10 = (bf16[128,8,128]{2,1,0:T(8,128)(2,1)S(1)}, bf16[128,8,128]{2,1,0:T(8,128)(2,1)S(1)}, u32[]{:S(2)}, u32[]{:S(2)}) collective-permute-start(bf16[128,8,128]{2,1,0:T(8,128)(2,1)S(1)} %broadcast_select_fusion.1.refs_4_), channel_id=1, source_target_pairs={{0,1},{1,0},{2,3},{3,2},{4,5},{5,4},{6,7},{7,6},{8,9},{9,8},{10,11... | collective-permute-start | bytes 786440 | tf_op jit(solution)/shard_map/ppermute | solution.py:26
  48.7 9.2 %collective-permute-start.22 = (bf16[128,8,128]{2,1,0:T(8,128)(2,1)S(1)}, bf16[128,8,128]{2,1,0:T(8,128)(2,1)S(1)}, u32[]{:S(2)}, u32[]{:S(2)}) collective-permute-start(bf16[128,8,128]{2,1,0:T(8,128)(2,1)S(1)} %collective-permute-done.21.refs_8_), channel_id=1, source_target_pairs={{0,4},{1,5},{2,6},{3,7},{4,0},{5,1},{6,2},{7,3},{8,12},{9,13},{10,... | collective-permute-start | bytes 786440 | tf_op jit(solution)/shard_map/ppermute | solution.py:26
  49.0 15.9 %collective-permute-start.19 = (bf16[128,8,128]{2,1,0:T(8,128)(2,1)S(1)}, bf16[128,8,128]{2,1,0:T(8,128)(2,1)S(1)}, u32[]{:S(2)}, u32[]{:S(2)}) collective-permute-start(bf16[128,8,128]{2,1,0:T(8,128)(2,1)S(1)} %broadcast_select_fusion.refs_4_), channel_id=1, source_target_pairs={{0,8},{1,9},{2,10},{3,11},{4,12},{5,13},{6,14},{7,15},{8,0},{9,1},... | collective-permute-start | bytes 786440 | tf_op jit(solution)/shard_map/ppermute | solution.py:26
  52.0 14.3 %collective-permute-start.14 = (bf16[128,8,128]{2,1,0:T(8,128)(2,1)S(1)}, bf16[128,8,128]{2,1,0:T(8,128)(2,1)S(1)}, u32[]{:S(2)}, u32[]{:S(2)}) collective-permute-start(bf16[128,8,128]{2,1,0:T(8,128)(2,1)S(1)} %collective-permute-done.13.refs_8_), channel_id=1, source_target_pairs={{0,1},{1,0},{2,3},{3,2},{4,5},{5,4},{6,7},{7,6},{8,9},{9,8},{10,11... | collective-permute-start | bytes 786440 | tf_op jit(solution)/shard_map/ppermute | solution.py:26
  53.6 14.7 %collective-permute-start.11 = (bf16[128,8,128]{2,1,0:T(8,128)(2,1)S(1)}, bf16[128,8,128]{2,1,0:T(8,128)(2,1)S(1)}, u32[]{:S(2)}, u32[]{:S(2)}) collective-permute-start(bf16[128,8,128]{2,1,0:T(8,128)(2,1)S(1)} %broadcast_select_fusion.1.refs_4_), channel_id=1, source_target_pairs={{0,2},{1,3},{2,0},{3,1},{4,6},{5,7},{6,4},{7,5},{8,10},{9,11},{10,... | collective-permute-start | bytes 786440 | tf_op jit(solution)/shard_map/ppermute | solution.py:26
  58.0 10.7 %collective-permute-start.23 = (bf16[128,8,128]{2,1,0:T(8,128)(2,1)S(1)}, bf16[128,8,128]{2,1,0:T(8,128)(2,1)S(1)}, u32[]{:S(2)}, u32[]{:S(2)}) collective-permute-start(bf16[128,8,128]{2,1,0:T(8,128)(2,1)S(1)} %collective-permute-done.21.refs_8_), channel_id=1, source_target_pairs={{0,8},{1,9},{2,10},{3,11},{4,12},{5,13},{6,14},{7,15},{8,0},{9,1},... | collective-permute-start | bytes 786440 | tf_op jit(solution)/shard_map/ppermute | solution.py:26
  64.9 9.1 %collective-permute-start.24 = (bf16[128,8,128]{2,1,0:T(8,128)(2,1)S(1)}, bf16[128,8,128]{2,1,0:T(8,128)(2,1)S(1)}, u32[]{:S(2)}, u32[]{:S(2)}) collective-permute-start(bf16[128,8,128]{2,1,0:T(8,128)(2,1)S(1)} %collective-permute-done.21.refs_8_), channel_id=1, source_target_pairs={{0,12},{1,13},{2,14},{3,15},{4,8},{5,9},{6,10},{7,11},{8,4},{9,5},... | collective-permute-start | bytes 786440 | tf_op jit(solution)/shard_map/ppermute | solution.py:26
  66.3 8.0 %collective-permute-start.15 = (bf16[128,8,128]{2,1,0:T(8,128)(2,1)S(1)}, bf16[128,8,128]{2,1,0:T(8,128)(2,1)S(1)}, u32[]{:S(2)}, u32[]{:S(2)}) collective-permute-start(bf16[128,8,128]{2,1,0:T(8,128)(2,1)S(1)} %collective-permute-done.13.refs_8_), channel_id=1, source_target_pairs={{0,2},{1,3},{2,0},{3,1},{4,6},{5,7},{6,4},{7,5},{8,10},{9,11},{10,... | collective-permute-start | bytes 786440 | tf_op jit(solution)/shard_map/ppermute | solution.py:26
  68.3 9.6 %collective-permute-start.16 = (bf16[128,8,128]{2,1,0:T(8,128)(2,1)S(1)}, bf16[128,8,128]{2,1,0:T(8,128)(2,1)S(1)}, u32[]{:S(2)}, u32[]{:S(2)}) collective-permute-start(bf16[128,8,128]{2,1,0:T(8,128)(2,1)S(1)} %collective-permute-done.13.refs_8_), channel_id=1, source_target_pairs={{0,3},{1,2},{2,1},{3,0},{4,7},{5,6},{6,5},{7,4},{8,11},{9,10},{10,... | collective-permute-start | bytes 786440 | tf_op jit(solution)/shard_map/ppermute | solution.py:26
  84.6 15.1 %collective-permute-start.25 = (bf16[2,520,256]{2,1,0:T(8,128)(2,1)S(1)}, bf16[2,520,256]{2,1,0:T(8,128)(2,1)S(1)}, u32[]{:S(2)}, u32[]{:S(2)}) collective-permute-start(bf16[2,520,256]{2,1,0:T(8,128)(2,1)S(1)} %get-tuple-element.97), channel_id=1, source_target_pairs={{0,4},{1,5},{2,6},{3,7},{4,0},{5,1},{6,2},{7,3},{8,12},{9,13},{10,... | collective-permute-start | bytes 1597448 | tf_op jit(solution)/shard_map/ppermute | solution.py:26
  85.2 25.5 %collective-permute-start.26 = (bf16[2,520,256]{2,1,0:T(8,128)(2,1)S(1)}, bf16[2,520,256]{2,1,0:T(8,128)(2,1)S(1)}, u32[]{:S(2)}, u32[]{:S(2)}) collective-permute-start(bf16[2,520,256]{2,1,0:T(8,128)(2,1)S(1)} %get-tuple-element.98), channel_id=1, source_target_pairs={{0,8},{1,9},{2,10},{3,11},{4,12},{5,13},{6,14},{7,15},{8,0},{9,1},... | collective-permute-start | bytes 1597448 | tf_op jit(solution)/shard_map/ppermute | solution.py:26
  88.2 25.2 %collective-permute-start.27 = (bf16[2,520,256]{2,1,0:T(8,128)(2,1)S(1)}, bf16[2,520,256]{2,1,0:T(8,128)(2,1)S(1)}, u32[]{:S(2)}, u32[]{:S(2)}) collective-permute-start(bf16[2,520,256]{2,1,0:T(8,128)(2,1)S(1)} %get-tuple-element.99), channel_id=1, source_target_pairs={{0,12},{1,13},{2,14},{3,15},{4,8},{5,9},{6,10},{7,11},{8,4},{9,5},... | collective-permute-start | bytes 1597448 | tf_op jit(solution)/shard_map/ppermute | solution.py:26
  96.1 17.3 %collective-permute-start.28 = (bf16[2,520,256]{2,1,0:T(8,128)(2,1)S(1)}, bf16[2,520,256]{2,1,0:T(8,128)(2,1)S(1)}, u32[]{:S(2)}, u32[]{:S(2)}) collective-permute-start(bf16[2,520,256]{2,1,0:T(8,128)(2,1)S(1)} %get-tuple-element.113), channel_id=1, source_target_pairs={{0,1},{1,0},{2,3},{3,2},{4,5},{5,4},{6,7},{7,6},{8,9},{9,8},{10,11... | collective-permute-start | bytes 1597448 | tf_op jit(solution)/shard_map/ppermute | solution.py:26
  97.7 22.6 %collective-permute-start.29 = (bf16[2,520,256]{2,1,0:T(8,128)(2,1)S(1)}, bf16[2,520,256]{2,1,0:T(8,128)(2,1)S(1)}, u32[]{:S(2)}, u32[]{:S(2)}) collective-permute-start(bf16[2,520,256]{2,1,0:T(8,128)(2,1)S(1)} %get-tuple-element.114), channel_id=1, source_target_pairs={{0,2},{1,3},{2,0},{3,1},{4,6},{5,7},{6,4},{7,5},{8,10},{9,11},{10,... | collective-permute-start | bytes 1597448 | tf_op jit(solution)/shard_map/ppermute | solution.py:26
  99.7 22.0 %collective-permute-start.30 = (bf16[2,520,256]{2,1,0:T(8,128)(2,1)S(1)}, bf16[2,520,256]{2,1,0:T(8,128)(2,1)S(1)}, u32[]{:S(2)}, u32[]{:S(2)}) collective-permute-start(bf16[2,520,256]{2,1,0:T(8,128)(2,1)S(1)} %get-tuple-element.115), channel_id=1, source_target_pairs={{0,3},{1,2},{2,1},{3,0},{4,7},{5,6},{6,5},{7,4},{8,11},{9,10},{10,... | collective-permute-start | bytes 1597448 | tf_op jit(solution)/shard_map/ppermute | solution.py:26

commit v3 on v2

--- a/solution.py
+++ b/solution.py
@@ -50,14 +50,49 @@
         whiten_kernel,
         out_shape=jax.ShapeDtypeStruct((LANE, CH, LANE), jnp.bfloat16),
         scratch_shapes=[pltpu.VMEM((LANE * CH, LANE), jnp.float32)],
-        compiler_params=vmem(12),
+        compiler_params=vmem(10),
         name="whiten",
     )(spectra)
 
 
+def pick_kernel(member_ref, partners_ref, *refs):
+    planes, out_ref = refs[:4], refs[4]
+    for r in range(2):
+        distance = partners_ref[r, member_ref[0]] >> 1
+        for d in range(4):
+
+            @pl.when(distance == d)
+            def _():
+                out_ref[r] = planes[d][...]
+
+
+def merge_kernel(member_ref, partners_ref, mine_ref, other_ref, out_ref):
+    for r in range(2):
+        swap = partners_ref[r, member_ref[0]] & 1
+
+        @pl.when(swap == 1)
+        def _():
+            out_ref[r] = other_ref[r]
+
+        @pl.when(swap == 0)
+        def _():
+            out_ref[r] = mine_ref[r]
+
+
+def choose(kernel, name, member, partners, arrays):
+    smem, whole = pl.BlockSpec(memory_space=pltpu.SMEM), pl.BlockSpec(memory_space=pltpu.VMEM)
+    return pl.pallas_call(
+        kernel,
+        in_specs=[smem, smem] + [whole] * len(arrays),
+        out_shape=jax.ShapeDtypeStruct((2, LANE, CH, LANE), jnp.bfloat16),
+        compiler_params=vmem(10),
+        name=name,
+    )(member, partners, *arrays)
+
+
 def corr_kernel(factor, *refs):
-    row_refs, col_refs, table_ref = refs[:4], refs[4:12], refs[12]
-    out_refs, rows, cross = refs[13:17], refs[17], refs[18]
+    row_refs, col_refs, table_ref = refs[:4], refs[4:8], refs[8]
+    out_refs, rows, cross = refs[9:13], refs[13], refs[14]
     lane = lax.broadcasted_iota(jnp.int32, (CH * LANE, LANE), 1)
     imag = lane // 16 % 2 == 1
     for d in range(4):
@@ -73,7 +108,9 @@
     blank = jnp.zeros((64, LANE), jnp.bfloat16)
 
     def step(g):
-        cols = jnp.concatenate([c[g].astype(jnp.float32) for c in col_refs], 0).astype(jnp.bfloat16)
+        cols = jnp.concatenate(
+            [c[n, g].astype(jnp.float32) for c in col_refs for n in range(2)], 0
+        ).astype(jnp.bfloat16)
         rhs = jnp.concatenate(
             [jnp.concatenate([cols, blank], 1), jnp.concatenate([blank, cols], 1)], 0
         )
@@ -121,7 +158,12 @@
             pltpu.VMEM((8 * 1024, LANE), jnp.float32),
             pltpu.VMEM((16, 1024, LANE), jnp.float32),
         ],
-        compiler_params=vmem(30),
+        compiler_params=vmem(24),
+        cost_estimate=pl.CostEstimate(
+            flops=2 * LANE * LANE * 256 * LANE + 16 * LAG_ROWS * 1024 * 256,
+            transcendentals=0,
+            bytes_accessed=7 * 1024 * 1024,
+        ),
         name="correlate",
     )(*row_blocks, *col_blocks, table)
 
@@ -132,10 +174,8 @@
         for half in range(2):
             i = i2 * 2 + half
             quad, at = i // 4, (i // 2) % 2 * LANE
+            wide = jnp.concatenate([p[quad, :, at : at + LANE] for p in parts], 1)
             for r in range(2):
-                wide = jnp.concatenate(
-                    [parts[r * 4 + d][quad, :, at : at + LANE] for d in range(4)], 1
-                )
                 ordered = jnp.dot(wide, order_ref[r, half], preferred_element_type=jnp.float32)
                 for tile in range(2):
                     buf[pl.ds(half * 4 * LAGS + tile * 2 + r, LAGS, stride=4), :] = ordered[
@@ -149,7 +189,7 @@
         finish_kernel,
         out_shape=jax.ShapeDtypeStruct((4, 8 * LAGS, LANE), jnp.bfloat16),
         scratch_shapes=[pltpu.VMEM((8 * LAGS, LANE), jnp.float32)],
-        compiler_params=vmem(24),
+        compiler_params=vmem(18),
         name="finish",
     )(*parts, order)
 
@@ -158,69 +198,66 @@
     lag = jnp.arange(LAG_ROWS, dtype=jnp.int32)[:, None]
     k = jnp.arange(2 * BINS, dtype=jnp.int32)[None, :]
     frequency = k % TAPS * LANE + k // 8
-    angles = jnp.mod(frequency * (lag - BINS // 2), 2 * BINS).astype(jnp.float32) * (math.pi / BINS)
-    values = jnp.where(k // TAPS % 2 == 0, jnp.cos(angles), -jnp.sin(angles))
+    n = frequency * (lag - BINS // 2) + k // TAPS % 2 * (BINS // 2)
+    turn = (n + BINS // 4) // (BINS // 2)
+    x = (n - turn * (BINS // 2)).astype(jnp.float32) * (math.pi / BINS)
+    x2 = x * x
+    cos, sin = jnp.float32(0), jnp.float32(0)
+    for power in range(10, -1, -2):
+        cos = cos * x2 + (-1) ** (power // 2) / math.factorial(power)
+        sin = sin * x2 + (-1) ** (power // 2) / math.factorial(power + 1)
+    values = jnp.where(turn % 2 == 0, cos, sin * x)
+    values = jnp.where((turn + 1) // 2 % 2 == 0, values, -values)
     return jnp.where(lag < LAGS, values, 0.0).astype(jnp.bfloat16)
 
 
 def column_order(member):
     z, x, y = member // 16, member // 4 % 4, member % 4
-    at = jnp.arange(512, dtype=jnp.int32)
-    d, half, block, ch = at // 128, at // 64 % 2, at // 8 % 8, at % 8
-    ez, e = block // 4, block % 4
-    first = (z ^ ez) * 128 + (x ^ d) * 32 + (y ^ e) * 8 + ch
-    second = (z ^ ez) * 128 + (x ^ e) * 32 + (y ^ d) * 8 + ch
-    target = jnp.stack([first, second], 0)[:, None, :, None]
+    at = jnp.arange(1024, dtype=jnp.int32)
+    far, d, half, e, turn, ch = at // 512, at // 128 % 4, at // 64 % 2, at // 16 % 4, at // 8 % 2, at % 8
+    dx, dy = jnp.where(far == 1, e, d), jnp.where(far == 1, d, e)
+    target = (z ^ far) * 128 + (x ^ dx) * 32 + (y ^ dy) * 8 + ch
+    target = target + 256 * half + 512 * turn
     column = jnp.arange(256, dtype=jnp.int32)[None, None, None, :]
     side = jnp.arange(2, dtype=jnp.int32)[None, :, None, None]
-    return ((target == column) & (half[None, None, :, None] == side)).astype(jnp.bfloat16)
+    turns = jnp.arange(2, dtype=jnp.int32)[:, None, None, None]
+    return (target[None, None, :, None] == column + 256 * side + 512 * turns).astype(jnp.bfloat16)
 
 
 def on_device(spectra, partners):
     member = lax.axis_index("mem").astype(jnp.int32)
     white = whiten(spectra)
-    planes = [white] + [xor_perm(white, "grp", 2 * d) for d in range(1, 4)]
     row_masks, col_masks = (4, 1), (1, 4)
-    order = column_order(member)
-    source, order = lax.optimization_barrier((white, order))
     rows = [[white, None, None, None], [white, None, None, None]]
+    source = white
     for d in (1, 3, 2):
         sent = [xor_perm(source, "mem", d * m) for m in row_masks]
         source, sent = lax.optimization_barrier((source, sent))
         rows[0][d], rows[1][d] = sent
+    planes = [white] + [xor_perm(white, "grp", 2 * d) for d in range(1, 4)]
     table = lag_table()
+    order = column_order(member)
     factor = math.sqrt(2.0 / (BINS * (COMP // 2)))
     planes, rows, table, order = lax.optimization_barrier((planes, rows, table, order))
-    mine = []
-    for r in range(2):
-        plane = partners[r, member] >> 1
-        mine.append(
-            jnp.where(
-                plane == 0,
-                planes[0],
-                jnp.where(plane == 1, planes[1], jnp.where(plane == 2, planes[2], planes[3])),
-            )
-        )
-    other = [xor_perm(m, "grp", 1) for m in mine]
-    near = [jnp.where((partners[r, member] & 1) == 1, other[r], mine[r]) for r in range(2)]
-    far = [xor_perm(b, "mem", 16) for b in near]
-    cols = [[None] * 8, [None] * 8]
-    sent = [[], []]
-    for block, sources in ((0, near), (4, far)):
-        for r in range(2):
-            cols[r][block] = sources[r]
-        for e in (1, 3, 2):
-            for r in range(2):
-                source = sources[r]
-                if len(sent[r]) >= 2:
-                    source, _ = lax.optimization_barrier((source, sent[r][-2]))
-                cols[r][block + e] = xor_perm(source, "mem", e * col_masks[r])
-                sent[r].append(cols[r][block + e])
-    cols = lax.optimization_barrier(cols)
+
+    mine = choose(pick_kernel, "pick", member.reshape(1), partners, planes)
+    other = xor_perm(mine, "grp", 1)
+    near = choose(merge_kernel, "merge", member.reshape(1), partners, [mine, other])
+    across = xor_perm(near, "mem", 16)
+    cols = [[near, None, None, None], [across, None, None, None]]
+    for e in (3, 1):
+        cols[0][e] = xor_perm(near, "mem", e * col_masks[0])
+    cols, near, across = lax.optimization_barrier((cols, near, across))
+    for e in (3, 1):
+        cols[1][e] = xor_perm(across, "mem", e * col_masks[1])
+    cols[0][2] = xor_perm(near, "mem", 2 * col_masks[0])
+    cols, across = lax.optimization_barrier((cols, across))
+    cols[1][2] = xor_perm(across, "mem", 2 * col_masks[1])
     parts = []
-    for r in range(2):
-        sums = correlate(rows[r], cols[r], table, factor)
-        parts += [sums[0]] + [xor_perm(sums[d], "mem", d * row_masks[r]) for d in range(1, 4)]
+    for n in range(2):
+        sums = correlate(rows[n], cols[n], table, factor)
+        parts += [sums[0]] + [xor_perm(sums[d], "mem", d * row_masks[n]) for d in range(1, 4)]
+        cols[1], sums = lax.optimization_barrier((cols[1], sums[0]))
     packed = finish(parts, order)
     result = packed.reshape(CH, LAGS, 2, 2, LANE)
     return jnp.transpose(result, (0, 3, 2, 4, 1)).reshape(CH, 2, 256, LAGS)

time: 128 us -> 128 us (level)
  waiting for transfers between devices: 42.7 us -> 60.7 us
  starting transfers between devices: 50.5 us -> 35.7 us
  Pallas kernels: 19.1 us -> 22.6 us
  between operations: 2.86 us -> 0.15 us
  other arithmetic: 9.81 us -> 7.66 us
    ppermute x31 -> x23, waiting for transfers between devices: 42.7 us -> 60.7 us  [xor_perm(): lax.ppermute(array, axis, [(i, i ^ mask) for i in range(lax.axis_size(axi...]
    ppermute x31 -> x23, starting transfers between devices: 50.5 us -> 35.7 us  [xor_perm(): lax.ppermute(array, axis, [(i, i ^ mask) for i in range(lax.axis_size(axi...]
    pallas_call x1, Pallas kernels: 4.92 us -> 7.1 us  [finish(): pl.pallas_call(finish_kernel, out_shape=jax.ShapeDtypeStruct((4, 8 * LAGS...]
    convert_element_type x1, other arithmetic: 9.13 us -> 7.08 us  [lag_table(): return jnp.where(lag < LAGS, values, 0.0).astype(jnp.bfloat16)]
  transfers between devices with their start and end apart: 31 -> 23, of which waited for: 17 -> 17; matrix products, arithmetic and copies ran while one was open for 8% -> 6% of each run, Pallas kernels for 5% -> 11%
where the time goes in v3:
time: 128 us
  waiting for transfers between devices  60.7 us (47%)
  starting transfers between devices  35.7 us (28%)
  Pallas kernels  22.6 us (18%)
  other arithmetic  7.66 us (6%)
    ppermute x23, waiting for transfers between devices, xor_perm(): lax.ppermute(array, axis, [(i, i ^ mask) for i in range(lax.axis_size(axi...  60.7 us
    ppermute x23, starting transfers between devices, xor_perm(): lax.ppermute(array, axis, [(i, i ^ mask) for i in range(lax.axis_size(axi...  35.7 us
    pallas_call x2, Pallas kernels, correlate(): pl.pallas_call(body, out_shape=[jax.ShapeDtypeStruct((2, LAG_ROWS, 256),...  13.4 us
    pallas_call x1, Pallas kernels, finish(): pl.pallas_call(finish_kernel, out_shape=jax.ShapeDtypeStruct((4, 8 * LAGS...  7.1 us
    convert_element_type x1, other arithmetic, lag_table(): return jnp.where(lag < LAGS, values, 0.0).astype(jnp.bfloat16)  7.08 us
  transfers between devices with their start and end apart: 23, of which 17 were waited for; matrix products, arithmetic and copies ran while one was open for 6% of the time, Pallas kernels for 11%

profile of v3, /device:TPU:8, one launch (start us, length us, event | category | flops | bytes accessed | tf_op | source)
XLA Modules:
  0.0 127.8 jit_solution(15453148127236914766)
XLA Ops:
  0.0 0.0 copy-start
  0.0 0.9 copy-done
  1.0 0.0 copy-start.1
  1.0 0.8 whiten.1.refs_0_
  1.8 2.3 %collective-permute-start.4 = (bf16[128,8,128]{2,1,0:T(8,128)(2,1)S(1)}, bf16[128,8,128]{2,1,0:T(8,128)(2,1)S(1)}, u32[]{:S(2)}, u32[]{:S(2)}) collective-permute-start(bf16[128,8,128]{2,1,0:T(8,128)(2,1)S(1)} %whiten.1.refs_0_), channel_id=1, source_target_pairs={{0,1},{1,0},{2,3},{3,2},{4,5},{5,4},{6,7},{7,6},{8,9},{9,8},{10,11... | collective-permute-start | bytes 786440 | tf_op jit(solution)/shard_map/ppermute | solution.py:26
  4.1 0.0 collective-permute-start.3
  4.1 6.1 %collective-permute-start.2 = (bf16[128,8,128]{2,1,0:T(8,128)(2,1)S(1)}, bf16[128,8,128]{2,1,0:T(8,128)(2,1)S(1)}, u32[]{:S(2)}, u32[]{:S(2)}) collective-permute-start(bf16[128,8,128]{2,1,0:T(8,128)(2,1)S(1)} %whiten.1.refs_0_), channel_id=1, source_target_pairs={{0,192},{32,224},{64,128},{96,160},{128,64},{160,96},{192,0},{224,... | collective-permute-start | bytes 786440 | tf_op jit(solution)/shard_map/ppermute | solution.py:26
  10.1 0.9 collective-permute-start.1
  11.0 1.5 %collective-permute-start = (bf16[128,8,128]{2,1,0:T(8,128)(2,1)S(1)}, bf16[128,8,128]{2,1,0:T(8,128)(2,1)S(1)}, u32[]{:S(2)}, u32[]{:S(2)}) collective-permute-start(bf16[128,8,128]{2,1,0:T(8,128)(2,1)S(1)} %whiten.1.refs_0_), channel_id=1, source_target_pairs={{0,64},{32,96},{64,0},{96,32},{128,192},{160,224},{192,128},{224,1... | collective-permute-start | bytes 786440 | tf_op jit(solution)/shard_map/ppermute | solution.py:26
  12.5 7.1 %fusion.7.refs_8_ = bf16[520,1024]{1,0:T(8,128)(2,1)S(1)} fusion(s32[1024]{0:T(1024)S(1)} %get-tuple-element.101, s32[520]{0:T(1024)S(1)} %iota_add_fusion, s32[1024]{0:T(1024)S(1)} %get-tuple-element.102, pred[520]{0:T(1024)(128)(4,1)S(1)} %iota_compare_fusion), kind=kLoop, calls=%fused_computation.23 | loop fusion | flops 48988160 | bytes 1075752 | tf_op jit(solution)/shard_map/convert_element_type | solution.py:211
  19.6 0.1 iota_add_fusion.1
  19.7 0.0 collective-permute-done.4.refs_1_
  19.7 0.0 collective-permute-done.3.refs_1_
  19.7 2.5 %collective-permute-start.6 = (bf16[128,8,128]{2,1,0:T(8,128)(2,1)S(1)}, bf16[128,8,128]{2,1,0:T(8,128)(2,1)S(1)}, u32[]{:S(2)}, u32[]{:S(2)}) collective-permute-start(bf16[128,8,128]{2,1,0:T(8,128)(2,1)S(1)} %whiten.1.refs_0_), channel_id=1, source_target_pairs={{0,3},{1,2},{2,1},{3,0},{4,7},{5,6},{6,5},{7,4},{8,11},{9,10},{10,... | collective-permute-start | bytes 786440 | tf_op jit(solution)/shard_map/ppermute | solution.py:26
  22.2 2.1 %collective-permute-start.5 = (bf16[128,8,128]{2,1,0:T(8,128)(2,1)S(1)}, bf16[128,8,128]{2,1,0:T(8,128)(2,1)S(1)}, u32[]{:S(2)}, u32[]{:S(2)}) collective-permute-start(bf16[128,8,128]{2,1,0:T(8,128)(2,1)S(1)} %whiten.1.refs_0_), channel_id=1, source_target_pairs={{0,12},{1,13},{2,14},{3,15},{4,8},{5,9},{6,10},{7,11},{8,4},{9,5},... | collective-permute-start | bytes 786440 | tf_op jit(solution)/shard_map/ppermute | solution.py:26
  24.3 0.1 broadcast_add_fusion
  24.4 3.0 %collective-permute-done.6.refs_3_ = bf16[128,8,128]{2,1,0:T(8,128)(2,1)S(1)} collective-permute-done((bf16[128,8,128]{2,1,0:T(8,128)(2,1)S(1)}, bf16[128,8,128]{2,1,0:T(8,128)(2,1)S(1)}, u32[]{:S(2)}, u32[]{:S(2)}) %collective-permute-start.6) | collective-permute-done | bytes 262176 | tf_op jit(solution)/shard_map/ppermute | solution.py:26
  27.4 2.7 %collective-permute-done.5.refs_3_ = bf16[128,8,128]{2,1,0:T(8,128)(2,1)S(1)} collective-permute-done((bf16[128,8,128]{2,1,0:T(8,128)(2,1)S(1)}, bf16[128,8,128]{2,1,0:T(8,128)(2,1)S(1)}, u32[]{:S(2)}, u32[]{:S(2)}) %collective-permute-start.5) | collective-permute-done | bytes 262176 | tf_op jit(solution)/shard_map/ppermute | solution.py:26
  30.0 1.2 collective-permute-start.8
  31.3 2.0 %collective-permute-start.7 = (bf16[128,8,128]{2,1,0:T(8,128)(2,1)S(1)}, bf16[128,8,128]{2,1,0:T(8,128)(2,1)S(1)}, u32[]{:S(2)}, u32[]{:S(2)}) collective-permute-start(bf16[128,8,128]{2,1,0:T(8,128)(2,1)S(1)} %whiten.1.refs_0_), channel_id=1, source_target_pairs={{0,8},{1,9},{2,10},{3,11},{4,12},{5,13},{6,14},{7,15},{8,0},{9,1},... | collective-permute-start | bytes 786440 | tf_op jit(solution)/shard_map/ppermute | solution.py:26
  33.2 0.4 compare_convert_fusion.refs_8_
  33.6 4.3 %collective-permute-done.8.refs_2_ = bf16[128,8,128]{2,1,0:T(8,128)(2,1)S(1)} collective-permute-done((bf16[128,8,128]{2,1,0:T(8,128)(2,1)S(1)}, bf16[128,8,128]{2,1,0:T(8,128)(2,1)S(1)}, u32[]{:S(2)}, u32[]{:S(2)}) %collective-permute-start.8) | collective-permute-done | bytes 262176 | tf_op jit(solution)/shard_map/ppermute | solution.py:26
  37.9 1.2 collective-permute-done.7.refs_2_
  39.1 0.0 collective-permute-done.2.refs_3_
  39.2 0.0 collective-permute-done.1.refs_2_
  39.2 0.0 collective-permute-done.refs_1_
  39.2 0.0 copy-done.1
  39.2 0.6 pick.1.mine_ref
  39.8 0.1 collective-permute-start.9
  39.9 1.9 %collective-permute-done.9.other_ref = bf16[2,128,8,128]{3,2,1,0:T(8,128)(2,1)S(1)} collective-permute-done((bf16[2,128,8,128]{3,2,1,0:T(8,128)(2,1)S(1)}, bf16[2,128,8,128]{3,2,1,0:T(8,128)(2,1)S(1)}, u32[]{:S(2)}, u32[]{:S(2)}) %collective-permute-start.9) | collective-permute-done | bytes 524320 | tf_op jit(solution)/shard_map/ppermute | solution.py:26
  41.8 0.6 merge.1.refs_4_
  42.4 1.1 collective-permute-start.12
  43.5 1.6 %collective-permute-start.11 = (bf16[2,128,8,128]{3,2,1,0:T(8,128)(2,1)S(1)}, bf16[2,128,8,128]{3,2,1,0:T(8,128)(2,1)S(1)}, u32[]{:S(2)}, u32[]{:S(2)}) collective-permute-start(bf16[2,128,8,128]{3,2,1,0:T(8,128)(2,1)S(1)} %merge.1.refs_4_), channel_id=1, source_target_pairs={{0,3},{1,2},{2,1},{3,0},{4,7},{5,6},{6,5},{7,4},{8,11},{9,10},{10,... | collective-permute-start | bytes 1572872 | tf_op jit(solution)/shard_map/ppermute | solution.py:26
  45.1 1.9 %collective-permute-start.10 = (bf16[2,128,8,128]{3,2,1,0:T(8,128)(2,1)S(1)}, bf16[2,128,8,128]{3,2,1,0:T(8,128)(2,1)S(1)}, u32[]{:S(2)}, u32[]{:S(2)}) collective-permute-start(bf16[2,128,8,128]{3,2,1,0:T(8,128)(2,1)S(1)} %merge.1.refs_4_), channel_id=1, source_target_pairs={{0,1},{1,0},{2,3},{3,2},{4,5},{5,4},{6,7},{7,6},{8,9},{9,8},{10,11... | collective-permute-start | bytes 1572872 | tf_op jit(solution)/shard_map/ppermute | solution.py:26
  47.0 9.5 %collective-permute-done.12.refs_4_ = bf16[2,128,8,128]{3,2,1,0:T(8,128)(2,1)S(1)} collective-permute-done((bf16[2,128,8,128]{3,2,1,0:T(8,128)(2,1)S(1)}, bf16[2,128,8,128]{3,2,1,0:T(8,128)(2,1)S(1)}, u32[]{:S(2)}, u32[]{:S(2)}) %collective-permute-start.12) | collective-permute-done | bytes 524320 | tf_op jit(solution)/shard_map/ppermute | solution.py:26
  56.5 0.7 collective-permute-done.11.refs_7_
  57.2 1.4 %collective-permute-done.10.refs_5_ = bf16[2,128,8,128]{3,2,1,0:T(8,128)(2,1)S(1)} collective-permute-done((bf16[2,128,8,128]{3,2,1,0:T(8,128)(2,1)S(1)}, bf16[2,128,8,128]{3,2,1,0:T(8,128)(2,1)S(1)}, u32[]{:S(2)}, u32[]{:S(2)}) %collective-permute-start.10) | collective-permute-done | bytes 524320 | tf_op jit(solution)/shard_map/ppermute | solution.py:26
  58.7 2.1 %collective-permute-start.13 = (bf16[2,128,8,128]{3,2,1,0:T(8,128)(2,1)S(1)}, bf16[2,128,8,128]{3,2,1,0:T(8,128)(2,1)S(1)}, u32[]{:S(2)}, u32[]{:S(2)}) collective-permute-start(bf16[2,128,8,128]{3,2,1,0:T(8,128)(2,1)S(1)} %merge.1.refs_4_), channel_id=1, source_target_pairs={{0,2},{1,3},{2,0},{3,1},{4,6},{5,7},{6,4},{7,5},{8,10},{9,11},{10,... | collective-permute-start | bytes 1572872 | tf_op jit(solution)/shard_map/ppermute | solution.py:26
  60.7 2.1 %collective-permute-start.15 = (bf16[2,128,8,128]{3,2,1,0:T(8,128)(2,1)S(1)}, bf16[2,128,8,128]{3,2,1,0:T(8,128)(2,1)S(1)}, u32[]{:S(2)}, u32[]{:S(2)}) collective-permute-start(bf16[2,128,8,128]{3,2,1,0:T(8,128)(2,1)S(1)} %collective-permute-done.12.refs_4_), channel_id=1, source_target_pairs={{0,12},{1,13},{2,14},{3,15},{4,8},{5,9},{6,10},{7,11},{8,4},{9,5},... | collective-permute-start | bytes 1572872 | tf_op jit(solution)/shard_map/ppermute | solution.py:26
  62.8 0.0 collective-permute-start.14
  62.8 10.0 %collective-permute-done.13.refs_6_ = bf16[2,128,8,128]{3,2,1,0:T(8,128)(2,1)S(1)} collective-permute-done((bf16[2,128,8,128]{3,2,1,0:T(8,128)(2,1)S(1)}, bf16[2,128,8,128]{3,2,1,0:T(8,128)(2,1)S(1)}, u32[]{:S(2)}, u32[]{:S(2)}) %collective-permute-start.13) | collective-permute-done | bytes 524320 | tf_op jit(solution)/shard_map/ppermute | solution.py:26
  72.8 1.6 %collective-permute-done.15.refs_7_ = bf16[2,128,8,128]{3,2,1,0:T(8,128)(2,1)S(1)} collective-permute-done((bf16[2,128,8,128]{3,2,1,0:T(8,128)(2,1)S(1)}, bf16[2,128,8,128]{3,2,1,0:T(8,128)(2,1)S(1)}, u32[]{:S(2)}, u32[]{:S(2)}) %collective-permute-start.15) | collective-permute-done | bytes 524320 | tf_op jit(solution)/shard_map/ppermute | solution.py:26
  74.5 0.6 collective-permute-done.14.refs_5_
  75.1 0.9 collective-permute-start.19
  75.9 6.7 %correlate.2 = (bf16[2,520,256]{2,1,0:T(8,128)(2,1)S(1)}, bf16[2,520,256]{2,1,0:T(8,128)(2,1)S(1)}, bf16[2,520,256]{2,1,0:T(8,128)(2,1)S(1)}, bf16[2,520,256]{2,1,0:T(8,128)(2,1)S(1)}) custom-call(bf16[128,8,128]{2,1,0:T(8,128)(2,1)S(1)} %whiten.1.refs_0_, bf16[128,8,128]{2,1,0:T(8,128)(2,1)S(1)} %collective-permute-done.3.refs_1_, ...), custom_call_target="tpu_custom_call" | custom-call | flops 3254779904 | bytes 7340032 | tf_op jit(solution)/shard_map/correlate/pallas_call | solution.py:154
  82.7 1.6 %collective-permute-start.16 = (bf16[2,520,256]{2,1,0:T(8,128)(2,1)S(1)}, bf16[2,520,256]{2,1,0:T(8,128)(2,1)S(1)}, u32[]{:S(2)}, u32[]{:S(2)}) collective-permute-start(bf16[2,520,256]{2,1,0:T(8,128)(2,1)S(1)} %get-tuple-element.81), channel_id=1, source_target_pairs={{0,4},{1,5},{2,6},{3,7},{4,0},{5,1},{6,2},{7,3},{8,12},{9,13},{10,... | collective-permute-start | bytes 1597448 | tf_op jit(solution)/shard_map/ppermute | solution.py:26
  84.2 2.1 %collective-permute-start.17 = (bf16[2,520,256]{2,1,0:T(8,128)(2,1)S(1)}, bf16[2,520,256]{2,1,0:T(8,128)(2,1)S(1)}, u32[]{:S(2)}, u32[]{:S(2)}) collective-permute-start(bf16[2,520,256]{2,1,0:T(8,128)(2,1)S(1)} %get-tuple-element.82), channel_id=1, source_target_pairs={{0,8},{1,9},{2,10},{3,11},{4,12},{5,13},{6,14},{7,15},{8,0},{9,1},... | collective-permute-start | bytes 1597448 | tf_op jit(solution)/shard_map/ppermute | solution.py:26
  86.3 1.1 collective-permute-start.18
  87.4 4.0 %collective-permute-done.19.refs_6_ = bf16[2,128,8,128]{3,2,1,0:T(8,128)(2,1)S(1)} collective-permute-done((bf16[2,128,8,128]{3,2,1,0:T(8,128)(2,1)S(1)}, bf16[2,128,8,128]{3,2,1,0:T(8,128)(2,1)S(1)}, u32[]{:S(2)}, u32[]{:S(2)}) %collective-permute-start.19) | collective-permute-done | bytes 524320 | tf_op jit(solution)/shard_map/ppermute | solution.py:26
  91.4 6.7 %correlate.3 = (bf16[2,520,256]{2,1,0:T(8,128)(2,1)S(1)}, bf16[2,520,256]{2,1,0:T(8,128)(2,1)S(1)}, bf16[2,520,256]{2,1,0:T(8,128)(2,1)S(1)}, bf16[2,520,256]{2,1,0:T(8,128)(2,1)S(1)}) custom-call(bf16[128,8,128]{2,1,0:T(8,128)(2,1)S(1)} %whiten.1.refs_0_, bf16[128,8,128]{2,1,0:T(8,128)(2,1)S(1)} %collective-permute-done.4.refs_1_, ...), custom_call_target="tpu_custom_call" | custom-call | flops 3254779904 | bytes 7340032 | tf_op jit(solution)/shard_map/correlate/pallas_call | solution.py:154
  98.2 0.1 collective-permute-start.20
  98.3 1.9 %collective-permute-start.21 = (bf16[2,520,256]{2,1,0:T(8,128)(2,1)S(1)}, bf16[2,520,256]{2,1,0:T(8,128)(2,1)S(1)}, u32[]{:S(2)}, u32[]{:S(2)}) collective-permute-start(bf16[2,520,256]{2,1,0:T(8,128)(2,1)S(1)} %get-tuple-element.98), channel_id=1, source_target_pairs={{0,2},{1,3},{2,0},{3,1},{4,6},{5,7},{6,4},{7,5},{8,10},{9,11},{10,... | collective-permute-start | bytes 1597448 | tf_op jit(solution)/shard_map/ppermute | solution.py:26
  100.2 1.5 %collective-permute-done.16.refs_1_ = bf16[2,520,256]{2,1,0:T(8,128)(2,1)S(1)} collective-permute-done((bf16[2,520,256]{2,1,0:T(8,128)(2,1)S(1)}, bf16[2,520,256]{2,1,0:T(8,128)(2,1)S(1)}, u32[]{:S(2)}, u32[]{:S(2)}) %collective-permute-start.16) | collective-permute-done | bytes 532512 | tf_op jit(solution)/shard_map/ppermute | solution.py:26
  101.7 0.8 collective-permute-start.22
  102.5 8.4 %collective-permute-done.17.refs_2_ = bf16[2,520,256]{2,1,0:T(8,128)(2,1)S(1)} collective-permute-done((bf16[2,520,256]{2,1,0:T(8,128)(2,1)S(1)}, bf16[2,520,256]{2,1,0:T(8,128)(2,1)S(1)}, u32[]{:S(2)}, u32[]{:S(2)}) %collective-permute-start.17) | collective-permute-done | bytes 532512 | tf_op jit(solution)/shard_map/ppermute | solution.py:26
  110.8 1.2 collective-permute-done.18.refs_3_
  112.1 0.0 collective-permute-done.20.refs_5_
  112.1 4.4 %collective-permute-done.21.refs_6_ = bf16[2,520,256]{2,1,0:T(8,128)(2,1)S(1)} collective-permute-done((bf16[2,520,256]{2,1,0:T(8,128)(2,1)S(1)}, bf16[2,520,256]{2,1,0:T(8,128)(2,1)S(1)}, u32[]{:S(2)}, u32[]{:S(2)}) %collective-permute-start.21) | collective-permute-done | bytes 532512 | tf_op jit(solution)/shard_map/ppermute | solution.py:26
  116.5 4.2 %collective-permute-done.22.refs_7_ = bf16[2,520,256]{2,1,0:T(8,128)(2,1)S(1)} collective-permute-done((bf16[2,520,256]{2,1,0:T(8,128)(2,1)S(1)}, bf16[2,520,256]{2,1,0:T(8,128)(2,1)S(1)}, u32[]{:S(2)}, u32[]{:S(2)}) %collective-permute-start.22) | collective-permute-done | bytes 532512 | tf_op jit(solution)/shard_map/ppermute | solution.py:26
  120.7 7.1 %finish.1 = bf16[4,4104,128]{2,1,0:T(8,128)(2,1)} custom-call(bf16[2,520,256]{2,1,0:T(8,128)(2,1)S(1)} %get-tuple-element.80.refs_0_, bf16[2,520,256]{2,1,0:T(8,128)(2,1)S(1)} %collective-permute-done.16.refs_1_, bf16[2,520,256]{2,1,0:T(8,128)(2,1)S(1)} %collective-permute-done.17.refs_2_, bf16[2,520,256]{2,1,0:T(8,128)(2,1)S(1)} %collective-permute-done.18.refs_3_, ...), custom_call_target="tpu_custom_call" | custom-call | tf_op jit(solution)/shard_map/finish/pallas_call | solution.py:188
  (6 shorter events, 0.0 us)
Async XLA Ops:
  0.0 0.9 copy-start
  1.0 38.2 %copy-start.1 = (s32[2,32]{1,0:T(2,128)S(1)}, s32[2,32]{1,0:T(2,128)}, u32[]{:S(2)}) copy-start(s32[2,32]{1,0:T(2,128)} %partners_ref.3) | copy-start | bytes 772
  1.8 17.9 %collective-permute-start.4 = (bf16[128,8,128]{2,1,0:T(8,128)(2,1)S(1)}, bf16[128,8,128]{2,1,0:T(8,128)(2,1)S(1)}, u32[]{:S(2)}, u32[]{:S(2)}) collective-permute-start(bf16[128,8,128]{2,1,0:T(8,128)(2,1)S(1)} %whiten.1.refs_0_), channel_id=1, source_target_pairs={{0,1},{1,0},{2,3},{3,2},{4,5},{5,4},{6,7},{7,6},{8,9},{9,8},{10,11... | collective-permute-start | bytes 786440 | tf_op jit(solution)/shard_map/ppermute | solution.py:26
  4.1 15.7 %collective-permute-start.3 = (bf16[128,8,128]{2,1,0:T(8,128)(2,1)S(1)}, bf16[128,8,128]{2,1,0:T(8,128)(2,1)S(1)}, u32[]{:S(2)}, u32[]{:S(2)}) collective-permute-start(bf16[128,8,128]{2,1,0:T(8,128)(2,1)S(1)} %whiten.1.refs_0_), channel_id=1, source_target_pairs={{0,4},{1,5},{2,6},{3,7},{4,0},{5,1},{6,2},{7,3},{8,12},{9,13},{10,... | collective-permute-start | bytes 786440 | tf_op jit(solution)/shard_map/ppermute | solution.py:26
  4.1 35.1 %collective-permute-start.2 = (bf16[128,8,128]{2,1,0:T(8,128)(2,1)S(1)}, bf16[128,8,128]{2,1,0:T(8,128)(2,1)S(1)}, u32[]{:S(2)}, u32[]{:S(2)}) collective-permute-start(bf16[128,8,128]{2,1,0:T(8,128)(2,1)S(1)} %whiten.1.refs_0_), channel_id=1, source_target_pairs={{0,192},{32,224},{64,128},{96,160},{128,64},{160,96},{192,0},{224,... | collective-permute-start | bytes 786440 | tf_op jit(solution)/shard_map/ppermute | solution.py:26
  10.1 29.0 %collective-permute-start.1 = (bf16[128,8,128]{2,1,0:T(8,128)(2,1)S(1)}, bf16[128,8,128]{2,1,0:T(8,128)(2,1)S(1)}, u32[]{:S(2)}, u32[]{:S(2)}) collective-permute-start(bf16[128,8,128]{2,1,0:T(8,128)(2,1)S(1)} %whiten.1.refs_0_), channel_id=1, source_target_pairs={{0,128},{32,160},{64,192},{96,224},{128,0},{160,32},{192,64},{224,... | collective-permute-start | bytes 786440 | tf_op jit(solution)/shard_map/ppermute | solution.py:26
  11.0 28.1 %collective-permute-start = (bf16[128,8,128]{2,1,0:T(8,128)(2,1)S(1)}, bf16[128,8,128]{2,1,0:T(8,128)(2,1)S(1)}, u32[]{:S(2)}, u32[]{:S(2)}) collective-permute-start(bf16[128,8,128]{2,1,0:T(8,128)(2,1)S(1)} %whiten.1.refs_0_), channel_id=1, source_target_pairs={{0,64},{32,96},{64,0},{96,32},{128,192},{160,224},{192,128},{224,1... | collective-permute-start | bytes 786440 | tf_op jit(solution)/shard_map/ppermute | solution.py:26
  19.7 7.6 %collective-permute-start.6 = (bf16[128,8,128]{2,1,0:T(8,128)(2,1)S(1)}, bf16[128,8,128]{2,1,0:T(8,128)(2,1)S(1)}, u32[]{:S(2)}, u32[]{:S(2)}) collective-permute-start(bf16[128,8,128]{2,1,0:T(8,128)(2,1)S(1)} %whiten.1.refs_0_), channel_id=1, source_target_pairs={{0,3},{1,2},{2,1},{3,0},{4,7},{5,6},{6,5},{7,4},{8,11},{9,10},{10,... | collective-permute-start | bytes 786440 | tf_op jit(solution)/shard_map/ppermute | solution.py:26
  22.2 7.9 %collective-permute-start.5 = (bf16[128,8,128]{2,1,0:T(8,128)(2,1)S(1)}, bf16[128,8,128]{2,1,0:T(8,128)(2,1)S(1)}, u32[]{:S(2)}, u32[]{:S(2)}) collective-permute-start(bf16[128,8,128]{2,1,0:T(8,128)(2,1)S(1)} %whiten.1.refs_0_), channel_id=1, source_target_pairs={{0,12},{1,13},{2,14},{3,15},{4,8},{5,9},{6,10},{7,11},{8,4},{9,5},... | collective-permute-start | bytes 786440 | tf_op jit(solution)/shard_map/ppermute | solution.py:26
  30.0 7.9 %collective-permute-start.8 = (bf16[128,8,128]{2,1,0:T(8,128)(2,1)S(1)}, bf16[128,8,128]{2,1,0:T(8,128)(2,1)S(1)}, u32[]{:S(2)}, u32[]{:S(2)}) collective-permute-start(bf16[128,8,128]{2,1,0:T(8,128)(2,1)S(1)} %whiten.1.refs_0_), channel_id=1, source_target_pairs={{0,2},{1,3},{2,0},{3,1},{4,6},{5,7},{6,4},{7,5},{8,10},{9,11},{10,... | collective-permute-start | bytes 786440 | tf_op jit(solution)/shard_map/ppermute | solution.py:26
  31.3 7.9 %collective-permute-start.7 = (bf16[128,8,128]{2,1,0:T(8,128)(2,1)S(1)}, bf16[128,8,128]{2,1,0:T(8,128)(2,1)S(1)}, u32[]{:S(2)}, u32[]{:S(2)}) collective-permute-start(bf16[128,8,128]{2,1,0:T(8,128)(2,1)S(1)} %whiten.1.refs_0_), channel_id=1, source_target_pairs={{0,8},{1,9},{2,10},{3,11},{4,12},{5,13},{6,14},{7,15},{8,0},{9,1},... | collective-permute-start | bytes 786440 | tf_op jit(solution)/shard_map/ppermute | solution.py:26
  39.8 2.0 %collective-permute-start.9 = (bf16[2,128,8,128]{3,2,1,0:T(8,128)(2,1)S(1)}, bf16[2,128,8,128]{3,2,1,0:T(8,128)(2,1)S(1)}, u32[]{:S(2)}, u32[]{:S(2)}) collective-permute-start(bf16[2,128,8,128]{3,2,1,0:T(8,128)(2,1)S(1)} %pick.1.mine_ref), channel_id=1, source_target_pairs={{0,32},{32,0},{64,96},{96,64},{128,160},{160,128},{192,224},{224,1... | collective-permute-start | bytes 1572872 | tf_op jit(solution)/shard_map/ppermute | solution.py:26
  42.4 14.1 %collective-permute-start.12 = (bf16[2,128,8,128]{3,2,1,0:T(8,128)(2,1)S(1)}, bf16[2,128,8,128]{3,2,1,0:T(8,128)(2,1)S(1)}, u32[]{:S(2)}, u32[]{:S(2)}) collective-permute-start(bf16[2,128,8,128]{3,2,1,0:T(8,128)(2,1)S(1)} %merge.1.refs_4_), channel_id=1, source_target_pairs={{0,16},{1,17},{2,18},{3,19},{4,20},{5,21},{6,22},{7,23},{8,24},{9,... | collective-permute-start | bytes 1572872 | tf_op jit(solution)/shard_map/ppermute | solution.py:26
  43.5 13.7 %collective-permute-start.11 = (bf16[2,128,8,128]{3,2,1,0:T(8,128)(2,1)S(1)}, bf16[2,128,8,128]{3,2,1,0:T(8,128)(2,1)S(1)}, u32[]{:S(2)}, u32[]{:S(2)}) collective-permute-start(bf16[2,128,8,128]{3,2,1,0:T(8,128)(2,1)S(1)} %merge.1.refs_4_), channel_id=1, source_target_pairs={{0,3},{1,2},{2,1},{3,0},{4,7},{5,6},{6,5},{7,4},{8,11},{9,10},{10,... | collective-permute-start | bytes 1572872 | tf_op jit(solution)/shard_map/ppermute | solution.py:26
  45.1 13.6 %collective-permute-start.10 = (bf16[2,128,8,128]{3,2,1,0:T(8,128)(2,1)S(1)}, bf16[2,128,8,128]{3,2,1,0:T(8,128)(2,1)S(1)}, u32[]{:S(2)}, u32[]{:S(2)}) collective-permute-start(bf16[2,128,8,128]{3,2,1,0:T(8,128)(2,1)S(1)} %merge.1.refs_4_), channel_id=1, source_target_pairs={{0,1},{1,0},{2,3},{3,2},{4,5},{5,4},{6,7},{7,6},{8,9},{9,8},{10,11... | collective-permute-start | bytes 1572872 | tf_op jit(solution)/shard_map/ppermute | solution.py:26
  58.7 14.2 %collective-permute-start.13 = (bf16[2,128,8,128]{3,2,1,0:T(8,128)(2,1)S(1)}, bf16[2,128,8,128]{3,2,1,0:T(8,128)(2,1)S(1)}, u32[]{:S(2)}, u32[]{:S(2)}) collective-permute-start(bf16[2,128,8,128]{3,2,1,0:T(8,128)(2,1)S(1)} %merge.1.refs_4_), channel_id=1, source_target_pairs={{0,2},{1,3},{2,0},{3,1},{4,6},{5,7},{6,4},{7,5},{8,10},{9,11},{10,... | collective-permute-start | bytes 1572872 | tf_op jit(solution)/shard_map/ppermute | solution.py:26
  60.7 13.7 %collective-permute-start.15 = (bf16[2,128,8,128]{3,2,1,0:T(8,128)(2,1)S(1)}, bf16[2,128,8,128]{3,2,1,0:T(8,128)(2,1)S(1)}, u32[]{:S(2)}, u32[]{:S(2)}) collective-permute-start(bf16[2,128,8,128]{3,2,1,0:T(8,128)(2,1)S(1)} %collective-permute-done.12.refs_4_), channel_id=1, source_target_pairs={{0,12},{1,13},{2,14},{3,15},{4,8},{5,9},{6,10},{7,11},{8,4},{9,5},... | collective-permute-start | bytes 1572872 | tf_op jit(solution)/shard_map/ppermute | solution.py:26
  62.8 12.3 %collective-permute-start.14 = (bf16[2,128,8,128]{3,2,1,0:T(8,128)(2,1)S(1)}, bf16[2,128,8,128]{3,2,1,0:T(8,128)(2,1)S(1)}, u32[]{:S(2)}, u32[]{:S(2)}) collective-permute-start(bf16[2,128,8,128]{3,2,1,0:T(8,128)(2,1)S(1)} %collective-permute-done.12.refs_4_), channel_id=1, source_target_pairs={{0,4},{1,5},{2,6},{3,7},{4,0},{5,1},{6,2},{7,3},{8,12},{9,13},{10,... | collective-permute-start | bytes 1572872 | tf_op jit(solution)/shard_map/ppermute | solution.py:26
  75.1 16.4 %collective-permute-start.19 = (bf16[2,128,8,128]{3,2,1,0:T(8,128)(2,1)S(1)}, bf16[2,128,8,128]{3,2,1,0:T(8,128)(2,1)S(1)}, u32[]{:S(2)}, u32[]{:S(2)}) collective-permute-start(bf16[2,128,8,128]{3,2,1,0:T(8,128)(2,1)S(1)} %collective-permute-done.12.refs_4_), channel_id=1, source_target_pairs={{0,8},{1,9},{2,10},{3,11},{4,12},{5,13},{6,14},{7,15},{8,0},{9,1},... | collective-permute-start | bytes 1572872 | tf_op jit(solution)/shard_map/ppermute | solution.py:26
  82.7 19.0 %collective-permute-start.16 = (bf16[2,520,256]{2,1,0:T(8,128)(2,1)S(1)}, bf16[2,520,256]{2,1,0:T(8,128)(2,1)S(1)}, u32[]{:S(2)}, u32[]{:S(2)}) collective-permute-start(bf16[2,520,256]{2,1,0:T(8,128)(2,1)S(1)} %get-tuple-element.81), channel_id=1, source_target_pairs={{0,4},{1,5},{2,6},{3,7},{4,0},{5,1},{6,2},{7,3},{8,12},{9,13},{10,... | collective-permute-start | bytes 1597448 | tf_op jit(solution)/shard_map/ppermute | solution.py:26
  84.2 26.6 %collective-permute-start.17 = (bf16[2,520,256]{2,1,0:T(8,128)(2,1)S(1)}, bf16[2,520,256]{2,1,0:T(8,128)(2,1)S(1)}, u32[]{:S(2)}, u32[]{:S(2)}) collective-permute-start(bf16[2,520,256]{2,1,0:T(8,128)(2,1)S(1)} %get-tuple-element.82), channel_id=1, source_target_pairs={{0,8},{1,9},{2,10},{3,11},{4,12},{5,13},{6,14},{7,15},{8,0},{9,1},... | collective-permute-start | bytes 1597448 | tf_op jit(solution)/shard_map/ppermute | solution.py:26
  86.3 25.8 %collective-permute-start.18 = (bf16[2,520,256]{2,1,0:T(8,128)(2,1)S(1)}, bf16[2,520,256]{2,1,0:T(8,128)(2,1)S(1)}, u32[]{:S(2)}, u32[]{:S(2)}) collective-permute-start(bf16[2,520,256]{2,1,0:T(8,128)(2,1)S(1)} %get-tuple-element.83), channel_id=1, source_target_pairs={{0,12},{1,13},{2,14},{3,15},{4,8},{5,9},{6,10},{7,11},{8,4},{9,5},... | collective-permute-start | bytes 1597448 | tf_op jit(solution)/shard_map/ppermute | solution.py:26
  98.2 13.9 %collective-permute-start.20 = (bf16[2,520,256]{2,1,0:T(8,128)(2,1)S(1)}, bf16[2,520,256]{2,1,0:T(8,128)(2,1)S(1)}, u32[]{:S(2)}, u32[]{:S(2)}) collective-permute-start(bf16[2,520,256]{2,1,0:T(8,128)(2,1)S(1)} %get-tuple-element.97), channel_id=1, source_target_pairs={{0,1},{1,0},{2,3},{3,2},{4,5},{5,4},{6,7},{7,6},{8,9},{9,8},{10,11... | collective-permute-start | bytes 1597448 | tf_op jit(solution)/shard_map/ppermute | solution.py:26
  98.3 18.2 %collective-permute-start.21 = (bf16[2,520,256]{2,1,0:T(8,128)(2,1)S(1)}, bf16[2,520,256]{2,1,0:T(8,128)(2,1)S(1)}, u32[]{:S(2)}, u32[]{:S(2)}) collective-permute-start(bf16[2,520,256]{2,1,0:T(8,128)(2,1)S(1)} %get-tuple-element.98), channel_id=1, source_target_pairs={{0,2},{1,3},{2,0},{3,1},{4,6},{5,7},{6,4},{7,5},{8,10},{9,11},{10,... | collective-permute-start | bytes 1597448 | tf_op jit(solution)/shard_map/ppermute | solution.py:26
  101.7 19.0 %collective-permute-start.22 = (bf16[2,520,256]{2,1,0:T(8,128)(2,1)S(1)}, bf16[2,520,256]{2,1,0:T(8,128)(2,1)S(1)}, u32[]{:S(2)}, u32[]{:S(2)}) collective-permute-start(bf16[2,520,256]{2,1,0:T(8,128)(2,1)S(1)} %get-tuple-element.99), channel_id=1, source_target_pairs={{0,3},{1,2},{2,1},{3,0},{4,7},{5,6},{6,5},{7,4},{8,11},{9,10},{10,... | collective-permute-start | bytes 1597448 | tf_op jit(solution)/shard_map/ppermute | solution.py:26

commit v4 on v3

--- a/solution.py
+++ b/solution.py
@@ -24,6 +24,11 @@
 
 def xor_perm(array, axis, mask):
     return lax.ppermute(array, axis, [(i, i ^ mask) for i in range(lax.axis_size(axis))])
+
+
+def ring_perm(array, shift):
+    size = lax.axis_size("grp")
+    return lax.ppermute(array, "grp", [(i, (i + 2 * shift) % size) for i in range(size)])
 
 
 def whiten_kernel(spectra_ref, out_ref, rows):
@@ -55,20 +60,25 @@
     )(spectra)
 
 
-def pick_kernel(member_ref, partners_ref, *refs):
-    planes, out_ref = refs[:4], refs[4]
+def pick_kernel(where_ref, partners_ref, *refs):
+    blocks, tops, out_ref = refs[:3], refs[3:5], refs[5]
+    here = where_ref[1]
     for r in range(2):
-        distance = partners_ref[r, member_ref[0]] >> 1
-        for d in range(4):
-
-            @pl.when(distance == d)
+        shift = ((here ^ (partners_ref[r, where_ref[0]] >> 1)) - here) & 3
+        for s in range(4):
+
+            @pl.when(shift == s)
             def _():
-                out_ref[r] = planes[d][...]
-
-
-def merge_kernel(member_ref, partners_ref, mine_ref, other_ref, out_ref):
+                if s == 2:
+                    out_ref[r, : LANE // 2] = tops[0][...]
+                    out_ref[r, LANE // 2 :] = tops[1][...]
+                else:
+                    out_ref[r] = blocks[s - (s > 2)][...]
+
+
+def merge_kernel(where_ref, partners_ref, mine_ref, other_ref, out_ref):
     for r in range(2):
-        swap = partners_ref[r, member_ref[0]] & 1
+        swap = partners_ref[r, where_ref[0]] & 1
 
         @pl.when(swap == 1)
         def _():
@@ -79,7 +89,7 @@
             out_ref[r] = mine_ref[r]
 
 
-def choose(kernel, name, member, partners, arrays):
+def choose(kernel, name, where, partners, arrays):
     smem, whole = pl.BlockSpec(memory_space=pltpu.SMEM), pl.BlockSpec(memory_space=pltpu.VMEM)
     return pl.pallas_call(
         kernel,
@@ -87,7 +97,7 @@
         out_shape=jax.ShapeDtypeStruct((2, LANE, CH, LANE), jnp.bfloat16),
         compiler_params=vmem(10),
         name=name,
-    )(member, partners, *arrays)
+    )(where, partners, *arrays)
 
 
 def corr_kernel(factor, *refs):
@@ -168,34 +178,41 @@
     )(*row_blocks, *col_blocks, table)
 
 
-def finish_kernel(*refs):
+def finish_kernel(member_ref, *refs):
     parts, order_ref, out_ref, buf = refs[:8], refs[8], refs[9], refs[10]
-    for i2 in range(4):
-        for half in range(2):
-            i = i2 * 2 + half
-            quad, at = i // 4, (i // 2) % 2 * LANE
-            wide = jnp.concatenate([p[quad, :, at : at + LANE] for p in parts], 1)
+    z = member_ref[0] // 16
+    pair = pl.program_id(0)
+    at = pl.multiple_of(pair % 2 * LANE, LANE)
+    for half in range(2):
+        for far in range(2):
+            wide = jnp.concatenate(
+                [p[pair // 2, :, pl.ds(at, LANE)] for p in parts[far * 4 : far * 4 + 4]], 1
+            )
+            ordered = jnp.dot(wide, order_ref[far, half], preferred_element_type=jnp.float32)
+            tile = z ^ far
             for r in range(2):
-                ordered = jnp.dot(wide, order_ref[r, half], preferred_element_type=jnp.float32)
-                for tile in range(2):
-                    buf[pl.ds(half * 4 * LAGS + tile * 2 + r, LAGS, stride=4), :] = ordered[
-                        :LAGS, tile * LANE : (tile + 1) * LANE
-                    ]
-        out_ref[i2] = buf[...].astype(jnp.bfloat16)
-
-
-def finish(parts, order):
+                buf[pl.ds(half * 4 * LAGS + tile * 2 + r, LAGS, stride=4), :] = ordered[
+                    :LAGS, r * LANE : (r + 1) * LANE
+                ]
+    out_ref[0] = buf[...].astype(jnp.bfloat16)
+
+
+def finish(member, parts, order):
+    whole = pl.BlockSpec(memory_space=pltpu.VMEM)
     return pl.pallas_call(
         finish_kernel,
+        grid=(4,),
+        in_specs=[pl.BlockSpec(memory_space=pltpu.SMEM)] + [whole] * 9,
+        out_specs=pl.BlockSpec((1, 8 * LAGS, LANE), lambda i: (i, 0, 0)),
         out_shape=jax.ShapeDtypeStruct((4, 8 * LAGS, LANE), jnp.bfloat16),
         scratch_shapes=[pltpu.VMEM((8 * LAGS, LANE), jnp.float32)],
         compiler_params=vmem(18),
         name="finish",
-    )(*parts, order)
-
-
-def lag_table():
-    lag = jnp.arange(LAG_ROWS, dtype=jnp.int32)[:, None]
+    )(member, *parts, order)
+
+
+def lag_table(zero):
+    lag = jnp.arange(LAG_ROWS, dtype=jnp.int32)[:, None] + zero
     k = jnp.arange(2 * BINS, dtype=jnp.int32)[None, :]
     frequency = k % TAPS * LANE + k // 8
     n = frequency * (lag - BINS // 2) + k // TAPS % 2 * (BINS // 2)
@@ -212,42 +229,50 @@
 
 
 def column_order(member):
-    z, x, y = member // 16, member // 4 % 4, member % 4
-    at = jnp.arange(1024, dtype=jnp.int32)
-    far, d, half, e, turn, ch = at // 512, at // 128 % 4, at // 64 % 2, at // 16 % 4, at // 8 % 2, at % 8
-    dx, dy = jnp.where(far == 1, e, d), jnp.where(far == 1, d, e)
-    target = (z ^ far) * 128 + (x ^ dx) * 32 + (y ^ dy) * 8 + ch
-    target = target + 256 * half + 512 * turn
+    x, y = member // 4 % 4, member % 4
+    at = jnp.arange(512, dtype=jnp.int32)
+    d, half, e, turn, ch = at // 128, at // 64 % 2, at // 16 % 4, at // 8 % 2, at % 8
+    first = (x ^ d) * 32 + (y ^ e) * 8 + ch
+    second = (x ^ e) * 32 + (y ^ d) * 8 + ch
+    target = jnp.stack([first, second], 0) + (128 * turn + 256 * half)[None]
     column = jnp.arange(256, dtype=jnp.int32)[None, None, None, :]
     side = jnp.arange(2, dtype=jnp.int32)[None, :, None, None]
-    turns = jnp.arange(2, dtype=jnp.int32)[:, None, None, None]
-    return (target[None, None, :, None] == column + 256 * side + 512 * turns).astype(jnp.bfloat16)
+    return (target[:, None, :, None] == column + 256 * side).astype(jnp.bfloat16)
 
 
 def on_device(spectra, partners):
     member = lax.axis_index("mem").astype(jnp.int32)
+    where = jnp.stack([member, lax.axis_index("grp").astype(jnp.int32) >> 1])
+    factor = math.sqrt(2.0 / (BINS * (COMP // 2)))
     white = whiten(spectra)
+
     row_masks, col_masks = (4, 1), (1, 4)
     rows = [[white, None, None, None], [white, None, None, None]]
-    source = white
-    for d in (1, 3, 2):
-        sent = [xor_perm(source, "mem", d * m) for m in row_masks]
-        source, sent = lax.optimization_barrier((source, sent))
-        rows[0][d], rows[1][d] = sent
-    planes = [white] + [xor_perm(white, "grp", 2 * d) for d in range(1, 4)]
-    table = lag_table()
-    order = column_order(member)
-    factor = math.sqrt(2.0 / (BINS * (COMP // 2)))
-    planes, rows, table, order = lax.optimization_barrier((planes, rows, table, order))
-
-    mine = choose(pick_kernel, "pick", member.reshape(1), partners, planes)
+
+    for d in (1, 3):
+        rows[1][d] = xor_perm(white, "mem", d * row_masks[1])
+    up, down = ring_perm(white, 1), ring_perm(white, -1)
+    up, down, rows, source = lax.optimization_barrier((up, down, rows, white))
+    for n in range(2):
+        rows[n][2] = xor_perm(source, "mem", 2 * row_masks[n])
+    tops = [ring_perm(up[: LANE // 2], 1), ring_perm(down[LANE // 2 :], -1)]
+    up, down, tops, rows, where = lax.optimization_barrier((up, down, tops, rows, where))
+
+    mine = choose(pick_kernel, "pick", where, partners, [white, down, up, *tops])
     other = xor_perm(mine, "grp", 1)
-    near = choose(merge_kernel, "merge", member.reshape(1), partners, [mine, other])
+    near = choose(merge_kernel, "merge", where, partners, [mine, other])
+    near, where, source = lax.optimization_barrier((near, where, white))
+    for d in (3, 1):
+        rows[0][d] = xor_perm(source, "mem", d * row_masks[0])
     across = xor_perm(near, "mem", 16)
     cols = [[near, None, None, None], [across, None, None, None]]
     for e in (3, 1):
         cols[0][e] = xor_perm(near, "mem", e * col_masks[0])
-    cols, near, across = lax.optimization_barrier((cols, near, across))
+    table = lag_table(where[0] - member)
+    order = column_order(where[0])
+    cols, rows, near, across, table, order = lax.optimization_barrier(
+        (cols, rows, near, across, table, order)
+    )
     for e in (3, 1):
         cols[1][e] = xor_perm(across, "mem", e * col_masks[1])
     cols[0][2] = xor_perm(near, "mem", 2 * col_masks[0])
@@ -258,7 +283,7 @@
         sums = correlate(rows[n], cols[n], table, factor)
         parts += [sums[0]] + [xor_perm(sums[d], "mem", d * row_masks[n]) for d in range(1, 4)]
         cols[1], sums = lax.optimization_barrier((cols[1], sums[0]))
-    packed = finish(parts, order)
+    packed = finish(member.reshape(1), parts, order)
     result = packed.reshape(CH, LAGS, 2, 2, LANE)
     return jnp.transpose(result, (0, 3, 2, 4, 1)).reshape(CH, 2, 256, LAGS)
 

time: 128 us -> 128 us (level)
    ppermute x23 -> x20, waiting for transfers between devices: 60.7 us -> 39.7 us  [xor_perm(): lax.ppermute(array, axis, [(i, i ^ mask) for i in range(lax.axis_size(axi...]
    ppermute x0 -> x4, waiting for transfers between devices: none -> 20.6 us  [ring_perm(): lax.ppermute(array, 'grp', [(i, (i + 2 * shift) % size) for i in range(si...]
    ppermute x23 -> x20, starting transfers between devices: 35.7 us -> 26.2 us  [xor_perm(): lax.ppermute(array, axis, [(i, i ^ mask) for i in range(lax.axis_size(axi...]
    ppermute x0 -> x4, starting transfers between devices: none -> 9.31 us  [ring_perm(): lax.ppermute(array, 'grp', [(i, (i + 2 * shift) % size) for i in range(si...]
    pallas_call x1, Pallas kernels: 7.1 us -> 4.89 us  [finish(): pl.pallas_call(finish_kernel, grid=(4,), in_specs=[pl.BlockSpec(memory_sp...]
  transfers between devices with their start and end apart: 23 -> 24, of which waited for: 17 -> 16; matrix products, arithmetic and copies ran while one was open for 6% -> 6% of each run, Pallas kernels for 11% -> 11%
where the time goes in v4:
time: 128 us; the launch traced here: 127 us
  waiting for transfers between devices  60.3 us (47%)
  starting transfers between devices  35.5 us (28%)
  Pallas kernels  21.4 us (17%)
  other arithmetic  7.48 us (6%)
  local copies, waits for them, and re-layouts  1.65 us (1%)
    ppermute x20, waiting for transfers between devices, xor_perm(): lax.ppermute(array, axis, [(i, i ^ mask) for i in range(lax.axis_size(axi...  39.7 us
    ppermute x20, starting transfers between devices, xor_perm(): lax.ppermute(array, axis, [(i, i ^ mask) for i in range(lax.axis_size(axi...  26.2 us
    ppermute x4, waiting for transfers between devices, ring_perm(): lax.ppermute(array, 'grp', [(i, (i + 2 * shift) % size) for i in range(si...  20.6 us
    pallas_call x2, Pallas kernels, correlate(): pl.pallas_call(body, out_shape=[jax.ShapeDtypeStruct((2, LAG_ROWS, 256),...  14.4 us
    ppermute x4, starting transfers between devices, ring_perm(): lax.ppermute(array, 'grp', [(i, (i + 2 * shift) % size) for i in range(si...  9.31 us
    convert_element_type x1, other arithmetic, lag_table(): return jnp.where(lag < LAGS, values, 0.0).astype(jnp.bfloat16)  7.04 us
    pallas_call x1, Pallas kernels, finish(): pl.pallas_call(finish_kernel, grid=(4,), in_specs=[pl.BlockSpec(memory_sp...  4.89 us
  transfers between devices with their start and end apart: 24, of which 16 were waited for; matrix products, arithmetic and copies ran while one was open for 6% of the time, Pallas kernels for 11%

profile of v4, /device:TPU:8, one launch (start us, length us, event | category | flops | bytes accessed | tf_op | source)
XLA Modules:
  0.0 126.7 jit_solution(10247092486236092945)
XLA Ops:
  0.0 0.0 copy-start
  0.0 0.9 copy-done
  1.0 0.0 copy-start.2
  1.0 0.8 whiten.1.refs_0_
  1.8 1.7 %collective-permute-start.3 = (bf16[128,8,128]{2,1,0:T(8,128)(2,1)S(1)}, bf16[128,8,128]{2,1,0:T(8,128)(2,1)S(1)}, u32[]{:S(2)}, u32[]{:S(2)}) collective-permute-start(bf16[128,8,128]{2,1,0:T(8,128)(2,1)S(1)} %whiten.1.refs_0_), channel_id=1, source_target_pairs={{0,3},{1,2},{2,1},{3,0},{4,7},{5,6},{6,5},{7,4},{8,11},{9,10},{10,... | collective-permute-start | bytes 786440 | tf_op jit(solution)/shard_map/ppermute | solution.py:26
  3.5 1.9 %collective-permute-start.2 = (bf16[128,8,128]{2,1,0:T(8,128)(2,1)S(1)}, bf16[128,8,128]{2,1,0:T(8,128)(2,1)S(1)}, u32[]{:S(2)}, u32[]{:S(2)}) collective-permute-start(bf16[128,8,128]{2,1,0:T(8,128)(2,1)S(1)} %whiten.1.refs_0_), channel_id=1, source_target_pairs={{0,1},{1,0},{2,3},{3,2},{4,5},{5,4},{6,7},{7,6},{8,9},{9,8},{10,11... | collective-permute-start | bytes 786440 | tf_op jit(solution)/shard_map/ppermute | solution.py:26
  5.3 6.3 %collective-permute-start.1 = (bf16[128,8,128]{2,1,0:T(8,128)(2,1)S(1)}, bf16[128,8,128]{2,1,0:T(8,128)(2,1)S(1)}, u32[]{:S(2)}, u32[]{:S(2)}) collective-permute-start(bf16[128,8,128]{2,1,0:T(8,128)(2,1)S(1)} %whiten.1.refs_0_), channel_id=1, source_target_pairs={{0,192},{32,224},{64,0},{96,32},{128,64},{160,96},{192,128},{224,1... | collective-permute-start | bytes 786440 | tf_op jit(solution)/shard_map/ppermute | solution.py:31
  11.6 0.0 collective-permute-start
  11.6 0.0 collective-permute-done.3.refs_3_
  11.6 0.0 collective-permute-done.2.refs_1_
  11.7 10.6 %collective-permute-done.1.refs_1_ = bf16[128,8,128]{2,1,0:T(8,128)(2,1)S(1)} collective-permute-done((bf16[128,8,128]{2,1,0:T(8,128)(2,1)S(1)}, bf16[128,8,128]{2,1,0:T(8,128)(2,1)S(1)}, u32[]{:S(2)}, u32[]{:S(2)}) %collective-permute-start.1) | collective-permute-done | bytes 262176 | tf_op jit(solution)/shard_map/ppermute | solution.py:31
  22.3 3.8 %collective-permute-done.refs_2_ = bf16[128,8,128]{2,1,0:T(8,128)(2,1)S(1)} collective-permute-done((bf16[128,8,128]{2,1,0:T(8,128)(2,1)S(1)}, bf16[128,8,128]{2,1,0:T(8,128)(2,1)S(1)}, u32[]{:S(2)}, u32[]{:S(2)}) %collective-permute-start) | collective-permute-done | bytes 262176 | tf_op jit(solution)/shard_map/ppermute | solution.py:31
  26.1 0.0 collective-permute-start.7
  26.2 3.0 %collective-permute-start.6 = (bf16[128,8,128]{2,1,0:T(8,128)(2,1)S(1)}, bf16[128,8,128]{2,1,0:T(8,128)(2,1)S(1)}, u32[]{:S(2)}, u32[]{:S(2)}) collective-permute-start(bf16[128,8,128]{2,1,0:T(8,128)(2,1)S(1)} %whiten.1.refs_0_), channel_id=1, source_target_pairs={{0,8},{1,9},{2,10},{3,11},{4,12},{5,13},{6,14},{7,15},{8,0},{9,1},... | collective-permute-start | bytes 786440 | tf_op jit(solution)/shard_map/ppermute | solution.py:26
  29.2 0.8 collective-permute-start.5
  30.0 2.2 %collective-permute-start.4 = (bf16[64,8,128]{2,1,0:T(8,128)(2,1)S(1)}, bf16[64,8,128]{2,1,0:T(8,128)(2,1)S(1)}, u32[]{:S(2)}, u32[]{:S(2)}) collective-permute-start(bf16[64,8,128]{2,1,0:T(8,128)(2,1)S(1)} %slice.10), channel_id=1, source_target_pairs={{0,64},{32,96},{64,128},{96,160},{128,192},{160,224},{192,0},{224,... | collective-permute-start | bytes 393224 | tf_op jit(solution)/shard_map/ppermute | solution.py:31
  32.2 0.1 pad_add_fusion.where_ref
  32.3 4.3 %collective-permute-done.5.refs_4_ = bf16[64,8,128]{2,1,0:T(8,128)(2,1)S(1)} collective-permute-done((bf16[64,8,128]{2,1,0:T(8,128)(2,1)S(1)}, bf16[64,8,128]{2,1,0:T(8,128)(2,1)S(1)}, u32[]{:S(2)}, u32[]{:S(2)}) %collective-permute-start.5) | collective-permute-done | bytes 131104 | tf_op jit(solution)/shard_map/ppermute | solution.py:31
  36.6 1.8 %collective-permute-done.4.refs_3_ = bf16[64,8,128]{2,1,0:T(8,128)(2,1)S(1)} collective-permute-done((bf16[64,8,128]{2,1,0:T(8,128)(2,1)S(1)}, bf16[64,8,128]{2,1,0:T(8,128)(2,1)S(1)}, u32[]{:S(2)}, u32[]{:S(2)}) %collective-permute-start.4) | collective-permute-done | bytes 131104 | tf_op jit(solution)/shard_map/ppermute | solution.py:31
  38.4 0.0 collective-permute-done.7.refs_2_
  38.4 0.0 collective-permute-done.6.refs_2_
  38.4 0.0 copy-start.1
  38.4 0.7 copy-done.1
  39.1 0.6 pick.1.mine_ref
  39.7 0.1 collective-permute-start.8
  39.8 0.1 iota_add_fusion.1
  39.9 1.8 %collective-permute-done.8.other_ref = bf16[2,128,8,128]{3,2,1,0:T(8,128)(2,1)S(1)} collective-permute-done((bf16[2,128,8,128]{3,2,1,0:T(8,128)(2,1)S(1)}, bf16[2,128,8,128]{3,2,1,0:T(8,128)(2,1)S(1)}, u32[]{:S(2)}, u32[]{:S(2)}) %collective-permute-start.8) | collective-permute-done | bytes 524320 | tf_op jit(solution)/shard_map/ppermute | solution.py:26
  41.7 0.0 copy-done.2
  41.7 0.6 merge.1.refs_4_
  42.6 1.2 collective-permute-start.13
  43.8 0.0 collective-permute-start.12
  43.8 0.0 collective-permute-start.11
  43.8 1.5 %collective-permute-start.10 = (bf16[2,128,8,128]{3,2,1,0:T(8,128)(2,1)S(1)}, bf16[2,128,8,128]{3,2,1,0:T(8,128)(2,1)S(1)}, u32[]{:S(2)}, u32[]{:S(2)}) collective-permute-start(bf16[2,128,8,128]{3,2,1,0:T(8,128)(2,1)S(1)} %merge.1.refs_4_), channel_id=1, source_target_pairs={{0,3},{1,2},{2,1},{3,0},{4,7},{5,6},{6,5},{7,4},{8,11},{9,10},{10,... | collective-permute-start | bytes 1572872 | tf_op jit(solution)/shard_map/ppermute | solution.py:26
  45.3 3.0 %collective-permute-start.9 = (bf16[2,128,8,128]{3,2,1,0:T(8,128)(2,1)S(1)}, bf16[2,128,8,128]{3,2,1,0:T(8,128)(2,1)S(1)}, u32[]{:S(2)}, u32[]{:S(2)}) collective-permute-start(bf16[2,128,8,128]{3,2,1,0:T(8,128)(2,1)S(1)} %merge.1.refs_4_), channel_id=1, source_target_pairs={{0,1},{1,0},{2,3},{3,2},{4,5},{5,4},{6,7},{7,6},{8,9},{9,8},{10,11... | collective-permute-start | bytes 1572872 | tf_op jit(solution)/shard_map/ppermute | solution.py:26
  48.3 7.0 %fusion.7.refs_8_ = bf16[520,1024]{1,0:T(8,128)(2,1)S(1)} fusion(s32[1024]{0:T(1024)S(1)} %get-tuple-element.120, s32[520]{0:T(1024)S(1)} %fusion.33, s32[1024]{0:T(1024)S(1)} %get-tuple-element.119, pred[520]{0:T(1024)(128)(4,1)S(1)} %fusion.34), kind=kLoop, calls=%fused_computation.22 | loop fusion | flops 48988160 | bytes 1075752 | tf_op jit(solution)/shard_map/convert_element_type | solution.py:228
  55.4 0.2 compare_convert_fusion.refs_8_
  55.6 0.0 collective-permute-done.13.refs_3_
  55.6 0.0 collective-permute-done.12.refs_1_
  55.6 1.9 %collective-permute-done.11.refs_4_ = bf16[2,128,8,128]{3,2,1,0:T(8,128)(2,1)S(1)} collective-permute-done((bf16[2,128,8,128]{3,2,1,0:T(8,128)(2,1)S(1)}, bf16[2,128,8,128]{3,2,1,0:T(8,128)(2,1)S(1)}, u32[]{:S(2)}, u32[]{:S(2)}) %collective-permute-start.11) | collective-permute-done | bytes 524320 | tf_op jit(solution)/shard_map/ppermute | solution.py:26
  57.5 0.0 collective-permute-done.10.refs_7_
  57.5 2.4 %collective-permute-done.9.refs_5_ = bf16[2,128,8,128]{3,2,1,0:T(8,128)(2,1)S(1)} collective-permute-done((bf16[2,128,8,128]{3,2,1,0:T(8,128)(2,1)S(1)}, bf16[2,128,8,128]{3,2,1,0:T(8,128)(2,1)S(1)}, u32[]{:S(2)}, u32[]{:S(2)}) %collective-permute-start.9) | collective-permute-done | bytes 524320 | tf_op jit(solution)/shard_map/ppermute | solution.py:26
  59.8 2.1 %collective-permute-start.14 = (bf16[2,128,8,128]{3,2,1,0:T(8,128)(2,1)S(1)}, bf16[2,128,8,128]{3,2,1,0:T(8,128)(2,1)S(1)}, u32[]{:S(2)}, u32[]{:S(2)}) collective-permute-start(bf16[2,128,8,128]{3,2,1,0:T(8,128)(2,1)S(1)} %merge.1.refs_4_), channel_id=1, source_target_pairs={{0,2},{1,3},{2,0},{3,1},{4,6},{5,7},{6,4},{7,5},{8,10},{9,11},{10,... | collective-permute-start | bytes 1572872 | tf_op jit(solution)/shard_map/ppermute | solution.py:26
  61.9 2.1 %collective-permute-start.16 = (bf16[2,128,8,128]{3,2,1,0:T(8,128)(2,1)S(1)}, bf16[2,128,8,128]{3,2,1,0:T(8,128)(2,1)S(1)}, u32[]{:S(2)}, u32[]{:S(2)}) collective-permute-start(bf16[2,128,8,128]{3,2,1,0:T(8,128)(2,1)S(1)} %collective-permute-done.11.refs_4_), channel_id=1, source_target_pairs={{0,12},{1,13},{2,14},{3,15},{4,8},{5,9},{6,10},{7,11},{8,4},{9,5},... | collective-permute-start | bytes 1572872 | tf_op jit(solution)/shard_map/ppermute | solution.py:26
  64.0 1.1 collective-permute-start.15
  65.1 8.9 %collective-permute-done.14.refs_6_ = bf16[2,128,8,128]{3,2,1,0:T(8,128)(2,1)S(1)} collective-permute-done((bf16[2,128,8,128]{3,2,1,0:T(8,128)(2,1)S(1)}, bf16[2,128,8,128]{3,2,1,0:T(8,128)(2,1)S(1)}, u32[]{:S(2)}, u32[]{:S(2)}) %collective-permute-start.14) | collective-permute-done | bytes 524320 | tf_op jit(solution)/shard_map/ppermute | solution.py:26
  74.1 1.5 %collective-permute-done.16.refs_7_ = bf16[2,128,8,128]{3,2,1,0:T(8,128)(2,1)S(1)} collective-permute-done((bf16[2,128,8,128]{3,2,1,0:T(8,128)(2,1)S(1)}, bf16[2,128,8,128]{3,2,1,0:T(8,128)(2,1)S(1)}, u32[]{:S(2)}, u32[]{:S(2)}) %collective-permute-start.16) | collective-permute-done | bytes 524320 | tf_op jit(solution)/shard_map/ppermute | solution.py:26
  75.6 0.6 collective-permute-done.15.refs_5_
  76.2 1.4 %collective-permute-start.20 = (bf16[2,128,8,128]{3,2,1,0:T(8,128)(2,1)S(1)}, bf16[2,128,8,128]{3,2,1,0:T(8,128)(2,1)S(1)}, u32[]{:S(2)}, u32[]{:S(2)}) collective-permute-start(bf16[2,128,8,128]{3,2,1,0:T(8,128)(2,1)S(1)} %collective-permute-done.11.refs_4_), channel_id=1, source_target_pairs={{0,8},{1,9},{2,10},{3,11},{4,12},{5,13},{6,14},{7,15},{8,0},{9,1},... | collective-permute-start | bytes 1572872 | tf_op jit(solution)/shard_map/ppermute | solution.py:26
  77.6 7.7 %correlate.2 = (bf16[2,520,256]{2,1,0:T(8,128)(2,1)S(1)}, bf16[2,520,256]{2,1,0:T(8,128)(2,1)S(1)}, bf16[2,520,256]{2,1,0:T(8,128)(2,1)S(1)}, bf16[2,520,256]{2,1,0:T(8,128)(2,1)S(1)}) custom-call(bf16[128,8,128]{2,1,0:T(8,128)(2,1)S(1)} %whiten.1.refs_0_, bf16[128,8,128]{2,1,0:T(8,128)(2,1)} %collective-permute-done.12.refs_1_, ...), custom_call_target="tpu_custom_call" | custom-call | flops 3254779904 | bytes 7340032 | tf_op jit(solution)/shard_map/correlate/pallas_call | solution.py:164
  85.3 1.0 collective-permute-start.17
  86.3 2.6 %collective-permute-start.18 = (bf16[2,520,256]{2,1,0:T(8,128)(2,1)S(1)}, bf16[2,520,256]{2,1,0:T(8,128)(2,1)S(1)}, u32[]{:S(2)}, u32[]{:S(2)}) collective-permute-start(bf16[2,520,256]{2,1,0:T(8,128)(2,1)S(1)} %get-tuple-element.100), channel_id=1, source_target_pairs={{0,8},{1,9},{2,10},{3,11},{4,12},{5,13},{6,14},{7,15},{8,0},{9,1},... | collective-permute-start | bytes 1597448 | tf_op jit(solution)/shard_map/ppermute | solution.py:26
  88.9 1.1 collective-permute-start.19
  90.1 1.4 %collective-permute-done.20.refs_6_ = bf16[2,128,8,128]{3,2,1,0:T(8,128)(2,1)S(1)} collective-permute-done((bf16[2,128,8,128]{3,2,1,0:T(8,128)(2,1)S(1)}, bf16[2,128,8,128]{3,2,1,0:T(8,128)(2,1)S(1)}, u32[]{:S(2)}, u32[]{:S(2)}) %collective-permute-start.20) | collective-permute-done | bytes 524320 | tf_op jit(solution)/shard_map/ppermute | solution.py:26
  91.4 6.7 %correlate.3 = (bf16[2,520,256]{2,1,0:T(8,128)(2,1)S(1)}, bf16[2,520,256]{2,1,0:T(8,128)(2,1)S(1)}, bf16[2,520,256]{2,1,0:T(8,128)(2,1)S(1)}, bf16[2,520,256]{2,1,0:T(8,128)(2,1)S(1)}) custom-call(bf16[128,8,128]{2,1,0:T(8,128)(2,1)S(1)} %whiten.1.refs_0_, bf16[128,8,128]{2,1,0:T(8,128)(2,1)S(1)} %collective-permute-done.2.refs_1_, ...), custom_call_target="tpu_custom_call" | custom-call | flops 3254779904 | bytes 7340032 | tf_op jit(solution)/shard_map/correlate/pallas_call | solution.py:164
  98.1 0.1 collective-permute-start.21
  98.2 1.9 %collective-permute-start.22 = (bf16[2,520,256]{2,1,0:T(8,128)(2,1)S(1)}, bf16[2,520,256]{2,1,0:T(8,128)(2,1)S(1)}, u32[]{:S(2)}, u32[]{:S(2)}) collective-permute-start(bf16[2,520,256]{2,1,0:T(8,128)(2,1)S(1)} %get-tuple-element.116), channel_id=1, source_target_pairs={{0,2},{1,3},{2,0},{3,1},{4,6},{5,7},{6,4},{7,5},{8,10},{9,11},{10,... | collective-permute-start | bytes 1597448 | tf_op jit(solution)/shard_map/ppermute | solution.py:26
  100.1 2.5 %collective-permute-done.17.refs_1_ = bf16[2,520,256]{2,1,0:T(8,128)(2,1)S(1)} collective-permute-done((bf16[2,520,256]{2,1,0:T(8,128)(2,1)S(1)}, bf16[2,520,256]{2,1,0:T(8,128)(2,1)S(1)}, u32[]{:S(2)}, u32[]{:S(2)}) %collective-permute-start.17) | collective-permute-done | bytes 532512 | tf_op jit(solution)/shard_map/ppermute | solution.py:26
  102.6 0.4 collective-permute-start.23
  103.0 8.9 %collective-permute-done.18.refs_2_ = bf16[2,520,256]{2,1,0:T(8,128)(2,1)S(1)} collective-permute-done((bf16[2,520,256]{2,1,0:T(8,128)(2,1)S(1)}, bf16[2,520,256]{2,1,0:T(8,128)(2,1)S(1)}, u32[]{:S(2)}, u32[]{:S(2)}) %collective-permute-start.18) | collective-permute-done | bytes 532512 | tf_op jit(solution)/shard_map/ppermute | solution.py:26
  111.8 1.2 collective-permute-done.19.refs_3_
  113.0 0.0 collective-permute-done.21.refs_5_
  113.0 5.6 %collective-permute-done.22.refs_6_ = bf16[2,520,256]{2,1,0:T(8,128)(2,1)S(1)} collective-permute-done((bf16[2,520,256]{2,1,0:T(8,128)(2,1)S(1)}, bf16[2,520,256]{2,1,0:T(8,128)(2,1)S(1)}, u32[]{:S(2)}, u32[]{:S(2)}) %collective-permute-start.22) | collective-permute-done | bytes 532512 | tf_op jit(solution)/shard_map/ppermute | solution.py:26
  118.7 3.1 %collective-permute-done.23.refs_7_ = bf16[2,520,256]{2,1,0:T(8,128)(2,1)S(1)} collective-permute-done((bf16[2,520,256]{2,1,0:T(8,128)(2,1)S(1)}, bf16[2,520,256]{2,1,0:T(8,128)(2,1)S(1)}, u32[]{:S(2)}, u32[]{:S(2)}) %collective-permute-start.23) | collective-permute-done | bytes 532512 | tf_op jit(solution)/shard_map/ppermute | solution.py:26
  121.8 4.9 %finish.1 = bf16[4,4104,128]{2,1,0:T(8,128)(2,1)} custom-call(s32[1]{0:T(128)} %bitcast.member_ref, bf16[2,520,256]{2,1,0:T(8,128)(2,1)S(1)} %get-tuple-element.98.refs_0_, bf16[2,520,256]{2,1,0:T(8,128)(2,1)S(1)} %collective-permute-done.17.refs_1_, bf16[2,520,256]{2,1,0:T(8,128)(2,1)S(1)} %collective-permute-done.18.refs_2_, ...), custom_call_target="tpu_custom_call" | custom-call | tf_op jit(solution)/shard_map/finish/pallas_call | solution.py:202
  (9 shorter events, 0.1 us)
Async XLA Ops:
  0.0 0.9 copy-start
  1.0 40.8 %copy-start.2 = (s32[2,32]{1,0:T(2,128)S(1)}, s32[2,32]{1,0:T(2,128)}, u32[]{:S(2)}) copy-start(s32[2,32]{1,0:T(2,128)} %partners_ref.3) | copy-start | bytes 772
  1.8 9.9 %collective-permute-start.3 = (bf16[128,8,128]{2,1,0:T(8,128)(2,1)S(1)}, bf16[128,8,128]{2,1,0:T(8,128)(2,1)S(1)}, u32[]{:S(2)}, u32[]{:S(2)}) collective-permute-start(bf16[128,8,128]{2,1,0:T(8,128)(2,1)S(1)} %whiten.1.refs_0_), channel_id=1, source_target_pairs={{0,3},{1,2},{2,1},{3,0},{4,7},{5,6},{6,5},{7,4},{8,11},{9,10},{10,... | collective-permute-start | bytes 786440 | tf_op jit(solution)/shard_map/ppermute | solution.py:26
  3.5 8.2 %collective-permute-start.2 = (bf16[128,8,128]{2,1,0:T(8,128)(2,1)S(1)}, bf16[128,8,128]{2,1,0:T(8,128)(2,1)S(1)}, u32[]{:S(2)}, u32[]{:S(2)}) collective-permute-start(bf16[128,8,128]{2,1,0:T(8,128)(2,1)S(1)} %whiten.1.refs_0_), channel_id=1, source_target_pairs={{0,1},{1,0},{2,3},{3,2},{4,5},{5,4},{6,7},{7,6},{8,9},{9,8},{10,11... | collective-permute-start | bytes 786440 | tf_op jit(solution)/shard_map/ppermute | solution.py:26
  5.3 17.0 %collective-permute-start.1 = (bf16[128,8,128]{2,1,0:T(8,128)(2,1)S(1)}, bf16[128,8,128]{2,1,0:T(8,128)(2,1)S(1)}, u32[]{:S(2)}, u32[]{:S(2)}) collective-permute-start(bf16[128,8,128]{2,1,0:T(8,128)(2,1)S(1)} %whiten.1.refs_0_), channel_id=1, source_target_pairs={{0,192},{32,224},{64,0},{96,32},{128,64},{160,96},{192,128},{224,1... | collective-permute-start | bytes 786440 | tf_op jit(solution)/shard_map/ppermute | solution.py:31
  11.6 14.5 %collective-permute-start = (bf16[128,8,128]{2,1,0:T(8,128)(2,1)S(1)}, bf16[128,8,128]{2,1,0:T(8,128)(2,1)S(1)}, u32[]{:S(2)}, u32[]{:S(2)}) collective-permute-start(bf16[128,8,128]{2,1,0:T(8,128)(2,1)S(1)} %whiten.1.refs_0_), channel_id=1, source_target_pairs={{0,64},{32,96},{64,128},{96,160},{128,192},{160,224},{192,0},{224,... | collective-permute-start | bytes 786440 | tf_op jit(solution)/shard_map/ppermute | solution.py:31
  26.1 12.3 %collective-permute-start.7 = (bf16[128,8,128]{2,1,0:T(8,128)(2,1)S(1)}, bf16[128,8,128]{2,1,0:T(8,128)(2,1)S(1)}, u32[]{:S(2)}, u32[]{:S(2)}) collective-permute-start(bf16[128,8,128]{2,1,0:T(8,128)(2,1)S(1)} %whiten.1.refs_0_), channel_id=1, source_target_pairs={{0,2},{1,3},{2,0},{3,1},{4,6},{5,7},{6,4},{7,5},{8,10},{9,11},{10,... | collective-permute-start | bytes 786440 | tf_op jit(solution)/shard_map/ppermute | solution.py:26
  26.2 12.2 %collective-permute-start.6 = (bf16[128,8,128]{2,1,0:T(8,128)(2,1)S(1)}, bf16[128,8,128]{2,1,0:T(8,128)(2,1)S(1)}, u32[]{:S(2)}, u32[]{:S(2)}) collective-permute-start(bf16[128,8,128]{2,1,0:T(8,128)(2,1)S(1)} %whiten.1.refs_0_), channel_id=1, source_target_pairs={{0,8},{1,9},{2,10},{3,11},{4,12},{5,13},{6,14},{7,15},{8,0},{9,1},... | collective-permute-start | bytes 786440 | tf_op jit(solution)/shard_map/ppermute | solution.py:26
  29.2 7.4 %collective-permute-start.5 = (bf16[64,8,128]{2,1,0:T(8,128)(2,1)S(1)}, bf16[64,8,128]{2,1,0:T(8,128)(2,1)S(1)}, u32[]{:S(2)}, u32[]{:S(2)}) collective-permute-start(bf16[64,8,128]{2,1,0:T(8,128)(2,1)S(1)} %slice.11), channel_id=1, source_target_pairs={{0,192},{32,224},{64,0},{96,32},{128,64},{160,96},{192,128},{224,1... | collective-permute-start | bytes 393224 | tf_op jit(solution)/shard_map/ppermute | solution.py:31
  30.0 8.4 %collective-permute-start.4 = (bf16[64,8,128]{2,1,0:T(8,128)(2,1)S(1)}, bf16[64,8,128]{2,1,0:T(8,128)(2,1)S(1)}, u32[]{:S(2)}, u32[]{:S(2)}) collective-permute-start(bf16[64,8,128]{2,1,0:T(8,128)(2,1)S(1)} %slice.10), channel_id=1, source_target_pairs={{0,64},{32,96},{64,128},{96,160},{128,192},{160,224},{192,0},{224,... | collective-permute-start | bytes 393224 | tf_op jit(solution)/shard_map/ppermute | solution.py:31
  38.4 0.7 copy-start.1
  39.7 2.0 %collective-permute-start.8 = (bf16[2,128,8,128]{3,2,1,0:T(8,128)(2,1)S(1)}, bf16[2,128,8,128]{3,2,1,0:T(8,128)(2,1)S(1)}, u32[]{:S(2)}, u32[]{:S(2)}) collective-permute-start(bf16[2,128,8,128]{3,2,1,0:T(8,128)(2,1)S(1)} %pick.1.mine_ref), channel_id=1, source_target_pairs={{0,32},{32,0},{64,96},{96,64},{128,160},{160,128},{192,224},{224,1... | collective-permute-start | bytes 1572872 | tf_op jit(solution)/shard_map/ppermute | solution.py:26
  42.6 13.0 %collective-permute-start.13 = (bf16[128,8,128]{2,1,0:T(8,128)(2,1)S(1)}, bf16[128,8,128]{2,1,0:T(8,128)(2,1)}, u32[]{:S(2)}, u32[]{:S(2)}) collective-permute-start(bf16[128,8,128]{2,1,0:T(8,128)(2,1)S(1)} %whiten.1.refs_0_), channel_id=1, source_target_pairs={{0,12},{1,13},{2,14},{3,15},{4,8},{5,9},{6,10},{7,11},{8,4},{9,5},... | collective-permute-start | bytes 786440 | tf_op jit(solution)/shard_map/ppermute | solution.py:26
  43.8 11.8 %collective-permute-start.12 = (bf16[128,8,128]{2,1,0:T(8,128)(2,1)S(1)}, bf16[128,8,128]{2,1,0:T(8,128)(2,1)}, u32[]{:S(2)}, u32[]{:S(2)}) collective-permute-start(bf16[128,8,128]{2,1,0:T(8,128)(2,1)S(1)} %whiten.1.refs_0_), channel_id=1, source_target_pairs={{0,4},{1,5},{2,6},{3,7},{4,0},{5,1},{6,2},{7,3},{8,12},{9,13},{10,... | collective-permute-start | bytes 786440 | tf_op jit(solution)/shard_map/ppermute | solution.py:26
  43.8 13.7 %collective-permute-start.11 = (bf16[2,128,8,128]{3,2,1,0:T(8,128)(2,1)S(1)}, bf16[2,128,8,128]{3,2,1,0:T(8,128)(2,1)S(1)}, u32[]{:S(2)}, u32[]{:S(2)}) collective-permute-start(bf16[2,128,8,128]{3,2,1,0:T(8,128)(2,1)S(1)} %merge.1.refs_4_), channel_id=1, source_target_pairs={{0,16},{1,17},{2,18},{3,19},{4,20},{5,21},{6,22},{7,23},{8,24},{9,... | collective-permute-start | bytes 1572872 | tf_op jit(solution)/shard_map/ppermute | solution.py:26
  43.8 13.7 %collective-permute-start.10 = (bf16[2,128,8,128]{3,2,1,0:T(8,128)(2,1)S(1)}, bf16[2,128,8,128]{3,2,1,0:T(8,128)(2,1)S(1)}, u32[]{:S(2)}, u32[]{:S(2)}) collective-permute-start(bf16[2,128,8,128]{3,2,1,0:T(8,128)(2,1)S(1)} %merge.1.refs_4_), channel_id=1, source_target_pairs={{0,3},{1,2},{2,1},{3,0},{4,7},{5,6},{6,5},{7,4},{8,11},{9,10},{10,... | collective-permute-start | bytes 1572872 | tf_op jit(solution)/shard_map/ppermute | solution.py:26
  45.3 14.5 %collective-permute-start.9 = (bf16[2,128,8,128]{3,2,1,0:T(8,128)(2,1)S(1)}, bf16[2,128,8,128]{3,2,1,0:T(8,128)(2,1)S(1)}, u32[]{:S(2)}, u32[]{:S(2)}) collective-permute-start(bf16[2,128,8,128]{3,2,1,0:T(8,128)(2,1)S(1)} %merge.1.refs_4_), channel_id=1, source_target_pairs={{0,1},{1,0},{2,3},{3,2},{4,5},{5,4},{6,7},{7,6},{8,9},{9,8},{10,11... | collective-permute-start | bytes 1572872 | tf_op jit(solution)/shard_map/ppermute | solution.py:26
  59.8 14.2 %collective-permute-start.14 = (bf16[2,128,8,128]{3,2,1,0:T(8,128)(2,1)S(1)}, bf16[2,128,8,128]{3,2,1,0:T(8,128)(2,1)S(1)}, u32[]{:S(2)}, u32[]{:S(2)}) collective-permute-start(bf16[2,128,8,128]{3,2,1,0:T(8,128)(2,1)S(1)} %merge.1.refs_4_), channel_id=1, source_target_pairs={{0,2},{1,3},{2,0},{3,1},{4,6},{5,7},{6,4},{7,5},{8,10},{9,11},{10,... | collective-permute-start | bytes 1572872 | tf_op jit(solution)/shard_map/ppermute | solution.py:26
  61.9 13.6 %collective-permute-start.16 = (bf16[2,128,8,128]{3,2,1,0:T(8,128)(2,1)S(1)}, bf16[2,128,8,128]{3,2,1,0:T(8,128)(2,1)S(1)}, u32[]{:S(2)}, u32[]{:S(2)}) collective-permute-start(bf16[2,128,8,128]{3,2,1,0:T(8,128)(2,1)S(1)} %collective-permute-done.11.refs_4_), channel_id=1, source_target_pairs={{0,12},{1,13},{2,14},{3,15},{4,8},{5,9},{6,10},{7,11},{8,4},{9,5},... | collective-permute-start | bytes 1572872 | tf_op jit(solution)/shard_map/ppermute | solution.py:26
  64.0 12.2 %collective-permute-start.15 = (bf16[2,128,8,128]{3,2,1,0:T(8,128)(2,1)S(1)}, bf16[2,128,8,128]{3,2,1,0:T(8,128)(2,1)S(1)}, u32[]{:S(2)}, u32[]{:S(2)}) collective-permute-start(bf16[2,128,8,128]{3,2,1,0:T(8,128)(2,1)S(1)} %collective-permute-done.11.refs_4_), channel_id=1, source_target_pairs={{0,4},{1,5},{2,6},{3,7},{4,0},{5,1},{6,2},{7,3},{8,12},{9,13},{10,... | collective-permute-start | bytes 1572872 | tf_op jit(solution)/shard_map/ppermute | solution.py:26
  76.2 15.3 %collective-permute-start.20 = (bf16[2,128,8,128]{3,2,1,0:T(8,128)(2,1)S(1)}, bf16[2,128,8,128]{3,2,1,0:T(8,128)(2,1)S(1)}, u32[]{:S(2)}, u32[]{:S(2)}) collective-permute-start(bf16[2,128,8,128]{3,2,1,0:T(8,128)(2,1)S(1)} %collective-permute-done.11.refs_4_), channel_id=1, source_target_pairs={{0,8},{1,9},{2,10},{3,11},{4,12},{5,13},{6,14},{7,15},{8,0},{9,1},... | collective-permute-start | bytes 1572872 | tf_op jit(solution)/shard_map/ppermute | solution.py:26
  85.3 17.3 %collective-permute-start.17 = (bf16[2,520,256]{2,1,0:T(8,128)(2,1)S(1)}, bf16[2,520,256]{2,1,0:T(8,128)(2,1)S(1)}, u32[]{:S(2)}, u32[]{:S(2)}) collective-permute-start(bf16[2,520,256]{2,1,0:T(8,128)(2,1)S(1)} %get-tuple-element.99), channel_id=1, source_target_pairs={{0,4},{1,5},{2,6},{3,7},{4,0},{5,1},{6,2},{7,3},{8,12},{9,13},{10,... | collective-permute-start | bytes 1597448 | tf_op jit(solution)/shard_map/ppermute | solution.py:26
  86.3 25.5 %collective-permute-start.18 = (bf16[2,520,256]{2,1,0:T(8,128)(2,1)S(1)}, bf16[2,520,256]{2,1,0:T(8,128)(2,1)S(1)}, u32[]{:S(2)}, u32[]{:S(2)}) collective-permute-start(bf16[2,520,256]{2,1,0:T(8,128)(2,1)S(1)} %get-tuple-element.100), channel_id=1, source_target_pairs={{0,8},{1,9},{2,10},{3,11},{4,12},{5,13},{6,14},{7,15},{8,0},{9,1},... | collective-permute-start | bytes 1597448 | tf_op jit(solution)/shard_map/ppermute | solution.py:26
  88.9 24.1 %collective-permute-start.19 = (bf16[2,520,256]{2,1,0:T(8,128)(2,1)S(1)}, bf16[2,520,256]{2,1,0:T(8,128)(2,1)S(1)}, u32[]{:S(2)}, u32[]{:S(2)}) collective-permute-start(bf16[2,520,256]{2,1,0:T(8,128)(2,1)S(1)} %get-tuple-element.101), channel_id=1, source_target_pairs={{0,12},{1,13},{2,14},{3,15},{4,8},{5,9},{6,10},{7,11},{8,4},{9,5},... | collective-permute-start | bytes 1597448 | tf_op jit(solution)/shard_map/ppermute | solution.py:26
  98.1 14.9 %collective-permute-start.21 = (bf16[2,520,256]{2,1,0:T(8,128)(2,1)S(1)}, bf16[2,520,256]{2,1,0:T(8,128)(2,1)S(1)}, u32[]{:S(2)}, u32[]{:S(2)}) collective-permute-start(bf16[2,520,256]{2,1,0:T(8,128)(2,1)S(1)} %get-tuple-element.115), channel_id=1, source_target_pairs={{0,1},{1,0},{2,3},{3,2},{4,5},{5,4},{6,7},{7,6},{8,9},{9,8},{10,11... | collective-permute-start | bytes 1597448 | tf_op jit(solution)/shard_map/ppermute | solution.py:26
  98.2 20.4 %collective-permute-start.22 = (bf16[2,520,256]{2,1,0:T(8,128)(2,1)S(1)}, bf16[2,520,256]{2,1,0:T(8,128)(2,1)S(1)}, u32[]{:S(2)}, u32[]{:S(2)}) collective-permute-start(bf16[2,520,256]{2,1,0:T(8,128)(2,1)S(1)} %get-tuple-element.116), channel_id=1, source_target_pairs={{0,2},{1,3},{2,0},{3,1},{4,6},{5,7},{6,4},{7,5},{8,10},{9,11},{10,... | collective-permute-start | bytes 1597448 | tf_op jit(solution)/shard_map/ppermute | solution.py:26
  102.6 19.3 %collective-permute-start.23 = (bf16[2,520,256]{2,1,0:T(8,128)(2,1)S(1)}, bf16[2,520,256]{2,1,0:T(8,128)(2,1)S(1)}, u32[]{:S(2)}, u32[]{:S(2)}) collective-permute-start(bf16[2,520,256]{2,1,0:T(8,128)(2,1)S(1)} %get-tuple-element.117), channel_id=1, source_target_pairs={{0,3},{1,2},{2,1},{3,0},{4,7},{5,6},{6,5},{7,4},{8,11},{9,10},{10,... | collective-permute-start | bytes 1597448 | tf_op jit(solution)/shard_map/ppermute | solution.py:26

commit v5 on v4

--- a/solution.py
+++ b/solution.py
@@ -249,35 +249,36 @@
     row_masks, col_masks = (4, 1), (1, 4)
     rows = [[white, None, None, None], [white, None, None, None]]
 
+    for d in (1, 2, 3):
+        rows[0][d] = xor_perm(white, "mem", d * row_masks[0])
+    up, down = ring_perm(white, 1), ring_perm(white, -1)
+    source, rows[0] = lax.optimization_barrier((white, rows[0]))
     for d in (1, 3):
-        rows[1][d] = xor_perm(white, "mem", d * row_masks[1])
-    up, down = ring_perm(white, 1), ring_perm(white, -1)
-    up, down, rows, source = lax.optimization_barrier((up, down, rows, white))
-    for n in range(2):
-        rows[n][2] = xor_perm(source, "mem", 2 * row_masks[n])
-    tops = [ring_perm(up[: LANE // 2], 1), ring_perm(down[LANE // 2 :], -1)]
-    up, down, tops, rows, where = lax.optimization_barrier((up, down, tops, rows, where))
+        rows[1][d] = xor_perm(source, "mem", d * row_masks[1])
+    rows, source, up, down = lax.optimization_barrier((rows, source, up, down))
+    source, *halves = lax.optimization_barrier((source, up[: LANE // 2], down[LANE // 2 :]))
+    rows[1][2] = xor_perm(source, "mem", 2 * row_masks[1])
+    tops = [ring_perm(halves[0], 1), ring_perm(halves[1], -1)]
+    rows, where, up, down, tops = lax.optimization_barrier((rows, where, up, down, tops))
 
     mine = choose(pick_kernel, "pick", where, partners, [white, down, up, *tops])
     other = xor_perm(mine, "grp", 1)
     near = choose(merge_kernel, "merge", where, partners, [mine, other])
-    near, where, source = lax.optimization_barrier((near, where, white))
-    for d in (3, 1):
-        rows[0][d] = xor_perm(source, "mem", d * row_masks[0])
+    near, where = lax.optimization_barrier((near, where))
     across = xor_perm(near, "mem", 16)
-    cols = [[near, None, None, None], [across, None, None, None]]
-    for e in (3, 1):
-        cols[0][e] = xor_perm(near, "mem", e * col_masks[0])
+    hop = xor_perm(near, "mem", 2 * col_masks[1])
+    near1, near3 = [xor_perm(near, "mem", e * col_masks[0]) for e in (1, 3)]
     table = lag_table(where[0] - member)
     order = column_order(where[0])
-    cols, rows, near, across, table, order = lax.optimization_barrier(
-        (cols, rows, near, across, table, order)
+    table, order, near, near1, near3, hop, across = lax.optimization_barrier(
+        (table, order, near, near1, near3, hop, across)
     )
-    for e in (3, 1):
-        cols[1][e] = xor_perm(across, "mem", e * col_masks[1])
-    cols[0][2] = xor_perm(near, "mem", 2 * col_masks[0])
-    cols, across = lax.optimization_barrier((cols, across))
-    cols[1][2] = xor_perm(across, "mem", 2 * col_masks[1])
+    near2 = xor_perm(near, "mem", 2 * col_masks[0])
+    far2 = xor_perm(hop, "mem", 16)
+    far3 = xor_perm(across, "mem", 3 * col_masks[1])
+    across, near2, far3, far2 = lax.optimization_barrier((across, near2, far3, far2))
+    far1 = xor_perm(across, "mem", col_masks[1])
+    cols = [[near, near1, near2, near3], [across, far1, far2, far3]]
     parts = []
     for n in range(2):
         sums = correlate(rows[n], cols[n], table, factor)

time: 128 us -> 131 us (1.023); the launches traced: 127 us -> 128 us
  starting transfers between devices: 35.5 us -> 41.3 us
  waiting for transfers between devices: 60.3 us -> 56.4 us
    ppermute x4, waiting for transfers between devices: 20.6 us -> 10.7 us  [ring_perm(): lax.ppermute(array, 'grp', [(i, (i + 2 * shift) % size) for i in range(si...]
    ppermute x20 -> x21, waiting for transfers between devices: 39.7 us -> 45.7 us  [xor_perm(): lax.ppermute(array, axis, [(i, i ^ mask) for i in range(lax.axis_size(axi...]
    ppermute x4, starting transfers between devices: 9.31 us -> 12.3 us  [ring_perm(): lax.ppermute(array, 'grp', [(i, (i + 2 * shift) % size) for i in range(si...]
    ppermute x20 -> x21, starting transfers between devices: 26.2 us -> 28.9 us  [xor_perm(): lax.ppermute(array, axis, [(i, i ^ mask) for i in range(lax.axis_size(axi...]
  transfers between devices with their start and end apart: 24 -> 25, of which waited for: 16 -> 19; matrix products, arithmetic and copies ran while one was open for 6% -> 6% of each run, Pallas kernels for 11% -> 10%
where the time goes in v5:
time: 131 us; the launch traced here: 128 us
  waiting for transfers between devices  56.4 us (43%)
  starting transfers between devices  41.3 us (32%)
  Pallas kernels  20.4 us (16%)
  other arithmetic  7.48 us (6%)
  local copies, waits for them, and re-layouts  2.37 us (2%)
    ppermute x21, waiting for transfers between devices, xor_perm(): lax.ppermute(array, axis, [(i, i ^ mask) for i in range(lax.axis_size(axi...  45.7 us
    ppermute x21, starting transfers between devices, xor_perm(): lax.ppermute(array, axis, [(i, i ^ mask) for i in range(lax.axis_size(axi...  28.9 us
    pallas_call x2, Pallas kernels, correlate(): pl.pallas_call(body, out_shape=[jax.ShapeDtypeStruct((2, LAG_ROWS, 256),...  13.4 us
    ppermute x4, starting transfers between devices, ring_perm(): lax.ppermute(array, 'grp', [(i, (i + 2 * shift) % size) for i in range(si...  12.3 us
    ppermute x4, waiting for transfers between devices, ring_perm(): lax.ppermute(array, 'grp', [(i, (i + 2 * shift) % size) for i in range(si...  10.7 us
    convert_element_type x1, other arithmetic, lag_table(): return jnp.where(lag < LAGS, values, 0.0).astype(jnp.bfloat16)  7.04 us
    pallas_call x1, Pallas kernels, finish(): pl.pallas_call(finish_kernel, grid=(4,), in_specs=[pl.BlockSpec(memory_sp...  4.88 us
  transfers between devices with their start and end apart: 25, of which 19 were waited for; matrix products, arithmetic and copies ran while one was open for 6% of the time, Pallas kernels for 10%

profile of v5, /device:TPU:8, one launch (start us, length us, event | category | flops | bytes accessed | tf_op | source)
XLA Modules:
  0.0 128.2 jit_solution(10785607253068487471)
XLA Ops:
  0.0 0.9 copy-done
  1.0 0.8 whiten.1.refs_0_
  1.8 2.8 %collective-permute-start.2 = (bf16[128,8,128]{2,1,0:T(8,128)(2,1)S(1)}, bf16[128,8,128]{2,1,0:T(8,128)(2,1)S(1)}, u32[]{:S(2)}, u32[]{:S(2)}) collective-permute-start(bf16[128,8,128]{2,1,0:T(8,128)(2,1)S(1)} %whiten.1.refs_0_), channel_id=1, source_target_pairs={{0,12},{1,13},{2,14},{3,15},{4,8},{5,9},{6,10},{7,11},{8,4},{9,5},... | collective-permute-start | bytes 786440 | tf_op jit(solution)/shard_map/ppermute | solution.py:26
  4.6 0.8 collective-permute-start.1
  5.4 0.5 collective-permute-start
  6.0 6.3 %collective-permute-start.6 = (bf16[128,8,128]{2,1,0:T(8,128)(2,1)S(1)}, bf16[128,8,128]{2,1,0:T(8,128)(2,1)S(1)}, u32[]{:S(2)}, u32[]{:S(2)}) collective-permute-start(bf16[128,8,128]{2,1,0:T(8,128)(2,1)S(1)} %whiten.1.refs_0_), channel_id=1, source_target_pairs={{0,192},{32,224},{64,0},{96,32},{128,64},{160,96},{192,128},{224,1... | collective-permute-start | bytes 786440 | tf_op jit(solution)/shard_map/ppermute | solution.py:31
  12.3 0.0 collective-permute-start.5
  12.3 4.5 %collective-permute-done.2.refs_3_ = bf16[128,8,128]{2,1,0:T(8,128)(2,1)S(1)} collective-permute-done((bf16[128,8,128]{2,1,0:T(8,128)(2,1)S(1)}, bf16[128,8,128]{2,1,0:T(8,128)(2,1)S(1)}, u32[]{:S(2)}, u32[]{:S(2)}) %collective-permute-start.2) | collective-permute-done | bytes 262176 | tf_op jit(solution)/shard_map/ppermute | solution.py:26
  16.8 0.0 collective-permute-done.1.refs_2_
  16.8 0.6 collective-permute-done.refs_1_
  17.4 0.7 copy-done.3
  18.1 1.6 %collective-permute-start.4 = (bf16[128,8,128]{2,1,0:T(8,128)(2,1)S(1)}, bf16[128,8,128]{2,1,0:T(8,128)(2,1)S(1)}, u32[]{:S(2)}, u32[]{:S(2)}) collective-permute-start(bf16[128,8,128]{2,1,0:T(8,128)(2,1)S(1)} %whiten.1.refs_0_), channel_id=1, source_target_pairs={{0,3},{1,2},{2,1},{3,0},{4,7},{5,6},{6,5},{7,4},{8,11},{9,10},{10,... | collective-permute-start | bytes 786440 | tf_op jit(solution)/shard_map/ppermute | solution.py:26
  19.7 1.9 %collective-permute-start.3 = (bf16[128,8,128]{2,1,0:T(8,128)(2,1)S(1)}, bf16[128,8,128]{2,1,0:T(8,128)(2,1)S(1)}, u32[]{:S(2)}, u32[]{:S(2)}) collective-permute-start(bf16[128,8,128]{2,1,0:T(8,128)(2,1)S(1)} %whiten.1.refs_0_), channel_id=1, source_target_pairs={{0,1},{1,0},{2,3},{3,2},{4,5},{5,4},{6,7},{7,6},{8,9},{9,8},{10,11... | collective-permute-start | bytes 786440 | tf_op jit(solution)/shard_map/ppermute | solution.py:26
  21.5 1.1 collective-permute-done.6.refs_1_
  22.6 3.8 %collective-permute-done.5.refs_2_ = bf16[128,8,128]{2,1,0:T(8,128)(2,1)S(1)} collective-permute-done((bf16[128,8,128]{2,1,0:T(8,128)(2,1)S(1)}, bf16[128,8,128]{2,1,0:T(8,128)(2,1)S(1)}, u32[]{:S(2)}, u32[]{:S(2)}) %collective-permute-start.5) | collective-permute-done | bytes 262176 | tf_op jit(solution)/shard_map/ppermute | solution.py:31
  26.5 0.0 collective-permute-done.4.refs_3_
  26.5 0.0 collective-permute-done.3.refs_1_
  26.5 2.4 %collective-permute-start.7 = (bf16[128,8,128]{2,1,0:T(8,128)(2,1)S(1)}, bf16[128,8,128]{2,1,0:T(8,128)(2,1)S(1)}, u32[]{:S(2)}, u32[]{:S(2)}) collective-permute-start(bf16[128,8,128]{2,1,0:T(8,128)(2,1)S(1)} %whiten.1.refs_0_), channel_id=1, source_target_pairs={{0,2},{1,3},{2,0},{3,1},{4,6},{5,7},{6,4},{7,5},{8,10},{9,11},{10,... | collective-permute-start | bytes 786440 | tf_op jit(solution)/shard_map/ppermute | solution.py:26
  28.9 3.0 %collective-permute-start.8 = (bf16[64,8,128]{2,1,0:T(8,128)(2,1)S(1)}, bf16[64,8,128]{2,1,0:T(8,128)(2,1)S(1)}, u32[]{:S(2)}, u32[]{:S(2)}) collective-permute-start(bf16[64,8,128]{2,1,0:T(8,128)(2,1)S(1)} %slice.10), channel_id=1, source_target_pairs={{0,64},{32,96},{64,128},{96,160},{128,192},{160,224},{192,0},{224,... | collective-permute-start | bytes 393224 | tf_op jit(solution)/shard_map/ppermute | solution.py:31
  31.9 3.0 %collective-permute-start.9 = (bf16[64,8,128]{2,1,0:T(8,128)(2,1)S(1)}, bf16[64,8,128]{2,1,0:T(8,128)(2,1)S(1)}, u32[]{:S(2)}, u32[]{:S(2)}) collective-permute-start(bf16[64,8,128]{2,1,0:T(8,128)(2,1)S(1)} %slice.11), channel_id=1, source_target_pairs={{0,192},{32,224},{64,0},{96,32},{128,64},{160,96},{192,128},{224,1... | collective-permute-start | bytes 393224 | tf_op jit(solution)/shard_map/ppermute | solution.py:31
  34.9 0.1 pad_add_fusion.where_ref
  35.0 4.3 %collective-permute-done.8.refs_3_ = bf16[64,8,128]{2,1,0:T(8,128)(2,1)S(1)} collective-permute-done((bf16[64,8,128]{2,1,0:T(8,128)(2,1)S(1)}, bf16[64,8,128]{2,1,0:T(8,128)(2,1)S(1)}, u32[]{:S(2)}, u32[]{:S(2)}) %collective-permute-start.8) | collective-permute-done | bytes 131104 | tf_op jit(solution)/shard_map/ppermute | solution.py:31
  39.3 1.5 %collective-permute-done.9.refs_4_ = bf16[64,8,128]{2,1,0:T(8,128)(2,1)S(1)} collective-permute-done((bf16[64,8,128]{2,1,0:T(8,128)(2,1)S(1)}, bf16[64,8,128]{2,1,0:T(8,128)(2,1)S(1)}, u32[]{:S(2)}, u32[]{:S(2)}) %collective-permute-start.9) | collective-permute-done | bytes 131104 | tf_op jit(solution)/shard_map/ppermute | solution.py:31
  40.7 0.0 collective-permute-done.7.refs_2_
  40.7 0.7 copy-done.1
  41.4 0.6 pick.1.mine_ref
  42.0 0.1 collective-permute-start.10
  42.2 0.1 iota_add_fusion.1
  42.2 1.8 %collective-permute-done.10.other_ref = bf16[2,128,8,128]{3,2,1,0:T(8,128)(2,1)S(1)} collective-permute-done((bf16[2,128,8,128]{3,2,1,0:T(8,128)(2,1)S(1)}, bf16[2,128,8,128]{3,2,1,0:T(8,128)(2,1)S(1)}, u32[]{:S(2)}, u32[]{:S(2)}) %collective-permute-start.10) | collective-permute-done | bytes 524320 | tf_op jit(solution)/shard_map/ppermute | solution.py:26
  44.0 0.0 copy-done.2
  44.0 0.6 merge.1.refs_4_
  44.9 0.5 collective-permute-start.14
  45.4 3.0 %collective-permute-start.13 = (bf16[2,128,8,128]{3,2,1,0:T(8,128)(2,1)S(1)}, bf16[2,128,8,128]{3,2,1,0:T(8,128)(2,1)}, u32[]{:S(2)}, u32[]{:S(2)}) collective-permute-start(bf16[2,128,8,128]{3,2,1,0:T(8,128)(2,1)S(1)} %merge.1.refs_4_), channel_id=1, source_target_pairs={{0,8},{1,9},{2,10},{3,11},{4,12},{5,13},{6,14},{7,15},{8,0},{9,1},... | collective-permute-start | bytes 1572872 | tf_op jit(solution)/shard_map/ppermute | solution.py:26
  48.4 1.2 collective-permute-start.12
  49.6 1.5 %collective-permute-start.11 = (bf16[2,128,8,128]{3,2,1,0:T(8,128)(2,1)S(1)}, bf16[2,128,8,128]{3,2,1,0:T(8,128)(2,1)S(1)}, u32[]{:S(2)}, u32[]{:S(2)}) collective-permute-start(bf16[2,128,8,128]{3,2,1,0:T(8,128)(2,1)S(1)} %merge.1.refs_4_), channel_id=1, source_target_pairs={{0,1},{1,0},{2,3},{3,2},{4,5},{5,4},{6,7},{7,6},{8,9},{9,8},{10,11... | collective-permute-start | bytes 1572872 | tf_op jit(solution)/shard_map/ppermute | solution.py:26
  51.1 7.0 %fusion.7.refs_8_ = bf16[520,1024]{1,0:T(8,128)(2,1)S(1)} fusion(s32[1024]{0:T(1024)S(1)} %get-tuple-element.118, s32[520]{0:T(1024)S(1)} %fusion.33, s32[1024]{0:T(1024)S(1)} %get-tuple-element.117, pred[520]{0:T(1024)(128)(4,1)S(1)} %fusion.34), kind=kLoop, calls=%fused_computation.22 | loop fusion | flops 48988160 | bytes 1075752 | tf_op jit(solution)/shard_map/convert_element_type | solution.py:228
  58.2 0.2 compare_convert_fusion.refs_8_
  58.5 0.5 collective-permute-done.14.refs_4_
  59.0 1.7 %collective-permute-done.13 = bf16[2,128,8,128]{3,2,1,0:T(8,128)(2,1)} collective-permute-done((bf16[2,128,8,128]{3,2,1,0:T(8,128)(2,1)S(1)}, bf16[2,128,8,128]{3,2,1,0:T(8,128)(2,1)}, u32[]{:S(2)}, u32[]{:S(2)}) %collective-permute-start.13) | collective-permute-done | bytes 524320 | tf_op jit(solution)/shard_map/ppermute | solution.py:26
  60.7 1.1 collective-permute-done.12.refs_7_
  61.8 0.9 collective-permute-done.11.refs_5_
  62.7 1.6 %collective-permute-start.17 = (bf16[2,128,8,128]{3,2,1,0:T(8,128)(2,1)}, bf16[2,128,8,128]{3,2,1,0:T(8,128)(2,1)S(1)}, u32[]{:S(2)}, u32[]{:S(2)}) collective-permute-start(bf16[2,128,8,128]{3,2,1,0:T(8,128)(2,1)} %collective-permute-done.13), channel_id=1, source_target_pairs={{0,16},{1,17},{2,18},{3,19},{4,20},{5,21},{6,22},{7,23},{8,24},{9,... | collective-permute-start | bytes 1572872 | tf_op jit(solution)/shard_map/ppermute | solution.py:26
  64.3 1.8 %collective-permute-start.15 = (bf16[2,128,8,128]{3,2,1,0:T(8,128)(2,1)S(1)}, bf16[2,128,8,128]{3,2,1,0:T(8,128)(2,1)S(1)}, u32[]{:S(2)}, u32[]{:S(2)}) collective-permute-start(bf16[2,128,8,128]{3,2,1,0:T(8,128)(2,1)S(1)} %merge.1.refs_4_), channel_id=1, source_target_pairs={{0,2},{1,3},{2,0},{3,1},{4,6},{5,7},{6,4},{7,5},{8,10},{9,11},{10,... | collective-permute-start | bytes 1572872 | tf_op jit(solution)/shard_map/ppermute | solution.py:26
  66.1 1.1 collective-permute-start.16
  67.3 7.9 %collective-permute-done.17.refs_6_ = bf16[2,128,8,128]{3,2,1,0:T(8,128)(2,1)S(1)} collective-permute-done((bf16[2,128,8,128]{3,2,1,0:T(8,128)(2,1)}, bf16[2,128,8,128]{3,2,1,0:T(8,128)(2,1)S(1)}, u32[]{:S(2)}, u32[]{:S(2)}) %collective-permute-start.17) | collective-permute-done | bytes 524320 | tf_op jit(solution)/shard_map/ppermute | solution.py:26
  75.2 2.6 %collective-permute-done.15.refs_6_ = bf16[2,128,8,128]{3,2,1,0:T(8,128)(2,1)S(1)} collective-permute-done((bf16[2,128,8,128]{3,2,1,0:T(8,128)(2,1)S(1)}, bf16[2,128,8,128]{3,2,1,0:T(8,128)(2,1)S(1)}, u32[]{:S(2)}, u32[]{:S(2)}) %collective-permute-start.15) | collective-permute-done | bytes 524320 | tf_op jit(solution)/shard_map/ppermute | solution.py:26
  77.7 1.5 %collective-permute-done.16.refs_7_ = bf16[2,128,8,128]{3,2,1,0:T(8,128)(2,1)S(1)} collective-permute-done((bf16[2,128,8,128]{3,2,1,0:T(8,128)(2,1)S(1)}, bf16[2,128,8,128]{3,2,1,0:T(8,128)(2,1)S(1)}, u32[]{:S(2)}, u32[]{:S(2)}) %collective-permute-start.16) | collective-permute-done | bytes 524320 | tf_op jit(solution)/shard_map/ppermute | solution.py:26
  79.3 0.0 collective-permute-start.21
  79.3 6.7 %correlate.2 = (bf16[2,520,256]{2,1,0:T(8,128)(2,1)S(1)}, bf16[2,520,256]{2,1,0:T(8,128)(2,1)S(1)}, bf16[2,520,256]{2,1,0:T(8,128)(2,1)S(1)}, bf16[2,520,256]{2,1,0:T(8,128)(2,1)S(1)}) custom-call(bf16[128,8,128]{2,1,0:T(8,128)(2,1)S(1)} %whiten.1.refs_0_, bf16[128,8,128]{2,1,0:T(8,128)(2,1)S(1)} %copy-done.4, ...), custom_call_target="tpu_custom_call" | custom-call | flops 3254779904 | bytes 7340032 | tf_op jit(solution)/shard_map/correlate/pallas_call | solution.py:164
  86.0 2.1 %collective-permute-start.18 = (bf16[2,520,256]{2,1,0:T(8,128)(2,1)S(1)}, bf16[2,520,256]{2,1,0:T(8,128)(2,1)S(1)}, u32[]{:S(2)}, u32[]{:S(2)}) collective-permute-start(bf16[2,520,256]{2,1,0:T(8,128)(2,1)S(1)} %get-tuple-element.98), channel_id=1, source_target_pairs={{0,4},{1,5},{2,6},{3,7},{4,0},{5,1},{6,2},{7,3},{8,12},{9,13},{10,... | collective-permute-start | bytes 1597448 | tf_op jit(solution)/shard_map/ppermute | solution.py:26
  88.1 0.8 collective-permute-start.19
  88.9 2.0 %collective-permute-start.20 = (bf16[2,520,256]{2,1,0:T(8,128)(2,1)S(1)}, bf16[2,520,256]{2,1,0:T(8,128)(2,1)S(1)}, u32[]{:S(2)}, u32[]{:S(2)}) collective-permute-start(bf16[2,520,256]{2,1,0:T(8,128)(2,1)S(1)} %get-tuple-element.100), channel_id=1, source_target_pairs={{0,12},{1,13},{2,14},{3,15},{4,8},{5,9},{6,10},{7,11},{8,4},{9,5},... | collective-permute-start | bytes 1597448 | tf_op jit(solution)/shard_map/ppermute | solution.py:26
  90.9 3.3 %collective-permute-done.21.refs_5_ = bf16[2,128,8,128]{3,2,1,0:T(8,128)(2,1)S(1)} collective-permute-done((bf16[2,128,8,128]{3,2,1,0:T(8,128)(2,1)S(1)}, bf16[2,128,8,128]{3,2,1,0:T(8,128)(2,1)S(1)}, u32[]{:S(2)}, u32[]{:S(2)}) %collective-permute-start.21) | collective-permute-done | bytes 524320 | tf_op jit(solution)/shard_map/ppermute | solution.py:26
  94.1 6.7 %correlate.3 = (bf16[2,520,256]{2,1,0:T(8,128)(2,1)S(1)}, bf16[2,520,256]{2,1,0:T(8,128)(2,1)S(1)}, bf16[2,520,256]{2,1,0:T(8,128)(2,1)S(1)}, bf16[2,520,256]{2,1,0:T(8,128)(2,1)S(1)}) custom-call(bf16[128,8,128]{2,1,0:T(8,128)(2,1)S(1)} %whiten.1.refs_0_, bf16[128,8,128]{2,1,0:T(8,128)(2,1)S(1)} %collective-permute-done.3.refs_1_, ...), custom_call_target="tpu_custom_call" | custom-call | flops 3254779904 | bytes 7340032 | tf_op jit(solution)/shard_map/correlate/pallas_call | solution.py:164
  100.9 0.9 collective-permute-start.22
  101.8 1.5 %collective-permute-start.23 = (bf16[2,520,256]{2,1,0:T(8,128)(2,1)S(1)}, bf16[2,520,256]{2,1,0:T(8,128)(2,1)S(1)}, u32[]{:S(2)}, u32[]{:S(2)}) collective-permute-start(bf16[2,520,256]{2,1,0:T(8,128)(2,1)S(1)} %get-tuple-element.114), channel_id=1, source_target_pairs={{0,2},{1,3},{2,0},{3,1},{4,6},{5,7},{6,4},{7,5},{8,10},{9,11},{10,... | collective-permute-start | bytes 1597448 | tf_op jit(solution)/shard_map/ppermute | solution.py:26
  103.2 2.3 %collective-permute-done.18.refs_1_ = bf16[2,520,256]{2,1,0:T(8,128)(2,1)S(1)} collective-permute-done((bf16[2,520,256]{2,1,0:T(8,128)(2,1)S(1)}, bf16[2,520,256]{2,1,0:T(8,128)(2,1)S(1)}, u32[]{:S(2)}, u32[]{:S(2)}) %collective-permute-start.18) | collective-permute-done | bytes 532512 | tf_op jit(solution)/shard_map/ppermute | solution.py:26
  105.5 0.8 collective-permute-start.24
  106.4 7.5 %collective-permute-done.19.refs_2_ = bf16[2,520,256]{2,1,0:T(8,128)(2,1)S(1)} collective-permute-done((bf16[2,520,256]{2,1,0:T(8,128)(2,1)S(1)}, bf16[2,520,256]{2,1,0:T(8,128)(2,1)S(1)}, u32[]{:S(2)}, u32[]{:S(2)}) %collective-permute-start.19) | collective-permute-done | bytes 532512 | tf_op jit(solution)/shard_map/ppermute | solution.py:26
  113.9 0.0 collective-permute-done.20.refs_3_
  113.9 0.0 collective-permute-done.22.refs_5_
  113.9 5.7 %collective-permute-done.23.refs_6_ = bf16[2,520,256]{2,1,0:T(8,128)(2,1)S(1)} collective-permute-done((bf16[2,520,256]{2,1,0:T(8,128)(2,1)S(1)}, bf16[2,520,256]{2,1,0:T(8,128)(2,1)S(1)}, u32[]{:S(2)}, u32[]{:S(2)}) %collective-permute-start.23) | collective-permute-done | bytes 532512 | tf_op jit(solution)/shard_map/ppermute | solution.py:26
  119.6 3.8 %collective-permute-done.24.refs_7_ = bf16[2,520,256]{2,1,0:T(8,128)(2,1)S(1)} collective-permute-done((bf16[2,520,256]{2,1,0:T(8,128)(2,1)S(1)}, bf16[2,520,256]{2,1,0:T(8,128)(2,1)S(1)}, u32[]{:S(2)}, u32[]{:S(2)}) %collective-permute-start.24) | collective-permute-done | bytes 532512 | tf_op jit(solution)/shard_map/ppermute | solution.py:26
  123.4 4.9 %finish.1 = bf16[4,4104,128]{2,1,0:T(8,128)(2,1)} custom-call(s32[1]{0:T(128)} %bitcast.member_ref, bf16[2,520,256]{2,1,0:T(8,128)(2,1)S(1)} %get-tuple-element.97.refs_0_, bf16[2,520,256]{2,1,0:T(8,128)(2,1)S(1)} %collective-permute-done.18.refs_1_, bf16[2,520,256]{2,1,0:T(8,128)(2,1)S(1)} %collective-permute-done.19.refs_2_, ...), custom_call_target="tpu_custom_call" | custom-call | tf_op jit(solution)/shard_map/finish/pallas_call | solution.py:202
  (19 shorter events, 0.1 us)
Async XLA Ops:
  0.0 0.9 copy-start
  1.0 43.1 %copy-start.2 = (s32[2,32]{1,0:T(2,128)S(1)}, s32[2,32]{1,0:T(2,128)}, u32[]{:S(2)}) copy-start(s32[2,32]{1,0:T(2,128)} %partners_ref.3) | copy-start | bytes 772
  1.8 15.0 %collective-permute-start.2 = (bf16[128,8,128]{2,1,0:T(8,128)(2,1)S(1)}, bf16[128,8,128]{2,1,0:T(8,128)(2,1)S(1)}, u32[]{:S(2)}, u32[]{:S(2)}) collective-permute-start(bf16[128,8,128]{2,1,0:T(8,128)(2,1)S(1)} %whiten.1.refs_0_), channel_id=1, source_target_pairs={{0,12},{1,13},{2,14},{3,15},{4,8},{5,9},{6,10},{7,11},{8,4},{9,5},... | collective-permute-start | bytes 786440 | tf_op jit(solution)/shard_map/ppermute | solution.py:26
  4.6 12.1 %collective-permute-start.1 = (bf16[128,8,128]{2,1,0:T(8,128)(2,1)S(1)}, bf16[128,8,128]{2,1,0:T(8,128)(2,1)S(1)}, u32[]{:S(2)}, u32[]{:S(2)}) collective-permute-start(bf16[128,8,128]{2,1,0:T(8,128)(2,1)S(1)} %whiten.1.refs_0_), channel_id=1, source_target_pairs={{0,8},{1,9},{2,10},{3,11},{4,12},{5,13},{6,14},{7,15},{8,0},{9,1},... | collective-permute-start | bytes 786440 | tf_op jit(solution)/shard_map/ppermute | solution.py:26
  5.4 11.9 %collective-permute-start = (bf16[128,8,128]{2,1,0:T(8,128)(2,1)S(1)}, bf16[128,8,128]{2,1,0:T(8,128)(2,1)S(1)}, u32[]{:S(2)}, u32[]{:S(2)}) collective-permute-start(bf16[128,8,128]{2,1,0:T(8,128)(2,1)S(1)} %whiten.1.refs_0_), channel_id=1, source_target_pairs={{0,4},{1,5},{2,6},{3,7},{4,0},{5,1},{6,2},{7,3},{8,12},{9,13},{10,... | collective-permute-start | bytes 786440 | tf_op jit(solution)/shard_map/ppermute | solution.py:26
  6.0 16.7 %collective-permute-start.6 = (bf16[128,8,128]{2,1,0:T(8,128)(2,1)S(1)}, bf16[128,8,128]{2,1,0:T(8,128)(2,1)S(1)}, u32[]{:S(2)}, u32[]{:S(2)}) collective-permute-start(bf16[128,8,128]{2,1,0:T(8,128)(2,1)S(1)} %whiten.1.refs_0_), channel_id=1, source_target_pairs={{0,192},{32,224},{64,0},{96,32},{128,64},{160,96},{192,128},{224,1... | collective-permute-start | bytes 786440 | tf_op jit(solution)/shard_map/ppermute | solution.py:31
  12.3 14.2 %collective-permute-start.5 = (bf16[128,8,128]{2,1,0:T(8,128)(2,1)S(1)}, bf16[128,8,128]{2,1,0:T(8,128)(2,1)S(1)}, u32[]{:S(2)}, u32[]{:S(2)}) collective-permute-start(bf16[128,8,128]{2,1,0:T(8,128)(2,1)S(1)} %whiten.1.refs_0_), channel_id=1, source_target_pairs={{0,64},{32,96},{64,128},{96,160},{128,192},{160,224},{192,0},{224,... | collective-permute-start | bytes 786440 | tf_op jit(solution)/shard_map/ppermute | solution.py:31
  17.4 0.7 copy-start.3
  18.1 8.4 %collective-permute-start.4 = (bf16[128,8,128]{2,1,0:T(8,128)(2,1)S(1)}, bf16[128,8,128]{2,1,0:T(8,128)(2,1)S(1)}, u32[]{:S(2)}, u32[]{:S(2)}) collective-permute-start(bf16[128,8,128]{2,1,0:T(8,128)(2,1)S(1)} %whiten.1.refs_0_), channel_id=1, source_target_pairs={{0,3},{1,2},{2,1},{3,0},{4,7},{5,6},{6,5},{7,4},{8,11},{9,10},{10,... | collective-permute-start | bytes 786440 | tf_op jit(solution)/shard_map/ppermute | solution.py:26
  19.7 6.8 %collective-permute-start.3 = (bf16[128,8,128]{2,1,0:T(8,128)(2,1)S(1)}, bf16[128,8,128]{2,1,0:T(8,128)(2,1)S(1)}, u32[]{:S(2)}, u32[]{:S(2)}) collective-permute-start(bf16[128,8,128]{2,1,0:T(8,128)(2,1)S(1)} %whiten.1.refs_0_), channel_id=1, source_target_pairs={{0,1},{1,0},{2,3},{3,2},{4,5},{5,4},{6,7},{7,6},{8,9},{9,8},{10,11... | collective-permute-start | bytes 786440 | tf_op jit(solution)/shard_map/ppermute | solution.py:26
  26.5 14.2 %collective-permute-start.7 = (bf16[128,8,128]{2,1,0:T(8,128)(2,1)S(1)}, bf16[128,8,128]{2,1,0:T(8,128)(2,1)S(1)}, u32[]{:S(2)}, u32[]{:S(2)}) collective-permute-start(bf16[128,8,128]{2,1,0:T(8,128)(2,1)S(1)} %whiten.1.refs_0_), channel_id=1, source_target_pairs={{0,2},{1,3},{2,0},{3,1},{4,6},{5,7},{6,4},{7,5},{8,10},{9,11},{10,... | collective-permute-start | bytes 786440 | tf_op jit(solution)/shard_map/ppermute | solution.py:26
  28.9 10.4 %collective-permute-start.8 = (bf16[64,8,128]{2,1,0:T(8,128)(2,1)S(1)}, bf16[64,8,128]{2,1,0:T(8,128)(2,1)S(1)}, u32[]{:S(2)}, u32[]{:S(2)}) collective-permute-start(bf16[64,8,128]{2,1,0:T(8,128)(2,1)S(1)} %slice.10), channel_id=1, source_target_pairs={{0,64},{32,96},{64,128},{96,160},{128,192},{160,224},{192,0},{224,... | collective-permute-start | bytes 393224 | tf_op jit(solution)/shard_map/ppermute | solution.py:31
  31.9 8.8 %collective-permute-start.9 = (bf16[64,8,128]{2,1,0:T(8,128)(2,1)S(1)}, bf16[64,8,128]{2,1,0:T(8,128)(2,1)S(1)}, u32[]{:S(2)}, u32[]{:S(2)}) collective-permute-start(bf16[64,8,128]{2,1,0:T(8,128)(2,1)S(1)} %slice.11), channel_id=1, source_target_pairs={{0,192},{32,224},{64,0},{96,32},{128,64},{160,96},{192,128},{224,1... | collective-permute-start | bytes 393224 | tf_op jit(solution)/shard_map/ppermute | solution.py:31
  40.7 0.7 copy-start.1
  41.4 3.5 %copy-start.5 = (bf16[128,8,128]{2,1,0:T(8,128)(2,1)}, bf16[128,8,128]{2,1,0:T(8,128)(2,1)S(1)}, u32[]{:S(2)}) copy-start(bf16[128,8,128]{2,1,0:T(8,128)(2,1)S(1)} %collective-permute-done.7.refs_2_) | copy-start | bytes 786436
  42.0 2.0 %collective-permute-start.10 = (bf16[2,128,8,128]{3,2,1,0:T(8,128)(2,1)S(1)}, bf16[2,128,8,128]{3,2,1,0:T(8,128)(2,1)S(1)}, u32[]{:S(2)}, u32[]{:S(2)}) collective-permute-start(bf16[2,128,8,128]{3,2,1,0:T(8,128)(2,1)S(1)} %pick.1.mine_ref), channel_id=1, source_target_pairs={{0,32},{32,0},{64,96},{96,64},{128,160},{160,128},{192,224},{224,1... | collective-permute-start | bytes 1572872 | tf_op jit(solution)/shard_map/ppermute | solution.py:26
  44.9 14.1 %collective-permute-start.14 = (bf16[2,128,8,128]{3,2,1,0:T(8,128)(2,1)S(1)}, bf16[2,128,8,128]{3,2,1,0:T(8,128)(2,1)S(1)}, u32[]{:S(2)}, u32[]{:S(2)}) collective-permute-start(bf16[2,128,8,128]{3,2,1,0:T(8,128)(2,1)S(1)} %merge.1.refs_4_), channel_id=1, source_target_pairs={{0,16},{1,17},{2,18},{3,19},{4,20},{5,21},{6,22},{7,23},{8,24},{9,... | collective-permute-start | bytes 1572872 | tf_op jit(solution)/shard_map/ppermute | solution.py:26
  45.4 15.3 %collective-permute-start.13 = (bf16[2,128,8,128]{3,2,1,0:T(8,128)(2,1)S(1)}, bf16[2,128,8,128]{3,2,1,0:T(8,128)(2,1)}, u32[]{:S(2)}, u32[]{:S(2)}) collective-permute-start(bf16[2,128,8,128]{3,2,1,0:T(8,128)(2,1)S(1)} %merge.1.refs_4_), channel_id=1, source_target_pairs={{0,8},{1,9},{2,10},{3,11},{4,12},{5,13},{6,14},{7,15},{8,0},{9,1},... | collective-permute-start | bytes 1572872 | tf_op jit(solution)/shard_map/ppermute | solution.py:26
  48.4 13.4 %collective-permute-start.12 = (bf16[2,128,8,128]{3,2,1,0:T(8,128)(2,1)S(1)}, bf16[2,128,8,128]{3,2,1,0:T(8,128)(2,1)S(1)}, u32[]{:S(2)}, u32[]{:S(2)}) collective-permute-start(bf16[2,128,8,128]{3,2,1,0:T(8,128)(2,1)S(1)} %merge.1.refs_4_), channel_id=1, source_target_pairs={{0,3},{1,2},{2,1},{3,0},{4,7},{5,6},{6,5},{7,4},{8,11},{9,10},{10,... | collective-permute-start | bytes 1572872 | tf_op jit(solution)/shard_map/ppermute | solution.py:26
  49.6 13.1 %collective-permute-start.11 = (bf16[2,128,8,128]{3,2,1,0:T(8,128)(2,1)S(1)}, bf16[2,128,8,128]{3,2,1,0:T(8,128)(2,1)S(1)}, u32[]{:S(2)}, u32[]{:S(2)}) collective-permute-start(bf16[2,128,8,128]{3,2,1,0:T(8,128)(2,1)S(1)} %merge.1.refs_4_), channel_id=1, source_target_pairs={{0,1},{1,0},{2,3},{3,2},{4,5},{5,4},{6,7},{7,6},{8,9},{9,8},{10,11... | collective-permute-start | bytes 1572872 | tf_op jit(solution)/shard_map/ppermute | solution.py:26
  51.1 28.2 %copy-start.4 = (bf16[128,8,128]{2,1,0:T(8,128)(2,1)S(1)}, bf16[128,8,128]{2,1,0:T(8,128)(2,1)}, u32[]{:S(2)}) copy-start(bf16[128,8,128]{2,1,0:T(8,128)(2,1)} %copy-done.3) | copy-start | bytes 786436
  58.4 35.7 %copy-start.6 = (bf16[128,8,128]{2,1,0:T(8,128)(2,1)S(1)}, bf16[128,8,128]{2,1,0:T(8,128)(2,1)}, u32[]{:S(2)}) copy-start(bf16[128,8,128]{2,1,0:T(8,128)(2,1)} %copy-done.5) | copy-start | bytes 786436
  62.7 12.4 %collective-permute-start.17 = (bf16[2,128,8,128]{3,2,1,0:T(8,128)(2,1)}, bf16[2,128,8,128]{3,2,1,0:T(8,128)(2,1)S(1)}, u32[]{:S(2)}, u32[]{:S(2)}) collective-permute-start(bf16[2,128,8,128]{3,2,1,0:T(8,128)(2,1)} %collective-permute-done.13), channel_id=1, source_target_pairs={{0,16},{1,17},{2,18},{3,19},{4,20},{5,21},{6,22},{7,23},{8,24},{9,... | collective-permute-start | bytes 1572872 | tf_op jit(solution)/shard_map/ppermute | solution.py:26
  64.3 13.4 %collective-permute-start.15 = (bf16[2,128,8,128]{3,2,1,0:T(8,128)(2,1)S(1)}, bf16[2,128,8,128]{3,2,1,0:T(8,128)(2,1)S(1)}, u32[]{:S(2)}, u32[]{:S(2)}) collective-permute-start(bf16[2,128,8,128]{3,2,1,0:T(8,128)(2,1)S(1)} %merge.1.refs_4_), channel_id=1, source_target_pairs={{0,2},{1,3},{2,0},{3,1},{4,6},{5,7},{6,4},{7,5},{8,10},{9,11},{10,... | collective-permute-start | bytes 1572872 | tf_op jit(solution)/shard_map/ppermute | solution.py:26
  66.1 13.1 %collective-permute-start.16 = (bf16[2,128,8,128]{3,2,1,0:T(8,128)(2,1)S(1)}, bf16[2,128,8,128]{3,2,1,0:T(8,128)(2,1)S(1)}, u32[]{:S(2)}, u32[]{:S(2)}) collective-permute-start(bf16[2,128,8,128]{3,2,1,0:T(8,128)(2,1)S(1)} %collective-permute-done.14.refs_4_), channel_id=1, source_target_pairs={{0,12},{1,13},{2,14},{3,15},{4,8},{5,9},{6,10},{7,11},{8,4},{9,5},... | collective-permute-start | bytes 1572872 | tf_op jit(solution)/shard_map/ppermute | solution.py:26
  79.3 14.9 %collective-permute-start.21 = (bf16[2,128,8,128]{3,2,1,0:T(8,128)(2,1)S(1)}, bf16[2,128,8,128]{3,2,1,0:T(8,128)(2,1)S(1)}, u32[]{:S(2)}, u32[]{:S(2)}) collective-permute-start(bf16[2,128,8,128]{3,2,1,0:T(8,128)(2,1)S(1)} %collective-permute-done.14.refs_4_), channel_id=1, source_target_pairs={{0,4},{1,5},{2,6},{3,7},{4,0},{5,1},{6,2},{7,3},{8,12},{9,13},{10,... | collective-permute-start | bytes 1572872 | tf_op jit(solution)/shard_map/ppermute | solution.py:26
  86.0 19.6 %collective-permute-start.18 = (bf16[2,520,256]{2,1,0:T(8,128)(2,1)S(1)}, bf16[2,520,256]{2,1,0:T(8,128)(2,1)S(1)}, u32[]{:S(2)}, u32[]{:S(2)}) collective-permute-start(bf16[2,520,256]{2,1,0:T(8,128)(2,1)S(1)} %get-tuple-element.98), channel_id=1, source_target_pairs={{0,4},{1,5},{2,6},{3,7},{4,0},{5,1},{6,2},{7,3},{8,12},{9,13},{10,... | collective-permute-start | bytes 1597448 | tf_op jit(solution)/shard_map/ppermute | solution.py:26
  88.1 25.8 %collective-permute-start.19 = (bf16[2,520,256]{2,1,0:T(8,128)(2,1)S(1)}, bf16[2,520,256]{2,1,0:T(8,128)(2,1)S(1)}, u32[]{:S(2)}, u32[]{:S(2)}) collective-permute-start(bf16[2,520,256]{2,1,0:T(8,128)(2,1)S(1)} %get-tuple-element.99), channel_id=1, source_target_pairs={{0,8},{1,9},{2,10},{3,11},{4,12},{5,13},{6,14},{7,15},{8,0},{9,1},... | collective-permute-start | bytes 1597448 | tf_op jit(solution)/shard_map/ppermute | solution.py:26
  88.9 25.0 %collective-permute-start.20 = (bf16[2,520,256]{2,1,0:T(8,128)(2,1)S(1)}, bf16[2,520,256]{2,1,0:T(8,128)(2,1)S(1)}, u32[]{:S(2)}, u32[]{:S(2)}) collective-permute-start(bf16[2,520,256]{2,1,0:T(8,128)(2,1)S(1)} %get-tuple-element.100), channel_id=1, source_target_pairs={{0,12},{1,13},{2,14},{3,15},{4,8},{5,9},{6,10},{7,11},{8,4},{9,5},... | collective-permute-start | bytes 1597448 | tf_op jit(solution)/shard_map/ppermute | solution.py:26
  100.9 13.0 %collective-permute-start.22 = (bf16[2,520,256]{2,1,0:T(8,128)(2,1)S(1)}, bf16[2,520,256]{2,1,0:T(8,128)(2,1)S(1)}, u32[]{:S(2)}, u32[]{:S(2)}) collective-permute-start(bf16[2,520,256]{2,1,0:T(8,128)(2,1)S(1)} %get-tuple-element.113), channel_id=1, source_target_pairs={{0,1},{1,0},{2,3},{3,2},{4,5},{5,4},{6,7},{7,6},{8,9},{9,8},{10,11... | collective-permute-start | bytes 1597448 | tf_op jit(solution)/shard_map/ppermute | solution.py:26
  101.8 17.8 %collective-permute-start.23 = (bf16[2,520,256]{2,1,0:T(8,128)(2,1)S(1)}, bf16[2,520,256]{2,1,0:T(8,128)(2,1)S(1)}, u32[]{:S(2)}, u32[]{:S(2)}) collective-permute-start(bf16[2,520,256]{2,1,0:T(8,128)(2,1)S(1)} %get-tuple-element.114), channel_id=1, source_target_pairs={{0,2},{1,3},{2,0},{3,1},{4,6},{5,7},{6,4},{7,5},{8,10},{9,11},{10,... | collective-permute-start | bytes 1597448 | tf_op jit(solution)/shard_map/ppermute | solution.py:26
  105.5 17.8 %collective-permute-start.24 = (bf16[2,520,256]{2,1,0:T(8,128)(2,1)S(1)}, bf16[2,520,256]{2,1,0:T(8,128)(2,1)S(1)}, u32[]{:S(2)}, u32[]{:S(2)}) collective-permute-start(bf16[2,520,256]{2,1,0:T(8,128)(2,1)S(1)} %get-tuple-element.115), channel_id=1, source_target_pairs={{0,3},{1,2},{2,1},{3,0},{4,7},{5,6},{6,5},{7,4},{8,11},{9,10},{10,... | collective-permute-start | bytes 1597448 | tf_op jit(solution)/shard_map/ppermute | solution.py:26

commit v6 on v5

--- a/solution.py
+++ b/solution.py
@@ -216,15 +216,15 @@
     k = jnp.arange(2 * BINS, dtype=jnp.int32)[None, :]
     frequency = k % TAPS * LANE + k // 8
     n = frequency * (lag - BINS // 2) + k // TAPS % 2 * (BINS // 2)
-    turn = (n + BINS // 4) // (BINS // 2)
-    x = (n - turn * (BINS // 2)).astype(jnp.float32) * (math.pi / BINS)
+    turn = (n + BINS // 4) >> 8
+    x = (n - (turn << 8)).astype(jnp.float32) * (math.pi / BINS)
     x2 = x * x
     cos, sin = jnp.float32(0), jnp.float32(0)
     for power in range(10, -1, -2):
         cos = cos * x2 + (-1) ** (power // 2) / math.factorial(power)
         sin = sin * x2 + (-1) ** (power // 2) / math.factorial(power + 1)
-    values = jnp.where(turn % 2 == 0, cos, sin * x)
-    values = jnp.where((turn + 1) // 2 % 2 == 0, values, -values)
+    values = jnp.where(turn & 1 == 0, cos, sin * x)
+    values = jnp.where((turn + 1) & 2 == 0, values, -values)
     return jnp.where(lag < LAGS, values, 0.0).astype(jnp.bfloat16)
 
 
@@ -242,7 +242,7 @@
 
 def on_device(spectra, partners):
     member = lax.axis_index("mem").astype(jnp.int32)
-    where = jnp.stack([member, lax.axis_index("grp").astype(jnp.int32) >> 1])
+    plane = lax.axis_index("grp").astype(jnp.int32) >> 1
     factor = math.sqrt(2.0 / (BINS * (COMP // 2)))
     white = whiten(spectra)
 
@@ -252,12 +252,12 @@
     for d in (1, 2, 3):
         rows[0][d] = xor_perm(white, "mem", d * row_masks[0])
     up, down = ring_perm(white, 1), ring_perm(white, -1)
-    source, rows[0] = lax.optimization_barrier((white, rows[0]))
-    for d in (1, 3):
+    rows, source, up, down = lax.optimization_barrier((rows, white, up, down))
+    member_now, *halves = lax.optimization_barrier((member, up[: LANE // 2], down[LANE // 2 :]))
+    where = jnp.stack([member_now, plane])
+    source, where = lax.optimization_barrier((source, where))
+    for d in (1, 2, 3):
         rows[1][d] = xor_perm(source, "mem", d * row_masks[1])
-    rows, source, up, down = lax.optimization_barrier((rows, source, up, down))
-    source, *halves = lax.optimization_barrier((source, up[: LANE // 2], down[LANE // 2 :]))
-    rows[1][2] = xor_perm(source, "mem", 2 * row_masks[1])
     tops = [ring_perm(halves[0], 1), ring_perm(halves[1], -1)]
     rows, where, up, down, tops = lax.optimization_barrier((rows, where, up, down, tops))
 
@@ -267,16 +267,16 @@
     near, where = lax.optimization_barrier((near, where))
     across = xor_perm(near, "mem", 16)
     hop = xor_perm(near, "mem", 2 * col_masks[1])
-    near1, near3 = [xor_perm(near, "mem", e * col_masks[0]) for e in (1, 3)]
+    order = column_order(where[0])
+    later, order = lax.optimization_barrier((near, order))
+    near1, near2, near3 = [xor_perm(later, "mem", e * col_masks[0]) for e in (1, 2, 3)]
     table = lag_table(where[0] - member)
-    order = column_order(where[0])
-    table, order, near, near1, near3, hop, across = lax.optimization_barrier(
-        (table, order, near, near1, near3, hop, across)
-    )
-    near2 = xor_perm(near, "mem", 2 * col_masks[0])
+    table, order, hop, across = lax.optimization_barrier((table, order, hop, across))
     far2 = xor_perm(hop, "mem", 16)
     far3 = xor_perm(across, "mem", 3 * col_masks[1])
-    across, near2, far3, far2 = lax.optimization_barrier((across, near2, far3, far2))
+    across, near1, near2, near3, far2, far3 = lax.optimization_barrier(
+        (across, near1, near2, near3, far2, far3)
+    )
     far1 = xor_perm(across, "mem", col_masks[1])
     cols = [[near, near1, near2, near3], [across, far1, far2, far3]]
     parts = []

time: 131 us -> 127 us (0.969)
  other arithmetic: 7.48 us -> 3.8 us
    ppermute x4, waiting for transfers between devices: 10.7 us -> 15.7 us  [ring_perm(): lax.ppermute(array, 'grp', [(i, (i + 2 * shift) % size) for i in range(si...]
    ppermute x21, waiting for transfers between devices: 45.7 us -> 42 us  [xor_perm(): lax.ppermute(array, axis, [(i, i ^ mask) for i in range(lax.axis_size(axi...]
    convert_element_type x1, other arithmetic: 7.04 us -> 3.36 us  [lag_table(): return jnp.where(lag < LAGS, values, 0.0).astype(jnp.bfloat16)]
    ppermute x21, starting transfers between devices: 28.9 us -> 31 us  [xor_perm(): lax.ppermute(array, axis, [(i, i ^ mask) for i in range(lax.axis_size(axi...]
    ppermute x4, starting transfers between devices: 12.3 us -> 10.5 us  [ring_perm(): lax.ppermute(array, 'grp', [(i, (i + 2 * shift) % size) for i in range(si...]
  transfers between devices with their start and end apart: 25 -> 25, of which waited for: 19 -> 16; matrix products, arithmetic and copies ran while one was open for 6% -> 3% of each run, Pallas kernels for 10% -> 11%
where the time goes in v6:
time: 127 us; the launch traced here: 125 us
  waiting for transfers between devices  57.7 us (45%)
  starting transfers between devices  41.5 us (33%)
  Pallas kernels  20.4 us (16%)
  other arithmetic  3.8 us (3%)
  local copies, waits for them, and re-layouts  1.65 us (1%)
    ppermute x21, waiting for transfers between devices, xor_perm(): lax.ppermute(array, axis, [(i, i ^ mask) for i in range(lax.axis_size(axi...  42 us
    ppermute x21, starting transfers between devices, xor_perm(): lax.ppermute(array, axis, [(i, i ^ mask) for i in range(lax.axis_size(axi...  31 us
    ppermute x4, waiting for transfers between devices, ring_perm(): lax.ppermute(array, 'grp', [(i, (i + 2 * shift) % size) for i in range(si...  15.7 us
    pallas_call x2, Pallas kernels, correlate(): pl.pallas_call(body, out_shape=[jax.ShapeDtypeStruct((2, LAG_ROWS, 256),...  13.4 us
    ppermute x4, starting transfers between devices, ring_perm(): lax.ppermute(array, 'grp', [(i, (i + 2 * shift) % size) for i in range(si...  10.5 us
    pallas_call x1, Pallas kernels, finish(): pl.pallas_call(finish_kernel, grid=(4,), in_specs=[pl.BlockSpec(memory_sp...  4.88 us
    convert_element_type x1, other arithmetic, lag_table(): return jnp.where(lag < LAGS, values, 0.0).astype(jnp.bfloat16)  3.36 us
  transfers between devices with their start and end apart: 25, of which 16 were waited for; matrix products, arithmetic and copies ran while one was open for 3% of the time, Pallas kernels for 11%

profile of v6, /device:TPU:8, one launch (start us, length us, event | category | flops | bytes accessed | tf_op | source)
XLA Modules:
  0.0 125.4 jit_solution(1015825567335227945)
XLA Ops:
  0.0 0.0 copy-start
  0.0 0.9 copy-done
  1.0 0.8 whiten.1.refs_0_
  1.8 6.4 %collective-permute-start.4 = (bf16[128,8,128]{2,1,0:T(8,128)(2,1)S(1)}, bf16[128,8,128]{2,1,0:T(8,128)(2,1)S(1)}, u32[]{:S(2)}, u32[]{:S(2)}) collective-permute-start(bf16[128,8,128]{2,1,0:T(8,128)(2,1)S(1)} %whiten.1.refs_0_), channel_id=1, source_target_pairs={{0,192},{32,224},{64,0},{96,32},{128,64},{160,96},{192,128},{224,1... | collective-permute-start | bytes 786440 | tf_op jit(solution)/shard_map/ppermute | solution.py:31
  8.2 0.0 collective-permute-start.3
  8.2 2.8 %collective-permute-start.2 = (bf16[128,8,128]{2,1,0:T(8,128)(2,1)S(1)}, bf16[128,8,128]{2,1,0:T(8,128)(2,1)S(1)}, u32[]{:S(2)}, u32[]{:S(2)}) collective-permute-start(bf16[128,8,128]{2,1,0:T(8,128)(2,1)S(1)} %whiten.1.refs_0_), channel_id=1, source_target_pairs={{0,12},{1,13},{2,14},{3,15},{4,8},{5,9},{6,10},{7,11},{8,4},{9,5},... | collective-permute-start | bytes 786440 | tf_op jit(solution)/shard_map/ppermute | solution.py:26
  10.9 0.8 collective-permute-start.1
  11.7 0.5 collective-permute-start
  12.3 7.1 %collective-permute-done.4.refs_1_ = bf16[128,8,128]{2,1,0:T(8,128)(2,1)S(1)} collective-permute-done((bf16[128,8,128]{2,1,0:T(8,128)(2,1)S(1)}, bf16[128,8,128]{2,1,0:T(8,128)(2,1)S(1)}, u32[]{:S(2)}, u32[]{:S(2)}) %collective-permute-start.4) | collective-permute-done | bytes 262176 | tf_op jit(solution)/shard_map/ppermute | solution.py:31
  19.4 3.8 %collective-permute-done.3.refs_2_ = bf16[128,8,128]{2,1,0:T(8,128)(2,1)S(1)} collective-permute-done((bf16[128,8,128]{2,1,0:T(8,128)(2,1)S(1)}, bf16[128,8,128]{2,1,0:T(8,128)(2,1)S(1)}, u32[]{:S(2)}, u32[]{:S(2)}) %collective-permute-start.3) | collective-permute-done | bytes 262176 | tf_op jit(solution)/shard_map/ppermute | solution.py:31
  23.2 0.0 collective-permute-done.2.refs_3_
  23.2 0.0 collective-permute-done.1.refs_2_
  23.2 0.2 collective-permute-done.refs_1_
  23.4 0.1 pad_add_fusion.where_ref
  23.5 1.6 %collective-permute-start.7 = (bf16[128,8,128]{2,1,0:T(8,128)(2,1)S(1)}, bf16[128,8,128]{2,1,0:T(8,128)(2,1)S(1)}, u32[]{:S(2)}, u32[]{:S(2)}) collective-permute-start(bf16[128,8,128]{2,1,0:T(8,128)(2,1)S(1)} %whiten.1.refs_0_), channel_id=1, source_target_pairs={{0,3},{1,2},{2,1},{3,0},{4,7},{5,6},{6,5},{7,4},{8,11},{9,10},{10,... | collective-permute-start | bytes 786440 | tf_op jit(solution)/shard_map/ppermute | solution.py:26
  25.1 0.9 collective-permute-start.6
  26.0 1.6 %collective-permute-start.5 = (bf16[128,8,128]{2,1,0:T(8,128)(2,1)S(1)}, bf16[128,8,128]{2,1,0:T(8,128)(2,1)S(1)}, u32[]{:S(2)}, u32[]{:S(2)}) collective-permute-start(bf16[128,8,128]{2,1,0:T(8,128)(2,1)S(1)} %whiten.1.refs_0_), channel_id=1, source_target_pairs={{0,1},{1,0},{2,3},{3,2},{4,5},{5,4},{6,7},{7,6},{8,9},{9,8},{10,11... | collective-permute-start | bytes 786440 | tf_op jit(solution)/shard_map/ppermute | solution.py:26
  27.6 1.5 %collective-permute-start.8 = (bf16[64,8,128]{2,1,0:T(8,128)(2,1)S(1)}, bf16[64,8,128]{2,1,0:T(8,128)(2,1)S(1)}, u32[]{:S(2)}, u32[]{:S(2)}) collective-permute-start(bf16[64,8,128]{2,1,0:T(8,128)(2,1)S(1)} %slice.10), channel_id=1, source_target_pairs={{0,64},{32,96},{64,128},{96,160},{128,192},{160,224},{192,0},{224,... | collective-permute-start | bytes 393224 | tf_op jit(solution)/shard_map/ppermute | solution.py:31
  29.2 2.6 %collective-permute-start.9 = (bf16[64,8,128]{2,1,0:T(8,128)(2,1)S(1)}, bf16[64,8,128]{2,1,0:T(8,128)(2,1)S(1)}, u32[]{:S(2)}, u32[]{:S(2)}) collective-permute-start(bf16[64,8,128]{2,1,0:T(8,128)(2,1)S(1)} %slice.11), channel_id=1, source_target_pairs={{0,192},{32,224},{64,0},{96,32},{128,64},{160,96},{192,128},{224,1... | collective-permute-start | bytes 393224 | tf_op jit(solution)/shard_map/ppermute | solution.py:31
  31.8 3.1 %collective-permute-done.8.refs_3_ = bf16[64,8,128]{2,1,0:T(8,128)(2,1)S(1)} collective-permute-done((bf16[64,8,128]{2,1,0:T(8,128)(2,1)S(1)}, bf16[64,8,128]{2,1,0:T(8,128)(2,1)S(1)}, u32[]{:S(2)}, u32[]{:S(2)}) %collective-permute-start.8) | collective-permute-done | bytes 131104 | tf_op jit(solution)/shard_map/ppermute | solution.py:31
  34.8 1.7 %collective-permute-done.9.refs_4_ = bf16[64,8,128]{2,1,0:T(8,128)(2,1)S(1)} collective-permute-done((bf16[64,8,128]{2,1,0:T(8,128)(2,1)S(1)}, bf16[64,8,128]{2,1,0:T(8,128)(2,1)S(1)}, u32[]{:S(2)}, u32[]{:S(2)}) %collective-permute-start.9) | collective-permute-done | bytes 131104 | tf_op jit(solution)/shard_map/ppermute | solution.py:31
  36.5 0.0 collective-permute-done.7.refs_3_
  36.5 0.0 collective-permute-done.6.refs_2_
  36.5 1.0 collective-permute-done.5.refs_1_
  37.6 0.7 copy-done.1
  38.3 0.6 pick.1.mine_ref
  38.9 0.1 collective-permute-start.10
  39.0 0.1 iota_add_fusion.1
  39.1 1.8 %collective-permute-done.10.other_ref = bf16[2,128,8,128]{3,2,1,0:T(8,128)(2,1)S(1)} collective-permute-done((bf16[2,128,8,128]{3,2,1,0:T(8,128)(2,1)S(1)}, bf16[2,128,8,128]{3,2,1,0:T(8,128)(2,1)S(1)}, u32[]{:S(2)}, u32[]{:S(2)}) %collective-permute-start.10) | collective-permute-done | bytes 524320 | tf_op jit(solution)/shard_map/ppermute | solution.py:26
  40.9 0.0 copy-done.2
  40.9 0.6 merge.1.refs_4_
  41.8 2.3 %collective-permute-start.12 = (bf16[2,128,8,128]{3,2,1,0:T(8,128)(2,1)S(1)}, bf16[2,128,8,128]{3,2,1,0:T(8,128)(2,1)S(1)}, u32[]{:S(2)}, u32[]{:S(2)}) collective-permute-start(bf16[2,128,8,128]{3,2,1,0:T(8,128)(2,1)S(1)} %merge.1.refs_4_), channel_id=1, source_target_pairs={{0,16},{1,17},{2,18},{3,19},{4,20},{5,21},{6,22},{7,23},{8,24},{9,... | collective-permute-start | bytes 1572872 | tf_op jit(solution)/shard_map/ppermute | solution.py:26
  44.0 3.0 %collective-permute-start.11 = (bf16[2,128,8,128]{3,2,1,0:T(8,128)(2,1)S(1)}, bf16[2,128,8,128]{3,2,1,0:T(8,128)(2,1)S(1)}, u32[]{:S(2)}, u32[]{:S(2)}) collective-permute-start(bf16[2,128,8,128]{3,2,1,0:T(8,128)(2,1)S(1)} %merge.1.refs_4_), channel_id=1, source_target_pairs={{0,8},{1,9},{2,10},{3,11},{4,12},{5,13},{6,14},{7,15},{8,0},{9,1},... | collective-permute-start | bytes 1572872 | tf_op jit(solution)/shard_map/ppermute | solution.py:26
  47.1 0.2 compare_convert_fusion.refs_8_
  47.3 1.7 %collective-permute-start.15 = (bf16[2,128,8,128]{3,2,1,0:T(8,128)(2,1)S(1)}, bf16[2,128,8,128]{3,2,1,0:T(8,128)(2,1)S(1)}, u32[]{:S(2)}, u32[]{:S(2)}) collective-permute-start(bf16[2,128,8,128]{3,2,1,0:T(8,128)(2,1)S(1)} %merge.1.refs_4_), channel_id=1, source_target_pairs={{0,3},{1,2},{2,1},{3,0},{4,7},{5,6},{6,5},{7,4},{8,11},{9,10},{10,... | collective-permute-start | bytes 1572872 | tf_op jit(solution)/shard_map/ppermute | solution.py:26
  49.0 1.1 collective-permute-start.14
  50.1 1.4 %collective-permute-start.13 = (bf16[2,128,8,128]{3,2,1,0:T(8,128)(2,1)S(1)}, bf16[2,128,8,128]{3,2,1,0:T(8,128)(2,1)S(1)}, u32[]{:S(2)}, u32[]{:S(2)}) collective-permute-start(bf16[2,128,8,128]{3,2,1,0:T(8,128)(2,1)S(1)} %merge.1.refs_4_), channel_id=1, source_target_pairs={{0,1},{1,0},{2,3},{3,2},{4,5},{5,4},{6,7},{7,6},{8,9},{9,8},{10,11... | collective-permute-start | bytes 1572872 | tf_op jit(solution)/shard_map/ppermute | solution.py:26
  51.5 3.4 %fusion.1.refs_8_ = bf16[520,1024]{1,0:T(8,128)(2,1)S(1)} fusion(s32[1024]{0:T(1024)S(1)} %get-tuple-element.110, s32[520]{0:T(1024)S(1)} %fusion.22, s32[1024]{0:T(1024)S(1)} %get-tuple-element.109, pred[520]{0:T(1024)(128)(4,1)S(1)} %fusion.23), kind=kLoop, calls=%fused_computation.2 | loop fusion | flops 22896640 | bytes 1075752 | tf_op jit(solution)/shard_map/convert_element_type | solution.py:228
  54.9 1.4 %collective-permute-done.12.refs_4_ = bf16[2,128,8,128]{3,2,1,0:T(8,128)(2,1)S(1)} collective-permute-done((bf16[2,128,8,128]{3,2,1,0:T(8,128)(2,1)S(1)}, bf16[2,128,8,128]{3,2,1,0:T(8,128)(2,1)S(1)}, u32[]{:S(2)}, u32[]{:S(2)}) %collective-permute-start.12) | collective-permute-done | bytes 524320 | tf_op jit(solution)/shard_map/ppermute | solution.py:26
  56.3 3.0 %collective-permute-done.11 = bf16[2,128,8,128]{3,2,1,0:T(8,128)(2,1)S(1)} collective-permute-done((bf16[2,128,8,128]{3,2,1,0:T(8,128)(2,1)S(1)}, bf16[2,128,8,128]{3,2,1,0:T(8,128)(2,1)S(1)}, u32[]{:S(2)}, u32[]{:S(2)}) %collective-permute-start.11) | collective-permute-done | bytes 524320 | tf_op jit(solution)/shard_map/ppermute | solution.py:26
  59.2 0.4 collective-permute-start.16
  59.6 2.8 %collective-permute-start.17 = (bf16[2,128,8,128]{3,2,1,0:T(8,128)(2,1)S(1)}, bf16[2,128,8,128]{3,2,1,0:T(8,128)(2,1)S(1)}, u32[]{:S(2)}, u32[]{:S(2)}) collective-permute-start(bf16[2,128,8,128]{3,2,1,0:T(8,128)(2,1)S(1)} %collective-permute-done.12.refs_4_), channel_id=1, source_target_pairs={{0,12},{1,13},{2,14},{3,15},{4,8},{5,9},{6,10},{7,11},{8,4},{9,5},... | collective-permute-start | bytes 1572872 | tf_op jit(solution)/shard_map/ppermute | solution.py:26
  62.4 9.7 %collective-permute-done.15.refs_7_ = bf16[2,128,8,128]{3,2,1,0:T(8,128)(2,1)S(1)} collective-permute-done((bf16[2,128,8,128]{3,2,1,0:T(8,128)(2,1)S(1)}, bf16[2,128,8,128]{3,2,1,0:T(8,128)(2,1)S(1)}, u32[]{:S(2)}, u32[]{:S(2)}) %collective-permute-start.15) | collective-permute-done | bytes 524320 | tf_op jit(solution)/shard_map/ppermute | solution.py:26
  72.1 0.0 collective-permute-done.14.refs_6_
  72.1 1.8 %collective-permute-done.13.refs_5_ = bf16[2,128,8,128]{3,2,1,0:T(8,128)(2,1)S(1)} collective-permute-done((bf16[2,128,8,128]{3,2,1,0:T(8,128)(2,1)S(1)}, bf16[2,128,8,128]{3,2,1,0:T(8,128)(2,1)S(1)}, u32[]{:S(2)}, u32[]{:S(2)}) %collective-permute-start.13) | collective-permute-done | bytes 524320 | tf_op jit(solution)/shard_map/ppermute | solution.py:26
  73.9 0.0 collective-permute-done.16.refs_6_
  73.9 0.0 collective-permute-done.17.refs_7_
  73.9 0.6 collective-permute-start.21
  74.5 6.7 %correlate.2 = (bf16[2,520,256]{2,1,0:T(8,128)(2,1)S(1)}, bf16[2,520,256]{2,1,0:T(8,128)(2,1)S(1)}, bf16[2,520,256]{2,1,0:T(8,128)(2,1)S(1)}, bf16[2,520,256]{2,1,0:T(8,128)(2,1)S(1)}) custom-call(bf16[128,8,128]{2,1,0:T(8,128)(2,1)S(1)} %whiten.1.refs_0_, bf16[128,8,128]{2,1,0:T(8,128)(2,1)S(1)} %collective-permute-done.refs_1_, ...), custom_call_target="tpu_custom_call" | custom-call | flops 3254779904 | bytes 7340032 | tf_op jit(solution)/shard_map/correlate/pallas_call | solution.py:164
  81.2 1.5 %collective-permute-start.18 = (bf16[2,520,256]{2,1,0:T(8,128)(2,1)S(1)}, bf16[2,520,256]{2,1,0:T(8,128)(2,1)S(1)}, u32[]{:S(2)}, u32[]{:S(2)}) collective-permute-start(bf16[2,520,256]{2,1,0:T(8,128)(2,1)S(1)} %get-tuple-element.90), channel_id=1, source_target_pairs={{0,4},{1,5},{2,6},{3,7},{4,0},{5,1},{6,2},{7,3},{8,12},{9,13},{10,... | collective-permute-start | bytes 1597448 | tf_op jit(solution)/shard_map/ppermute | solution.py:26
  82.7 1.8 %collective-permute-start.19 = (bf16[2,520,256]{2,1,0:T(8,128)(2,1)S(1)}, bf16[2,520,256]{2,1,0:T(8,128)(2,1)S(1)}, u32[]{:S(2)}, u32[]{:S(2)}) collective-permute-start(bf16[2,520,256]{2,1,0:T(8,128)(2,1)S(1)} %get-tuple-element.91), channel_id=1, source_target_pairs={{0,8},{1,9},{2,10},{3,11},{4,12},{5,13},{6,14},{7,15},{8,0},{9,1},... | collective-permute-start | bytes 1597448 | tf_op jit(solution)/shard_map/ppermute | solution.py:26
  84.5 1.4 %collective-permute-start.20 = (bf16[2,520,256]{2,1,0:T(8,128)(2,1)S(1)}, bf16[2,520,256]{2,1,0:T(8,128)(2,1)S(1)}, u32[]{:S(2)}, u32[]{:S(2)}) collective-permute-start(bf16[2,520,256]{2,1,0:T(8,128)(2,1)S(1)} %get-tuple-element.92), channel_id=1, source_target_pairs={{0,12},{1,13},{2,14},{3,15},{4,8},{5,9},{6,10},{7,11},{8,4},{9,5},... | collective-permute-start | bytes 1597448 | tf_op jit(solution)/shard_map/ppermute | solution.py:26
  86.0 2.8 %collective-permute-done.21.refs_5_ = bf16[2,128,8,128]{3,2,1,0:T(8,128)(2,1)S(1)} collective-permute-done((bf16[2,128,8,128]{3,2,1,0:T(8,128)(2,1)S(1)}, bf16[2,128,8,128]{3,2,1,0:T(8,128)(2,1)S(1)}, u32[]{:S(2)}, u32[]{:S(2)}) %collective-permute-start.21) | collective-permute-done | bytes 524320 | tf_op jit(solution)/shard_map/ppermute | solution.py:26
  88.8 6.7 %correlate.3 = (bf16[2,520,256]{2,1,0:T(8,128)(2,1)S(1)}, bf16[2,520,256]{2,1,0:T(8,128)(2,1)S(1)}, bf16[2,520,256]{2,1,0:T(8,128)(2,1)S(1)}, bf16[2,520,256]{2,1,0:T(8,128)(2,1)S(1)}) custom-call(bf16[128,8,128]{2,1,0:T(8,128)(2,1)S(1)} %whiten.1.refs_0_, bf16[128,8,128]{2,1,0:T(8,128)(2,1)S(1)} %collective-permute-done.5.refs_1_, ...), custom_call_target="tpu_custom_call" | custom-call | flops 3254779904 | bytes 7340032 | tf_op jit(solution)/shard_map/correlate/pallas_call | solution.py:164
  95.5 0.7 collective-permute-start.22
  96.2 2.4 %collective-permute-start.23 = (bf16[2,520,256]{2,1,0:T(8,128)(2,1)S(1)}, bf16[2,520,256]{2,1,0:T(8,128)(2,1)S(1)}, u32[]{:S(2)}, u32[]{:S(2)}) collective-permute-start(bf16[2,520,256]{2,1,0:T(8,128)(2,1)S(1)} %get-tuple-element.106), channel_id=1, source_target_pairs={{0,2},{1,3},{2,0},{3,1},{4,6},{5,7},{6,4},{7,5},{8,10},{9,11},{10,... | collective-permute-start | bytes 1597448 | tf_op jit(solution)/shard_map/ppermute | solution.py:26
  98.6 1.6 %collective-permute-done.18.refs_1_ = bf16[2,520,256]{2,1,0:T(8,128)(2,1)S(1)} collective-permute-done((bf16[2,520,256]{2,1,0:T(8,128)(2,1)S(1)}, bf16[2,520,256]{2,1,0:T(8,128)(2,1)S(1)}, u32[]{:S(2)}, u32[]{:S(2)}) %collective-permute-start.18) | collective-permute-done | bytes 532512 | tf_op jit(solution)/shard_map/ppermute | solution.py:26
  100.2 1.6 %collective-permute-start.24 = (bf16[2,520,256]{2,1,0:T(8,128)(2,1)S(1)}, bf16[2,520,256]{2,1,0:T(8,128)(2,1)S(1)}, u32[]{:S(2)}, u32[]{:S(2)}) collective-permute-start(bf16[2,520,256]{2,1,0:T(8,128)(2,1)S(1)} %get-tuple-element.107), channel_id=1, source_target_pairs={{0,3},{1,2},{2,1},{3,0},{4,7},{5,6},{6,5},{7,4},{8,11},{9,10},{10,... | collective-permute-start | bytes 1597448 | tf_op jit(solution)/shard_map/ppermute | solution.py:26
  101.8 8.4 %collective-permute-done.19.refs_2_ = bf16[2,520,256]{2,1,0:T(8,128)(2,1)S(1)} collective-permute-done((bf16[2,520,256]{2,1,0:T(8,128)(2,1)S(1)}, bf16[2,520,256]{2,1,0:T(8,128)(2,1)S(1)}, u32[]{:S(2)}, u32[]{:S(2)}) %collective-permute-start.19) | collective-permute-done | bytes 532512 | tf_op jit(solution)/shard_map/ppermute | solution.py:26
  110.1 0.0 collective-permute-done.20.refs_3_
  110.1 0.0 collective-permute-done.22.refs_5_
  110.2 7.6 %collective-permute-done.23.refs_6_ = bf16[2,520,256]{2,1,0:T(8,128)(2,1)S(1)} collective-permute-done((bf16[2,520,256]{2,1,0:T(8,128)(2,1)S(1)}, bf16[2,520,256]{2,1,0:T(8,128)(2,1)S(1)}, u32[]{:S(2)}, u32[]{:S(2)}) %collective-permute-start.23) | collective-permute-done | bytes 532512 | tf_op jit(solution)/shard_map/ppermute | solution.py:26
  117.8 2.7 %collective-permute-done.24.refs_7_ = bf16[2,520,256]{2,1,0:T(8,128)(2,1)S(1)} collective-permute-done((bf16[2,520,256]{2,1,0:T(8,128)(2,1)S(1)}, bf16[2,520,256]{2,1,0:T(8,128)(2,1)S(1)}, u32[]{:S(2)}, u32[]{:S(2)}) %collective-permute-start.24) | collective-permute-done | bytes 532512 | tf_op jit(solution)/shard_map/ppermute | solution.py:26
  120.5 4.9 %finish.1 = bf16[4,4104,128]{2,1,0:T(8,128)(2,1)} custom-call(s32[1]{0:T(128)} %bitcast.member_ref, bf16[2,520,256]{2,1,0:T(8,128)(2,1)S(1)} %get-tuple-element.89.refs_0_, bf16[2,520,256]{2,1,0:T(8,128)(2,1)S(1)} %collective-permute-done.18.refs_1_, bf16[2,520,256]{2,1,0:T(8,128)(2,1)S(1)} %collective-permute-done.19.refs_2_, ...), custom_call_target="tpu_custom_call" | custom-call | tf_op jit(solution)/shard_map/finish/pallas_call | solution.py:202
  (11 shorter events, 0.1 us)
Async XLA Ops:
  0.0 0.9 copy-start
  1.0 40.0 %copy-start.2 = (s32[2,32]{1,0:T(2,128)S(1)}, s32[2,32]{1,0:T(2,128)}, u32[]{:S(2)}) copy-start(s32[2,32]{1,0:T(2,128)} %partners_ref.3) | copy-start | bytes 772
  1.8 17.6 %collective-permute-start.4 = (bf16[128,8,128]{2,1,0:T(8,128)(2,1)S(1)}, bf16[128,8,128]{2,1,0:T(8,128)(2,1)S(1)}, u32[]{:S(2)}, u32[]{:S(2)}) collective-permute-start(bf16[128,8,128]{2,1,0:T(8,128)(2,1)S(1)} %whiten.1.refs_0_), channel_id=1, source_target_pairs={{0,192},{32,224},{64,0},{96,32},{128,64},{160,96},{192,128},{224,1... | collective-permute-start | bytes 786440 | tf_op jit(solution)/shard_map/ppermute | solution.py:31
  8.2 15.0 %collective-permute-start.3 = (bf16[128,8,128]{2,1,0:T(8,128)(2,1)S(1)}, bf16[128,8,128]{2,1,0:T(8,128)(2,1)S(1)}, u32[]{:S(2)}, u32[]{:S(2)}) collective-permute-start(bf16[128,8,128]{2,1,0:T(8,128)(2,1)S(1)} %whiten.1.refs_0_), channel_id=1, source_target_pairs={{0,64},{32,96},{64,128},{96,160},{128,192},{160,224},{192,0},{224,... | collective-permute-start | bytes 786440 | tf_op jit(solution)/shard_map/ppermute | solution.py:31
  8.2 15.0 %collective-permute-start.2 = (bf16[128,8,128]{2,1,0:T(8,128)(2,1)S(1)}, bf16[128,8,128]{2,1,0:T(8,128)(2,1)S(1)}, u32[]{:S(2)}, u32[]{:S(2)}) collective-permute-start(bf16[128,8,128]{2,1,0:T(8,128)(2,1)S(1)} %whiten.1.refs_0_), channel_id=1, source_target_pairs={{0,12},{1,13},{2,14},{3,15},{4,8},{5,9},{6,10},{7,11},{8,4},{9,5},... | collective-permute-start | bytes 786440 | tf_op jit(solution)/shard_map/ppermute | solution.py:26
  10.9 12.3 %collective-permute-start.1 = (bf16[128,8,128]{2,1,0:T(8,128)(2,1)S(1)}, bf16[128,8,128]{2,1,0:T(8,128)(2,1)S(1)}, u32[]{:S(2)}, u32[]{:S(2)}) collective-permute-start(bf16[128,8,128]{2,1,0:T(8,128)(2,1)S(1)} %whiten.1.refs_0_), channel_id=1, source_target_pairs={{0,8},{1,9},{2,10},{3,11},{4,12},{5,13},{6,14},{7,15},{8,0},{9,1},... | collective-permute-start | bytes 786440 | tf_op jit(solution)/shard_map/ppermute | solution.py:26
  11.7 11.7 %collective-permute-start = (bf16[128,8,128]{2,1,0:T(8,128)(2,1)S(1)}, bf16[128,8,128]{2,1,0:T(8,128)(2,1)S(1)}, u32[]{:S(2)}, u32[]{:S(2)}) collective-permute-start(bf16[128,8,128]{2,1,0:T(8,128)(2,1)S(1)} %whiten.1.refs_0_), channel_id=1, source_target_pairs={{0,4},{1,5},{2,6},{3,7},{4,0},{5,1},{6,2},{7,3},{8,12},{9,13},{10,... | collective-permute-start | bytes 786440 | tf_op jit(solution)/shard_map/ppermute | solution.py:26
  23.5 13.0 %collective-permute-start.7 = (bf16[128,8,128]{2,1,0:T(8,128)(2,1)S(1)}, bf16[128,8,128]{2,1,0:T(8,128)(2,1)S(1)}, u32[]{:S(2)}, u32[]{:S(2)}) collective-permute-start(bf16[128,8,128]{2,1,0:T(8,128)(2,1)S(1)} %whiten.1.refs_0_), channel_id=1, source_target_pairs={{0,3},{1,2},{2,1},{3,0},{4,7},{5,6},{6,5},{7,4},{8,11},{9,10},{10,... | collective-permute-start | bytes 786440 | tf_op jit(solution)/shard_map/ppermute | solution.py:26
  25.1 11.4 %collective-permute-start.6 = (bf16[128,8,128]{2,1,0:T(8,128)(2,1)S(1)}, bf16[128,8,128]{2,1,0:T(8,128)(2,1)S(1)}, u32[]{:S(2)}, u32[]{:S(2)}) collective-permute-start(bf16[128,8,128]{2,1,0:T(8,128)(2,1)S(1)} %whiten.1.refs_0_), channel_id=1, source_target_pairs={{0,2},{1,3},{2,0},{3,1},{4,6},{5,7},{6,4},{7,5},{8,10},{9,11},{10,... | collective-permute-start | bytes 786440 | tf_op jit(solution)/shard_map/ppermute | solution.py:26
  26.0 11.5 %collective-permute-start.5 = (bf16[128,8,128]{2,1,0:T(8,128)(2,1)S(1)}, bf16[128,8,128]{2,1,0:T(8,128)(2,1)S(1)}, u32[]{:S(2)}, u32[]{:S(2)}) collective-permute-start(bf16[128,8,128]{2,1,0:T(8,128)(2,1)S(1)} %whiten.1.refs_0_), channel_id=1, source_target_pairs={{0,1},{1,0},{2,3},{3,2},{4,5},{5,4},{6,7},{7,6},{8,9},{9,8},{10,11... | collective-permute-start | bytes 786440 | tf_op jit(solution)/shard_map/ppermute | solution.py:26
  27.6 7.2 %collective-permute-start.8 = (bf16[64,8,128]{2,1,0:T(8,128)(2,1)S(1)}, bf16[64,8,128]{2,1,0:T(8,128)(2,1)S(1)}, u32[]{:S(2)}, u32[]{:S(2)}) collective-permute-start(bf16[64,8,128]{2,1,0:T(8,128)(2,1)S(1)} %slice.10), channel_id=1, source_target_pairs={{0,64},{32,96},{64,128},{96,160},{128,192},{160,224},{192,0},{224,... | collective-permute-start | bytes 393224 | tf_op jit(solution)/shard_map/ppermute | solution.py:31
  29.2 7.4 %collective-permute-start.9 = (bf16[64,8,128]{2,1,0:T(8,128)(2,1)S(1)}, bf16[64,8,128]{2,1,0:T(8,128)(2,1)S(1)}, u32[]{:S(2)}, u32[]{:S(2)}) collective-permute-start(bf16[64,8,128]{2,1,0:T(8,128)(2,1)S(1)} %slice.11), channel_id=1, source_target_pairs={{0,192},{32,224},{64,0},{96,32},{128,64},{160,96},{192,128},{224,1... | collective-permute-start | bytes 393224 | tf_op jit(solution)/shard_map/ppermute | solution.py:31
  37.6 0.7 copy-start.1
  38.9 2.0 %collective-permute-start.10 = (bf16[2,128,8,128]{3,2,1,0:T(8,128)(2,1)S(1)}, bf16[2,128,8,128]{3,2,1,0:T(8,128)(2,1)S(1)}, u32[]{:S(2)}, u32[]{:S(2)}) collective-permute-start(bf16[2,128,8,128]{3,2,1,0:T(8,128)(2,1)S(1)} %pick.1.mine_ref), channel_id=1, source_target_pairs={{0,32},{32,0},{64,96},{96,64},{128,160},{160,128},{192,224},{224,1... | collective-permute-start | bytes 1572872 | tf_op jit(solution)/shard_map/ppermute | solution.py:26
  41.8 14.5 %collective-permute-start.12 = (bf16[2,128,8,128]{3,2,1,0:T(8,128)(2,1)S(1)}, bf16[2,128,8,128]{3,2,1,0:T(8,128)(2,1)S(1)}, u32[]{:S(2)}, u32[]{:S(2)}) collective-permute-start(bf16[2,128,8,128]{3,2,1,0:T(8,128)(2,1)S(1)} %merge.1.refs_4_), channel_id=1, source_target_pairs={{0,16},{1,17},{2,18},{3,19},{4,20},{5,21},{6,22},{7,23},{8,24},{9,... | collective-permute-start | bytes 1572872 | tf_op jit(solution)/shard_map/ppermute | solution.py:26
  44.0 15.2 %collective-permute-start.11 = (bf16[2,128,8,128]{3,2,1,0:T(8,128)(2,1)S(1)}, bf16[2,128,8,128]{3,2,1,0:T(8,128)(2,1)S(1)}, u32[]{:S(2)}, u32[]{:S(2)}) collective-permute-start(bf16[2,128,8,128]{3,2,1,0:T(8,128)(2,1)S(1)} %merge.1.refs_4_), channel_id=1, source_target_pairs={{0,8},{1,9},{2,10},{3,11},{4,12},{5,13},{6,14},{7,15},{8,0},{9,1},... | collective-permute-start | bytes 1572872 | tf_op jit(solution)/shard_map/ppermute | solution.py:26
  47.3 24.7 %collective-permute-start.15 = (bf16[2,128,8,128]{3,2,1,0:T(8,128)(2,1)S(1)}, bf16[2,128,8,128]{3,2,1,0:T(8,128)(2,1)S(1)}, u32[]{:S(2)}, u32[]{:S(2)}) collective-permute-start(bf16[2,128,8,128]{3,2,1,0:T(8,128)(2,1)S(1)} %merge.1.refs_4_), channel_id=1, source_target_pairs={{0,3},{1,2},{2,1},{3,0},{4,7},{5,6},{6,5},{7,4},{8,11},{9,10},{10,... | collective-permute-start | bytes 1572872 | tf_op jit(solution)/shard_map/ppermute | solution.py:26
  49.0 23.1 %collective-permute-start.14 = (bf16[2,128,8,128]{3,2,1,0:T(8,128)(2,1)S(1)}, bf16[2,128,8,128]{3,2,1,0:T(8,128)(2,1)S(1)}, u32[]{:S(2)}, u32[]{:S(2)}) collective-permute-start(bf16[2,128,8,128]{3,2,1,0:T(8,128)(2,1)S(1)} %merge.1.refs_4_), channel_id=1, source_target_pairs={{0,2},{1,3},{2,0},{3,1},{4,6},{5,7},{6,4},{7,5},{8,10},{9,11},{10,... | collective-permute-start | bytes 1572872 | tf_op jit(solution)/shard_map/ppermute | solution.py:26
  50.1 23.8 %collective-permute-start.13 = (bf16[2,128,8,128]{3,2,1,0:T(8,128)(2,1)S(1)}, bf16[2,128,8,128]{3,2,1,0:T(8,128)(2,1)S(1)}, u32[]{:S(2)}, u32[]{:S(2)}) collective-permute-start(bf16[2,128,8,128]{3,2,1,0:T(8,128)(2,1)S(1)} %merge.1.refs_4_), channel_id=1, source_target_pairs={{0,1},{1,0},{2,3},{3,2},{4,5},{5,4},{6,7},{7,6},{8,9},{9,8},{10,11... | collective-permute-start | bytes 1572872 | tf_op jit(solution)/shard_map/ppermute | solution.py:26
  59.2 14.7 %collective-permute-start.16 = (bf16[2,128,8,128]{3,2,1,0:T(8,128)(2,1)S(1)}, bf16[2,128,8,128]{3,2,1,0:T(8,128)(2,1)S(1)}, u32[]{:S(2)}, u32[]{:S(2)}) collective-permute-start(bf16[2,128,8,128]{3,2,1,0:T(8,128)(2,1)S(1)} %collective-permute-done.11), channel_id=1, source_target_pairs={{0,16},{1,17},{2,18},{3,19},{4,20},{5,21},{6,22},{7,23},{8,24},{9,... | collective-permute-start | bytes 1572872 | tf_op jit(solution)/shard_map/ppermute | solution.py:26
  59.6 14.3 %collective-permute-start.17 = (bf16[2,128,8,128]{3,2,1,0:T(8,128)(2,1)S(1)}, bf16[2,128,8,128]{3,2,1,0:T(8,128)(2,1)S(1)}, u32[]{:S(2)}, u32[]{:S(2)}) collective-permute-start(bf16[2,128,8,128]{3,2,1,0:T(8,128)(2,1)S(1)} %collective-permute-done.12.refs_4_), channel_id=1, source_target_pairs={{0,12},{1,13},{2,14},{3,15},{4,8},{5,9},{6,10},{7,11},{8,4},{9,5},... | collective-permute-start | bytes 1572872 | tf_op jit(solution)/shard_map/ppermute | solution.py:26
  73.9 14.9 %collective-permute-start.21 = (bf16[2,128,8,128]{3,2,1,0:T(8,128)(2,1)S(1)}, bf16[2,128,8,128]{3,2,1,0:T(8,128)(2,1)S(1)}, u32[]{:S(2)}, u32[]{:S(2)}) collective-permute-start(bf16[2,128,8,128]{3,2,1,0:T(8,128)(2,1)S(1)} %collective-permute-done.12.refs_4_), channel_id=1, source_target_pairs={{0,4},{1,5},{2,6},{3,7},{4,0},{5,1},{6,2},{7,3},{8,12},{9,13},{10,... | collective-permute-start | bytes 1572872 | tf_op jit(solution)/shard_map/ppermute | solution.py:26
  81.2 19.0 %collective-permute-start.18 = (bf16[2,520,256]{2,1,0:T(8,128)(2,1)S(1)}, bf16[2,520,256]{2,1,0:T(8,128)(2,1)S(1)}, u32[]{:S(2)}, u32[]{:S(2)}) collective-permute-start(bf16[2,520,256]{2,1,0:T(8,128)(2,1)S(1)} %get-tuple-element.90), channel_id=1, source_target_pairs={{0,4},{1,5},{2,6},{3,7},{4,0},{5,1},{6,2},{7,3},{8,12},{9,13},{10,... | collective-permute-start | bytes 1597448 | tf_op jit(solution)/shard_map/ppermute | solution.py:26
  82.7 27.4 %collective-permute-start.19 = (bf16[2,520,256]{2,1,0:T(8,128)(2,1)S(1)}, bf16[2,520,256]{2,1,0:T(8,128)(2,1)S(1)}, u32[]{:S(2)}, u32[]{:S(2)}) collective-permute-start(bf16[2,520,256]{2,1,0:T(8,128)(2,1)S(1)} %get-tuple-element.91), channel_id=1, source_target_pairs={{0,8},{1,9},{2,10},{3,11},{4,12},{5,13},{6,14},{7,15},{8,0},{9,1},... | collective-permute-start | bytes 1597448 | tf_op jit(solution)/shard_map/ppermute | solution.py:26
  84.5 25.6 %collective-permute-start.20 = (bf16[2,520,256]{2,1,0:T(8,128)(2,1)S(1)}, bf16[2,520,256]{2,1,0:T(8,128)(2,1)S(1)}, u32[]{:S(2)}, u32[]{:S(2)}) collective-permute-start(bf16[2,520,256]{2,1,0:T(8,128)(2,1)S(1)} %get-tuple-element.92), channel_id=1, source_target_pairs={{0,12},{1,13},{2,14},{3,15},{4,8},{5,9},{6,10},{7,11},{8,4},{9,5},... | collective-permute-start | bytes 1597448 | tf_op jit(solution)/shard_map/ppermute | solution.py:26
  95.5 14.7 %collective-permute-start.22 = (bf16[2,520,256]{2,1,0:T(8,128)(2,1)S(1)}, bf16[2,520,256]{2,1,0:T(8,128)(2,1)S(1)}, u32[]{:S(2)}, u32[]{:S(2)}) collective-permute-start(bf16[2,520,256]{2,1,0:T(8,128)(2,1)S(1)} %get-tuple-element.105), channel_id=1, source_target_pairs={{0,1},{1,0},{2,3},{3,2},{4,5},{5,4},{6,7},{7,6},{8,9},{9,8},{10,11... | collective-permute-start | bytes 1597448 | tf_op jit(solution)/shard_map/ppermute | solution.py:26
  96.2 21.6 %collective-permute-start.23 = (bf16[2,520,256]{2,1,0:T(8,128)(2,1)S(1)}, bf16[2,520,256]{2,1,0:T(8,128)(2,1)S(1)}, u32[]{:S(2)}, u32[]{:S(2)}) collective-permute-start(bf16[2,520,256]{2,1,0:T(8,128)(2,1)S(1)} %get-tuple-element.106), channel_id=1, source_target_pairs={{0,2},{1,3},{2,0},{3,1},{4,6},{5,7},{6,4},{7,5},{8,10},{9,11},{10,... | collective-permute-start | bytes 1597448 | tf_op jit(solution)/shard_map/ppermute | solution.py:26
  100.2 20.3 %collective-permute-start.24 = (bf16[2,520,256]{2,1,0:T(8,128)(2,1)S(1)}, bf16[2,520,256]{2,1,0:T(8,128)(2,1)S(1)}, u32[]{:S(2)}, u32[]{:S(2)}) collective-permute-start(bf16[2,520,256]{2,1,0:T(8,128)(2,1)S(1)} %get-tuple-element.107), channel_id=1, source_target_pairs={{0,3},{1,2},{2,1},{3,0},{4,7},{5,6},{6,5},{7,4},{8,11},{9,10},{10,... | collective-permute-start | bytes 1597448 | tf_op jit(solution)/shard_map/ppermute | solution.py:26

commit v7 on v6

--- a/solution.py
+++ b/solution.py
@@ -100,13 +100,13 @@
     )(where, partners, *arrays)
 
 
-def corr_kernel(factor, *refs):
-    row_refs, col_refs, table_ref = refs[:4], refs[4:8], refs[8]
-    out_refs, rows, cross = refs[9:13], refs[13], refs[14]
+def corr_kernel(factor, place_ref, row_ref, *refs):
+    col_refs, table_ref = refs[:4], refs[4]
+    out_refs, rows, cross = refs[5:9], refs[9], refs[10]
     lane = lax.broadcasted_iota(jnp.int32, (CH * LANE, LANE), 1)
     imag = lane // 16 % 2 == 1
     for d in range(4):
-        own = row_refs[d][...].astype(jnp.float32).reshape(CH * LANE, LANE)
+        own = row_ref[place_ref[0] ^ d].astype(jnp.float32).reshape(CH * LANE, LANE)
         rows[pl.ds(d * 1024, 1024), :] = own
         rows[pl.ds(4096 + d * 1024, 1024), :] = jnp.where(
             imag, -pltpu.roll(own, 16, 1), pltpu.roll(own, LANE - 16, 1)
@@ -157,25 +157,27 @@
             out_refs[d][quad] = (lags * factor).astype(jnp.bfloat16)
 
 
-def correlate(row_blocks, col_blocks, table, factor):
+def correlate(place, row_blocks, col_blocks, table, factor):
     def body(*refs):
         corr_kernel(factor, *refs)
 
+    whole = pl.BlockSpec(memory_space=pltpu.VMEM)
     return pl.pallas_call(
         body,
+        in_specs=[pl.BlockSpec(memory_space=pltpu.SMEM)] + [whole] * 6,
         out_shape=[jax.ShapeDtypeStruct((2, LAG_ROWS, 256), jnp.bfloat16)] * 4,
         scratch_shapes=[
             pltpu.VMEM((8 * 1024, LANE), jnp.float32),
             pltpu.VMEM((16, 1024, LANE), jnp.float32),
         ],
-        compiler_params=vmem(24),
+        compiler_params=vmem(20),
         cost_estimate=pl.CostEstimate(
             flops=2 * LANE * LANE * 256 * LANE + 16 * LAG_ROWS * 1024 * 256,
             transcendentals=0,
             bytes_accessed=7 * 1024 * 1024,
         ),
         name="correlate",
-    )(*row_blocks, *col_blocks, table)
+    )(place, row_blocks, *col_blocks, table)
 
 
 def finish_kernel(member_ref, *refs):
@@ -247,19 +249,20 @@
     white = whiten(spectra)
 
     row_masks, col_masks = (4, 1), (1, 4)
-    rows = [[white, None, None, None], [white, None, None, None]]
-
-    for d in (1, 2, 3):
-        rows[0][d] = xor_perm(white, "mem", d * row_masks[0])
+    members = range(lax.axis_size("mem"))
+    lines = [
+        [[m ^ (d * mask) for d in range(4)] for m in members if m & (3 * mask) == 0] for mask in row_masks
+    ]
+    rows = [
+        lax.all_gather(white, "mem", axis_index_groups=groups).reshape(4, LANE, CH, LANE)
+        for groups in lines
+    ]
+    places = [(member // mask % 4).reshape(1) for mask in row_masks]
     up, down = ring_perm(white, 1), ring_perm(white, -1)
-    rows, source, up, down = lax.optimization_barrier((rows, white, up, down))
-    member_now, *halves = lax.optimization_barrier((member, up[: LANE // 2], down[LANE // 2 :]))
+    member_now, up, down = lax.optimization_barrier((member, up, down))
+    tops = [ring_perm(up[: LANE // 2], 1), ring_perm(down[LANE // 2 :], -1)]
     where = jnp.stack([member_now, plane])
-    source, where = lax.optimization_barrier((source, where))
-    for d in (1, 2, 3):
-        rows[1][d] = xor_perm(source, "mem", d * row_masks[1])
-    tops = [ring_perm(halves[0], 1), ring_perm(halves[1], -1)]
-    rows, where, up, down, tops = lax.optimization_barrier((rows, where, up, down, tops))
+    where, up, down, tops = lax.optimization_barrier((where, up, down, tops))
 
     mine = choose(pick_kernel, "pick", where, partners, [white, down, up, *tops])
     other = xor_perm(mine, "grp", 1)
@@ -281,7 +284,7 @@
     cols = [[near, near1, near2, near3], [across, far1, far2, far3]]
     parts = []
     for n in range(2):
-        sums = correlate(rows[n], cols[n], table, factor)
+        sums = correlate(places[n], rows[n], cols[n], table, factor)
         parts += [sums[0]] + [xor_perm(sums[d], "mem", d * row_masks[n]) for d in range(1, 4)]
         cols[1], sums = lax.optimization_barrier((cols[1], sums[0]))
     packed = finish(member.reshape(1), parts, order)

time: 127 us -> 154 us (1.21)
  between operations: 0.35 us -> 13.7 us
  waiting for transfers between devices: 57.7 us -> 67.9 us
  starting transfers between devices: 41.5 us -> 33 us
  local copies, waits for them, and re-layouts: 1.65 us -> 7.53 us
  Pallas kernels: 20.4 us -> 25.6 us
    ppermute x21 -> x15, starting transfers between devices: 31 us -> 22.2 us  [xor_perm(): lax.ppermute(array, axis, [(i, i ^ mask) for i in range(lax.axis_size(axi...]
    ppermute x21 -> x15, waiting for transfers between devices: 42 us -> 48.8 us  [xor_perm(): lax.ppermute(array, axis, [(i, i ^ mask) for i in range(lax.axis_size(axi...]
    unnamed x6 -> x18, local copies, waits for them, and re-layouts: 1.63 us -> 7.51 us
    ppermute x4, waiting for transfers between devices: 15.7 us -> 19.1 us  [ring_perm(): lax.ppermute(array, 'grp', [(i, (i + 2 * shift) % size) for i in range(si...]
    pallas_call x2, Pallas kernels: 13.4 us -> 16.2 us  [correlate(): pl.pallas_call(body, in_specs=[pl.BlockSpec(memory_space=pltpu.SMEM)] + [...]
  transfers between devices with their start and end apart: 25 -> 21, of which waited for: 16 -> 15; matrix products, arithmetic and copies ran while one was open for 3% -> 3% of each run, Pallas kernels for 11% -> 12%
where the time goes in v7:
time: 154 us; the launch traced here: 152 us
  waiting for transfers between devices  67.9 us (44%)
  starting transfers between devices  33 us (21%)
  Pallas kernels  25.6 us (17%)
  between operations  13.7 us (9%)
  local copies, waits for them, and re-layouts  7.53 us (5%)
  other arithmetic  3.8 us (2%)
    ppermute x15, waiting for transfers between devices, xor_perm(): lax.ppermute(array, axis, [(i, i ^ mask) for i in range(lax.axis_size(axi...  48.8 us
    ppermute x15, starting transfers between devices, xor_perm(): lax.ppermute(array, axis, [(i, i ^ mask) for i in range(lax.axis_size(axi...  22.2 us
    ppermute x4, waiting for transfers between devices, ring_perm(): lax.ppermute(array, 'grp', [(i, (i + 2 * shift) % size) for i in range(si...  19.1 us
    pallas_call x2, Pallas kernels, correlate(): pl.pallas_call(body, in_specs=[pl.BlockSpec(memory_space=pltpu.SMEM)] + [...  16.2 us
    ppermute x4, starting transfers between devices, ring_perm(): lax.ppermute(array, 'grp', [(i, (i + 2 * shift) % size) for i in range(si...  10.8 us
    unnamed x18, local copies, waits for them, and re-layouts  7.51 us
    pallas_call x1, Pallas kernels, finish(): pl.pallas_call(finish_kernel, grid=(4,), in_specs=[pl.BlockSpec(memory_sp...  6.16 us
    convert_element_type x1, other arithmetic, lag_table(): return jnp.where(lag < LAGS, values, 0.0).astype(jnp.bfloat16)  3.36 us
  transfers between devices with their start and end apart: 21, of which 15 were waited for; matrix products, arithmetic and copies ran while one was open for 3% of the time, Pallas kernels for 12%

profile of v7, /device:TPU:8, one launch (start us, length us, event | category | flops | bytes accessed | tf_op | source)
XLA Modules:
  0.0 151.6 jit_solution(8347325319767509498)
XLA Ops:
  6.5 0.0 all-gather.5.cloned.1.call-start
  6.5 0.0 copy-start
  6.5 0.9 copy-done
  7.5 0.0 copy-start.2
  7.5 1.5 %whiten.1.refs_0_ = bf16[128,8,128]{2,1,0:T(8,128)(2,1)} custom-call(bf16[8,2,16,512]{3,2,1,0:T(8,128)(2,1)S(1)} %copy-done), custom_call_target="tpu_custom_call" | custom-call | tf_op jit(solution)/shard_map/whiten/pallas_call | solution.py:54
  9.0 0.0 all-gather.5.cloned.1.call-update
  9.0 0.0 all-gather.7.cloned.1.call-start
  9.1 3.3 %collective-permute-start = (bf16[128,8,128]{2,1,0:T(8,128)(2,1)}, bf16[128,8,128]{2,1,0:T(8,128)(2,1)S(1)}, u32[]{:S(2)}, u32[]{:S(2)}) collective-permute-start(bf16[128,8,128]{2,1,0:T(8,128)(2,1)} %whiten.1.refs_0_), channel_id=1, source_target_pairs={{0,64},{32,96},{64,128},{96,160},{128,192},{160,224},{192,0},{224,... | collective-permute-start | bytes 786440 | tf_op jit(solution)/shard_map/ppermute | solution.py:31
  12.4 3.1 %collective-permute-start.1 = (bf16[128,8,128]{2,1,0:T(8,128)(2,1)}, bf16[128,8,128]{2,1,0:T(8,128)(2,1)S(1)}, u32[]{:S(2)}, u32[]{:S(2)}) collective-permute-start(bf16[128,8,128]{2,1,0:T(8,128)(2,1)} %whiten.1.refs_0_), channel_id=1, source_target_pairs={{0,192},{32,224},{64,0},{96,32},{128,64},{160,96},{192,128},{224,1... | collective-permute-start | bytes 786440 | tf_op jit(solution)/shard_map/ppermute | solution.py:31
  15.6 8.4 %collective-permute-done.refs_2_ = bf16[128,8,128]{2,1,0:T(8,128)(2,1)S(1)} collective-permute-done((bf16[128,8,128]{2,1,0:T(8,128)(2,1)}, bf16[128,8,128]{2,1,0:T(8,128)(2,1)S(1)}, u32[]{:S(2)}, u32[]{:S(2)}) %collective-permute-start) | collective-permute-done | bytes 262176 | tf_op jit(solution)/shard_map/ppermute | solution.py:31
  24.0 4.8 %collective-permute-done.1.refs_1_ = bf16[128,8,128]{2,1,0:T(8,128)(2,1)S(1)} collective-permute-done((bf16[128,8,128]{2,1,0:T(8,128)(2,1)}, bf16[128,8,128]{2,1,0:T(8,128)(2,1)S(1)}, u32[]{:S(2)}, u32[]{:S(2)}) %collective-permute-start.1) | collective-permute-done | bytes 262176 | tf_op jit(solution)/shard_map/ppermute | solution.py:31
  28.8 3.8 %collective-permute-start.2 = (bf16[64,8,128]{2,1,0:T(8,128)(2,1)S(1)}, bf16[64,8,128]{2,1,0:T(8,128)(2,1)S(1)}, u32[]{:S(2)}, u32[]{:S(2)}) collective-permute-start(bf16[64,8,128]{2,1,0:T(8,128)(2,1)S(1)} %slice.10), channel_id=1, source_target_pairs={{0,64},{32,96},{64,128},{96,160},{128,192},{160,224},{192,0},{224,... | collective-permute-start | bytes 393224 | tf_op jit(solution)/shard_map/ppermute | solution.py:31
  32.6 0.5 collective-permute-start.3
  33.1 0.0 all-gather.7.cloned.1.call-update
  33.2 0.1 pad_add_fusion.where_ref
  33.2 4.4 %collective-permute-done.2.refs_3_ = bf16[64,8,128]{2,1,0:T(8,128)(2,1)S(1)} collective-permute-done((bf16[64,8,128]{2,1,0:T(8,128)(2,1)S(1)}, bf16[64,8,128]{2,1,0:T(8,128)(2,1)S(1)}, u32[]{:S(2)}, u32[]{:S(2)}) %collective-permute-start.2) | collective-permute-done | bytes 131104 | tf_op jit(solution)/shard_map/ppermute | solution.py:31
  37.6 1.5 collective-permute-done.3.refs_4_
  39.1 0.7 copy-done.1
  39.8 1.0 pick.1.mine_ref
  40.8 0.1 collective-permute-start.4
  40.9 0.1 iota_add_fusion.1
  41.0 1.8 %collective-permute-done.4.other_ref = bf16[2,128,8,128]{3,2,1,0:T(8,128)(2,1)S(1)} collective-permute-done((bf16[2,128,8,128]{3,2,1,0:T(8,128)(2,1)S(1)}, bf16[2,128,8,128]{3,2,1,0:T(8,128)(2,1)S(1)}, u32[]{:S(2)}, u32[]{:S(2)}) %collective-permute-start.4) | collective-permute-done | bytes 524320 | tf_op jit(solution)/shard_map/ppermute | solution.py:26
  42.8 0.0 copy-done.2
  42.8 0.6 merge.1.refs_2_
  43.7 3.1 %collective-permute-start.5 = (bf16[2,128,8,128]{3,2,1,0:T(8,128)(2,1)S(1)}, bf16[2,128,8,128]{3,2,1,0:T(8,128)(2,1)}, u32[]{:S(2)}, u32[]{:S(2)}) collective-permute-start(bf16[2,128,8,128]{3,2,1,0:T(8,128)(2,1)S(1)} %merge.1.refs_2_), channel_id=1, source_target_pairs={{0,8},{1,9},{2,10},{3,11},{4,12},{5,13},{6,14},{7,15},{8,0},{9,1},... | collective-permute-start | bytes 1572872 | tf_op jit(solution)/shard_map/ppermute | solution.py:26
  46.8 2.1 %collective-permute-start.6 = (bf16[2,128,8,128]{3,2,1,0:T(8,128)(2,1)S(1)}, bf16[2,128,8,128]{3,2,1,0:T(8,128)(2,1)}, u32[]{:S(2)}, u32[]{:S(2)}) collective-permute-start(bf16[2,128,8,128]{3,2,1,0:T(8,128)(2,1)S(1)} %merge.1.refs_2_), channel_id=1, source_target_pairs={{0,16},{1,17},{2,18},{3,19},{4,20},{5,21},{6,22},{7,23},{8,24},{9,... | collective-permute-start | bytes 1572872 | tf_op jit(solution)/shard_map/ppermute | solution.py:26
  48.9 0.2 compare_convert_fusion.refs_8_
  49.1 0.5 collective-permute-start.7
  49.7 2.6 %collective-permute-start.8 = (bf16[2,128,8,128]{3,2,1,0:T(8,128)(2,1)S(1)}, bf16[2,128,8,128]{3,2,1,0:T(8,128)(2,1)}, u32[]{:S(2)}, u32[]{:S(2)}) collective-permute-start(bf16[2,128,8,128]{3,2,1,0:T(8,128)(2,1)S(1)} %merge.1.refs_2_), channel_id=1, source_target_pairs={{0,2},{1,3},{2,0},{3,1},{4,6},{5,7},{6,4},{7,5},{8,10},{9,11},{10,... | collective-permute-start | bytes 1572872 | tf_op jit(solution)/shard_map/ppermute | solution.py:26
  52.3 0.4 collective-permute-start.9
  52.7 3.4 %fusion.1.refs_6_ = bf16[520,1024]{1,0:T(8,128)(2,1)S(1)} fusion(s32[1024]{0:T(1024)S(1)} %get-tuple-element.74, s32[520]{0:T(1024)S(1)} %fusion.22, s32[1024]{0:T(1024)S(1)} %get-tuple-element.73, pred[520]{0:T(1024)(128)(4,1)S(1)} %fusion.23), kind=kLoop, calls=%fused_computation.2 | loop fusion | flops 22896640 | bytes 1075752 | tf_op jit(solution)/shard_map/convert_element_type | solution.py:230
  56.1 3.2 %collective-permute-done.5 = bf16[2,128,8,128]{3,2,1,0:T(8,128)(2,1)} collective-permute-done((bf16[2,128,8,128]{3,2,1,0:T(8,128)(2,1)S(1)}, bf16[2,128,8,128]{3,2,1,0:T(8,128)(2,1)}, u32[]{:S(2)}, u32[]{:S(2)}) %collective-permute-start.5) | collective-permute-done | bytes 524320 | tf_op jit(solution)/shard_map/ppermute | solution.py:26
  59.3 1.6 %collective-permute-done.6.refs_2_ = bf16[2,128,8,128]{3,2,1,0:T(8,128)(2,1)} collective-permute-done((bf16[2,128,8,128]{3,2,1,0:T(8,128)(2,1)S(1)}, bf16[2,128,8,128]{3,2,1,0:T(8,128)(2,1)}, u32[]{:S(2)}, u32[]{:S(2)}) %collective-permute-start.6) | collective-permute-done | bytes 524320 | tf_op jit(solution)/shard_map/ppermute | solution.py:26
  60.9 1.7 %collective-permute-start.10 = (bf16[2,128,8,128]{3,2,1,0:T(8,128)(2,1)}, bf16[2,128,8,128]{3,2,1,0:T(8,128)(2,1)S(1)}, u32[]{:S(2)}, u32[]{:S(2)}) collective-permute-start(bf16[2,128,8,128]{3,2,1,0:T(8,128)(2,1)} %collective-permute-done.5), channel_id=1, source_target_pairs={{0,16},{1,17},{2,18},{3,19},{4,20},{5,21},{6,22},{7,23},{8,24},{9,... | collective-permute-start | bytes 1572872 | tf_op jit(solution)/shard_map/ppermute | solution.py:26
  62.7 1.5 %collective-permute-start.11 = (bf16[2,128,8,128]{3,2,1,0:T(8,128)(2,1)}, bf16[2,128,8,128]{3,2,1,0:T(8,128)(2,1)}, u32[]{:S(2)}, u32[]{:S(2)}) collective-permute-start(bf16[2,128,8,128]{3,2,1,0:T(8,128)(2,1)} %collective-permute-done.6.refs_2_), channel_id=1, source_target_pairs={{0,12},{1,13},{2,14},{3,15},{4,8},{5,9},{6,10},{7,11},{8,4},{9,5},... | collective-permute-start | bytes 1572872 | tf_op jit(solution)/shard_map/ppermute | solution.py:26
  64.2 8.4 %collective-permute-done.7.refs_3_ = bf16[2,128,8,128]{3,2,1,0:T(8,128)(2,1)} collective-permute-done((bf16[2,128,8,128]{3,2,1,0:T(8,128)(2,1)S(1)}, bf16[2,128,8,128]{3,2,1,0:T(8,128)(2,1)}, u32[]{:S(2)}, u32[]{:S(2)}) %collective-permute-start.7) | collective-permute-done | bytes 524320 | tf_op jit(solution)/shard_map/ppermute | solution.py:26
  72.6 10.9 %collective-permute-done.8.refs_4_ = bf16[2,128,8,128]{3,2,1,0:T(8,128)(2,1)} collective-permute-done((bf16[2,128,8,128]{3,2,1,0:T(8,128)(2,1)S(1)}, bf16[2,128,8,128]{3,2,1,0:T(8,128)(2,1)}, u32[]{:S(2)}, u32[]{:S(2)}) %collective-permute-start.8) | collective-permute-done | bytes 524320 | tf_op jit(solution)/shard_map/ppermute | solution.py:26
  83.5 1.4 collective-permute-done.9.refs_5_
  84.9 0.0 collective-permute-done.10.refs_4_
  84.9 0.8 copy-done.7
  85.7 0.0 collective-permute-done.11.refs_5_
  85.7 0.6 collective-permute-start.15
  86.3 1.2 copy-done.4
  87.5 8.1 %correlate.2 = (bf16[2,520,256]{2,1,0:T(8,128)(2,1)S(1)}, bf16[2,520,256]{2,1,0:T(8,128)(2,1)}, bf16[2,520,256]{2,1,0:T(8,128)(2,1)S(1)}, bf16[2,520,256]{2,1,0:T(8,128)(2,1)S(1)}) custom-call(s32[1]{0:T(128)} %bitcast.1.refs_0_, bf16[4,128,8,128]{3,2,1,0:T(8,128)(2,1)S(1)} %bitcast.20, bf16[2,128,8,128]{3,2,1,0:T(8,128)(2,1)S(1)} %merge.1.refs_2_, ...), custom_call_target="tpu_custom_call" | custom-call | flops 3254779904 | bytes 7340032 | tf_op jit(solution)/shard_map/correlate/pallas_call | solution.py:165
  95.6 0.0 copy-start.5
  95.6 0.8 copy-done.5
  96.4 0.8 copy-done.6
  97.2 1.4 collective-permute-start.12
  98.7 0.6 collective-permute-start.13
  99.3 2.7 %collective-permute-start.14 = (bf16[2,520,256]{2,1,0:T(8,128)(2,1)}, bf16[2,520,256]{2,1,0:T(8,128)(2,1)}, u32[]{:S(2)}, u32[]{:S(2)}) collective-permute-start(bf16[2,520,256]{2,1,0:T(8,128)(2,1)} %copy-done.5), channel_id=1, source_target_pairs={{0,12},{1,13},{2,14},{3,15},{4,8},{5,9},{6,10},{7,11},{8,4},{9,5},... | collective-permute-start | bytes 1597448 | tf_op jit(solution)/shard_map/ppermute | solution.py:26
  101.9 0.0 collective-permute-done.15.refs_3_
  101.9 1.2 copy-done.3
  103.2 1.0 copy-done.8
  104.2 8.1 %correlate.3 = (bf16[2,520,256]{2,1,0:T(8,128)(2,1)S(1)}, bf16[2,520,256]{2,1,0:T(8,128)(2,1)S(1)}, bf16[2,520,256]{2,1,0:T(8,128)(2,1)S(1)}, bf16[2,520,256]{2,1,0:T(8,128)(2,1)S(1)}) custom-call(s32[1]{0:T(128)} %bitcast.6.refs_0_, bf16[4,128,8,128]{3,2,1,0:T(8,128)(2,1)S(1)} %bitcast.19, bf16[2,128,8,128]{3,2,1,0:T(8,128)(2,1)} %collective-permute-done.6.refs_2_, ...), custom_call_target="tpu_custom_call" | custom-call | flops 3254779904 | bytes 7340032 | tf_op jit(solution)/shard_map/correlate/pallas_call | solution.py:165
  112.3 3.2 %collective-permute-start.16 = (bf16[2,520,256]{2,1,0:T(8,128)(2,1)S(1)}, bf16[2,520,256]{2,1,0:T(8,128)(2,1)S(1)}, u32[]{:S(2)}, u32[]{:S(2)}) collective-permute-start(bf16[2,520,256]{2,1,0:T(8,128)(2,1)S(1)} %get-tuple-element.69), channel_id=1, source_target_pairs={{0,1},{1,0},{2,3},{3,2},{4,5},{5,4},{6,7},{7,6},{8,9},{9,8},{10,11... | collective-permute-start | bytes 1597448 | tf_op jit(solution)/shard_map/ppermute | solution.py:26
  115.5 0.0 collective-permute-start.17
  115.5 0.0 collective-permute-done.12.refs_1_
  115.5 1.6 %collective-permute-start.18 = (bf16[2,520,256]{2,1,0:T(8,128)(2,1)S(1)}, bf16[2,520,256]{2,1,0:T(8,128)(2,1)S(1)}, u32[]{:S(2)}, u32[]{:S(2)}) collective-permute-start(bf16[2,520,256]{2,1,0:T(8,128)(2,1)S(1)} %get-tuple-element.71), channel_id=1, source_target_pairs={{0,3},{1,2},{2,1},{3,0},{4,7},{5,6},{6,5},{7,4},{8,11},{9,10},{10,... | collective-permute-start | bytes 1597448 | tf_op jit(solution)/shard_map/ppermute | solution.py:26
  117.1 3.4 %collective-permute-done.13.refs_2_ = bf16[2,520,256]{2,1,0:T(8,128)(2,1)} collective-permute-done((bf16[2,520,256]{2,1,0:T(8,128)(2,1)}, bf16[2,520,256]{2,1,0:T(8,128)(2,1)}, u32[]{:S(2)}, u32[]{:S(2)}) %collective-permute-start.13) | collective-permute-done | bytes 532512 | tf_op jit(solution)/shard_map/ppermute | solution.py:26
  120.5 2.3 %collective-permute-done.14.refs_3_ = bf16[2,520,256]{2,1,0:T(8,128)(2,1)} collective-permute-done((bf16[2,520,256]{2,1,0:T(8,128)(2,1)}, bf16[2,520,256]{2,1,0:T(8,128)(2,1)}, u32[]{:S(2)}, u32[]{:S(2)}) %collective-permute-start.14) | collective-permute-done | bytes 532512 | tf_op jit(solution)/shard_map/ppermute | solution.py:26
  122.9 5.7 %collective-permute-done.16.refs_5_ = bf16[2,520,256]{2,1,0:T(8,128)(2,1)S(1)} collective-permute-done((bf16[2,520,256]{2,1,0:T(8,128)(2,1)S(1)}, bf16[2,520,256]{2,1,0:T(8,128)(2,1)S(1)}, u32[]{:S(2)}, u32[]{:S(2)}) %collective-permute-start.16) | collective-permute-done | bytes 532512 | tf_op jit(solution)/shard_map/ppermute | solution.py:26
  128.5 7.9 %collective-permute-done.17.refs_6_ = bf16[2,520,256]{2,1,0:T(8,128)(2,1)S(1)} collective-permute-done((bf16[2,520,256]{2,1,0:T(8,128)(2,1)S(1)}, bf16[2,520,256]{2,1,0:T(8,128)(2,1)S(1)}, u32[]{:S(2)}, u32[]{:S(2)}) %collective-permute-start.17) | collective-permute-done | bytes 532512 | tf_op jit(solution)/shard_map/ppermute | solution.py:26
  136.4 2.2 %collective-permute-done.18.refs_7_ = bf16[2,520,256]{2,1,0:T(8,128)(2,1)S(1)} collective-permute-done((bf16[2,520,256]{2,1,0:T(8,128)(2,1)S(1)}, bf16[2,520,256]{2,1,0:T(8,128)(2,1)S(1)}, u32[]{:S(2)}, u32[]{:S(2)}) %collective-permute-start.18) | collective-permute-done | bytes 532512 | tf_op jit(solution)/shard_map/ppermute | solution.py:26
  138.6 6.2 %finish.1 = bf16[4,4104,128]{2,1,0:T(8,128)(2,1)} custom-call(s32[1]{0:T(128)} %bitcast.member_ref, bf16[2,520,256]{2,1,0:T(8,128)(2,1)S(1)} %get-tuple-element.57.refs_0_, bf16[2,520,256]{2,1,0:T(8,128)(2,1)S(1)} %collective-permute-done.12.refs_1_, bf16[2,520,256]{2,1,0:T(8,128)(2,1)} %collective-permute-done.13.refs_2_, ...), custom_call_target="tpu_custom_call" | custom-call | tf_op jit(solution)/shard_map/finish/pallas_call | solution.py:204
  (17 shorter events, 0.1 us)
Async XLA Ops:
  6.5 79.7 %all-gather.5.cloned.1.call-start = ((), (), s32[]{:S(2)}) async-start(), calls=%async_computation | async-start | bytes 1310720 | tf_op jit(solution)/shard_map/all_gather | solution.py:257
  6.5 0.9 copy-start
  7.5 35.3 %copy-start.2 = (s32[2,32]{1,0:T(2,128)S(1)}, s32[2,32]{1,0:T(2,128)}, u32[]{:S(2)}) copy-start(s32[2,32]{1,0:T(2,128)} %partners_ref.3) | copy-start | bytes 772
  9.0 92.9 %all-gather.7.cloned.1.call-start = ((), (), s32[]{:S(2)}) async-start(), calls=%async_computation.1 | async-start | bytes 1310720 | tf_op jit(solution)/shard_map/all_gather | solution.py:257
  9.1 14.9 %collective-permute-start = (bf16[128,8,128]{2,1,0:T(8,128)(2,1)}, bf16[128,8,128]{2,1,0:T(8,128)(2,1)S(1)}, u32[]{:S(2)}, u32[]{:S(2)}) collective-permute-start(bf16[128,8,128]{2,1,0:T(8,128)(2,1)} %whiten.1.refs_0_), channel_id=1, source_target_pairs={{0,64},{32,96},{64,128},{96,160},{128,192},{160,224},{192,0},{224,... | collective-permute-start | bytes 786440 | tf_op jit(solution)/shard_map/ppermute | solution.py:31
  12.4 16.4 %collective-permute-start.1 = (bf16[128,8,128]{2,1,0:T(8,128)(2,1)}, bf16[128,8,128]{2,1,0:T(8,128)(2,1)S(1)}, u32[]{:S(2)}, u32[]{:S(2)}) collective-permute-start(bf16[128,8,128]{2,1,0:T(8,128)(2,1)} %whiten.1.refs_0_), channel_id=1, source_target_pairs={{0,192},{32,224},{64,0},{96,32},{128,64},{160,96},{192,128},{224,1... | collective-permute-start | bytes 786440 | tf_op jit(solution)/shard_map/ppermute | solution.py:31
  28.8 8.8 %collective-permute-start.2 = (bf16[64,8,128]{2,1,0:T(8,128)(2,1)S(1)}, bf16[64,8,128]{2,1,0:T(8,128)(2,1)S(1)}, u32[]{:S(2)}, u32[]{:S(2)}) collective-permute-start(bf16[64,8,128]{2,1,0:T(8,128)(2,1)S(1)} %slice.10), channel_id=1, source_target_pairs={{0,64},{32,96},{64,128},{96,160},{128,192},{160,224},{192,0},{224,... | collective-permute-start | bytes 393224 | tf_op jit(solution)/shard_map/ppermute | solution.py:31
  32.6 6.4 %collective-permute-start.3 = (bf16[64,8,128]{2,1,0:T(8,128)(2,1)S(1)}, bf16[64,8,128]{2,1,0:T(8,128)(2,1)S(1)}, u32[]{:S(2)}, u32[]{:S(2)}) collective-permute-start(bf16[64,8,128]{2,1,0:T(8,128)(2,1)S(1)} %slice.11), channel_id=1, source_target_pairs={{0,192},{32,224},{64,0},{96,32},{128,64},{160,96},{192,128},{224,1... | collective-permute-start | bytes 393224 | tf_op jit(solution)/shard_map/ppermute | solution.py:31
  39.1 0.7 copy-start.1
  40.8 2.0 %collective-permute-start.4 = (bf16[2,128,8,128]{3,2,1,0:T(8,128)(2,1)S(1)}, bf16[2,128,8,128]{3,2,1,0:T(8,128)(2,1)S(1)}, u32[]{:S(2)}, u32[]{:S(2)}) collective-permute-start(bf16[2,128,8,128]{3,2,1,0:T(8,128)(2,1)S(1)} %pick.1.mine_ref), channel_id=1, source_target_pairs={{0,32},{32,0},{64,96},{96,64},{128,160},{160,128},{192,224},{224,1... | collective-permute-start | bytes 1572872 | tf_op jit(solution)/shard_map/ppermute | solution.py:26
  43.7 15.7 %collective-permute-start.5 = (bf16[2,128,8,128]{3,2,1,0:T(8,128)(2,1)S(1)}, bf16[2,128,8,128]{3,2,1,0:T(8,128)(2,1)}, u32[]{:S(2)}, u32[]{:S(2)}) collective-permute-start(bf16[2,128,8,128]{3,2,1,0:T(8,128)(2,1)S(1)} %merge.1.refs_2_), channel_id=1, source_target_pairs={{0,8},{1,9},{2,10},{3,11},{4,12},{5,13},{6,14},{7,15},{8,0},{9,1},... | collective-permute-start | bytes 1572872 | tf_op jit(solution)/shard_map/ppermute | solution.py:26
  46.8 14.1 %collective-permute-start.6 = (bf16[2,128,8,128]{3,2,1,0:T(8,128)(2,1)S(1)}, bf16[2,128,8,128]{3,2,1,0:T(8,128)(2,1)}, u32[]{:S(2)}, u32[]{:S(2)}) collective-permute-start(bf16[2,128,8,128]{3,2,1,0:T(8,128)(2,1)S(1)} %merge.1.refs_2_), channel_id=1, source_target_pairs={{0,16},{1,17},{2,18},{3,19},{4,20},{5,21},{6,22},{7,23},{8,24},{9,... | collective-permute-start | bytes 1572872 | tf_op jit(solution)/shard_map/ppermute | solution.py:26
  49.1 23.5 %collective-permute-start.7 = (bf16[2,128,8,128]{3,2,1,0:T(8,128)(2,1)S(1)}, bf16[2,128,8,128]{3,2,1,0:T(8,128)(2,1)}, u32[]{:S(2)}, u32[]{:S(2)}) collective-permute-start(bf16[2,128,8,128]{3,2,1,0:T(8,128)(2,1)S(1)} %merge.1.refs_2_), channel_id=1, source_target_pairs={{0,1},{1,0},{2,3},{3,2},{4,5},{5,4},{6,7},{7,6},{8,9},{9,8},{10,11... | collective-permute-start | bytes 1572872 | tf_op jit(solution)/shard_map/ppermute | solution.py:26
  49.7 33.8 %collective-permute-start.8 = (bf16[2,128,8,128]{3,2,1,0:T(8,128)(2,1)S(1)}, bf16[2,128,8,128]{3,2,1,0:T(8,128)(2,1)}, u32[]{:S(2)}, u32[]{:S(2)}) collective-permute-start(bf16[2,128,8,128]{3,2,1,0:T(8,128)(2,1)S(1)} %merge.1.refs_2_), channel_id=1, source_target_pairs={{0,2},{1,3},{2,0},{3,1},{4,6},{5,7},{6,4},{7,5},{8,10},{9,11},{10,... | collective-permute-start | bytes 1572872 | tf_op jit(solution)/shard_map/ppermute | solution.py:26
  52.3 32.6 %collective-permute-start.9 = (bf16[2,128,8,128]{3,2,1,0:T(8,128)(2,1)S(1)}, bf16[2,128,8,128]{3,2,1,0:T(8,128)(2,1)}, u32[]{:S(2)}, u32[]{:S(2)}) collective-permute-start(bf16[2,128,8,128]{3,2,1,0:T(8,128)(2,1)S(1)} %merge.1.refs_2_), channel_id=1, source_target_pairs={{0,3},{1,2},{2,1},{3,0},{4,7},{5,6},{6,5},{7,4},{8,11},{9,10},{10,... | collective-permute-start | bytes 1572872 | tf_op jit(solution)/shard_map/ppermute | solution.py:26
  60.9 24.0 %collective-permute-start.10 = (bf16[2,128,8,128]{3,2,1,0:T(8,128)(2,1)}, bf16[2,128,8,128]{3,2,1,0:T(8,128)(2,1)S(1)}, u32[]{:S(2)}, u32[]{:S(2)}) collective-permute-start(bf16[2,128,8,128]{3,2,1,0:T(8,128)(2,1)} %collective-permute-done.5), channel_id=1, source_target_pairs={{0,16},{1,17},{2,18},{3,19},{4,20},{5,21},{6,22},{7,23},{8,24},{9,... | collective-permute-start | bytes 1572872 | tf_op jit(solution)/shard_map/ppermute | solution.py:26
  62.7 23.0 %collective-permute-start.11 = (bf16[2,128,8,128]{3,2,1,0:T(8,128)(2,1)}, bf16[2,128,8,128]{3,2,1,0:T(8,128)(2,1)}, u32[]{:S(2)}, u32[]{:S(2)}) collective-permute-start(bf16[2,128,8,128]{3,2,1,0:T(8,128)(2,1)} %collective-permute-done.6.refs_2_), channel_id=1, source_target_pairs={{0,12},{1,13},{2,14},{3,15},{4,8},{5,9},{6,10},{7,11},{8,4},{9,5},... | collective-permute-start | bytes 1572872 | tf_op jit(solution)/shard_map/ppermute | solution.py:26
  84.9 0.8 copy-start.7
  85.7 16.3 %collective-permute-start.15 = (bf16[2,128,8,128]{3,2,1,0:T(8,128)(2,1)}, bf16[2,128,8,128]{3,2,1,0:T(8,128)(2,1)}, u32[]{:S(2)}, u32[]{:S(2)}) collective-permute-start(bf16[2,128,8,128]{3,2,1,0:T(8,128)(2,1)} %collective-permute-done.6.refs_2_), channel_id=1, source_target_pairs={{0,4},{1,5},{2,6},{3,7},{4,0},{5,1},{6,2},{7,3},{8,12},{9,13},{10,... | collective-permute-start | bytes 1572872 | tf_op jit(solution)/shard_map/ppermute | solution.py:26
  86.3 1.2 copy-start.4
  95.6 0.8 copy-start.5
  96.4 0.8 copy-start.6
  97.2 18.3 %collective-permute-start.12 = (bf16[2,520,256]{2,1,0:T(8,128)(2,1)}, bf16[2,520,256]{2,1,0:T(8,128)(2,1)S(1)}, u32[]{:S(2)}, u32[]{:S(2)}) collective-permute-start(bf16[2,520,256]{2,1,0:T(8,128)(2,1)} %get-tuple-element.58), channel_id=1, source_target_pairs={{0,4},{1,5},{2,6},{3,7},{4,0},{5,1},{6,2},{7,3},{8,12},{9,13},{10,... | collective-permute-start | bytes 1597448 | tf_op jit(solution)/shard_map/ppermute | solution.py:26
  98.7 21.9 %collective-permute-start.13 = (bf16[2,520,256]{2,1,0:T(8,128)(2,1)}, bf16[2,520,256]{2,1,0:T(8,128)(2,1)}, u32[]{:S(2)}, u32[]{:S(2)}) collective-permute-start(bf16[2,520,256]{2,1,0:T(8,128)(2,1)} %copy-done.6), channel_id=1, source_target_pairs={{0,8},{1,9},{2,10},{3,11},{4,12},{5,13},{6,14},{7,15},{8,0},{9,1},... | collective-permute-start | bytes 1597448 | tf_op jit(solution)/shard_map/ppermute | solution.py:26
  99.3 23.6 %collective-permute-start.14 = (bf16[2,520,256]{2,1,0:T(8,128)(2,1)}, bf16[2,520,256]{2,1,0:T(8,128)(2,1)}, u32[]{:S(2)}, u32[]{:S(2)}) collective-permute-start(bf16[2,520,256]{2,1,0:T(8,128)(2,1)} %copy-done.5), channel_id=1, source_target_pairs={{0,12},{1,13},{2,14},{3,15},{4,8},{5,9},{6,10},{7,11},{8,4},{9,5},... | collective-permute-start | bytes 1597448 | tf_op jit(solution)/shard_map/ppermute | solution.py:26
  101.9 1.2 copy-start.3
  103.2 1.0 copy-start.8
  112.3 16.2 %collective-permute-start.16 = (bf16[2,520,256]{2,1,0:T(8,128)(2,1)S(1)}, bf16[2,520,256]{2,1,0:T(8,128)(2,1)S(1)}, u32[]{:S(2)}, u32[]{:S(2)}) collective-permute-start(bf16[2,520,256]{2,1,0:T(8,128)(2,1)S(1)} %get-tuple-element.69), channel_id=1, source_target_pairs={{0,1},{1,0},{2,3},{3,2},{4,5},{5,4},{6,7},{7,6},{8,9},{9,8},{10,11... | collective-permute-start | bytes 1597448 | tf_op jit(solution)/shard_map/ppermute | solution.py:26
  115.5 20.9 %collective-permute-start.17 = (bf16[2,520,256]{2,1,0:T(8,128)(2,1)S(1)}, bf16[2,520,256]{2,1,0:T(8,128)(2,1)S(1)}, u32[]{:S(2)}, u32[]{:S(2)}) collective-permute-start(bf16[2,520,256]{2,1,0:T(8,128)(2,1)S(1)} %get-tuple-element.70), channel_id=1, source_target_pairs={{0,2},{1,3},{2,0},{3,1},{4,6},{5,7},{6,4},{7,5},{8,10},{9,11},{10,... | collective-permute-start | bytes 1597448 | tf_op jit(solution)/shard_map/ppermute | solution.py:26
  115.5 23.0 %collective-permute-start.18 = (bf16[2,520,256]{2,1,0:T(8,128)(2,1)S(1)}, bf16[2,520,256]{2,1,0:T(8,128)(2,1)S(1)}, u32[]{:S(2)}, u32[]{:S(2)}) collective-permute-start(bf16[2,520,256]{2,1,0:T(8,128)(2,1)S(1)} %get-tuple-element.71), channel_id=1, source_target_pairs={{0,3},{1,2},{2,1},{3,0},{4,7},{5,6},{6,5},{7,4},{8,11},{9,10},{10,... | collective-permute-start | bytes 1597448 | tf_op jit(solution)/shard_map/ppermute | solution.py:26
Sparse Core Ops, SparseCore 0:
  9.2 29.3 all-gather.4
  40.4 33.5 all-gather.6

commit v8 on v6

--- a/solution.py
+++ b/solution.py
@@ -15,7 +15,7 @@
 TAPS = BINS // LANE
 LAGS = BINS + 1
 LAG_ROWS = 520
-UNROLL = 16
+UNROLL = 32
 
 
 def vmem(mib):
@@ -24,11 +24,6 @@
 
 def xor_perm(array, axis, mask):
     return lax.ppermute(array, axis, [(i, i ^ mask) for i in range(lax.axis_size(axis))])
-
-
-def ring_perm(array, shift):
-    size = lax.axis_size("grp")
-    return lax.ppermute(array, "grp", [(i, (i + 2 * shift) % size) for i in range(size)])
 
 
 def whiten_kernel(spectra_ref, out_ref, rows):
@@ -60,25 +55,19 @@
     )(spectra)
 
 
-def pick_kernel(where_ref, partners_ref, *refs):
-    blocks, tops, out_ref = refs[:3], refs[3:5], refs[5]
-    here = where_ref[1]
+def pick_kernel(offsets_ref, *refs):
+    planes, out_ref = refs[:4], refs[4]
     for r in range(2):
-        shift = ((here ^ (partners_ref[r, where_ref[0]] >> 1)) - here) & 3
-        for s in range(4):
-
-            @pl.when(shift == s)
+        for d in range(4):
+
+            @pl.when(offsets_ref[r] >> 1 == d)
             def _():
-                if s == 2:
-                    out_ref[r, : LANE // 2] = tops[0][...]
-                    out_ref[r, LANE // 2 :] = tops[1][...]
-                else:
-                    out_ref[r] = blocks[s - (s > 2)][...]
-
-
-def merge_kernel(where_ref, partners_ref, mine_ref, other_ref, out_ref):
+                out_ref[r] = planes[d][...]
+
+
+def merge_kernel(offsets_ref, mine_ref, other_ref, out_ref):
     for r in range(2):
-        swap = partners_ref[r, where_ref[0]] & 1
+        swap = offsets_ref[r] & 1
 
         @pl.when(swap == 1)
         def _():
@@ -89,15 +78,15 @@
             out_ref[r] = mine_ref[r]
 
 
-def choose(kernel, name, where, partners, arrays):
+def choose(kernel, name, offsets, arrays):
     smem, whole = pl.BlockSpec(memory_space=pltpu.SMEM), pl.BlockSpec(memory_space=pltpu.VMEM)
     return pl.pallas_call(
         kernel,
-        in_specs=[smem, smem] + [whole] * len(arrays),
+        in_specs=[smem] + [whole] * len(arrays),
         out_shape=jax.ShapeDtypeStruct((2, LANE, CH, LANE), jnp.bfloat16),
         compiler_params=vmem(10),
         name=name,
-    )(where, partners, *arrays)
+    )(offsets, *arrays)
 
 
 def corr_kernel(factor, *refs):
@@ -211,8 +200,8 @@
     )(member, *parts, order)
 
 
-def lag_table(zero):
-    lag = jnp.arange(LAG_ROWS, dtype=jnp.int32)[:, None] + zero
+def lag_table():
+    lag = jnp.arange(LAG_ROWS, dtype=jnp.int32)[:, None]
     k = jnp.arange(2 * BINS, dtype=jnp.int32)[None, :]
     frequency = k % TAPS * LANE + k // 8
     n = frequency * (lag - BINS // 2) + k // TAPS % 2 * (BINS // 2)
@@ -242,36 +231,34 @@
 
 def on_device(spectra, partners):
     member = lax.axis_index("mem").astype(jnp.int32)
-    plane = lax.axis_index("grp").astype(jnp.int32) >> 1
     factor = math.sqrt(2.0 / (BINS * (COMP // 2)))
     white = whiten(spectra)
 
     row_masks, col_masks = (4, 1), (1, 4)
     rows = [[white, None, None, None], [white, None, None, None]]
 
-    for d in (1, 2, 3):
-        rows[0][d] = xor_perm(white, "mem", d * row_masks[0])
-    up, down = ring_perm(white, 1), ring_perm(white, -1)
-    rows, source, up, down = lax.optimization_barrier((rows, white, up, down))
-    member_now, *halves = lax.optimization_barrier((member, up[: LANE // 2], down[LANE // 2 :]))
-    where = jnp.stack([member_now, plane])
-    source, where = lax.optimization_barrier((source, where))
-    for d in (1, 2, 3):
-        rows[1][d] = xor_perm(source, "mem", d * row_masks[1])
-    tops = [ring_perm(halves[0], 1), ring_perm(halves[1], -1)]
-    rows, where, up, down, tops = lax.optimization_barrier((rows, where, up, down, tops))
-
-    mine = choose(pick_kernel, "pick", where, partners, [white, down, up, *tops])
+    plane1, plane2, plane3 = [xor_perm(white, "grp", 2 * d) for d in (1, 2, 3)]
+    source = white
+    for d in (1, 3, 2):
+        sent = [xor_perm(source, "mem", d * mask) for mask in row_masks]
+        source, sent = lax.optimization_barrier((source, sent))
+        rows[0][d], rows[1][d] = sent
+    offsets = lax.dynamic_index_in_dim(partners, member, 1, keepdims=False)
+    table = lag_table()
+    table, rows, offsets, white, plane1, plane3, plane2 = lax.optimization_barrier(
+        (table, rows, offsets, white, plane1, plane3, plane2)
+    )
+
+    mine = choose(pick_kernel, "pick", offsets, [white, plane1, plane2, plane3])
     other = xor_perm(mine, "grp", 1)
-    near = choose(merge_kernel, "merge", where, partners, [mine, other])
-    near, where = lax.optimization_barrier((near, where))
+    near = choose(merge_kernel, "merge", offsets, [mine, other])
+    near, member_now = lax.optimization_barrier((near, member))
     across = xor_perm(near, "mem", 16)
     hop = xor_perm(near, "mem", 2 * col_masks[1])
-    order = column_order(where[0])
+    order = column_order(member_now)
     later, order = lax.optimization_barrier((near, order))
     near1, near2, near3 = [xor_perm(later, "mem", e * col_masks[0]) for e in (1, 2, 3)]
-    table = lag_table(where[0] - member)
-    table, order, hop, across = lax.optimization_barrier((table, order, hop, across))
+    order, hop, across = lax.optimization_barrier((order, hop, across))
     far2 = xor_perm(hop, "mem", 16)
     far3 = xor_perm(across, "mem", 3 * col_masks[1])
     across, near1, near2, near3, far2, far3 = lax.optimization_barrier(

time: 127 us -> 121 us (0.953)
  waiting for transfers between devices: 57.7 us -> 53.2 us
    ppermute x4 -> x0, waiting for transfers between devices: 15.7 us -> none  [ring_perm(): lax.ppermute(array, 'grp', [(i, (i + 2 * shift) % size) for i in range(si...]
    ppermute x21 -> x24, waiting for transfers between devices: 42 us -> 53.2 us  [xor_perm(): lax.ppermute(array, axis, [(i, i ^ mask) for i in range(lax.axis_size(axi...]
    ppermute x4 -> x0, starting transfers between devices: 10.5 us -> none  [ring_perm(): lax.ppermute(array, 'grp', [(i, (i + 2 * shift) % size) for i in range(si...]
    ppermute x21 -> x24, starting transfers between devices: 31 us -> 41 us  [xor_perm(): lax.ppermute(array, axis, [(i, i ^ mask) for i in range(lax.axis_size(axi...]
  transfers between devices with their start and end apart: 25 -> 24, of which waited for: 16 -> 18; matrix products, arithmetic and copies ran while one was open for 3% -> 3% of each run, Pallas kernels for 11% -> 11%
where the time goes in v8:
time: 121 us; the launch traced here: 120 us
  waiting for transfers between devices  53.2 us (44%)
  starting transfers between devices  41 us (34%)
  Pallas kernels  20.2 us (17%)
  other arithmetic  3.74 us (3%)
  local copies, waits for them, and re-layouts  2.11 us (2%)
    ppermute x24, waiting for transfers between devices, xor_perm(): lax.ppermute(array, axis, [(i, i ^ mask) for i in range(lax.axis_size(axi...  53.2 us
    ppermute x24, starting transfers between devices, xor_perm(): lax.ppermute(array, axis, [(i, i ^ mask) for i in range(lax.axis_size(axi...  41 us
    pallas_call x2, Pallas kernels, correlate(): pl.pallas_call(body, out_shape=[jax.ShapeDtypeStruct((2, LAG_ROWS, 256),...  13.3 us
    pallas_call x1, Pallas kernels, finish(): pl.pallas_call(finish_kernel, grid=(4,), in_specs=[pl.BlockSpec(memory_sp...  4.87 us
    convert_element_type x1, other arithmetic, lag_table(): return jnp.where(lag < LAGS, values, 0.0).astype(jnp.bfloat16)  3.36 us
  transfers between devices with their start and end apart: 24, of which 18 were waited for; matrix products, arithmetic and copies ran while one was open for 3% of the time, Pallas kernels for 11%

profile of v8, /device:TPU:8, one launch (start us, length us, event | category | flops | bytes accessed | tf_op | source)
XLA Modules:
  0.0 120.4 jit_solution(11330139841950850509)
XLA Ops:
  0.0 0.0 copy-start
  0.0 0.0 copy-start.1
  0.0 1.0 copy-done.1
  1.0 0.8 whiten.1.refs_0_
  1.8 2.3 %collective-permute-start.1 = (bf16[128,8,128]{2,1,0:T(8,128)(2,1)S(1)}, bf16[128,8,128]{2,1,0:T(8,128)(2,1)S(1)}, u32[]{:S(2)}, u32[]{:S(2)}) collective-permute-start(bf16[128,8,128]{2,1,0:T(8,128)(2,1)S(1)} %whiten.1.refs_0_), channel_id=1, source_target_pairs={{0,1},{1,0},{2,3},{3,2},{4,5},{5,4},{6,7},{7,6},{8,9},{9,8},{10,11... | collective-permute-start | bytes 786440 | tf_op jit(solution)/shard_map/ppermute | solution.py:26
  4.1 0.0 collective-permute-start
  4.1 6.9 %collective-permute-start.8 = (bf16[128,8,128]{2,1,0:T(8,128)(2,1)S(1)}, bf16[128,8,128]{2,1,0:T(8,128)(2,1)S(1)}, u32[]{:S(2)}, u32[]{:S(2)}) collective-permute-start(bf16[128,8,128]{2,1,0:T(8,128)(2,1)S(1)} %whiten.1.refs_0_), channel_id=1, source_target_pairs={{0,128},{32,160},{64,192},{96,224},{128,0},{160,32},{192,64},{224,... | collective-permute-start | bytes 786440 | tf_op jit(solution)/shard_map/ppermute | solution.py:26
  11.0 0.0 collective-permute-start.7
  11.0 1.5 %collective-permute-start.6 = (bf16[128,8,128]{2,1,0:T(8,128)(2,1)S(1)}, bf16[128,8,128]{2,1,0:T(8,128)(2,1)S(1)}, u32[]{:S(2)}, u32[]{:S(2)}) collective-permute-start(bf16[128,8,128]{2,1,0:T(8,128)(2,1)S(1)} %whiten.1.refs_0_), channel_id=1, source_target_pairs={{0,64},{32,96},{64,0},{96,32},{128,192},{160,224},{192,128},{224,1... | collective-permute-start | bytes 786440 | tf_op jit(solution)/shard_map/ppermute | solution.py:26
  12.5 0.0 collective-permute-done.1.refs_1_
  12.5 0.0 collective-permute-done.refs_1_
  12.5 2.4 %collective-permute-start.3 = (bf16[128,8,128]{2,1,0:T(8,128)(2,1)S(1)}, bf16[128,8,128]{2,1,0:T(8,128)(2,1)S(1)}, u32[]{:S(2)}, u32[]{:S(2)}) collective-permute-start(bf16[128,8,128]{2,1,0:T(8,128)(2,1)S(1)} %whiten.1.refs_0_), channel_id=1, source_target_pairs={{0,3},{1,2},{2,1},{3,0},{4,7},{5,6},{6,5},{7,4},{8,11},{9,10},{10,... | collective-permute-start | bytes 786440 | tf_op jit(solution)/shard_map/ppermute | solution.py:26
  14.9 2.1 %collective-permute-start.2 = (bf16[128,8,128]{2,1,0:T(8,128)(2,1)S(1)}, bf16[128,8,128]{2,1,0:T(8,128)(2,1)S(1)}, u32[]{:S(2)}, u32[]{:S(2)}) collective-permute-start(bf16[128,8,128]{2,1,0:T(8,128)(2,1)S(1)} %whiten.1.refs_0_), channel_id=1, source_target_pairs={{0,12},{1,13},{2,14},{3,15},{4,8},{5,9},{6,10},{7,11},{8,4},{9,5},... | collective-permute-start | bytes 786440 | tf_op jit(solution)/shard_map/ppermute | solution.py:26
  17.0 3.1 %collective-permute-done.3.refs_3_ = bf16[128,8,128]{2,1,0:T(8,128)(2,1)S(1)} collective-permute-done((bf16[128,8,128]{2,1,0:T(8,128)(2,1)S(1)}, bf16[128,8,128]{2,1,0:T(8,128)(2,1)S(1)}, u32[]{:S(2)}, u32[]{:S(2)}) %collective-permute-start.3) | collective-permute-done | bytes 262176 | tf_op jit(solution)/shard_map/ppermute | solution.py:26
  20.1 2.7 %collective-permute-done.2.refs_3_ = bf16[128,8,128]{2,1,0:T(8,128)(2,1)S(1)} collective-permute-done((bf16[128,8,128]{2,1,0:T(8,128)(2,1)S(1)}, bf16[128,8,128]{2,1,0:T(8,128)(2,1)S(1)}, u32[]{:S(2)}, u32[]{:S(2)}) %collective-permute-start.2) | collective-permute-done | bytes 262176 | tf_op jit(solution)/shard_map/ppermute | solution.py:26
  22.8 1.2 %collective-permute-start.5 = (bf16[128,8,128]{2,1,0:T(8,128)(2,1)S(1)}, bf16[128,8,128]{2,1,0:T(8,128)(2,1)S(1)}, u32[]{:S(2)}, u32[]{:S(2)}) collective-permute-start(bf16[128,8,128]{2,1,0:T(8,128)(2,1)S(1)} %whiten.1.refs_0_), channel_id=1, source_target_pairs={{0,2},{1,3},{2,0},{3,1},{4,6},{5,7},{6,4},{7,5},{8,10},{9,11},{10,... | collective-permute-start | bytes 786440 | tf_op jit(solution)/shard_map/ppermute | solution.py:26
  24.0 2.0 %collective-permute-start.4 = (bf16[128,8,128]{2,1,0:T(8,128)(2,1)S(1)}, bf16[128,8,128]{2,1,0:T(8,128)(2,1)}, u32[]{:S(2)}, u32[]{:S(2)}) collective-permute-start(bf16[128,8,128]{2,1,0:T(8,128)(2,1)S(1)} %whiten.1.refs_0_), channel_id=1, source_target_pairs={{0,8},{1,9},{2,10},{3,11},{4,12},{5,13},{6,14},{7,15},{8,0},{9,1},... | collective-permute-start | bytes 786440 | tf_op jit(solution)/shard_map/ppermute | solution.py:26
  26.0 3.4 %fusion.1.refs_8_ = bf16[520,1024]{1,0:T(8,128)(2,1)S(1)} fusion(s32[1024]{0:T(1024)S(1)} %get-tuple-element.100, s32[520]{0:T(1024)S(1)} %iota_add_fusion, s32[1024]{0:T(1024)S(1)} %get-tuple-element.99, pred[520]{0:T(1024)(128)(4,1)S(1)} %iota_compare_fusion), kind=kLoop, calls=%fused_computation.2 | loop fusion | flops 22896640 | bytes 1075752 | tf_op jit(solution)/shard_map/convert_element_type | solution.py:217
  29.3 0.0 copy-done
  29.4 0.2 dynamic-slice_reduce_fusion.offsets_ref
  29.5 1.1 collective-permute-done.5.refs_2_
  30.7 1.3 %collective-permute-done.4.refs_2_ = bf16[128,8,128]{2,1,0:T(8,128)(2,1)} collective-permute-done((bf16[128,8,128]{2,1,0:T(8,128)(2,1)S(1)}, bf16[128,8,128]{2,1,0:T(8,128)(2,1)}, u32[]{:S(2)}, u32[]{:S(2)}) %collective-permute-start.4) | collective-permute-done | bytes 262176 | tf_op jit(solution)/shard_map/ppermute | solution.py:26
  32.0 0.0 collective-permute-done.8.refs_2_
  32.0 0.5 collective-permute-done.7.refs_3_
  32.5 1.5 %collective-permute-done.6.refs_1_ = bf16[128,8,128]{2,1,0:T(8,128)(2,1)S(1)} collective-permute-done((bf16[128,8,128]{2,1,0:T(8,128)(2,1)S(1)}, bf16[128,8,128]{2,1,0:T(8,128)(2,1)S(1)}, u32[]{:S(2)}, u32[]{:S(2)}) %collective-permute-start.6) | collective-permute-done | bytes 262176 | tf_op jit(solution)/shard_map/ppermute | solution.py:26
  34.0 0.6 pick.1.mine_ref
  34.7 0.1 collective-permute-start.9
  34.8 0.1 iota_add_fusion.1
  34.9 1.8 %collective-permute-done.9.other_ref = bf16[2,128,8,128]{3,2,1,0:T(8,128)(2,1)S(1)} collective-permute-done((bf16[2,128,8,128]{3,2,1,0:T(8,128)(2,1)S(1)}, bf16[2,128,8,128]{3,2,1,0:T(8,128)(2,1)S(1)}, u32[]{:S(2)}, u32[]{:S(2)}) %collective-permute-start.9) | collective-permute-done | bytes 524320 | tf_op jit(solution)/shard_map/ppermute | solution.py:26
  36.7 0.6 merge.1.refs_4_
  37.3 0.0 copy-done.2
  37.3 0.7 collective-permute-start.11
  38.0 2.7 %collective-permute-start.10 = (bf16[2,128,8,128]{3,2,1,0:T(8,128)(2,1)S(1)}, bf16[2,128,8,128]{3,2,1,0:T(8,128)(2,1)}, u32[]{:S(2)}, u32[]{:S(2)}) collective-permute-start(bf16[2,128,8,128]{3,2,1,0:T(8,128)(2,1)S(1)} %merge.1.refs_4_), channel_id=1, source_target_pairs={{0,8},{1,9},{2,10},{3,11},{4,12},{5,13},{6,14},{7,15},{8,0},{9,1},... | collective-permute-start | bytes 1572872 | tf_op jit(solution)/shard_map/ppermute | solution.py:26
  40.8 0.2 compare_convert_fusion.refs_8_
  41.1 2.5 %collective-permute-start.14 = (bf16[2,128,8,128]{3,2,1,0:T(8,128)(2,1)S(1)}, bf16[2,128,8,128]{3,2,1,0:T(8,128)(2,1)S(1)}, u32[]{:S(2)}, u32[]{:S(2)}) collective-permute-start(bf16[2,128,8,128]{3,2,1,0:T(8,128)(2,1)S(1)} %merge.1.refs_4_), channel_id=1, source_target_pairs={{0,3},{1,2},{2,1},{3,0},{4,7},{5,6},{6,5},{7,4},{8,11},{9,10},{10,... | collective-permute-start | bytes 1572872 | tf_op jit(solution)/shard_map/ppermute | solution.py:26
  43.6 1.2 %collective-permute-start.13 = (bf16[2,128,8,128]{3,2,1,0:T(8,128)(2,1)S(1)}, bf16[2,128,8,128]{3,2,1,0:T(8,128)(2,1)S(1)}, u32[]{:S(2)}, u32[]{:S(2)}) collective-permute-start(bf16[2,128,8,128]{3,2,1,0:T(8,128)(2,1)S(1)} %merge.1.refs_4_), channel_id=1, source_target_pairs={{0,2},{1,3},{2,0},{3,1},{4,6},{5,7},{6,4},{7,5},{8,10},{9,11},{10,... | collective-permute-start | bytes 1572872 | tf_op jit(solution)/shard_map/ppermute | solution.py:26
  44.8 0.9 collective-permute-start.12
  45.7 5.6 %collective-permute-done.11.refs_4_ = bf16[2,128,8,128]{3,2,1,0:T(8,128)(2,1)S(1)} collective-permute-done((bf16[2,128,8,128]{3,2,1,0:T(8,128)(2,1)S(1)}, bf16[2,128,8,128]{3,2,1,0:T(8,128)(2,1)S(1)}, u32[]{:S(2)}, u32[]{:S(2)}) %collective-permute-start.11) | collective-permute-done | bytes 524320 | tf_op jit(solution)/shard_map/ppermute | solution.py:26
  51.4 2.0 %collective-permute-done.10 = bf16[2,128,8,128]{3,2,1,0:T(8,128)(2,1)} collective-permute-done((bf16[2,128,8,128]{3,2,1,0:T(8,128)(2,1)S(1)}, bf16[2,128,8,128]{3,2,1,0:T(8,128)(2,1)}, u32[]{:S(2)}, u32[]{:S(2)}) %collective-permute-start.10) | collective-permute-done | bytes 524320 | tf_op jit(solution)/shard_map/ppermute | solution.py:26
  53.3 1.4 %collective-permute-start.15 = (bf16[2,128,8,128]{3,2,1,0:T(8,128)(2,1)}, bf16[2,128,8,128]{3,2,1,0:T(8,128)(2,1)S(1)}, u32[]{:S(2)}, u32[]{:S(2)}) collective-permute-start(bf16[2,128,8,128]{3,2,1,0:T(8,128)(2,1)} %collective-permute-done.10), channel_id=1, source_target_pairs={{0,16},{1,17},{2,18},{3,19},{4,20},{5,21},{6,22},{7,23},{8,24},{9,... | collective-permute-start | bytes 1572872 | tf_op jit(solution)/shard_map/ppermute | solution.py:26
  54.7 2.1 %collective-permute-start.16 = (bf16[2,128,8,128]{3,2,1,0:T(8,128)(2,1)S(1)}, bf16[2,128,8,128]{3,2,1,0:T(8,128)(2,1)S(1)}, u32[]{:S(2)}, u32[]{:S(2)}) collective-permute-start(bf16[2,128,8,128]{3,2,1,0:T(8,128)(2,1)S(1)} %collective-permute-done.11.refs_4_), channel_id=1, source_target_pairs={{0,12},{1,13},{2,14},{3,15},{4,8},{5,9},{6,10},{7,11},{8,4},{9,5},... | collective-permute-start | bytes 1572872 | tf_op jit(solution)/shard_map/ppermute | solution.py:26
  56.8 9.7 %collective-permute-done.14.refs_7_ = bf16[2,128,8,128]{3,2,1,0:T(8,128)(2,1)S(1)} collective-permute-done((bf16[2,128,8,128]{3,2,1,0:T(8,128)(2,1)S(1)}, bf16[2,128,8,128]{3,2,1,0:T(8,128)(2,1)S(1)}, u32[]{:S(2)}, u32[]{:S(2)}) %collective-permute-start.14) | collective-permute-done | bytes 524320 | tf_op jit(solution)/shard_map/ppermute | solution.py:26
  66.5 0.0 collective-permute-done.13.refs_6_
  66.5 1.9 %collective-permute-done.12.refs_5_ = bf16[2,128,8,128]{3,2,1,0:T(8,128)(2,1)S(1)} collective-permute-done((bf16[2,128,8,128]{3,2,1,0:T(8,128)(2,1)S(1)}, bf16[2,128,8,128]{3,2,1,0:T(8,128)(2,1)S(1)}, u32[]{:S(2)}, u32[]{:S(2)}) %collective-permute-start.12) | collective-permute-done | bytes 524320 | tf_op jit(solution)/shard_map/ppermute | solution.py:26
  68.4 0.0 collective-permute-done.15.refs_6_
  68.4 0.1 collective-permute-done.16.refs_7_
  68.5 0.2 collective-permute-start.20
  68.6 0.9 copy-done.3
  69.6 7.1 %correlate.2 = (bf16[2,520,256]{2,1,0:T(8,128)(2,1)S(1)}, bf16[2,520,256]{2,1,0:T(8,128)(2,1)S(1)}, bf16[2,520,256]{2,1,0:T(8,128)(2,1)S(1)}, bf16[2,520,256]{2,1,0:T(8,128)(2,1)S(1)}) custom-call(bf16[128,8,128]{2,1,0:T(8,128)(2,1)S(1)} %whiten.1.refs_0_, bf16[128,8,128]{2,1,0:T(8,128)(2,1)S(1)} %collective-permute-done.refs_1_, ...), custom_call_target="tpu_custom_call" | custom-call | flops 3254779904 | bytes 7340032 | tf_op jit(solution)/shard_map/correlate/pallas_call | solution.py:153
  76.7 2.0 %collective-permute-start.17 = (bf16[2,520,256]{2,1,0:T(8,128)(2,1)S(1)}, bf16[2,520,256]{2,1,0:T(8,128)(2,1)S(1)}, u32[]{:S(2)}, u32[]{:S(2)}) collective-permute-start(bf16[2,520,256]{2,1,0:T(8,128)(2,1)S(1)} %get-tuple-element.80), channel_id=1, source_target_pairs={{0,4},{1,5},{2,6},{3,7},{4,0},{5,1},{6,2},{7,3},{8,12},{9,13},{10,... | collective-permute-start | bytes 1597448 | tf_op jit(solution)/shard_map/ppermute | solution.py:26
  78.6 1.6 %collective-permute-start.18 = (bf16[2,520,256]{2,1,0:T(8,128)(2,1)S(1)}, bf16[2,520,256]{2,1,0:T(8,128)(2,1)S(1)}, u32[]{:S(2)}, u32[]{:S(2)}) collective-permute-start(bf16[2,520,256]{2,1,0:T(8,128)(2,1)S(1)} %get-tuple-element.81), channel_id=1, source_target_pairs={{0,8},{1,9},{2,10},{3,11},{4,12},{5,13},{6,14},{7,15},{8,0},{9,1},... | collective-permute-start | bytes 1597448 | tf_op jit(solution)/shard_map/ppermute | solution.py:26
  80.2 1.2 %collective-permute-start.19 = (bf16[2,520,256]{2,1,0:T(8,128)(2,1)S(1)}, bf16[2,520,256]{2,1,0:T(8,128)(2,1)S(1)}, u32[]{:S(2)}, u32[]{:S(2)}) collective-permute-start(bf16[2,520,256]{2,1,0:T(8,128)(2,1)S(1)} %get-tuple-element.82), channel_id=1, source_target_pairs={{0,12},{1,13},{2,14},{3,15},{4,8},{5,9},{6,10},{7,11},{8,4},{9,5},... | collective-permute-start | bytes 1597448 | tf_op jit(solution)/shard_map/ppermute | solution.py:26
  81.4 1.9 %collective-permute-done.20.refs_5_ = bf16[2,128,8,128]{3,2,1,0:T(8,128)(2,1)S(1)} collective-permute-done((bf16[2,128,8,128]{3,2,1,0:T(8,128)(2,1)S(1)}, bf16[2,128,8,128]{3,2,1,0:T(8,128)(2,1)S(1)}, u32[]{:S(2)}, u32[]{:S(2)}) %collective-permute-start.20) | collective-permute-done | bytes 524320 | tf_op jit(solution)/shard_map/ppermute | solution.py:26
  83.3 6.2 %correlate.3 = (bf16[2,520,256]{2,1,0:T(8,128)(2,1)S(1)}, bf16[2,520,256]{2,1,0:T(8,128)(2,1)S(1)}, bf16[2,520,256]{2,1,0:T(8,128)(2,1)S(1)}, bf16[2,520,256]{2,1,0:T(8,128)(2,1)S(1)}) custom-call(bf16[128,8,128]{2,1,0:T(8,128)(2,1)S(1)} %whiten.1.refs_0_, bf16[128,8,128]{2,1,0:T(8,128)(2,1)S(1)} %collective-permute-done.1.refs_1_, ...), custom_call_target="tpu_custom_call" | custom-call | flops 3254779904 | bytes 7340032 | tf_op jit(solution)/shard_map/correlate/pallas_call | solution.py:153
  89.5 1.5 %collective-permute-start.21 = (bf16[2,520,256]{2,1,0:T(8,128)(2,1)S(1)}, bf16[2,520,256]{2,1,0:T(8,128)(2,1)S(1)}, u32[]{:S(2)}, u32[]{:S(2)}) collective-permute-start(bf16[2,520,256]{2,1,0:T(8,128)(2,1)S(1)} %get-tuple-element.95), channel_id=1, source_target_pairs={{0,1},{1,0},{2,3},{3,2},{4,5},{5,4},{6,7},{7,6},{8,9},{9,8},{10,11... | collective-permute-start | bytes 1597448 | tf_op jit(solution)/shard_map/ppermute | solution.py:26
  91.0 2.3 %collective-permute-start.22 = (bf16[2,520,256]{2,1,0:T(8,128)(2,1)S(1)}, bf16[2,520,256]{2,1,0:T(8,128)(2,1)S(1)}, u32[]{:S(2)}, u32[]{:S(2)}) collective-permute-start(bf16[2,520,256]{2,1,0:T(8,128)(2,1)S(1)} %get-tuple-element.96), channel_id=1, source_target_pairs={{0,2},{1,3},{2,0},{3,1},{4,6},{5,7},{6,4},{7,5},{8,10},{9,11},{10,... | collective-permute-start | bytes 1597448 | tf_op jit(solution)/shard_map/ppermute | solution.py:26
  93.3 1.4 %collective-permute-done.17.refs_1_ = bf16[2,520,256]{2,1,0:T(8,128)(2,1)S(1)} collective-permute-done((bf16[2,520,256]{2,1,0:T(8,128)(2,1)S(1)}, bf16[2,520,256]{2,1,0:T(8,128)(2,1)S(1)}, u32[]{:S(2)}, u32[]{:S(2)}) %collective-permute-start.17) | collective-permute-done | bytes 532512 | tf_op jit(solution)/shard_map/ppermute | solution.py:26
  94.7 2.2 %collective-permute-start.23 = (bf16[2,520,256]{2,1,0:T(8,128)(2,1)S(1)}, bf16[2,520,256]{2,1,0:T(8,128)(2,1)S(1)}, u32[]{:S(2)}, u32[]{:S(2)}) collective-permute-start(bf16[2,520,256]{2,1,0:T(8,128)(2,1)S(1)} %get-tuple-element.97), channel_id=1, source_target_pairs={{0,3},{1,2},{2,1},{3,0},{4,7},{5,6},{6,5},{7,4},{8,11},{9,10},{10,... | collective-permute-start | bytes 1597448 | tf_op jit(solution)/shard_map/ppermute | solution.py:26
  97.0 7.5 %collective-permute-done.18.refs_2_ = bf16[2,520,256]{2,1,0:T(8,128)(2,1)S(1)} collective-permute-done((bf16[2,520,256]{2,1,0:T(8,128)(2,1)S(1)}, bf16[2,520,256]{2,1,0:T(8,128)(2,1)S(1)}, u32[]{:S(2)}, u32[]{:S(2)}) %collective-permute-start.18) | collective-permute-done | bytes 532512 | tf_op jit(solution)/shard_map/ppermute | solution.py:26
  104.4 0.0 collective-permute-done.19.refs_3_
  104.4 0.2 collective-permute-done.21.refs_5_
  104.7 7.3 %collective-permute-done.22.refs_6_ = bf16[2,520,256]{2,1,0:T(8,128)(2,1)S(1)} collective-permute-done((bf16[2,520,256]{2,1,0:T(8,128)(2,1)S(1)}, bf16[2,520,256]{2,1,0:T(8,128)(2,1)S(1)}, u32[]{:S(2)}, u32[]{:S(2)}) %collective-permute-start.22) | collective-permute-done | bytes 532512 | tf_op jit(solution)/shard_map/ppermute | solution.py:26
  111.9 3.6 %collective-permute-done.23.refs_7_ = bf16[2,520,256]{2,1,0:T(8,128)(2,1)S(1)} collective-permute-done((bf16[2,520,256]{2,1,0:T(8,128)(2,1)S(1)}, bf16[2,520,256]{2,1,0:T(8,128)(2,1)S(1)}, u32[]{:S(2)}, u32[]{:S(2)}) %collective-permute-start.23) | collective-permute-done | bytes 532512 | tf_op jit(solution)/shard_map/ppermute | solution.py:26
  115.5 4.9 %finish.1 = bf16[4,4104,128]{2,1,0:T(8,128)(2,1)} custom-call(s32[1]{0:T(128)} %bitcast.member_ref, bf16[2,520,256]{2,1,0:T(8,128)(2,1)S(1)} %get-tuple-element.79.refs_0_, bf16[2,520,256]{2,1,0:T(8,128)(2,1)S(1)} %collective-permute-done.17.refs_1_, bf16[2,520,256]{2,1,0:T(8,128)(2,1)S(1)} %collective-permute-done.18.refs_2_, ...), custom_call_target="tpu_custom_call" | custom-call | tf_op jit(solution)/shard_map/finish/pallas_call | solution.py:191
  (10 shorter events, 0.1 us)
Async XLA Ops:
  0.0 29.3 %copy-start = (s32[2,32]{1,0:T(2,128)S(1)}, s32[2,32]{1,0:T(2,128)}, u32[]{:S(2)}) copy-start(s32[2,32]{1,0:T(2,128)} %param.3) | copy-start | bytes 772
  0.0 1.0 copy-start.1
  1.8 10.7 %collective-permute-start.1 = (bf16[128,8,128]{2,1,0:T(8,128)(2,1)S(1)}, bf16[128,8,128]{2,1,0:T(8,128)(2,1)S(1)}, u32[]{:S(2)}, u32[]{:S(2)}) collective-permute-start(bf16[128,8,128]{2,1,0:T(8,128)(2,1)S(1)} %whiten.1.refs_0_), channel_id=1, source_target_pairs={{0,1},{1,0},{2,3},{3,2},{4,5},{5,4},{6,7},{7,6},{8,9},{9,8},{10,11... | collective-permute-start | bytes 786440 | tf_op jit(solution)/shard_map/ppermute | solution.py:26
  4.1 8.4 %collective-permute-start = (bf16[128,8,128]{2,1,0:T(8,128)(2,1)S(1)}, bf16[128,8,128]{2,1,0:T(8,128)(2,1)S(1)}, u32[]{:S(2)}, u32[]{:S(2)}) collective-permute-start(bf16[128,8,128]{2,1,0:T(8,128)(2,1)S(1)} %whiten.1.refs_0_), channel_id=1, source_target_pairs={{0,4},{1,5},{2,6},{3,7},{4,0},{5,1},{6,2},{7,3},{8,12},{9,13},{10,... | collective-permute-start | bytes 786440 | tf_op jit(solution)/shard_map/ppermute | solution.py:26
  4.1 27.9 %collective-permute-start.8 = (bf16[128,8,128]{2,1,0:T(8,128)(2,1)S(1)}, bf16[128,8,128]{2,1,0:T(8,128)(2,1)S(1)}, u32[]{:S(2)}, u32[]{:S(2)}) collective-permute-start(bf16[128,8,128]{2,1,0:T(8,128)(2,1)S(1)} %whiten.1.refs_0_), channel_id=1, source_target_pairs={{0,128},{32,160},{64,192},{96,224},{128,0},{160,32},{192,64},{224,... | collective-permute-start | bytes 786440 | tf_op jit(solution)/shard_map/ppermute | solution.py:26
  11.0 21.5 %collective-permute-start.7 = (bf16[128,8,128]{2,1,0:T(8,128)(2,1)S(1)}, bf16[128,8,128]{2,1,0:T(8,128)(2,1)S(1)}, u32[]{:S(2)}, u32[]{:S(2)}) collective-permute-start(bf16[128,8,128]{2,1,0:T(8,128)(2,1)S(1)} %whiten.1.refs_0_), channel_id=1, source_target_pairs={{0,192},{32,224},{64,128},{96,160},{128,64},{160,96},{192,0},{224,... | collective-permute-start | bytes 786440 | tf_op jit(solution)/shard_map/ppermute | solution.py:26
  11.0 23.0 %collective-permute-start.6 = (bf16[128,8,128]{2,1,0:T(8,128)(2,1)S(1)}, bf16[128,8,128]{2,1,0:T(8,128)(2,1)S(1)}, u32[]{:S(2)}, u32[]{:S(2)}) collective-permute-start(bf16[128,8,128]{2,1,0:T(8,128)(2,1)S(1)} %whiten.1.refs_0_), channel_id=1, source_target_pairs={{0,64},{32,96},{64,0},{96,32},{128,192},{160,224},{192,128},{224,1... | collective-permute-start | bytes 786440 | tf_op jit(solution)/shard_map/ppermute | solution.py:26
  12.5 7.6 %collective-permute-start.3 = (bf16[128,8,128]{2,1,0:T(8,128)(2,1)S(1)}, bf16[128,8,128]{2,1,0:T(8,128)(2,1)S(1)}, u32[]{:S(2)}, u32[]{:S(2)}) collective-permute-start(bf16[128,8,128]{2,1,0:T(8,128)(2,1)S(1)} %whiten.1.refs_0_), channel_id=1, source_target_pairs={{0,3},{1,2},{2,1},{3,0},{4,7},{5,6},{6,5},{7,4},{8,11},{9,10},{10,... | collective-permute-start | bytes 786440 | tf_op jit(solution)/shard_map/ppermute | solution.py:26
  14.9 7.9 %collective-permute-start.2 = (bf16[128,8,128]{2,1,0:T(8,128)(2,1)S(1)}, bf16[128,8,128]{2,1,0:T(8,128)(2,1)S(1)}, u32[]{:S(2)}, u32[]{:S(2)}) collective-permute-start(bf16[128,8,128]{2,1,0:T(8,128)(2,1)S(1)} %whiten.1.refs_0_), channel_id=1, source_target_pairs={{0,12},{1,13},{2,14},{3,15},{4,8},{5,9},{6,10},{7,11},{8,4},{9,5},... | collective-permute-start | bytes 786440 | tf_op jit(solution)/shard_map/ppermute | solution.py:26
  22.8 14.5 %copy-start.2 = (bf16[128,8,128]{2,1,0:T(8,128)(2,1)}, bf16[128,8,128]{2,1,0:T(8,128)(2,1)S(1)}, u32[]{:S(2)}) copy-start(bf16[128,8,128]{2,1,0:T(8,128)(2,1)S(1)} %collective-permute-done.2.refs_3_) | copy-start | bytes 786436
  22.8 7.9 %collective-permute-start.5 = (bf16[128,8,128]{2,1,0:T(8,128)(2,1)S(1)}, bf16[128,8,128]{2,1,0:T(8,128)(2,1)S(1)}, u32[]{:S(2)}, u32[]{:S(2)}) collective-permute-start(bf16[128,8,128]{2,1,0:T(8,128)(2,1)S(1)} %whiten.1.refs_0_), channel_id=1, source_target_pairs={{0,2},{1,3},{2,0},{3,1},{4,6},{5,7},{6,4},{7,5},{8,10},{9,11},{10,... | collective-permute-start | bytes 786440 | tf_op jit(solution)/shard_map/ppermute | solution.py:26
  24.0 8.0 %collective-permute-start.4 = (bf16[128,8,128]{2,1,0:T(8,128)(2,1)S(1)}, bf16[128,8,128]{2,1,0:T(8,128)(2,1)}, u32[]{:S(2)}, u32[]{:S(2)}) collective-permute-start(bf16[128,8,128]{2,1,0:T(8,128)(2,1)S(1)} %whiten.1.refs_0_), channel_id=1, source_target_pairs={{0,8},{1,9},{2,10},{3,11},{4,12},{5,13},{6,14},{7,15},{8,0},{9,1},... | collective-permute-start | bytes 786440 | tf_op jit(solution)/shard_map/ppermute | solution.py:26
  34.7 2.0 %collective-permute-start.9 = (bf16[2,128,8,128]{3,2,1,0:T(8,128)(2,1)S(1)}, bf16[2,128,8,128]{3,2,1,0:T(8,128)(2,1)S(1)}, u32[]{:S(2)}, u32[]{:S(2)}) collective-permute-start(bf16[2,128,8,128]{3,2,1,0:T(8,128)(2,1)S(1)} %pick.1.mine_ref), channel_id=1, source_target_pairs={{0,32},{32,0},{64,96},{96,64},{128,160},{160,128},{192,224},{224,1... | collective-permute-start | bytes 1572872 | tf_op jit(solution)/shard_map/ppermute | solution.py:26
  37.3 14.1 %collective-permute-start.11 = (bf16[2,128,8,128]{3,2,1,0:T(8,128)(2,1)S(1)}, bf16[2,128,8,128]{3,2,1,0:T(8,128)(2,1)S(1)}, u32[]{:S(2)}, u32[]{:S(2)}) collective-permute-start(bf16[2,128,8,128]{3,2,1,0:T(8,128)(2,1)S(1)} %merge.1.refs_4_), channel_id=1, source_target_pairs={{0,16},{1,17},{2,18},{3,19},{4,20},{5,21},{6,22},{7,23},{8,24},{9,... | collective-permute-start | bytes 1572872 | tf_op jit(solution)/shard_map/ppermute | solution.py:26
  38.0 15.3 %collective-permute-start.10 = (bf16[2,128,8,128]{3,2,1,0:T(8,128)(2,1)S(1)}, bf16[2,128,8,128]{3,2,1,0:T(8,128)(2,1)}, u32[]{:S(2)}, u32[]{:S(2)}) collective-permute-start(bf16[2,128,8,128]{3,2,1,0:T(8,128)(2,1)S(1)} %merge.1.refs_4_), channel_id=1, source_target_pairs={{0,8},{1,9},{2,10},{3,11},{4,12},{5,13},{6,14},{7,15},{8,0},{9,1},... | collective-permute-start | bytes 1572872 | tf_op jit(solution)/shard_map/ppermute | solution.py:26
  41.1 25.4 %collective-permute-start.14 = (bf16[2,128,8,128]{3,2,1,0:T(8,128)(2,1)S(1)}, bf16[2,128,8,128]{3,2,1,0:T(8,128)(2,1)S(1)}, u32[]{:S(2)}, u32[]{:S(2)}) collective-permute-start(bf16[2,128,8,128]{3,2,1,0:T(8,128)(2,1)S(1)} %merge.1.refs_4_), channel_id=1, source_target_pairs={{0,3},{1,2},{2,1},{3,0},{4,7},{5,6},{6,5},{7,4},{8,11},{9,10},{10,... | collective-permute-start | bytes 1572872 | tf_op jit(solution)/shard_map/ppermute | solution.py:26
  43.6 22.9 %collective-permute-start.13 = (bf16[2,128,8,128]{3,2,1,0:T(8,128)(2,1)S(1)}, bf16[2,128,8,128]{3,2,1,0:T(8,128)(2,1)S(1)}, u32[]{:S(2)}, u32[]{:S(2)}) collective-permute-start(bf16[2,128,8,128]{3,2,1,0:T(8,128)(2,1)S(1)} %merge.1.refs_4_), channel_id=1, source_target_pairs={{0,2},{1,3},{2,0},{3,1},{4,6},{5,7},{6,4},{7,5},{8,10},{9,11},{10,... | collective-permute-start | bytes 1572872 | tf_op jit(solution)/shard_map/ppermute | solution.py:26
  44.8 23.6 %collective-permute-start.12 = (bf16[2,128,8,128]{3,2,1,0:T(8,128)(2,1)S(1)}, bf16[2,128,8,128]{3,2,1,0:T(8,128)(2,1)S(1)}, u32[]{:S(2)}, u32[]{:S(2)}) collective-permute-start(bf16[2,128,8,128]{3,2,1,0:T(8,128)(2,1)S(1)} %merge.1.refs_4_), channel_id=1, source_target_pairs={{0,1},{1,0},{2,3},{3,2},{4,5},{5,4},{6,7},{7,6},{8,9},{9,8},{10,11... | collective-permute-start | bytes 1572872 | tf_op jit(solution)/shard_map/ppermute | solution.py:26
  53.3 15.1 %collective-permute-start.15 = (bf16[2,128,8,128]{3,2,1,0:T(8,128)(2,1)}, bf16[2,128,8,128]{3,2,1,0:T(8,128)(2,1)S(1)}, u32[]{:S(2)}, u32[]{:S(2)}) collective-permute-start(bf16[2,128,8,128]{3,2,1,0:T(8,128)(2,1)} %collective-permute-done.10), channel_id=1, source_target_pairs={{0,16},{1,17},{2,18},{3,19},{4,20},{5,21},{6,22},{7,23},{8,24},{9,... | collective-permute-start | bytes 1572872 | tf_op jit(solution)/shard_map/ppermute | solution.py:26
  54.7 13.7 %collective-permute-start.16 = (bf16[2,128,8,128]{3,2,1,0:T(8,128)(2,1)S(1)}, bf16[2,128,8,128]{3,2,1,0:T(8,128)(2,1)S(1)}, u32[]{:S(2)}, u32[]{:S(2)}) collective-permute-start(bf16[2,128,8,128]{3,2,1,0:T(8,128)(2,1)S(1)} %collective-permute-done.11.refs_4_), channel_id=1, source_target_pairs={{0,12},{1,13},{2,14},{3,15},{4,8},{5,9},{6,10},{7,11},{8,4},{9,5},... | collective-permute-start | bytes 1572872 | tf_op jit(solution)/shard_map/ppermute | solution.py:26
  68.5 14.9 %collective-permute-start.20 = (bf16[2,128,8,128]{3,2,1,0:T(8,128)(2,1)S(1)}, bf16[2,128,8,128]{3,2,1,0:T(8,128)(2,1)S(1)}, u32[]{:S(2)}, u32[]{:S(2)}) collective-permute-start(bf16[2,128,8,128]{3,2,1,0:T(8,128)(2,1)S(1)} %collective-permute-done.11.refs_4_), channel_id=1, source_target_pairs={{0,4},{1,5},{2,6},{3,7},{4,0},{5,1},{6,2},{7,3},{8,12},{9,13},{10,... | collective-permute-start | bytes 1572872 | tf_op jit(solution)/shard_map/ppermute | solution.py:26
  68.6 0.9 copy-start.3
  76.7 18.1 %collective-permute-start.17 = (bf16[2,520,256]{2,1,0:T(8,128)(2,1)S(1)}, bf16[2,520,256]{2,1,0:T(8,128)(2,1)S(1)}, u32[]{:S(2)}, u32[]{:S(2)}) collective-permute-start(bf16[2,520,256]{2,1,0:T(8,128)(2,1)S(1)} %get-tuple-element.80), channel_id=1, source_target_pairs={{0,4},{1,5},{2,6},{3,7},{4,0},{5,1},{6,2},{7,3},{8,12},{9,13},{10,... | collective-permute-start | bytes 1597448 | tf_op jit(solution)/shard_map/ppermute | solution.py:26
  78.6 25.8 %collective-permute-start.18 = (bf16[2,520,256]{2,1,0:T(8,128)(2,1)S(1)}, bf16[2,520,256]{2,1,0:T(8,128)(2,1)S(1)}, u32[]{:S(2)}, u32[]{:S(2)}) collective-permute-start(bf16[2,520,256]{2,1,0:T(8,128)(2,1)S(1)} %get-tuple-element.81), channel_id=1, source_target_pairs={{0,8},{1,9},{2,10},{3,11},{4,12},{5,13},{6,14},{7,15},{8,0},{9,1},... | collective-permute-start | bytes 1597448 | tf_op jit(solution)/shard_map/ppermute | solution.py:26
  80.2 24.2 %collective-permute-start.19 = (bf16[2,520,256]{2,1,0:T(8,128)(2,1)S(1)}, bf16[2,520,256]{2,1,0:T(8,128)(2,1)S(1)}, u32[]{:S(2)}, u32[]{:S(2)}) collective-permute-start(bf16[2,520,256]{2,1,0:T(8,128)(2,1)S(1)} %get-tuple-element.82), channel_id=1, source_target_pairs={{0,12},{1,13},{2,14},{3,15},{4,8},{5,9},{6,10},{7,11},{8,4},{9,5},... | collective-permute-start | bytes 1597448 | tf_op jit(solution)/shard_map/ppermute | solution.py:26
  89.5 15.1 %collective-permute-start.21 = (bf16[2,520,256]{2,1,0:T(8,128)(2,1)S(1)}, bf16[2,520,256]{2,1,0:T(8,128)(2,1)S(1)}, u32[]{:S(2)}, u32[]{:S(2)}) collective-permute-start(bf16[2,520,256]{2,1,0:T(8,128)(2,1)S(1)} %get-tuple-element.95), channel_id=1, source_target_pairs={{0,1},{1,0},{2,3},{3,2},{4,5},{5,4},{6,7},{7,6},{8,9},{9,8},{10,11... | collective-permute-start | bytes 1597448 | tf_op jit(solution)/shard_map/ppermute | solution.py:26
  91.0 20.9 %collective-permute-start.22 = (bf16[2,520,256]{2,1,0:T(8,128)(2,1)S(1)}, bf16[2,520,256]{2,1,0:T(8,128)(2,1)S(1)}, u32[]{:S(2)}, u32[]{:S(2)}) collective-permute-start(bf16[2,520,256]{2,1,0:T(8,128)(2,1)S(1)} %get-tuple-element.96), channel_id=1, source_target_pairs={{0,2},{1,3},{2,0},{3,1},{4,6},{5,7},{6,4},{7,5},{8,10},{9,11},{10,... | collective-permute-start | bytes 1597448 | tf_op jit(solution)/shard_map/ppermute | solution.py:26
  94.7 20.8 %collective-permute-start.23 = (bf16[2,520,256]{2,1,0:T(8,128)(2,1)S(1)}, bf16[2,520,256]{2,1,0:T(8,128)(2,1)S(1)}, u32[]{:S(2)}, u32[]{:S(2)}) collective-permute-start(bf16[2,520,256]{2,1,0:T(8,128)(2,1)S(1)} %get-tuple-element.97), channel_id=1, source_target_pairs={{0,3},{1,2},{2,1},{3,0},{4,7},{5,6},{6,5},{7,4},{8,11},{9,10},{10,... | collective-permute-start | bytes 1597448 | tf_op jit(solution)/shard_map/ppermute | solution.py:26

commit v9 on v8

--- a/solution.py
+++ b/solution.py
@@ -256,14 +256,11 @@
     across = xor_perm(near, "mem", 16)
     hop = xor_perm(near, "mem", 2 * col_masks[1])
     order = column_order(member_now)
-    later, order = lax.optimization_barrier((near, order))
-    near1, near2, near3 = [xor_perm(later, "mem", e * col_masks[0]) for e in (1, 2, 3)]
+    near1, near2, near3 = [xor_perm(near, "mem", e * col_masks[0]) for e in (1, 2, 3)]
     order, hop, across = lax.optimization_barrier((order, hop, across))
     far2 = xor_perm(hop, "mem", 16)
     far3 = xor_perm(across, "mem", 3 * col_masks[1])
-    across, near1, near2, near3, far2, far3 = lax.optimization_barrier(
-        (across, near1, near2, near3, far2, far3)
-    )
+    across, near1, near2, near3 = lax.optimization_barrier((across, near1, near2, near3))
     far1 = xor_perm(across, "mem", col_masks[1])
     cols = [[near, near1, near2, near3], [across, far1, far2, far3]]
     parts = []

time: 121 us -> 120 us (level)
  waiting for transfers between devices: 53.2 us -> 47.4 us
  local copies, waits for them, and re-layouts: 2.11 us -> 6.83 us
    ppermute x24, waiting for transfers between devices: 53.2 us -> 47.4 us  [xor_perm(): lax.ppermute(array, axis, [(i, i ^ mask) for i in range(lax.axis_size(axi...]
    unnamed x8 -> x28, local copies, waits for them, and re-layouts: 1.92 us -> 6.64 us
  transfers between devices with their start and end apart: 24 -> 24, of which waited for: 18 -> 14; matrix products, arithmetic and copies ran while one was open for 3% -> 3% of each run, Pallas kernels for 11% -> 11%
where the time goes in v9:
time: 120 us; the launch traced here: 118 us
  waiting for transfers between devices  47.4 us (40%)
  starting transfers between devices  40.1 us (33%)
  Pallas kernels  20.3 us (17%)
  local copies, waits for them, and re-layouts  6.83 us (6%)
  other arithmetic  3.74 us (3%)
    ppermute x24, waiting for transfers between devices, xor_perm(): lax.ppermute(array, axis, [(i, i ^ mask) for i in range(lax.axis_size(axi...  47.4 us
    ppermute x24, starting transfers between devices, xor_perm(): lax.ppermute(array, axis, [(i, i ^ mask) for i in range(lax.axis_size(axi...  40.1 us
    pallas_call x2, Pallas kernels, correlate(): pl.pallas_call(body, out_shape=[jax.ShapeDtypeStruct((2, LAG_ROWS, 256),...  13.3 us
    unnamed x28, local copies, waits for them, and re-layouts  6.64 us
    pallas_call x1, Pallas kernels, finish(): pl.pallas_call(finish_kernel, grid=(4,), in_specs=[pl.BlockSpec(memory_sp...  4.88 us
    convert_element_type x1, other arithmetic, lag_table(): return jnp.where(lag < LAGS, values, 0.0).astype(jnp.bfloat16)  3.36 us
  transfers between devices with their start and end apart: 24, of which 14 were waited for; matrix products, arithmetic and copies ran while one was open for 3% of the time, Pallas kernels for 11%

profile of v9, /device:TPU:8, one launch (start us, length us, event | category | flops | bytes accessed | tf_op | source)
XLA Modules:
  0.0 118.5 jit_solution(13216056637563108718)
XLA Ops:
  0.0 1.0 copy-done.1
  1.0 0.8 whiten.1.refs_0_
  1.8 2.3 %collective-permute-start.1 = (bf16[128,8,128]{2,1,0:T(8,128)(2,1)S(1)}, bf16[128,8,128]{2,1,0:T(8,128)(2,1)S(1)}, u32[]{:S(2)}, u32[]{:S(2)}) collective-permute-start(bf16[128,8,128]{2,1,0:T(8,128)(2,1)S(1)} %whiten.1.refs_0_), channel_id=1, source_target_pairs={{0,1},{1,0},{2,3},{3,2},{4,5},{5,4},{6,7},{7,6},{8,9},{9,8},{10,11... | collective-permute-start | bytes 786440 | tf_op jit(solution)/shard_map/ppermute | solution.py:26
  4.1 0.0 collective-permute-start
  4.1 6.9 %collective-permute-start.8 = (bf16[128,8,128]{2,1,0:T(8,128)(2,1)S(1)}, bf16[128,8,128]{2,1,0:T(8,128)(2,1)S(1)}, u32[]{:S(2)}, u32[]{:S(2)}) collective-permute-start(bf16[128,8,128]{2,1,0:T(8,128)(2,1)S(1)} %whiten.1.refs_0_), channel_id=1, source_target_pairs={{0,128},{32,160},{64,192},{96,224},{128,0},{160,32},{192,64},{224,... | collective-permute-start | bytes 786440 | tf_op jit(solution)/shard_map/ppermute | solution.py:26
  11.0 0.0 collective-permute-start.7
  11.0 1.5 %collective-permute-start.6 = (bf16[128,8,128]{2,1,0:T(8,128)(2,1)S(1)}, bf16[128,8,128]{2,1,0:T(8,128)(2,1)S(1)}, u32[]{:S(2)}, u32[]{:S(2)}) collective-permute-start(bf16[128,8,128]{2,1,0:T(8,128)(2,1)S(1)} %whiten.1.refs_0_), channel_id=1, source_target_pairs={{0,64},{32,96},{64,0},{96,32},{128,192},{160,224},{192,128},{224,1... | collective-permute-start | bytes 786440 | tf_op jit(solution)/shard_map/ppermute | solution.py:26
  12.5 0.0 collective-permute-done.1.refs_1_
  12.5 0.7 copy-done.2
  13.2 0.0 collective-permute-done.refs_1_
  13.2 0.7 copy-done.6
  13.9 2.4 %collective-permute-start.3 = (bf16[128,8,128]{2,1,0:T(8,128)(2,1)S(1)}, bf16[128,8,128]{2,1,0:T(8,128)(2,1)S(1)}, u32[]{:S(2)}, u32[]{:S(2)}) collective-permute-start(bf16[128,8,128]{2,1,0:T(8,128)(2,1)S(1)} %whiten.1.refs_0_), channel_id=1, source_target_pairs={{0,3},{1,2},{2,1},{3,0},{4,7},{5,6},{6,5},{7,4},{8,11},{9,10},{10,... | collective-permute-start | bytes 786440 | tf_op jit(solution)/shard_map/ppermute | solution.py:26
  16.3 2.1 %collective-permute-start.2 = (bf16[128,8,128]{2,1,0:T(8,128)(2,1)S(1)}, bf16[128,8,128]{2,1,0:T(8,128)(2,1)S(1)}, u32[]{:S(2)}, u32[]{:S(2)}) collective-permute-start(bf16[128,8,128]{2,1,0:T(8,128)(2,1)S(1)} %whiten.1.refs_0_), channel_id=1, source_target_pairs={{0,12},{1,13},{2,14},{3,15},{4,8},{5,9},{6,10},{7,11},{8,4},{9,5},... | collective-permute-start | bytes 786440 | tf_op jit(solution)/shard_map/ppermute | solution.py:26
  18.4 3.1 %collective-permute-done.3.refs_3_ = bf16[128,8,128]{2,1,0:T(8,128)(2,1)S(1)} collective-permute-done((bf16[128,8,128]{2,1,0:T(8,128)(2,1)S(1)}, bf16[128,8,128]{2,1,0:T(8,128)(2,1)S(1)}, u32[]{:S(2)}, u32[]{:S(2)}) %collective-permute-start.3) | collective-permute-done | bytes 262176 | tf_op jit(solution)/shard_map/ppermute | solution.py:26
  21.5 0.7 copy-done.4
  22.2 2.0 %collective-permute-done.2.refs_3_ = bf16[128,8,128]{2,1,0:T(8,128)(2,1)S(1)} collective-permute-done((bf16[128,8,128]{2,1,0:T(8,128)(2,1)S(1)}, bf16[128,8,128]{2,1,0:T(8,128)(2,1)S(1)}, u32[]{:S(2)}, u32[]{:S(2)}) %collective-permute-start.2) | collective-permute-done | bytes 262176 | tf_op jit(solution)/shard_map/ppermute | solution.py:26
  24.2 0.7 copy-done.10
  24.9 1.2 %collective-permute-start.5 = (bf16[128,8,128]{2,1,0:T(8,128)(2,1)S(1)}, bf16[128,8,128]{2,1,0:T(8,128)(2,1)S(1)}, u32[]{:S(2)}, u32[]{:S(2)}) collective-permute-start(bf16[128,8,128]{2,1,0:T(8,128)(2,1)S(1)} %whiten.1.refs_0_), channel_id=1, source_target_pairs={{0,2},{1,3},{2,0},{3,1},{4,6},{5,7},{6,4},{7,5},{8,10},{9,11},{10,... | collective-permute-start | bytes 786440 | tf_op jit(solution)/shard_map/ppermute | solution.py:26
  26.1 2.7 %collective-permute-start.4 = (bf16[128,8,128]{2,1,0:T(8,128)(2,1)S(1)}, bf16[128,8,128]{2,1,0:T(8,128)(2,1)S(1)}, u32[]{:S(2)}, u32[]{:S(2)}) collective-permute-start(bf16[128,8,128]{2,1,0:T(8,128)(2,1)S(1)} %whiten.1.refs_0_), channel_id=1, source_target_pairs={{0,8},{1,9},{2,10},{3,11},{4,12},{5,13},{6,14},{7,15},{8,0},{9,1},... | collective-permute-start | bytes 786440 | tf_op jit(solution)/shard_map/ppermute | solution.py:26
  28.8 3.4 %fusion.1.refs_8_ = bf16[520,1024]{1,0:T(8,128)(2,1)S(1)} fusion(s32[1024]{0:T(1024)S(1)} %get-tuple-element.92, s32[520]{0:T(1024)S(1)} %iota_add_fusion, s32[1024]{0:T(1024)S(1)} %get-tuple-element.91, pred[520]{0:T(1024)(128)(4,1)S(1)} %iota_compare_fusion), kind=kLoop, calls=%fused_computation.2 | loop fusion | flops 22896640 | bytes 1075752 | tf_op jit(solution)/shard_map/convert_element_type | solution.py:217
  32.2 0.2 dynamic-slice_reduce_fusion.offsets_ref
  32.3 0.4 collective-permute-done.5.refs_2_
  32.8 1.2 %collective-permute-done.4.refs_2_ = bf16[128,8,128]{2,1,0:T(8,128)(2,1)S(1)} collective-permute-done((bf16[128,8,128]{2,1,0:T(8,128)(2,1)S(1)}, bf16[128,8,128]{2,1,0:T(8,128)(2,1)S(1)}, u32[]{:S(2)}, u32[]{:S(2)}) %collective-permute-start.4) | collective-permute-done | bytes 262176 | tf_op jit(solution)/shard_map/ppermute | solution.py:26
  34.0 0.0 collective-permute-done.8.refs_2_
  34.0 0.0 collective-permute-done.7.refs_3_
  34.0 0.0 collective-permute-done.6.refs_1_
  34.0 0.6 pick.1.mine_ref
  34.7 0.1 collective-permute-start.9
  34.8 0.1 iota_add_fusion.1
  34.9 1.8 %collective-permute-done.9.other_ref = bf16[2,128,8,128]{3,2,1,0:T(8,128)(2,1)S(1)} collective-permute-done((bf16[2,128,8,128]{3,2,1,0:T(8,128)(2,1)S(1)}, bf16[2,128,8,128]{3,2,1,0:T(8,128)(2,1)S(1)}, u32[]{:S(2)}, u32[]{:S(2)}) %collective-permute-start.9) | collective-permute-done | bytes 524320 | tf_op jit(solution)/shard_map/ppermute | solution.py:26
  36.7 0.6 merge.1.refs_4_
  37.3 2.5 %collective-permute-start.14 = (bf16[2,128,8,128]{3,2,1,0:T(8,128)(2,1)S(1)}, bf16[2,128,8,128]{3,2,1,0:T(8,128)(2,1)S(1)}, u32[]{:S(2)}, u32[]{:S(2)}) collective-permute-start(bf16[2,128,8,128]{3,2,1,0:T(8,128)(2,1)S(1)} %merge.1.refs_4_), channel_id=1, source_target_pairs={{0,3},{1,2},{2,1},{3,0},{4,7},{5,6},{6,5},{7,4},{8,11},{9,10},{10,... | collective-permute-start | bytes 1572872 | tf_op jit(solution)/shard_map/ppermute | solution.py:26
  39.8 1.2 %collective-permute-start.13 = (bf16[2,128,8,128]{3,2,1,0:T(8,128)(2,1)S(1)}, bf16[2,128,8,128]{3,2,1,0:T(8,128)(2,1)S(1)}, u32[]{:S(2)}, u32[]{:S(2)}) collective-permute-start(bf16[2,128,8,128]{3,2,1,0:T(8,128)(2,1)S(1)} %merge.1.refs_4_), channel_id=1, source_target_pairs={{0,2},{1,3},{2,0},{3,1},{4,6},{5,7},{6,4},{7,5},{8,10},{9,11},{10,... | collective-permute-start | bytes 1572872 | tf_op jit(solution)/shard_map/ppermute | solution.py:26
  41.1 0.9 collective-permute-start.12
  42.0 0.6 collective-permute-start.11
  42.6 2.7 %collective-permute-start.10 = (bf16[2,128,8,128]{3,2,1,0:T(8,128)(2,1)S(1)}, bf16[2,128,8,128]{3,2,1,0:T(8,128)(2,1)}, u32[]{:S(2)}, u32[]{:S(2)}) collective-permute-start(bf16[2,128,8,128]{3,2,1,0:T(8,128)(2,1)S(1)} %merge.1.refs_4_), channel_id=1, source_target_pairs={{0,8},{1,9},{2,10},{3,11},{4,12},{5,13},{6,14},{7,15},{8,0},{9,1},... | collective-permute-start | bytes 1572872 | tf_op jit(solution)/shard_map/ppermute | solution.py:26
  45.4 0.2 compare_convert_fusion.refs_8_
  45.7 9.7 %collective-permute-done.11.refs_4_ = bf16[2,128,8,128]{3,2,1,0:T(8,128)(2,1)S(1)} collective-permute-done((bf16[2,128,8,128]{3,2,1,0:T(8,128)(2,1)S(1)}, bf16[2,128,8,128]{3,2,1,0:T(8,128)(2,1)S(1)}, u32[]{:S(2)}, u32[]{:S(2)}) %collective-permute-start.11) | collective-permute-done | bytes 524320 | tf_op jit(solution)/shard_map/ppermute | solution.py:26
  55.4 2.0 %collective-permute-done.10 = bf16[2,128,8,128]{3,2,1,0:T(8,128)(2,1)} collective-permute-done((bf16[2,128,8,128]{3,2,1,0:T(8,128)(2,1)S(1)}, bf16[2,128,8,128]{3,2,1,0:T(8,128)(2,1)}, u32[]{:S(2)}, u32[]{:S(2)}) %collective-permute-start.10) | collective-permute-done | bytes 524320 | tf_op jit(solution)/shard_map/ppermute | solution.py:26
  57.4 2.1 %collective-permute-start.20 = (bf16[2,128,8,128]{3,2,1,0:T(8,128)(2,1)S(1)}, bf16[2,128,8,128]{3,2,1,0:T(8,128)(2,1)S(1)}, u32[]{:S(2)}, u32[]{:S(2)}) collective-permute-start(bf16[2,128,8,128]{3,2,1,0:T(8,128)(2,1)S(1)} %collective-permute-done.11.refs_4_), channel_id=1, source_target_pairs={{0,12},{1,13},{2,14},{3,15},{4,8},{5,9},{6,10},{7,11},{8,4},{9,5},... | collective-permute-start | bytes 1572872 | tf_op jit(solution)/shard_map/ppermute | solution.py:26
  59.5 3.8 %collective-permute-done.14.refs_7_ = bf16[2,128,8,128]{3,2,1,0:T(8,128)(2,1)S(1)} collective-permute-done((bf16[2,128,8,128]{3,2,1,0:T(8,128)(2,1)S(1)}, bf16[2,128,8,128]{3,2,1,0:T(8,128)(2,1)S(1)}, u32[]{:S(2)}, u32[]{:S(2)}) %collective-permute-start.14) | collective-permute-done | bytes 524320 | tf_op jit(solution)/shard_map/ppermute | solution.py:26
  63.3 0.0 collective-permute-done.13.refs_6_
  63.3 2.0 %collective-permute-done.12.refs_5_ = bf16[2,128,8,128]{3,2,1,0:T(8,128)(2,1)} collective-permute-done((bf16[2,128,8,128]{3,2,1,0:T(8,128)(2,1)S(1)}, bf16[2,128,8,128]{3,2,1,0:T(8,128)(2,1)}, u32[]{:S(2)}, u32[]{:S(2)}) %collective-permute-start.12) | collective-permute-done | bytes 524320 | tf_op jit(solution)/shard_map/ppermute | solution.py:26
  65.3 0.5 collective-permute-start.18
  65.8 0.6 collective-permute-start.19
  66.5 0.9 copy-done.7
  67.4 0.9 copy-done.11
  68.4 0.9 copy-done.13
  69.3 7.2 %correlate.2 = (bf16[2,520,256]{2,1,0:T(8,128)(2,1)S(1)}, bf16[2,520,256]{2,1,0:T(8,128)(2,1)S(1)}, bf16[2,520,256]{2,1,0:T(8,128)(2,1)S(1)}, bf16[2,520,256]{2,1,0:T(8,128)(2,1)S(1)}) custom-call(bf16[128,8,128]{2,1,0:T(8,128)(2,1)S(1)} %whiten.1.refs_0_, bf16[128,8,128]{2,1,0:T(8,128)(2,1)S(1)} %copy-done.7, bf16[128,8,128]{2,1,0:T(8,128)(2,1)S(1)} %copy-done.13, ...), custom_call_target="tpu_custom_call" | custom-call | flops 3254779904 | bytes 7340032 | tf_op jit(solution)/shard_map/correlate/pallas_call | solution.py:153
  76.5 1.6 %collective-permute-start.15 = (bf16[2,520,256]{2,1,0:T(8,128)(2,1)S(1)}, bf16[2,520,256]{2,1,0:T(8,128)(2,1)S(1)}, u32[]{:S(2)}, u32[]{:S(2)}) collective-permute-start(bf16[2,520,256]{2,1,0:T(8,128)(2,1)S(1)} %get-tuple-element.73), channel_id=1, source_target_pairs={{0,4},{1,5},{2,6},{3,7},{4,0},{5,1},{6,2},{7,3},{8,12},{9,13},{10,... | collective-permute-start | bytes 1597448 | tf_op jit(solution)/shard_map/ppermute | solution.py:26
  78.1 2.7 %collective-permute-start.16 = (bf16[2,520,256]{2,1,0:T(8,128)(2,1)S(1)}, bf16[2,520,256]{2,1,0:T(8,128)(2,1)S(1)}, u32[]{:S(2)}, u32[]{:S(2)}) collective-permute-start(bf16[2,520,256]{2,1,0:T(8,128)(2,1)S(1)} %get-tuple-element.74), channel_id=1, source_target_pairs={{0,8},{1,9},{2,10},{3,11},{4,12},{5,13},{6,14},{7,15},{8,0},{9,1},... | collective-permute-start | bytes 1597448 | tf_op jit(solution)/shard_map/ppermute | solution.py:26
  80.8 0.0 collective-permute-done.18.refs_5_
  80.8 0.5 collective-permute-start.17
  81.3 0.0 collective-permute-done.19.refs_6_
  81.3 6.2 %correlate.3 = (bf16[2,520,256]{2,1,0:T(8,128)(2,1)S(1)}, bf16[2,520,256]{2,1,0:T(8,128)(2,1)S(1)}, bf16[2,520,256]{2,1,0:T(8,128)(2,1)S(1)}, bf16[2,520,256]{2,1,0:T(8,128)(2,1)S(1)}) custom-call(bf16[128,8,128]{2,1,0:T(8,128)(2,1)S(1)} %whiten.1.refs_0_, bf16[128,8,128]{2,1,0:T(8,128)(2,1)S(1)} %copy-done.3, bf16[128,8,128]{2,1,0:T(8,128)(2,1)S(1)} %copy-done.9, ...), custom_call_target="tpu_custom_call" | custom-call | flops 3254779904 | bytes 7340032 | tf_op jit(solution)/shard_map/correlate/pallas_call | solution.py:153
  87.5 0.9 collective-permute-start.21
  88.4 2.2 %collective-permute-start.22 = (bf16[2,520,256]{2,1,0:T(8,128)(2,1)S(1)}, bf16[2,520,256]{2,1,0:T(8,128)(2,1)S(1)}, u32[]{:S(2)}, u32[]{:S(2)}) collective-permute-start(bf16[2,520,256]{2,1,0:T(8,128)(2,1)S(1)} %get-tuple-element.88), channel_id=1, source_target_pairs={{0,2},{1,3},{2,0},{3,1},{4,6},{5,7},{6,4},{7,5},{8,10},{9,11},{10,... | collective-permute-start | bytes 1597448 | tf_op jit(solution)/shard_map/ppermute | solution.py:26
  90.6 1.0 collective-permute-done.15.refs_1_
  91.6 1.6 %collective-permute-start.23 = (bf16[2,520,256]{2,1,0:T(8,128)(2,1)S(1)}, bf16[2,520,256]{2,1,0:T(8,128)(2,1)S(1)}, u32[]{:S(2)}, u32[]{:S(2)}) collective-permute-start(bf16[2,520,256]{2,1,0:T(8,128)(2,1)S(1)} %get-tuple-element.89), channel_id=1, source_target_pairs={{0,3},{1,2},{2,1},{3,0},{4,7},{5,6},{6,5},{7,4},{8,11},{9,10},{10,... | collective-permute-start | bytes 1597448 | tf_op jit(solution)/shard_map/ppermute | solution.py:26
  93.3 9.8 %collective-permute-done.16.refs_2_ = bf16[2,520,256]{2,1,0:T(8,128)(2,1)S(1)} collective-permute-done((bf16[2,520,256]{2,1,0:T(8,128)(2,1)S(1)}, bf16[2,520,256]{2,1,0:T(8,128)(2,1)S(1)}, u32[]{:S(2)}, u32[]{:S(2)}) %collective-permute-start.16) | collective-permute-done | bytes 532512 | tf_op jit(solution)/shard_map/ppermute | solution.py:26
  103.1 2.6 %collective-permute-done.17.refs_3_ = bf16[2,520,256]{2,1,0:T(8,128)(2,1)S(1)} collective-permute-done((bf16[2,520,256]{2,1,0:T(8,128)(2,1)S(1)}, bf16[2,520,256]{2,1,0:T(8,128)(2,1)S(1)}, u32[]{:S(2)}, u32[]{:S(2)}) %collective-permute-start.17) | collective-permute-done | bytes 532512 | tf_op jit(solution)/shard_map/ppermute | solution.py:26
  105.6 6.1 %collective-permute-done.22.refs_6_ = bf16[2,520,256]{2,1,0:T(8,128)(2,1)S(1)} collective-permute-done((bf16[2,520,256]{2,1,0:T(8,128)(2,1)S(1)}, bf16[2,520,256]{2,1,0:T(8,128)(2,1)S(1)}, u32[]{:S(2)}, u32[]{:S(2)}) %collective-permute-start.22) | collective-permute-done | bytes 532512 | tf_op jit(solution)/shard_map/ppermute | solution.py:26
  111.8 1.8 %collective-permute-done.23.refs_7_ = bf16[2,520,256]{2,1,0:T(8,128)(2,1)S(1)} collective-permute-done((bf16[2,520,256]{2,1,0:T(8,128)(2,1)S(1)}, bf16[2,520,256]{2,1,0:T(8,128)(2,1)S(1)}, u32[]{:S(2)}, u32[]{:S(2)}) %collective-permute-start.23) | collective-permute-done | bytes 532512 | tf_op jit(solution)/shard_map/ppermute | solution.py:26
  113.6 4.9 %finish.1 = bf16[4,4104,128]{2,1,0:T(8,128)(2,1)} custom-call(s32[1]{0:T(128)} %bitcast.member_ref, bf16[2,520,256]{2,1,0:T(8,128)(2,1)S(1)} %get-tuple-element.72.refs_0_, bf16[2,520,256]{2,1,0:T(8,128)(2,1)S(1)} %collective-permute-done.15.refs_1_, bf16[2,520,256]{2,1,0:T(8,128)(2,1)S(1)} %collective-permute-done.16.refs_2_, ...), custom_call_target="tpu_custom_call" | custom-call | tf_op jit(solution)/shard_map/finish/pallas_call | solution.py:191
  (30 shorter events, 0.1 us)
Async XLA Ops:
  0.0 32.2 %copy-start = (s32[2,32]{1,0:T(2,128)S(1)}, s32[2,32]{1,0:T(2,128)}, u32[]{:S(2)}) copy-start(s32[2,32]{1,0:T(2,128)} %param.3) | copy-start | bytes 772
  0.0 1.0 copy-start.1
  1.8 10.7 %collective-permute-start.1 = (bf16[128,8,128]{2,1,0:T(8,128)(2,1)S(1)}, bf16[128,8,128]{2,1,0:T(8,128)(2,1)S(1)}, u32[]{:S(2)}, u32[]{:S(2)}) collective-permute-start(bf16[128,8,128]{2,1,0:T(8,128)(2,1)S(1)} %whiten.1.refs_0_), channel_id=1, source_target_pairs={{0,1},{1,0},{2,3},{3,2},{4,5},{5,4},{6,7},{7,6},{8,9},{9,8},{10,11... | collective-permute-start | bytes 786440 | tf_op jit(solution)/shard_map/ppermute | solution.py:26
  4.1 9.1 %collective-permute-start = (bf16[128,8,128]{2,1,0:T(8,128)(2,1)S(1)}, bf16[128,8,128]{2,1,0:T(8,128)(2,1)S(1)}, u32[]{:S(2)}, u32[]{:S(2)}) collective-permute-start(bf16[128,8,128]{2,1,0:T(8,128)(2,1)S(1)} %whiten.1.refs_0_), channel_id=1, source_target_pairs={{0,4},{1,5},{2,6},{3,7},{4,0},{5,1},{6,2},{7,3},{8,12},{9,13},{10,... | collective-permute-start | bytes 786440 | tf_op jit(solution)/shard_map/ppermute | solution.py:26
  4.1 29.9 %collective-permute-start.8 = (bf16[128,8,128]{2,1,0:T(8,128)(2,1)S(1)}, bf16[128,8,128]{2,1,0:T(8,128)(2,1)S(1)}, u32[]{:S(2)}, u32[]{:S(2)}) collective-permute-start(bf16[128,8,128]{2,1,0:T(8,128)(2,1)S(1)} %whiten.1.refs_0_), channel_id=1, source_target_pairs={{0,128},{32,160},{64,192},{96,224},{128,0},{160,32},{192,64},{224,... | collective-permute-start | bytes 786440 | tf_op jit(solution)/shard_map/ppermute | solution.py:26
  11.0 23.0 %collective-permute-start.7 = (bf16[128,8,128]{2,1,0:T(8,128)(2,1)S(1)}, bf16[128,8,128]{2,1,0:T(8,128)(2,1)S(1)}, u32[]{:S(2)}, u32[]{:S(2)}) collective-permute-start(bf16[128,8,128]{2,1,0:T(8,128)(2,1)S(1)} %whiten.1.refs_0_), channel_id=1, source_target_pairs={{0,192},{32,224},{64,128},{96,160},{128,64},{160,96},{192,0},{224,... | collective-permute-start | bytes 786440 | tf_op jit(solution)/shard_map/ppermute | solution.py:26
  11.0 23.0 %collective-permute-start.6 = (bf16[128,8,128]{2,1,0:T(8,128)(2,1)S(1)}, bf16[128,8,128]{2,1,0:T(8,128)(2,1)S(1)}, u32[]{:S(2)}, u32[]{:S(2)}) collective-permute-start(bf16[128,8,128]{2,1,0:T(8,128)(2,1)S(1)} %whiten.1.refs_0_), channel_id=1, source_target_pairs={{0,64},{32,96},{64,0},{96,32},{128,192},{160,224},{192,128},{224,1... | collective-permute-start | bytes 786440 | tf_op jit(solution)/shard_map/ppermute | solution.py:26
  12.5 0.7 copy-start.2
  13.2 0.7 copy-start.6
  13.9 7.6 %collective-permute-start.3 = (bf16[128,8,128]{2,1,0:T(8,128)(2,1)S(1)}, bf16[128,8,128]{2,1,0:T(8,128)(2,1)S(1)}, u32[]{:S(2)}, u32[]{:S(2)}) collective-permute-start(bf16[128,8,128]{2,1,0:T(8,128)(2,1)S(1)} %whiten.1.refs_0_), channel_id=1, source_target_pairs={{0,3},{1,2},{2,1},{3,0},{4,7},{5,6},{6,5},{7,4},{8,11},{9,10},{10,... | collective-permute-start | bytes 786440 | tf_op jit(solution)/shard_map/ppermute | solution.py:26
  16.3 7.9 %collective-permute-start.2 = (bf16[128,8,128]{2,1,0:T(8,128)(2,1)S(1)}, bf16[128,8,128]{2,1,0:T(8,128)(2,1)S(1)}, u32[]{:S(2)}, u32[]{:S(2)}) collective-permute-start(bf16[128,8,128]{2,1,0:T(8,128)(2,1)S(1)} %whiten.1.refs_0_), channel_id=1, source_target_pairs={{0,12},{1,13},{2,14},{3,15},{4,8},{5,9},{6,10},{7,11},{8,4},{9,5},... | collective-permute-start | bytes 786440 | tf_op jit(solution)/shard_map/ppermute | solution.py:26
  21.5 0.7 copy-start.4
  24.2 0.7 copy-start.10
  24.9 7.9 %collective-permute-start.5 = (bf16[128,8,128]{2,1,0:T(8,128)(2,1)S(1)}, bf16[128,8,128]{2,1,0:T(8,128)(2,1)S(1)}, u32[]{:S(2)}, u32[]{:S(2)}) collective-permute-start(bf16[128,8,128]{2,1,0:T(8,128)(2,1)S(1)} %whiten.1.refs_0_), channel_id=1, source_target_pairs={{0,2},{1,3},{2,0},{3,1},{4,6},{5,7},{6,4},{7,5},{8,10},{9,11},{10,... | collective-permute-start | bytes 786440 | tf_op jit(solution)/shard_map/ppermute | solution.py:26
  26.1 7.9 %collective-permute-start.4 = (bf16[128,8,128]{2,1,0:T(8,128)(2,1)S(1)}, bf16[128,8,128]{2,1,0:T(8,128)(2,1)S(1)}, u32[]{:S(2)}, u32[]{:S(2)}) collective-permute-start(bf16[128,8,128]{2,1,0:T(8,128)(2,1)S(1)} %whiten.1.refs_0_), channel_id=1, source_target_pairs={{0,8},{1,9},{2,10},{3,11},{4,12},{5,13},{6,14},{7,15},{8,0},{9,1},... | collective-permute-start | bytes 786440 | tf_op jit(solution)/shard_map/ppermute | solution.py:26
  32.8 8.3 %copy-start.8 = (bf16[128,8,128]{2,1,0:T(8,128)(2,1)}, bf16[128,8,128]{2,1,0:T(8,128)(2,1)S(1)}, u32[]{:S(2)}) copy-start(bf16[128,8,128]{2,1,0:T(8,128)(2,1)S(1)} %collective-permute-done.5.refs_2_) | copy-start | bytes 786436
  34.0 3.3 %copy-start.12 = (bf16[128,8,128]{2,1,0:T(8,128)(2,1)}, bf16[128,8,128]{2,1,0:T(8,128)(2,1)S(1)}, u32[]{:S(2)}) copy-start(bf16[128,8,128]{2,1,0:T(8,128)(2,1)S(1)} %collective-permute-done.4.refs_2_) | copy-start | bytes 786436
  34.7 2.0 %collective-permute-start.9 = (bf16[2,128,8,128]{3,2,1,0:T(8,128)(2,1)S(1)}, bf16[2,128,8,128]{3,2,1,0:T(8,128)(2,1)S(1)}, u32[]{:S(2)}, u32[]{:S(2)}) collective-permute-start(bf16[2,128,8,128]{3,2,1,0:T(8,128)(2,1)S(1)} %pick.1.mine_ref), channel_id=1, source_target_pairs={{0,32},{32,0},{64,96},{96,64},{128,160},{160,128},{192,224},{224,1... | collective-permute-start | bytes 1572872 | tf_op jit(solution)/shard_map/ppermute | solution.py:26
  37.3 26.0 %collective-permute-start.14 = (bf16[2,128,8,128]{3,2,1,0:T(8,128)(2,1)S(1)}, bf16[2,128,8,128]{3,2,1,0:T(8,128)(2,1)S(1)}, u32[]{:S(2)}, u32[]{:S(2)}) collective-permute-start(bf16[2,128,8,128]{3,2,1,0:T(8,128)(2,1)S(1)} %merge.1.refs_4_), channel_id=1, source_target_pairs={{0,3},{1,2},{2,1},{3,0},{4,7},{5,6},{6,5},{7,4},{8,11},{9,10},{10,... | collective-permute-start | bytes 1572872 | tf_op jit(solution)/shard_map/ppermute | solution.py:26
  39.8 23.5 %collective-permute-start.13 = (bf16[2,128,8,128]{3,2,1,0:T(8,128)(2,1)S(1)}, bf16[2,128,8,128]{3,2,1,0:T(8,128)(2,1)S(1)}, u32[]{:S(2)}, u32[]{:S(2)}) collective-permute-start(bf16[2,128,8,128]{3,2,1,0:T(8,128)(2,1)S(1)} %merge.1.refs_4_), channel_id=1, source_target_pairs={{0,2},{1,3},{2,0},{3,1},{4,6},{5,7},{6,4},{7,5},{8,10},{9,11},{10,... | collective-permute-start | bytes 1572872 | tf_op jit(solution)/shard_map/ppermute | solution.py:26
  41.1 24.3 %collective-permute-start.12 = (bf16[2,128,8,128]{3,2,1,0:T(8,128)(2,1)S(1)}, bf16[2,128,8,128]{3,2,1,0:T(8,128)(2,1)}, u32[]{:S(2)}, u32[]{:S(2)}) collective-permute-start(bf16[2,128,8,128]{3,2,1,0:T(8,128)(2,1)S(1)} %merge.1.refs_4_), channel_id=1, source_target_pairs={{0,1},{1,0},{2,3},{3,2},{4,5},{5,4},{6,7},{7,6},{8,9},{9,8},{10,11... | collective-permute-start | bytes 1572872 | tf_op jit(solution)/shard_map/ppermute | solution.py:26
  42.0 13.4 %collective-permute-start.11 = (bf16[2,128,8,128]{3,2,1,0:T(8,128)(2,1)S(1)}, bf16[2,128,8,128]{3,2,1,0:T(8,128)(2,1)S(1)}, u32[]{:S(2)}, u32[]{:S(2)}) collective-permute-start(bf16[2,128,8,128]{3,2,1,0:T(8,128)(2,1)S(1)} %merge.1.refs_4_), channel_id=1, source_target_pairs={{0,16},{1,17},{2,18},{3,19},{4,20},{5,21},{6,22},{7,23},{8,24},{9,... | collective-permute-start | bytes 1572872 | tf_op jit(solution)/shard_map/ppermute | solution.py:26
  42.6 14.7 %collective-permute-start.10 = (bf16[2,128,8,128]{3,2,1,0:T(8,128)(2,1)S(1)}, bf16[2,128,8,128]{3,2,1,0:T(8,128)(2,1)}, u32[]{:S(2)}, u32[]{:S(2)}) collective-permute-start(bf16[2,128,8,128]{3,2,1,0:T(8,128)(2,1)S(1)} %merge.1.refs_4_), channel_id=1, source_target_pairs={{0,8},{1,9},{2,10},{3,11},{4,12},{5,13},{6,14},{7,15},{8,0},{9,1},... | collective-permute-start | bytes 1572872 | tf_op jit(solution)/shard_map/ppermute | solution.py:26
  45.4 35.9 %copy-start.9 = (bf16[128,8,128]{2,1,0:T(8,128)(2,1)S(1)}, bf16[128,8,128]{2,1,0:T(8,128)(2,1)}, u32[]{:S(2)}) copy-start(bf16[128,8,128]{2,1,0:T(8,128)(2,1)} %copy-done.8) | copy-start | bytes 786436
  45.7 35.6 %copy-start.3 = (bf16[128,8,128]{2,1,0:T(8,128)(2,1)S(1)}, bf16[128,8,128]{2,1,0:T(8,128)(2,1)}, u32[]{:S(2)}) copy-start(bf16[128,8,128]{2,1,0:T(8,128)(2,1)} %copy-done.2) | copy-start | bytes 786436
  45.7 35.6 %copy-start.5 = (bf16[128,8,128]{2,1,0:T(8,128)(2,1)S(1)}, bf16[128,8,128]{2,1,0:T(8,128)(2,1)}, u32[]{:S(2)}) copy-start(bf16[128,8,128]{2,1,0:T(8,128)(2,1)} %copy-done.4) | copy-start | bytes 786436
  57.4 23.9 %collective-permute-start.20 = (bf16[2,128,8,128]{3,2,1,0:T(8,128)(2,1)S(1)}, bf16[2,128,8,128]{3,2,1,0:T(8,128)(2,1)S(1)}, u32[]{:S(2)}, u32[]{:S(2)}) collective-permute-start(bf16[2,128,8,128]{3,2,1,0:T(8,128)(2,1)S(1)} %collective-permute-done.11.refs_4_), channel_id=1, source_target_pairs={{0,12},{1,13},{2,14},{3,15},{4,8},{5,9},{6,10},{7,11},{8,4},{9,5},... | collective-permute-start | bytes 1572872 | tf_op jit(solution)/shard_map/ppermute | solution.py:26
  65.3 15.5 %collective-permute-start.18 = (bf16[2,128,8,128]{3,2,1,0:T(8,128)(2,1)S(1)}, bf16[2,128,8,128]{3,2,1,0:T(8,128)(2,1)S(1)}, u32[]{:S(2)}, u32[]{:S(2)}) collective-permute-start(bf16[2,128,8,128]{3,2,1,0:T(8,128)(2,1)S(1)} %collective-permute-done.11.refs_4_), channel_id=1, source_target_pairs={{0,4},{1,5},{2,6},{3,7},{4,0},{5,1},{6,2},{7,3},{8,12},{9,13},{10,... | collective-permute-start | bytes 1572872 | tf_op jit(solution)/shard_map/ppermute | solution.py:26
  65.8 15.5 %collective-permute-start.19 = (bf16[2,128,8,128]{3,2,1,0:T(8,128)(2,1)}, bf16[2,128,8,128]{3,2,1,0:T(8,128)(2,1)S(1)}, u32[]{:S(2)}, u32[]{:S(2)}) collective-permute-start(bf16[2,128,8,128]{3,2,1,0:T(8,128)(2,1)} %collective-permute-done.10), channel_id=1, source_target_pairs={{0,16},{1,17},{2,18},{3,19},{4,20},{5,21},{6,22},{7,23},{8,24},{9,... | collective-permute-start | bytes 1572872 | tf_op jit(solution)/shard_map/ppermute | solution.py:26
  66.5 0.9 copy-start.7
  67.4 0.9 copy-start.11
  68.4 0.9 copy-start.13
  76.5 15.1 %collective-permute-start.15 = (bf16[2,520,256]{2,1,0:T(8,128)(2,1)S(1)}, bf16[2,520,256]{2,1,0:T(8,128)(2,1)S(1)}, u32[]{:S(2)}, u32[]{:S(2)}) collective-permute-start(bf16[2,520,256]{2,1,0:T(8,128)(2,1)S(1)} %get-tuple-element.73), channel_id=1, source_target_pairs={{0,4},{1,5},{2,6},{3,7},{4,0},{5,1},{6,2},{7,3},{8,12},{9,13},{10,... | collective-permute-start | bytes 1597448 | tf_op jit(solution)/shard_map/ppermute | solution.py:26
  78.1 25.0 %collective-permute-start.16 = (bf16[2,520,256]{2,1,0:T(8,128)(2,1)S(1)}, bf16[2,520,256]{2,1,0:T(8,128)(2,1)S(1)}, u32[]{:S(2)}, u32[]{:S(2)}) collective-permute-start(bf16[2,520,256]{2,1,0:T(8,128)(2,1)S(1)} %get-tuple-element.74), channel_id=1, source_target_pairs={{0,8},{1,9},{2,10},{3,11},{4,12},{5,13},{6,14},{7,15},{8,0},{9,1},... | collective-permute-start | bytes 1597448 | tf_op jit(solution)/shard_map/ppermute | solution.py:26
  80.8 24.8 %collective-permute-start.17 = (bf16[2,520,256]{2,1,0:T(8,128)(2,1)S(1)}, bf16[2,520,256]{2,1,0:T(8,128)(2,1)S(1)}, u32[]{:S(2)}, u32[]{:S(2)}) collective-permute-start(bf16[2,520,256]{2,1,0:T(8,128)(2,1)S(1)} %get-tuple-element.75), channel_id=1, source_target_pairs={{0,12},{1,13},{2,14},{3,15},{4,8},{5,9},{6,10},{7,11},{8,4},{9,5},... | collective-permute-start | bytes 1597448 | tf_op jit(solution)/shard_map/ppermute | solution.py:26
  87.5 18.2 %collective-permute-start.21 = (bf16[2,520,256]{2,1,0:T(8,128)(2,1)S(1)}, bf16[2,520,256]{2,1,0:T(8,128)(2,1)S(1)}, u32[]{:S(2)}, u32[]{:S(2)}) collective-permute-start(bf16[2,520,256]{2,1,0:T(8,128)(2,1)S(1)} %get-tuple-element.87), channel_id=1, source_target_pairs={{0,1},{1,0},{2,3},{3,2},{4,5},{5,4},{6,7},{7,6},{8,9},{9,8},{10,11... | collective-permute-start | bytes 1597448 | tf_op jit(solution)/shard_map/ppermute | solution.py:26
  88.4 23.4 %collective-permute-start.22 = (bf16[2,520,256]{2,1,0:T(8,128)(2,1)S(1)}, bf16[2,520,256]{2,1,0:T(8,128)(2,1)S(1)}, u32[]{:S(2)}, u32[]{:S(2)}) collective-permute-start(bf16[2,520,256]{2,1,0:T(8,128)(2,1)S(1)} %get-tuple-element.88), channel_id=1, source_target_pairs={{0,2},{1,3},{2,0},{3,1},{4,6},{5,7},{6,4},{7,5},{8,10},{9,11},{10,... | collective-permute-start | bytes 1597448 | tf_op jit(solution)/shard_map/ppermute | solution.py:26
  91.6 22.0 %collective-permute-start.23 = (bf16[2,520,256]{2,1,0:T(8,128)(2,1)S(1)}, bf16[2,520,256]{2,1,0:T(8,128)(2,1)S(1)}, u32[]{:S(2)}, u32[]{:S(2)}) collective-permute-start(bf16[2,520,256]{2,1,0:T(8,128)(2,1)S(1)} %get-tuple-element.89), channel_id=1, source_target_pairs={{0,3},{1,2},{2,1},{3,0},{4,7},{5,6},{6,5},{7,4},{8,11},{9,10},{10,... | collective-permute-start | bytes 1597448 | tf_op jit(solution)/shard_map/ppermute | solution.py:26

commit v10 on v9

--- a/solution.py
+++ b/solution.py
@@ -87,6 +87,19 @@
         compiler_params=vmem(10),
         name=name,
     )(offsets, *arrays)
+
+
+def hold(blocks):
+    def body(*refs):
+        for n in range(3):
+            refs[3 + n][...] = refs[n][...]
+
+    return pl.pallas_call(
+        body,
+        out_shape=[jax.ShapeDtypeStruct((LANE, CH, LANE), jnp.bfloat16)] * 3,
+        compiler_params=vmem(6),
+        name="hold",
+    )(*blocks)
 
 
 def corr_kernel(factor, *refs):
@@ -252,12 +265,14 @@
     mine = choose(pick_kernel, "pick", offsets, [white, plane1, plane2, plane3])
     other = xor_perm(mine, "grp", 1)
     near = choose(merge_kernel, "merge", offsets, [mine, other])
-    near, member_now = lax.optimization_barrier((near, member))
+    near, member_now, kept = lax.optimization_barrier((near, member, rows[0][1:]))
+    kept = hold(kept)
     across = xor_perm(near, "mem", 16)
     hop = xor_perm(near, "mem", 2 * col_masks[1])
     order = column_order(member_now)
     near1, near2, near3 = [xor_perm(near, "mem", e * col_masks[0]) for e in (1, 2, 3)]
-    order, hop, across = lax.optimization_barrier((order, hop, across))
+    kept, order, hop, across = lax.optimization_barrier((kept, order, hop, across))
+    rows[0][1:] = kept
     far2 = xor_perm(hop, "mem", 16)
     far3 = xor_perm(across, "mem", 3 * col_masks[1])
     across, near1, near2, near3 = lax.optimization_barrier((across, near1, near2, near3))

time: 120 us -> 119 us (level)
  local copies, waits for them, and re-layouts: 6.83 us -> 1.86 us
  waiting for transfers between devices: 47.4 us -> 50.5 us
  starting transfers between devices: 40.1 us -> 41.7 us
    unnamed x28 -> x12, local copies, waits for them, and re-layouts: 6.64 us -> 1.68 us
    ppermute x24, waiting for transfers between devices: 47.4 us -> 50.5 us  [xor_perm(): lax.ppermute(array, axis, [(i, i ^ mask) for i in range(lax.axis_size(axi...]
    ppermute x24, starting transfers between devices: 40.1 us -> 41.7 us  [xor_perm(): lax.ppermute(array, axis, [(i, i ^ mask) for i in range(lax.axis_size(axi...]
  transfers between devices with their start and end apart: 24 -> 24, of which waited for: 14 -> 17; matrix products, arithmetic and copies ran while one was open for 3% -> 3% of each run, Pallas kernels for 11% -> 12%
where the time goes in v10:
time: 119 us
  waiting for transfers between devices  50.5 us (42%)
  starting transfers between devices  41.7 us (35%)
  Pallas kernels  20.6 us (17%)
  other arithmetic  3.74 us (3%)
  local copies, waits for them, and re-layouts  1.86 us (2%)
    ppermute x24, waiting for transfers between devices, xor_perm(): lax.ppermute(array, axis, [(i, i ^ mask) for i in range(lax.axis_size(axi...  50.5 us
    ppermute x24, starting transfers between devices, xor_perm(): lax.ppermute(array, axis, [(i, i ^ mask) for i in range(lax.axis_size(axi...  41.7 us
    pallas_call x2, Pallas kernels, correlate(): pl.pallas_call(body, out_shape=[jax.ShapeDtypeStruct((2, LAG_ROWS, 256),...  13.6 us
    pallas_call x1, Pallas kernels, finish(): pl.pallas_call(finish_kernel, grid=(4,), in_specs=[pl.BlockSpec(memory_sp...  4.88 us
    convert_element_type x1, other arithmetic, lag_table(): return jnp.where(lag < LAGS, values, 0.0).astype(jnp.bfloat16)  3.36 us
  transfers between devices with their start and end apart: 24, of which 17 were waited for; matrix products, arithmetic and copies ran while one was open for 3% of the time, Pallas kernels for 12%

profile of v10, /device:TPU:8, one launch (start us, length us, event | category | flops | bytes accessed | tf_op | source)
XLA Modules:
  0.0 118.5 jit_solution(2980496105362028693)
XLA Ops:
  0.0 0.0 copy-start
  0.0 1.0 copy-done.1
  1.0 0.8 whiten.1.refs_0_
  1.8 2.3 %collective-permute-start.1 = (bf16[128,8,128]{2,1,0:T(8,128)(2,1)S(1)}, bf16[128,8,128]{2,1,0:T(8,128)(2,1)S(1)}, u32[]{:S(2)}, u32[]{:S(2)}) collective-permute-start(bf16[128,8,128]{2,1,0:T(8,128)(2,1)S(1)} %whiten.1.refs_0_), channel_id=1, source_target_pairs={{0,1},{1,0},{2,3},{3,2},{4,5},{5,4},{6,7},{7,6},{8,9},{9,8},{10,11... | collective-permute-start | bytes 786440 | tf_op jit(solution)/shard_map/ppermute | solution.py:26
  4.1 0.0 collective-permute-start
  4.1 6.9 %collective-permute-start.8 = (bf16[128,8,128]{2,1,0:T(8,128)(2,1)S(1)}, bf16[128,8,128]{2,1,0:T(8,128)(2,1)S(1)}, u32[]{:S(2)}, u32[]{:S(2)}) collective-permute-start(bf16[128,8,128]{2,1,0:T(8,128)(2,1)S(1)} %whiten.1.refs_0_), channel_id=1, source_target_pairs={{0,128},{32,160},{64,192},{96,224},{128,0},{160,32},{192,64},{224,... | collective-permute-start | bytes 786440 | tf_op jit(solution)/shard_map/ppermute | solution.py:26
  11.0 0.0 collective-permute-start.7
  11.0 1.5 %collective-permute-start.6 = (bf16[128,8,128]{2,1,0:T(8,128)(2,1)S(1)}, bf16[128,8,128]{2,1,0:T(8,128)(2,1)S(1)}, u32[]{:S(2)}, u32[]{:S(2)}) collective-permute-start(bf16[128,8,128]{2,1,0:T(8,128)(2,1)S(1)} %whiten.1.refs_0_), channel_id=1, source_target_pairs={{0,64},{32,96},{64,0},{96,32},{128,192},{160,224},{192,128},{224,1... | collective-permute-start | bytes 786440 | tf_op jit(solution)/shard_map/ppermute | solution.py:26
  12.5 0.0 collective-permute-done.1.refs_1_
  12.5 0.0 collective-permute-done.refs_0_
  12.5 2.4 %collective-permute-start.3 = (bf16[128,8,128]{2,1,0:T(8,128)(2,1)S(1)}, bf16[128,8,128]{2,1,0:T(8,128)(2,1)S(1)}, u32[]{:S(2)}, u32[]{:S(2)}) collective-permute-start(bf16[128,8,128]{2,1,0:T(8,128)(2,1)S(1)} %whiten.1.refs_0_), channel_id=1, source_target_pairs={{0,3},{1,2},{2,1},{3,0},{4,7},{5,6},{6,5},{7,4},{8,11},{9,10},{10,... | collective-permute-start | bytes 786440 | tf_op jit(solution)/shard_map/ppermute | solution.py:26
  14.9 2.1 %collective-permute-start.2 = (bf16[128,8,128]{2,1,0:T(8,128)(2,1)S(1)}, bf16[128,8,128]{2,1,0:T(8,128)(2,1)S(1)}, u32[]{:S(2)}, u32[]{:S(2)}) collective-permute-start(bf16[128,8,128]{2,1,0:T(8,128)(2,1)S(1)} %whiten.1.refs_0_), channel_id=1, source_target_pairs={{0,12},{1,13},{2,14},{3,15},{4,8},{5,9},{6,10},{7,11},{8,4},{9,5},... | collective-permute-start | bytes 786440 | tf_op jit(solution)/shard_map/ppermute | solution.py:26
  17.0 3.1 %collective-permute-done.3.refs_3_ = bf16[128,8,128]{2,1,0:T(8,128)(2,1)S(1)} collective-permute-done((bf16[128,8,128]{2,1,0:T(8,128)(2,1)S(1)}, bf16[128,8,128]{2,1,0:T(8,128)(2,1)S(1)}, u32[]{:S(2)}, u32[]{:S(2)}) %collective-permute-start.3) | collective-permute-done | bytes 262176 | tf_op jit(solution)/shard_map/ppermute | solution.py:26
  20.1 0.7 copy-done.2
  20.8 2.0 %collective-permute-done.2.refs_2_ = bf16[128,8,128]{2,1,0:T(8,128)(2,1)S(1)} collective-permute-done((bf16[128,8,128]{2,1,0:T(8,128)(2,1)S(1)}, bf16[128,8,128]{2,1,0:T(8,128)(2,1)S(1)}, u32[]{:S(2)}, u32[]{:S(2)}) %collective-permute-start.2) | collective-permute-done | bytes 262176 | tf_op jit(solution)/shard_map/ppermute | solution.py:26
  22.8 1.2 %collective-permute-start.5 = (bf16[128,8,128]{2,1,0:T(8,128)(2,1)S(1)}, bf16[128,8,128]{2,1,0:T(8,128)(2,1)S(1)}, u32[]{:S(2)}, u32[]{:S(2)}) collective-permute-start(bf16[128,8,128]{2,1,0:T(8,128)(2,1)S(1)} %whiten.1.refs_0_), channel_id=1, source_target_pairs={{0,2},{1,3},{2,0},{3,1},{4,6},{5,7},{6,4},{7,5},{8,10},{9,11},{10,... | collective-permute-start | bytes 786440 | tf_op jit(solution)/shard_map/ppermute | solution.py:26
  24.0 2.7 %collective-permute-start.4 = (bf16[128,8,128]{2,1,0:T(8,128)(2,1)S(1)}, bf16[128,8,128]{2,1,0:T(8,128)(2,1)S(1)}, u32[]{:S(2)}, u32[]{:S(2)}) collective-permute-start(bf16[128,8,128]{2,1,0:T(8,128)(2,1)S(1)} %whiten.1.refs_0_), channel_id=1, source_target_pairs={{0,8},{1,9},{2,10},{3,11},{4,12},{5,13},{6,14},{7,15},{8,0},{9,1},... | collective-permute-start | bytes 786440 | tf_op jit(solution)/shard_map/ppermute | solution.py:26
  26.7 3.4 %fusion.1.refs_8_ = bf16[520,1024]{1,0:T(8,128)(2,1)S(1)} fusion(s32[1024]{0:T(1024)S(1)} %get-tuple-element.110, s32[520]{0:T(1024)S(1)} %iota_add_fusion, s32[1024]{0:T(1024)S(1)} %get-tuple-element.109, pred[520]{0:T(1024)(128)(4,1)S(1)} %iota_compare_fusion), kind=kLoop, calls=%fused_computation.2 | loop fusion | flops 22896640 | bytes 1075752 | tf_op jit(solution)/shard_map/convert_element_type | solution.py:230
  30.0 0.0 copy-done
  30.1 0.2 dynamic-slice_reduce_fusion.offsets_ref
  30.2 0.4 collective-permute-done.5.refs_2_
  30.7 1.2 %collective-permute-done.4.refs_1_ = bf16[128,8,128]{2,1,0:T(8,128)(2,1)S(1)} collective-permute-done((bf16[128,8,128]{2,1,0:T(8,128)(2,1)S(1)}, bf16[128,8,128]{2,1,0:T(8,128)(2,1)S(1)}, u32[]{:S(2)}, u32[]{:S(2)}) %collective-permute-start.4) | collective-permute-done | bytes 262176 | tf_op jit(solution)/shard_map/ppermute | solution.py:26
  31.9 0.0 collective-permute-done.8.refs_2_
  31.9 0.6 collective-permute-done.7.refs_3_
  32.5 1.5 %collective-permute-done.6.refs_1_ = bf16[128,8,128]{2,1,0:T(8,128)(2,1)S(1)} collective-permute-done((bf16[128,8,128]{2,1,0:T(8,128)(2,1)S(1)}, bf16[128,8,128]{2,1,0:T(8,128)(2,1)S(1)}, u32[]{:S(2)}, u32[]{:S(2)}) %collective-permute-start.6) | collective-permute-done | bytes 262176 | tf_op jit(solution)/shard_map/ppermute | solution.py:26
  34.0 0.6 pick.1.mine_ref
  34.7 0.1 collective-permute-start.9
  34.8 0.1 iota_add_fusion.1
  34.9 1.8 %collective-permute-done.9.other_ref = bf16[2,128,8,128]{3,2,1,0:T(8,128)(2,1)S(1)} collective-permute-done((bf16[2,128,8,128]{3,2,1,0:T(8,128)(2,1)S(1)}, bf16[2,128,8,128]{3,2,1,0:T(8,128)(2,1)S(1)}, u32[]{:S(2)}, u32[]{:S(2)}) %collective-permute-start.9) | collective-permute-done | bytes 524320 | tf_op jit(solution)/shard_map/ppermute | solution.py:26
  36.7 0.6 merge.1.refs_4_
  37.3 2.5 %collective-permute-start.14 = (bf16[2,128,8,128]{3,2,1,0:T(8,128)(2,1)S(1)}, bf16[2,128,8,128]{3,2,1,0:T(8,128)(2,1)}, u32[]{:S(2)}, u32[]{:S(2)}) collective-permute-start(bf16[2,128,8,128]{3,2,1,0:T(8,128)(2,1)S(1)} %merge.1.refs_4_), channel_id=1, source_target_pairs={{0,3},{1,2},{2,1},{3,0},{4,7},{5,6},{6,5},{7,4},{8,11},{9,10},{10,... | collective-permute-start | bytes 1572872 | tf_op jit(solution)/shard_map/ppermute | solution.py:26
  39.8 1.2 %collective-permute-start.13 = (bf16[2,128,8,128]{3,2,1,0:T(8,128)(2,1)S(1)}, bf16[2,128,8,128]{3,2,1,0:T(8,128)(2,1)}, u32[]{:S(2)}, u32[]{:S(2)}) collective-permute-start(bf16[2,128,8,128]{3,2,1,0:T(8,128)(2,1)S(1)} %merge.1.refs_4_), channel_id=1, source_target_pairs={{0,2},{1,3},{2,0},{3,1},{4,6},{5,7},{6,4},{7,5},{8,10},{9,11},{10,... | collective-permute-start | bytes 1572872 | tf_op jit(solution)/shard_map/ppermute | solution.py:26
  41.0 0.0 copy-done.4
  41.0 0.9 collective-permute-start.12
  42.0 0.6 collective-permute-start.11
  42.6 2.7 %collective-permute-start.10 = (bf16[2,128,8,128]{3,2,1,0:T(8,128)(2,1)S(1)}, bf16[2,128,8,128]{3,2,1,0:T(8,128)(2,1)}, u32[]{:S(2)}, u32[]{:S(2)}) collective-permute-start(bf16[2,128,8,128]{3,2,1,0:T(8,128)(2,1)S(1)} %merge.1.refs_4_), channel_id=1, source_target_pairs={{0,8},{1,9},{2,10},{3,11},{4,12},{5,13},{6,14},{7,15},{8,0},{9,1},... | collective-permute-start | bytes 1572872 | tf_op jit(solution)/shard_map/ppermute | solution.py:26
  45.4 0.1 hold.1
  45.5 0.2 compare_convert_fusion.refs_8_
  45.7 9.7 %collective-permute-done.11.refs_4_ = bf16[2,128,8,128]{3,2,1,0:T(8,128)(2,1)S(1)} collective-permute-done((bf16[2,128,8,128]{3,2,1,0:T(8,128)(2,1)S(1)}, bf16[2,128,8,128]{3,2,1,0:T(8,128)(2,1)S(1)}, u32[]{:S(2)}, u32[]{:S(2)}) %collective-permute-start.11) | collective-permute-done | bytes 524320 | tf_op jit(solution)/shard_map/ppermute | solution.py:26
  55.4 2.0 %collective-permute-done.10 = bf16[2,128,8,128]{3,2,1,0:T(8,128)(2,1)} collective-permute-done((bf16[2,128,8,128]{3,2,1,0:T(8,128)(2,1)S(1)}, bf16[2,128,8,128]{3,2,1,0:T(8,128)(2,1)}, u32[]{:S(2)}, u32[]{:S(2)}) %collective-permute-start.10) | collective-permute-done | bytes 524320 | tf_op jit(solution)/shard_map/ppermute | solution.py:26
  57.4 2.1 %collective-permute-start.20 = (bf16[2,128,8,128]{3,2,1,0:T(8,128)(2,1)S(1)}, bf16[2,128,8,128]{3,2,1,0:T(8,128)(2,1)S(1)}, u32[]{:S(2)}, u32[]{:S(2)}) collective-permute-start(bf16[2,128,8,128]{3,2,1,0:T(8,128)(2,1)S(1)} %collective-permute-done.11.refs_4_), channel_id=1, source_target_pairs={{0,12},{1,13},{2,14},{3,15},{4,8},{5,9},{6,10},{7,11},{8,4},{9,5},... | collective-permute-start | bytes 1572872 | tf_op jit(solution)/shard_map/ppermute | solution.py:26
  59.5 3.9 %collective-permute-done.14.refs_7_ = bf16[2,128,8,128]{3,2,1,0:T(8,128)(2,1)} collective-permute-done((bf16[2,128,8,128]{3,2,1,0:T(8,128)(2,1)S(1)}, bf16[2,128,8,128]{3,2,1,0:T(8,128)(2,1)}, u32[]{:S(2)}, u32[]{:S(2)}) %collective-permute-start.14) | collective-permute-done | bytes 524320 | tf_op jit(solution)/shard_map/ppermute | solution.py:26
  63.4 0.0 collective-permute-done.13.refs_6_
  63.4 1.9 %collective-permute-done.12.refs_5_ = bf16[2,128,8,128]{3,2,1,0:T(8,128)(2,1)} collective-permute-done((bf16[2,128,8,128]{3,2,1,0:T(8,128)(2,1)S(1)}, bf16[2,128,8,128]{3,2,1,0:T(8,128)(2,1)}, u32[]{:S(2)}, u32[]{:S(2)}) %collective-permute-start.12) | collective-permute-done | bytes 524320 | tf_op jit(solution)/shard_map/ppermute | solution.py:26
  65.3 0.5 collective-permute-start.18
  65.8 0.6 collective-permute-start.19
  66.5 7.5 %correlate.2 = (bf16[2,520,256]{2,1,0:T(8,128)(2,1)S(1)}, bf16[2,520,256]{2,1,0:T(8,128)(2,1)S(1)}, bf16[2,520,256]{2,1,0:T(8,128)(2,1)S(1)}, bf16[2,520,256]{2,1,0:T(8,128)(2,1)S(1)}) custom-call(bf16[128,8,128]{2,1,0:T(8,128)(2,1)S(1)} %whiten.1.refs_0_, bf16[128,8,128]{2,1,0:T(8,128)(2,1)S(1)} %get-tuple-element.82.refs_1_, ...), custom_call_target="tpu_custom_call" | custom-call | flops 3254779904 | bytes 7340032 | tf_op jit(solution)/shard_map/correlate/pallas_call | solution.py:166
  74.0 1.5 %collective-permute-start.15 = (bf16[2,520,256]{2,1,0:T(8,128)(2,1)S(1)}, bf16[2,520,256]{2,1,0:T(8,128)(2,1)S(1)}, u32[]{:S(2)}, u32[]{:S(2)}) collective-permute-start(bf16[2,520,256]{2,1,0:T(8,128)(2,1)S(1)} %get-tuple-element.91), channel_id=1, source_target_pairs={{0,4},{1,5},{2,6},{3,7},{4,0},{5,1},{6,2},{7,3},{8,12},{9,13},{10,... | collective-permute-start | bytes 1597448 | tf_op jit(solution)/shard_map/ppermute | solution.py:26
  75.5 2.8 %collective-permute-start.16 = (bf16[2,520,256]{2,1,0:T(8,128)(2,1)S(1)}, bf16[2,520,256]{2,1,0:T(8,128)(2,1)S(1)}, u32[]{:S(2)}, u32[]{:S(2)}) collective-permute-start(bf16[2,520,256]{2,1,0:T(8,128)(2,1)S(1)} %get-tuple-element.92), channel_id=1, source_target_pairs={{0,8},{1,9},{2,10},{3,11},{4,12},{5,13},{6,14},{7,15},{8,0},{9,1},... | collective-permute-start | bytes 1597448 | tf_op jit(solution)/shard_map/ppermute | solution.py:26
  78.3 1.9 %collective-permute-done.18.refs_5_ = bf16[2,128,8,128]{3,2,1,0:T(8,128)(2,1)S(1)} collective-permute-done((bf16[2,128,8,128]{3,2,1,0:T(8,128)(2,1)S(1)}, bf16[2,128,8,128]{3,2,1,0:T(8,128)(2,1)S(1)}, u32[]{:S(2)}, u32[]{:S(2)}) %collective-permute-start.18) | collective-permute-done | bytes 524320 | tf_op jit(solution)/shard_map/ppermute | solution.py:26
  80.2 2.1 %collective-permute-start.17 = (bf16[2,520,256]{2,1,0:T(8,128)(2,1)S(1)}, bf16[2,520,256]{2,1,0:T(8,128)(2,1)S(1)}, u32[]{:S(2)}, u32[]{:S(2)}) collective-permute-start(bf16[2,520,256]{2,1,0:T(8,128)(2,1)S(1)} %get-tuple-element.93), channel_id=1, source_target_pairs={{0,12},{1,13},{2,14},{3,15},{4,8},{5,9},{6,10},{7,11},{8,4},{9,5},... | collective-permute-start | bytes 1597448 | tf_op jit(solution)/shard_map/ppermute | solution.py:26
  82.3 0.0 collective-permute-done.19.refs_6_
  82.3 0.0 collective-permute-done.20.refs_7_
  82.3 6.1 %correlate.3 = (bf16[2,520,256]{2,1,0:T(8,128)(2,1)S(1)}, bf16[2,520,256]{2,1,0:T(8,128)(2,1)S(1)}, bf16[2,520,256]{2,1,0:T(8,128)(2,1)S(1)}, bf16[2,520,256]{2,1,0:T(8,128)(2,1)S(1)}) custom-call(bf16[128,8,128]{2,1,0:T(8,128)(2,1)S(1)} %whiten.1.refs_0_, bf16[128,8,128]{2,1,0:T(8,128)(2,1)S(1)} %collective-permute-done.1.refs_1_, ...), custom_call_target="tpu_custom_call" | custom-call | flops 3254779904 | bytes 7340032 | tf_op jit(solution)/shard_map/correlate/pallas_call | solution.py:166
  88.4 0.9 collective-permute-start.21
  89.3 2.3 %collective-permute-start.22 = (bf16[2,520,256]{2,1,0:T(8,128)(2,1)S(1)}, bf16[2,520,256]{2,1,0:T(8,128)(2,1)S(1)}, u32[]{:S(2)}, u32[]{:S(2)}) collective-permute-start(bf16[2,520,256]{2,1,0:T(8,128)(2,1)S(1)} %get-tuple-element.106), channel_id=1, source_target_pairs={{0,2},{1,3},{2,0},{3,1},{4,6},{5,7},{6,4},{7,5},{8,10},{9,11},{10,... | collective-permute-start | bytes 1597448 | tf_op jit(solution)/shard_map/ppermute | solution.py:26
  91.6 0.0 collective-permute-done.15.refs_1_
  91.6 1.6 %collective-permute-start.23 = (bf16[2,520,256]{2,1,0:T(8,128)(2,1)S(1)}, bf16[2,520,256]{2,1,0:T(8,128)(2,1)S(1)}, u32[]{:S(2)}, u32[]{:S(2)}) collective-permute-start(bf16[2,520,256]{2,1,0:T(8,128)(2,1)S(1)} %get-tuple-element.107), channel_id=1, source_target_pairs={{0,3},{1,2},{2,1},{3,0},{4,7},{5,6},{6,5},{7,4},{8,11},{9,10},{10,... | collective-permute-start | bytes 1597448 | tf_op jit(solution)/shard_map/ppermute | solution.py:26
  93.2 9.7 %collective-permute-done.16.refs_2_ = bf16[2,520,256]{2,1,0:T(8,128)(2,1)S(1)} collective-permute-done((bf16[2,520,256]{2,1,0:T(8,128)(2,1)S(1)}, bf16[2,520,256]{2,1,0:T(8,128)(2,1)S(1)}, u32[]{:S(2)}, u32[]{:S(2)}) %collective-permute-start.16) | collective-permute-done | bytes 532512 | tf_op jit(solution)/shard_map/ppermute | solution.py:26
  102.9 0.6 collective-permute-done.17.refs_3_
  103.5 0.1 collective-permute-done.21.refs_5_
  103.5 7.4 %collective-permute-done.22.refs_6_ = bf16[2,520,256]{2,1,0:T(8,128)(2,1)S(1)} collective-permute-done((bf16[2,520,256]{2,1,0:T(8,128)(2,1)S(1)}, bf16[2,520,256]{2,1,0:T(8,128)(2,1)S(1)}, u32[]{:S(2)}, u32[]{:S(2)}) %collective-permute-start.22) | collective-permute-done | bytes 532512 | tf_op jit(solution)/shard_map/ppermute | solution.py:26
  110.9 2.7 %collective-permute-done.23.refs_7_ = bf16[2,520,256]{2,1,0:T(8,128)(2,1)S(1)} collective-permute-done((bf16[2,520,256]{2,1,0:T(8,128)(2,1)S(1)}, bf16[2,520,256]{2,1,0:T(8,128)(2,1)S(1)}, u32[]{:S(2)}, u32[]{:S(2)}) %collective-permute-start.23) | collective-permute-done | bytes 532512 | tf_op jit(solution)/shard_map/ppermute | solution.py:26
  113.7 4.9 %finish.1 = bf16[4,4104,128]{2,1,0:T(8,128)(2,1)} custom-call(s32[1]{0:T(128)} %bitcast.member_ref, bf16[2,520,256]{2,1,0:T(8,128)(2,1)S(1)} %get-tuple-element.90.refs_0_, bf16[2,520,256]{2,1,0:T(8,128)(2,1)S(1)} %collective-permute-done.15.refs_1_, bf16[2,520,256]{2,1,0:T(8,128)(2,1)S(1)} %collective-permute-done.16.refs_2_, ...), custom_call_target="tpu_custom_call" | custom-call | tf_op jit(solution)/shard_map/finish/pallas_call | solution.py:204
  (15 shorter events, 0.1 us)
Async XLA Ops:
  0.0 30.0 %copy-start = (s32[2,32]{1,0:T(2,128)S(1)}, s32[2,32]{1,0:T(2,128)}, u32[]{:S(2)}) copy-start(s32[2,32]{1,0:T(2,128)} %param.3) | copy-start | bytes 772
  0.0 1.0 copy-start.1
  1.8 10.7 %collective-permute-start.1 = (bf16[128,8,128]{2,1,0:T(8,128)(2,1)S(1)}, bf16[128,8,128]{2,1,0:T(8,128)(2,1)S(1)}, u32[]{:S(2)}, u32[]{:S(2)}) collective-permute-start(bf16[128,8,128]{2,1,0:T(8,128)(2,1)S(1)} %whiten.1.refs_0_), channel_id=1, source_target_pairs={{0,1},{1,0},{2,3},{3,2},{4,5},{5,4},{6,7},{7,6},{8,9},{9,8},{10,11... | collective-permute-start | bytes 786440 | tf_op jit(solution)/shard_map/ppermute | solution.py:26
  4.1 8.4 %collective-permute-start = (bf16[128,8,128]{2,1,0:T(8,128)(2,1)S(1)}, bf16[128,8,128]{2,1,0:T(8,128)(2,1)S(1)}, u32[]{:S(2)}, u32[]{:S(2)}) collective-permute-start(bf16[128,8,128]{2,1,0:T(8,128)(2,1)S(1)} %whiten.1.refs_0_), channel_id=1, source_target_pairs={{0,4},{1,5},{2,6},{3,7},{4,0},{5,1},{6,2},{7,3},{8,12},{9,13},{10,... | collective-permute-start | bytes 786440 | tf_op jit(solution)/shard_map/ppermute | solution.py:26
  4.1 27.8 %collective-permute-start.8 = (bf16[128,8,128]{2,1,0:T(8,128)(2,1)S(1)}, bf16[128,8,128]{2,1,0:T(8,128)(2,1)S(1)}, u32[]{:S(2)}, u32[]{:S(2)}) collective-permute-start(bf16[128,8,128]{2,1,0:T(8,128)(2,1)S(1)} %whiten.1.refs_0_), channel_id=1, source_target_pairs={{0,128},{32,160},{64,192},{96,224},{128,0},{160,32},{192,64},{224,... | collective-permute-start | bytes 786440 | tf_op jit(solution)/shard_map/ppermute | solution.py:26
  11.0 21.5 %collective-permute-start.7 = (bf16[128,8,128]{2,1,0:T(8,128)(2,1)S(1)}, bf16[128,8,128]{2,1,0:T(8,128)(2,1)S(1)}, u32[]{:S(2)}, u32[]{:S(2)}) collective-permute-start(bf16[128,8,128]{2,1,0:T(8,128)(2,1)S(1)} %whiten.1.refs_0_), channel_id=1, source_target_pairs={{0,192},{32,224},{64,128},{96,160},{128,64},{160,96},{192,0},{224,... | collective-permute-start | bytes 786440 | tf_op jit(solution)/shard_map/ppermute | solution.py:26
  11.0 23.0 %collective-permute-start.6 = (bf16[128,8,128]{2,1,0:T(8,128)(2,1)S(1)}, bf16[128,8,128]{2,1,0:T(8,128)(2,1)S(1)}, u32[]{:S(2)}, u32[]{:S(2)}) collective-permute-start(bf16[128,8,128]{2,1,0:T(8,128)(2,1)S(1)} %whiten.1.refs_0_), channel_id=1, source_target_pairs={{0,64},{32,96},{64,0},{96,32},{128,192},{160,224},{192,128},{224,1... | collective-permute-start | bytes 786440 | tf_op jit(solution)/shard_map/ppermute | solution.py:26
  12.5 7.6 %collective-permute-start.3 = (bf16[128,8,128]{2,1,0:T(8,128)(2,1)S(1)}, bf16[128,8,128]{2,1,0:T(8,128)(2,1)S(1)}, u32[]{:S(2)}, u32[]{:S(2)}) collective-permute-start(bf16[128,8,128]{2,1,0:T(8,128)(2,1)S(1)} %whiten.1.refs_0_), channel_id=1, source_target_pairs={{0,3},{1,2},{2,1},{3,0},{4,7},{5,6},{6,5},{7,4},{8,11},{9,10},{10,... | collective-permute-start | bytes 786440 | tf_op jit(solution)/shard_map/ppermute | solution.py:26
  14.9 7.9 %collective-permute-start.2 = (bf16[128,8,128]{2,1,0:T(8,128)(2,1)S(1)}, bf16[128,8,128]{2,1,0:T(8,128)(2,1)S(1)}, u32[]{:S(2)}, u32[]{:S(2)}) collective-permute-start(bf16[128,8,128]{2,1,0:T(8,128)(2,1)S(1)} %whiten.1.refs_0_), channel_id=1, source_target_pairs={{0,12},{1,13},{2,14},{3,15},{4,8},{5,9},{6,10},{7,11},{8,4},{9,5},... | collective-permute-start | bytes 786440 | tf_op jit(solution)/shard_map/ppermute | solution.py:26
  20.1 0.7 copy-start.2
  22.8 7.9 %collective-permute-start.5 = (bf16[128,8,128]{2,1,0:T(8,128)(2,1)S(1)}, bf16[128,8,128]{2,1,0:T(8,128)(2,1)S(1)}, u32[]{:S(2)}, u32[]{:S(2)}) collective-permute-start(bf16[128,8,128]{2,1,0:T(8,128)(2,1)S(1)} %whiten.1.refs_0_), channel_id=1, source_target_pairs={{0,2},{1,3},{2,0},{3,1},{4,6},{5,7},{6,4},{7,5},{8,10},{9,11},{10,... | collective-permute-start | bytes 786440 | tf_op jit(solution)/shard_map/ppermute | solution.py:26
  24.0 7.9 %collective-permute-start.4 = (bf16[128,8,128]{2,1,0:T(8,128)(2,1)S(1)}, bf16[128,8,128]{2,1,0:T(8,128)(2,1)S(1)}, u32[]{:S(2)}, u32[]{:S(2)}) collective-permute-start(bf16[128,8,128]{2,1,0:T(8,128)(2,1)S(1)} %whiten.1.refs_0_), channel_id=1, source_target_pairs={{0,8},{1,9},{2,10},{3,11},{4,12},{5,13},{6,14},{7,15},{8,0},{9,1},... | collective-permute-start | bytes 786440 | tf_op jit(solution)/shard_map/ppermute | solution.py:26
  30.7 10.4 %copy-start.4 = (bf16[128,8,128]{2,1,0:T(8,128)(2,1)}, bf16[128,8,128]{2,1,0:T(8,128)(2,1)S(1)}, u32[]{:S(2)}) copy-start(bf16[128,8,128]{2,1,0:T(8,128)(2,1)S(1)} %collective-permute-done.5.refs_2_) | copy-start | bytes 786436
  34.7 2.0 %collective-permute-start.9 = (bf16[2,128,8,128]{3,2,1,0:T(8,128)(2,1)S(1)}, bf16[2,128,8,128]{3,2,1,0:T(8,128)(2,1)S(1)}, u32[]{:S(2)}, u32[]{:S(2)}) collective-permute-start(bf16[2,128,8,128]{3,2,1,0:T(8,128)(2,1)S(1)} %pick.1.mine_ref), channel_id=1, source_target_pairs={{0,32},{32,0},{64,96},{96,64},{128,160},{160,128},{192,224},{224,1... | collective-permute-start | bytes 1572872 | tf_op jit(solution)/shard_map/ppermute | solution.py:26
  37.3 26.1 %collective-permute-start.14 = (bf16[2,128,8,128]{3,2,1,0:T(8,128)(2,1)S(1)}, bf16[2,128,8,128]{3,2,1,0:T(8,128)(2,1)}, u32[]{:S(2)}, u32[]{:S(2)}) collective-permute-start(bf16[2,128,8,128]{3,2,1,0:T(8,128)(2,1)S(1)} %merge.1.refs_4_), channel_id=1, source_target_pairs={{0,3},{1,2},{2,1},{3,0},{4,7},{5,6},{6,5},{7,4},{8,11},{9,10},{10,... | collective-permute-start | bytes 1572872 | tf_op jit(solution)/shard_map/ppermute | solution.py:26
  39.8 23.6 %collective-permute-start.13 = (bf16[2,128,8,128]{3,2,1,0:T(8,128)(2,1)S(1)}, bf16[2,128,8,128]{3,2,1,0:T(8,128)(2,1)}, u32[]{:S(2)}, u32[]{:S(2)}) collective-permute-start(bf16[2,128,8,128]{3,2,1,0:T(8,128)(2,1)S(1)} %merge.1.refs_4_), channel_id=1, source_target_pairs={{0,2},{1,3},{2,0},{3,1},{4,6},{5,7},{6,4},{7,5},{8,10},{9,11},{10,... | collective-permute-start | bytes 1572872 | tf_op jit(solution)/shard_map/ppermute | solution.py:26
  41.0 24.3 %collective-permute-start.12 = (bf16[2,128,8,128]{3,2,1,0:T(8,128)(2,1)S(1)}, bf16[2,128,8,128]{3,2,1,0:T(8,128)(2,1)}, u32[]{:S(2)}, u32[]{:S(2)}) collective-permute-start(bf16[2,128,8,128]{3,2,1,0:T(8,128)(2,1)S(1)} %merge.1.refs_4_), channel_id=1, source_target_pairs={{0,1},{1,0},{2,3},{3,2},{4,5},{5,4},{6,7},{7,6},{8,9},{9,8},{10,11... | collective-permute-start | bytes 1572872 | tf_op jit(solution)/shard_map/ppermute | solution.py:26
  42.0 13.4 %collective-permute-start.11 = (bf16[2,128,8,128]{3,2,1,0:T(8,128)(2,1)S(1)}, bf16[2,128,8,128]{3,2,1,0:T(8,128)(2,1)S(1)}, u32[]{:S(2)}, u32[]{:S(2)}) collective-permute-start(bf16[2,128,8,128]{3,2,1,0:T(8,128)(2,1)S(1)} %merge.1.refs_4_), channel_id=1, source_target_pairs={{0,16},{1,17},{2,18},{3,19},{4,20},{5,21},{6,22},{7,23},{8,24},{9,... | collective-permute-start | bytes 1572872 | tf_op jit(solution)/shard_map/ppermute | solution.py:26
  42.6 14.7 %collective-permute-start.10 = (bf16[2,128,8,128]{3,2,1,0:T(8,128)(2,1)S(1)}, bf16[2,128,8,128]{3,2,1,0:T(8,128)(2,1)}, u32[]{:S(2)}, u32[]{:S(2)}) collective-permute-start(bf16[2,128,8,128]{3,2,1,0:T(8,128)(2,1)S(1)} %merge.1.refs_4_), channel_id=1, source_target_pairs={{0,8},{1,9},{2,10},{3,11},{4,12},{5,13},{6,14},{7,15},{8,0},{9,1},... | collective-permute-start | bytes 1572872 | tf_op jit(solution)/shard_map/ppermute | solution.py:26
  57.4 24.9 %copy-start.3 = (bf16[128,8,128]{2,1,0:T(8,128)(2,1)S(1)}, bf16[128,8,128]{2,1,0:T(8,128)(2,1)}, u32[]{:S(2)}) copy-start(bf16[128,8,128]{2,1,0:T(8,128)(2,1)} %copy-done.2) | copy-start | bytes 786436
  57.4 24.9 %copy-start.5 = (bf16[128,8,128]{2,1,0:T(8,128)(2,1)S(1)}, bf16[128,8,128]{2,1,0:T(8,128)(2,1)}, u32[]{:S(2)}) copy-start(bf16[128,8,128]{2,1,0:T(8,128)(2,1)} %copy-done.4) | copy-start | bytes 786436
  57.4 24.9 %collective-permute-start.20 = (bf16[2,128,8,128]{3,2,1,0:T(8,128)(2,1)S(1)}, bf16[2,128,8,128]{3,2,1,0:T(8,128)(2,1)S(1)}, u32[]{:S(2)}, u32[]{:S(2)}) collective-permute-start(bf16[2,128,8,128]{3,2,1,0:T(8,128)(2,1)S(1)} %collective-permute-done.11.refs_4_), channel_id=1, source_target_pairs={{0,12},{1,13},{2,14},{3,15},{4,8},{5,9},{6,10},{7,11},{8,4},{9,5},... | collective-permute-start | bytes 1572872 | tf_op jit(solution)/shard_map/ppermute | solution.py:26
  65.3 14.9 %collective-permute-start.18 = (bf16[2,128,8,128]{3,2,1,0:T(8,128)(2,1)S(1)}, bf16[2,128,8,128]{3,2,1,0:T(8,128)(2,1)S(1)}, u32[]{:S(2)}, u32[]{:S(2)}) collective-permute-start(bf16[2,128,8,128]{3,2,1,0:T(8,128)(2,1)S(1)} %collective-permute-done.11.refs_4_), channel_id=1, source_target_pairs={{0,4},{1,5},{2,6},{3,7},{4,0},{5,1},{6,2},{7,3},{8,12},{9,13},{10,... | collective-permute-start | bytes 1572872 | tf_op jit(solution)/shard_map/ppermute | solution.py:26
  65.8 16.4 %collective-permute-start.19 = (bf16[2,128,8,128]{3,2,1,0:T(8,128)(2,1)}, bf16[2,128,8,128]{3,2,1,0:T(8,128)(2,1)S(1)}, u32[]{:S(2)}, u32[]{:S(2)}) collective-permute-start(bf16[2,128,8,128]{3,2,1,0:T(8,128)(2,1)} %collective-permute-done.10), channel_id=1, source_target_pairs={{0,16},{1,17},{2,18},{3,19},{4,20},{5,21},{6,22},{7,23},{8,24},{9,... | collective-permute-start | bytes 1572872 | tf_op jit(solution)/shard_map/ppermute | solution.py:26
  74.0 17.6 %collective-permute-start.15 = (bf16[2,520,256]{2,1,0:T(8,128)(2,1)S(1)}, bf16[2,520,256]{2,1,0:T(8,128)(2,1)S(1)}, u32[]{:S(2)}, u32[]{:S(2)}) collective-permute-start(bf16[2,520,256]{2,1,0:T(8,128)(2,1)S(1)} %get-tuple-element.91), channel_id=1, source_target_pairs={{0,4},{1,5},{2,6},{3,7},{4,0},{5,1},{6,2},{7,3},{8,12},{9,13},{10,... | collective-permute-start | bytes 1597448 | tf_op jit(solution)/shard_map/ppermute | solution.py:26
  75.5 27.4 %collective-permute-start.16 = (bf16[2,520,256]{2,1,0:T(8,128)(2,1)S(1)}, bf16[2,520,256]{2,1,0:T(8,128)(2,1)S(1)}, u32[]{:S(2)}, u32[]{:S(2)}) collective-permute-start(bf16[2,520,256]{2,1,0:T(8,128)(2,1)S(1)} %get-tuple-element.92), channel_id=1, source_target_pairs={{0,8},{1,9},{2,10},{3,11},{4,12},{5,13},{6,14},{7,15},{8,0},{9,1},... | collective-permute-start | bytes 1597448 | tf_op jit(solution)/shard_map/ppermute | solution.py:26
  80.2 23.3 %collective-permute-start.17 = (bf16[2,520,256]{2,1,0:T(8,128)(2,1)S(1)}, bf16[2,520,256]{2,1,0:T(8,128)(2,1)S(1)}, u32[]{:S(2)}, u32[]{:S(2)}) collective-permute-start(bf16[2,520,256]{2,1,0:T(8,128)(2,1)S(1)} %get-tuple-element.93), channel_id=1, source_target_pairs={{0,12},{1,13},{2,14},{3,15},{4,8},{5,9},{6,10},{7,11},{8,4},{9,5},... | collective-permute-start | bytes 1597448 | tf_op jit(solution)/shard_map/ppermute | solution.py:26
  88.4 15.1 %collective-permute-start.21 = (bf16[2,520,256]{2,1,0:T(8,128)(2,1)S(1)}, bf16[2,520,256]{2,1,0:T(8,128)(2,1)S(1)}, u32[]{:S(2)}, u32[]{:S(2)}) collective-permute-start(bf16[2,520,256]{2,1,0:T(8,128)(2,1)S(1)} %get-tuple-element.105), channel_id=1, source_target_pairs={{0,1},{1,0},{2,3},{3,2},{4,5},{5,4},{6,7},{7,6},{8,9},{9,8},{10,11... | collective-permute-start | bytes 1597448 | tf_op jit(solution)/shard_map/ppermute | solution.py:26
  89.3 21.6 %collective-permute-start.22 = (bf16[2,520,256]{2,1,0:T(8,128)(2,1)S(1)}, bf16[2,520,256]{2,1,0:T(8,128)(2,1)S(1)}, u32[]{:S(2)}, u32[]{:S(2)}) collective-permute-start(bf16[2,520,256]{2,1,0:T(8,128)(2,1)S(1)} %get-tuple-element.106), channel_id=1, source_target_pairs={{0,2},{1,3},{2,0},{3,1},{4,6},{5,7},{6,4},{7,5},{8,10},{9,11},{10,... | collective-permute-start | bytes 1597448 | tf_op jit(solution)/shard_map/ppermute | solution.py:26
  91.6 22.1 %collective-permute-start.23 = (bf16[2,520,256]{2,1,0:T(8,128)(2,1)S(1)}, bf16[2,520,256]{2,1,0:T(8,128)(2,1)S(1)}, u32[]{:S(2)}, u32[]{:S(2)}) collective-permute-start(bf16[2,520,256]{2,1,0:T(8,128)(2,1)S(1)} %get-tuple-element.107), channel_id=1, source_target_pairs={{0,3},{1,2},{2,1},{3,0},{4,7},{5,6},{6,5},{7,4},{8,11},{9,10},{10,... | collective-permute-start | bytes 1597448 | tf_op jit(solution)/shard_map/ppermute | solution.py:26
